TPU v7x, 32 devices: a whole 2x2x4 slice. The times are simulated.
32 devices in a mesh: groups: 2 (over y), expert: 4 (over z), dp: 4 (over x, core).
Axes of the slice: x: 2, y: 2, z: 4, core: 2. Of those that a mesh axis runs over, the one named last changes fastest.
Arguments:
- tokens: bfloat16 [4096, 2048], P(('groups', 'expert', 'dp')), parts along dimension 0, may hold values from -6 to 6
- cotangent: bfloat16 [4096, 2048], P(('groups', 'expert', 'dp')), parts along dimension 0, may hold values from -1.5 to 1.5
- expert_ids: int32 [4096, 8], P(('groups', 'expert', 'dp')), parts along dimension 0, may hold values from 0 to 127, all different within a row; in each aligned block of 128 rows (0 to 127, 128 to 255, ...) at most 16 rows name the same one
- gate_probs: float32 [4096, 8], P(('groups', 'expert', 'dp')), parts along dimension 0, may hold values from 0.05 to 0.6
- w_gate: bfloat16 [4, 2048, 384], P('expert', 'dp'), may hold values from -0.125 to 0.125
- w_up: bfloat16 [4, 2048, 384], P('expert', 'dp'), may hold values from -0.125 to 0.125
- w_down: bfloat16 [4, 384, 2048], P('expert', None, 'dp'), may hold values from -0.3125 to 0.3125
Outputs:
- mixed: bfloat16 [4096, 2048], P(('groups', 'expert', 'dp')), parts along dimension 0
- grad_tokens: bfloat16 [4096, 2048], P(('groups', 'expert', 'dp')), parts along dimension 0
- grad_gates: float32 [4096, 8], P(('groups', 'expert', 'dp')), parts along dimension 0
- grad_w_gate: bfloat16 [8, 2048, 384], P(('groups', 'expert'), 'dp'), parts along dimension 0
- grad_w_up: bfloat16 [8, 2048, 384], P(('groups', 'expert'), 'dp'), parts along dimension 0
- grad_w_down: bfloat16 [8, 384, 2048], P(('groups', 'expert'), None, 'dp'), parts along dimension 0
There are 2 independent parts, one for each index of `groups`. A program takes and returns all parts, laid end to end along the dimension named above; an argument that names none is the same for every part. Nothing has to cross between parts.
Inputs may be any that keep to these rules, and one draw needn't show every extreme that they name: `expert_ids`: each token names 8 different experts. In the rows of one device (aligned blocks of 128 tokens) no expert is named more than 16 times, and in every draw some expert is named exactly 16 times in some block.
All inputs are finite; a program needn't handle non-finite values.
Results may differ from a plain program's by a relative error of at most 0.0058.
Values may be sent and summed in bfloat16 or wider, within the bound.
No kernel may reach another device: no remote copies, remote signals or barrier semaphores. Data moves between devices by JAX's collectives and lax.ppermute only.
A program may use at most 128 MiB of HBM per device.

v0:
```python
import jax
import jax.numpy as jnp
from jax import lax
from jax.sharding import PartitionSpec as P

EXPERTS = 128


def dot_last(left, right):
    return lax.dot_general(
        left, right, (((1,), (1,)), ((), ())), preferred_element_type=jnp.float32
    )


def expert_rows(rows_x, rows_dy, gate_full, up_full, down_full):
    gate_part = jnp.dot(rows_x, gate_full, preferred_element_type=jnp.float32)
    up_part = jnp.dot(rows_x, up_full, preferred_element_type=jnp.float32)
    sigmoid_gate = jax.nn.sigmoid(gate_part)
    activated = gate_part * sigmoid_gate
    hidden = (activated * up_part).astype(jnp.bfloat16)
    expert_out = jnp.dot(hidden, down_full, preferred_element_type=jnp.float32).astype(jnp.bfloat16)
    back_hidden = dot_last(rows_dy, down_full)
    d_gate = (
        back_hidden * up_part * sigmoid_gate * (1.0 + gate_part * (1.0 - sigmoid_gate))
    ).astype(jnp.bfloat16)
    d_up = (back_hidden * activated).astype(jnp.bfloat16)
    d_rows = (dot_last(d_gate, gate_full) + dot_last(d_up, up_full)).astype(jnp.bfloat16)
    return (hidden, expert_out, d_gate, d_up, d_rows)


def on_device(tokens, cotangent, expert_ids, gate_probs, w_gate, w_up, w_down):
    expert_count = lax.axis_size("expert")
    dp_count = lax.axis_size("dp")
    token_rows, model_width = tokens.shape
    top_count = expert_ids.shape[1]
    slice_width = w_gate.shape[1]
    hidden_width = w_gate.shape[2]
    capacity = 2 * token_rows * top_count // EXPERTS
    slot_total = expert_count * capacity
    flat_ids = expert_ids.reshape(-1)
    onehot = (flat_ids[:, None] == jnp.arange(EXPERTS, dtype=jnp.int32)[None, :]).astype(jnp.int32)
    running = jnp.cumsum(onehot, axis=0)
    slot_index = jnp.sum(running * onehot, axis=1) - 1
    in_wave = flat_ids < expert_count
    position = jnp.where(in_wave, flat_ids * capacity + slot_index, slot_total)
    matched = position[:, None] == jnp.arange(slot_total, dtype=jnp.int32)[None, :]
    owner_row = jnp.arange(token_rows * top_count, dtype=jnp.int32) // top_count
    source = jnp.sum(jnp.where(matched, owner_row[:, None], 0), axis=0)
    filled = jnp.any(matched, axis=0)
    zero_value = jnp.zeros((), jnp.bfloat16)
    send_x = jnp.where(filled[:, None], jnp.take(tokens, source, axis=0), zero_value).reshape(
        expert_count, capacity, model_width
    )
    send_dy = jnp.where(filled[:, None], jnp.take(cotangent, source, axis=0), zero_value).reshape(
        expert_count, capacity, model_width
    )
    gate_full, up_full, down_full = (
        lax.all_gather(w_gate, "dp", axis=1, tiled=True),
        lax.all_gather(w_up, "dp", axis=1, tiled=True),
        lax.all_gather(w_down, "dp", axis=2, tiled=True),
    )
    gate_full = gate_full[0]
    up_full = up_full[0]
    down_full = down_full[0]
    got_x, got_dy = (
        lax.all_to_all(send_x, "expert", split_axis=0, concat_axis=0, tiled=True),
        lax.all_to_all(send_dy, "expert", split_axis=0, concat_axis=0, tiled=True),
    )
    rows_x = got_x.reshape(slot_total, model_width)
    rows_dy = got_dy.reshape(slot_total, model_width)
    hidden, expert_out, d_gate, d_up, d_rows = expert_rows(
        rows_x, rows_dy, gate_full, up_full, down_full
    )
    back_out, back_rows = (
        lax.all_to_all(
            expert_out.reshape(expert_count, capacity, model_width),
            "expert",
            split_axis=0,
            concat_axis=0,
            tiled=True,
        ),
        lax.all_to_all(
            d_rows.reshape(expert_count, capacity, model_width),
            "expert",
            split_axis=0,
            concat_axis=0,
            tiled=True,
        ),
    )
    back_out = back_out.reshape(slot_total, model_width)
    back_rows = back_rows.reshape(slot_total, model_width)
    matched_three = matched.reshape(token_rows, top_count, slot_total)
    weight_table = jnp.sum(jnp.where(matched_three, gate_probs[:, :, None], 0.0), axis=1)
    mixed = jnp.dot(
        weight_table, back_out.astype(jnp.float32), precision=lax.Precision.HIGHEST
    ).astype(jnp.bfloat16)
    grad_tokens = jnp.dot(
        weight_table, back_rows.astype(jnp.float32), precision=lax.Precision.HIGHEST
    ).astype(jnp.bfloat16)
    inner_table = dot_last(cotangent, back_out)
    grad_gates = jnp.sum(jnp.where(matched_three, inner_table[:, None, :], 0.0), axis=2)
    local_gate = jnp.einsum("sd,sf->df", rows_x, d_gate, preferred_element_type=jnp.float32).astype(
        jnp.bfloat16
    )
    local_up = jnp.einsum("sd,sf->df", rows_x, d_up, preferred_element_type=jnp.float32).astype(
        jnp.bfloat16
    )
    local_down = jnp.einsum(
        "sd,sf->df", rows_dy, hidden, preferred_element_type=jnp.float32
    ).astype(jnp.bfloat16)
    got_gate, got_up, got_down = (
        lax.all_to_all(
            local_gate.reshape(dp_count, slice_width, hidden_width),
            "dp",
            split_axis=0,
            concat_axis=0,
            tiled=True,
        ),
        lax.all_to_all(
            local_up.reshape(dp_count, slice_width, hidden_width),
            "dp",
            split_axis=0,
            concat_axis=0,
            tiled=True,
        ),
        lax.all_to_all(
            local_down.reshape(dp_count, slice_width, hidden_width),
            "dp",
            split_axis=0,
            concat_axis=0,
            tiled=True,
        ),
    )
    grad_w_gate = jnp.sum(got_gate.astype(jnp.float32), axis=0).astype(jnp.bfloat16)[None]
    grad_w_up = jnp.sum(got_up.astype(jnp.float32), axis=0).astype(jnp.bfloat16)[None]
    grad_w_down = jnp.sum(got_down.astype(jnp.float32), axis=0).T.astype(jnp.bfloat16)[None]
    return (mixed, grad_tokens, grad_gates, grad_w_gate, grad_w_up, grad_w_down)


def solution(mesh):
    in_specs = (
        P(("groups", "expert", "dp"), None),
        P(("groups", "expert", "dp"), None),
        P(("groups", "expert", "dp"), None),
        P(("groups", "expert", "dp"), None),
        P("expert", "dp", None),
        P("expert", "dp", None),
        P("expert", None, "dp"),
    )
    out_specs = (
        P(("groups", "expert", "dp"), None),
        P(("groups", "expert", "dp"), None),
        P(("groups", "expert", "dp"), None),
        P(("groups", "expert"), "dp", None),
        P(("groups", "expert"), "dp", None),
        P(("groups", "expert"), None, "dp"),
    )
    return jax.shard_map(
        on_device, mesh=mesh, in_specs=in_specs, out_specs=out_specs, check_vma=False
    )
```

profile of v0, /device:TPU:0, one launch (start us, length us, event | category | flops | bytes accessed | tf_op | source)
XLA Modules:
  0.0 183.9 jit_solution(1787334633764432873)
XLA Ops:
  7.2 0.0 copy-start
  7.2 0.0 all-gather.4.cloned.1.call-start
  7.2 0.7 all-gather.4.cloned.1.call-update
  7.9 0.0 all-gather.6.cloned.1.call-start
  8.0 0.7 all-gather.6.cloned.1.call-update
  8.7 0.0 all-gather.8.cloned.1.call-start
  8.7 0.7 all-gather.8.cloned.1.call-update
  9.4 0.8 copy.47
  10.2 0.1 eq.49
  10.3 0.1 eq.45
  10.4 0.1 copy.49
  10.5 0.2 fusion.12
  10.8 0.1 copy.50
  10.9 0.0 copy-start.1
  10.9 0.4 fusion.11
  11.3 0.1 select_reduce_fusion.1
  11.4 0.0 copy-done
  11.4 0.7 gather_fusion.1
  12.2 0.0 copy-done.1
  12.2 0.7 gather_fusion
  12.9 0.1 fusion.14
  13.1 0.8 select_select_fusion
  13.9 15.0 %all_to_all.35 = bf16[4,16,2048]{2,1,0:T(8,128)(2,1)S(1)} all-to-all(bf16[4,16,2048]{2,1,0:T(8,128)(2,1)S(1)} %bitcast.74), channel_id=1, replica_groups=mesh['groups'=2,'expert'=4,'dp'=4] {'expert'}, dimensions={0} | all-to-all | bytes 524288 | tf_op jit(solution)/shard_map/all_to_all | solution.py:66
  28.9 3.4 %all-to-all-start.2 = ((bf16[4,16,2048]{2,1,0:T(8,128)(2,1)}), bf16[4,16,2048]{2,1,0:T(8,128)(2,1)S(1)}, u32[]{:S(2)}, u32[]{:S(2)}) async-start(bf16[4,16,2048]{2,1,0:T(8,128)(2,1)} %bitcast.10), calls=%async_computation.2 | async-start | bytes 524288 | tf_op jit(solution)/shard_map/all_to_all | solution.py:67
  32.3 0.0 all-gather.4.cloned.1.call-done
  32.3 1.8 fusion.9
  34.1 19.1 %all-gather.6.cloned.1.call-done = bf16[1,2048,384]{2,1,0:T(8,128)(2,1)} async-done(((bf16[1,512,384]{2,1,0:T(8,128)(2,1)}), bf16[1,2048,384]{2,1,0:T(8,128)(2,1)}) %all-gather.6.cloned.1.call-update) | async-done | bytes 1572880 | tf_op jit(solution)/shard_map/all_gather | solution.py:59
  53.2 1.8 fusion.5
  55.0 0.0 all-to-all-done.2
  55.0 19.5 %all-gather.8.cloned.1.call-done = bf16[1,384,2048]{2,1,0:T(8,128)(2,1)} async-done(((bf16[1,384,512]{2,1,0:T(8,128)(2,1)}), bf16[1,384,2048]{2,1,0:T(8,128)(2,1)}) %all-gather.8.cloned.1.call-update) | async-done | bytes 1572880 | tf_op jit(solution)/shard_map/all_gather | solution.py:60
  74.5 0.0 copy-start.2
  74.5 2.1 %multiply_convert_fusion = (bf16[64,384]{1,0:T(8,128)(2,1)S(1)}, bf16[64,384]{1,0:T(8,128)(2,1)S(1)}, bf16[64,384]{1,0:T(8,128)(2,1)S(1)}) fusion(f32[64,384]{1,0:T(8,128)S(1)} %fusion.9, f32[64,384]{1,0:T(8,128)S(1)} %fusion.5, bf16[64,2048]{1,0:T(8,128)(2,1)S(1)} %bitcast.70, bf16[1,384,2048]{2,1,0:T(8,128)(2,1)} %all-gather.8.cloned.1.call-done), kind=kOutput, calls=%fused_computation.37 | convolution fusion | flops 101031936 | bytes 2179072 | tf_op jit(solution)/shard_map/dot_general | solution.py:10
  76.6 0.0 copy-done.2
  76.6 1.1 convolution_convert_fusion.5
  77.7 0.0 copy-start.3
  77.7 4.7 %all-to-all-start.1 = ((bf16[4,16,2048]{2,1,0:T(8,128)(2,1)}), bf16[4,16,2048]{2,1,0:T(8,128)(2,1)S(1)}, u32[]{:S(2)}, u32[]{:S(2)}) async-start(bf16[4,16,2048]{2,1,0:T(8,128)(2,1)} %bitcast.8), calls=%async_computation.1 | async-start | bytes 524288 | tf_op jit(solution)/shard_map/all_to_all | solution.py:75
  82.5 2.0 %fusion.7 = f32[64,2048]{1,0:T(8,128)S(1)} fusion(bf16[64,384]{1,0:T(8,128)(2,1)S(1)} %get-tuple-element.28, bf16[1,2048,384]{2,1,0:T(8,128)(2,1)} %all-gather.4.cloned.1.call-done), kind=kOutput, calls=%fused_computation.16 | convolution fusion | flops 100663296 | bytes 2146304 | tf_op jit(solution)/shard_map/dot_general | solution.py:10
  84.5 0.0 copy-done.3
  84.5 1.3 fusion
  85.8 6.0 %all-to-all-done.1 = bf16[4,16,2048]{2,1,0:T(8,128)(2,1)S(1)} async-done(((bf16[4,16,2048]{2,1,0:T(8,128)(2,1)}), bf16[4,16,2048]{2,1,0:T(8,128)(2,1)S(1)}, u32[]{:S(2)}, u32[]{:S(2)}) %all-to-all-start.1) | async-done | bytes 262176 | tf_op jit(solution)/shard_map/all_to_all | solution.py:75
  91.8 3.4 %all-to-all-start.3 = ((bf16[4,16,2048]{2,1,0:T(8,128)(2,1)}), bf16[4,16,2048]{2,1,0:T(8,128)(2,1)S(1)}, u32[]{:S(2)}, u32[]{:S(2)}) async-start(bf16[4,16,2048]{2,1,0:T(8,128)(2,1)} %bitcast.12), calls=%async_computation.3 | async-start | bytes 524288 | tf_op jit(solution)/shard_map/all_to_all | solution.py:82
  95.2 1.8 convolution_convert_fusion.2
  97.0 5.1 %all-to-all-done.3 = bf16[4,16,2048]{2,1,0:T(8,128)(2,1)S(1)} async-done(((bf16[4,16,2048]{2,1,0:T(8,128)(2,1)}), bf16[4,16,2048]{2,1,0:T(8,128)(2,1)S(1)}, u32[]{:S(2)}, u32[]{:S(2)}) %all-to-all-start.3) | async-done | bytes 262176 | tf_op jit(solution)/shard_map/all_to_all | solution.py:82
  102.1 3.6 %all-to-all-start.4 = ((bf16[4,512,384]{2,1,0:T(8,128)(2,1)}), bf16[4,512,384]{2,1,0:T(8,128)(2,1)S(1)}, u32[]{:S(2)}, u32[]{:S(2)}) async-start(bf16[4,512,384]{2,1,0:T(8,128)(2,1)} %bitcast.67), calls=%async_computation.4 | async-start | bytes 3145728 | tf_op jit(solution)/shard_map/all_to_all | solution.py:112
  105.7 1.8 convolution_convert_fusion
  107.4 18.3 %all-to-all-done.4 = bf16[4,512,384]{2,1,0:T(8,128)(2,1)S(1)} async-done(((bf16[4,512,384]{2,1,0:T(8,128)(2,1)}), bf16[4,512,384]{2,1,0:T(8,128)(2,1)S(1)}, u32[]{:S(2)}, u32[]{:S(2)}) %all-to-all-start.4) | async-done | bytes 1572896 | tf_op jit(solution)/shard_map/all_to_all | solution.py:112
  125.7 4.3 %all-to-all-start.6 = ((bf16[4,512,384]{2,1,0:T(8,128)(2,1)}), bf16[4,512,384]{2,1,0:T(8,128)(2,1)}, u32[]{:S(2)}, u32[]{:S(2)}) async-start(bf16[4,512,384]{2,1,0:T(8,128)(2,1)} %bitcast.66), calls=%async_computation.6 | async-start | bytes 3145728 | tf_op jit(solution)/shard_map/all_to_all | solution.py:126
  130.1 1.8 convolution_convert_fusion.1
  131.8 18.4 %all-to-all-done.6 = bf16[4,512,384]{2,1,0:T(8,128)(2,1)} async-done(((bf16[4,512,384]{2,1,0:T(8,128)(2,1)}), bf16[4,512,384]{2,1,0:T(8,128)(2,1)}, u32[]{:S(2)}, u32[]{:S(2)}) %all-to-all-start.6) | async-done | bytes 1572896 | tf_op jit(solution)/shard_map/all_to_all | solution.py:126
  150.2 0.0 copy-start.4
  150.2 0.0 copy-start.5
  150.2 4.5 %all-to-all-start.5 = ((bf16[4,512,384]{2,1,0:T(8,128)(2,1)}), bf16[4,512,384]{2,1,0:T(8,128)(2,1)}, u32[]{:S(2)}, u32[]{:S(2)}) async-start(bf16[4,512,384]{2,1,0:T(8,128)(2,1)} %bitcast.65), calls=%async_computation.5 | async-start | bytes 3145728 | tf_op jit(solution)/shard_map/all_to_all | solution.py:119
  154.7 0.1 sub.16
  154.8 0.0 copy-done.4
  154.8 0.3 convolution_bitcast_fusion
  155.2 0.0 copy-done.5
  155.2 0.6 select_reduce_fusion
  155.8 1.4 convolution_convert_fusion.4
  157.2 1.4 convolution_convert_fusion.3
  158.7 1.8 reduce_sum.78
  160.5 0.9 copy.52
  161.4 1.1 reduce_sum.76
  162.5 12.4 %all-to-all-done.5 = bf16[4,512,384]{2,1,0:T(8,128)(2,1)} async-done(((bf16[4,512,384]{2,1,0:T(8,128)(2,1)}), bf16[4,512,384]{2,1,0:T(8,128)(2,1)}, u32[]{:S(2)}, u32[]{:S(2)}) %all-to-all-start.5) | async-done | bytes 1572896 | tf_op jit(solution)/shard_map/all_to_all | solution.py:119
  174.8 2.5 %reduce_sum.77 = bf16[512,384]{1,0:T(8,128)(2,1)} reduce(bf16[4,512,384]{2,1,0:T(8,128)(2,1)} %all-to-all-done.5, bf16[]{:T(256)} %constant.50.clone.1), dimensions={0}, to_apply=%region_8.10 | reduce | flops 589824 | bytes 1966082 | tf_op jit(solution)/shard_map/reduce_sum | solution.py:135
  (10 shorter events, 0.2 us)
Async XLA Ops:
  7.2 4.3 %copy-start = (bf16[128,2048]{1,0:T(8,128)(2,1)S(1)}, bf16[128,2048]{1,0:T(8,128)(2,1)}, u32[]{:S(2)}) copy-start(bf16[128,2048]{1,0:T(8,128)(2,1)} %param.10) | copy-start | bytes 1572868
  7.2 25.2 %all-gather.4.cloned.1.call-start = ((), (), s32[]{:S(2)}) async-start(), calls=%async_computation.7 | async-start | bytes 1966080 | tf_op jit(solution)/shard_map/all_gather | solution.py:58
  7.9 45.3 %all-gather.6.cloned.1.call-start = ((), (), s32[]{:S(2)}) async-start(), calls=%async_computation.8 | async-start | bytes 1966080 | tf_op jit(solution)/shard_map/all_gather | solution.py:59
  8.7 65.8 %all-gather.8.cloned.1.call-start = ((), (), s32[]{:S(2)}) async-start(), calls=%async_computation.9 | async-start | bytes 1966080 | tf_op jit(solution)/shard_map/all_gather | solution.py:60
  10.9 1.3 copy-start.1
  28.9 26.1 %all-to-all-start.2 = ((bf16[4,16,2048]{2,1,0:T(8,128)(2,1)}), bf16[4,16,2048]{2,1,0:T(8,128)(2,1)S(1)}, u32[]{:S(2)}, u32[]{:S(2)}) async-start(bf16[4,16,2048]{2,1,0:T(8,128)(2,1)} %bitcast.10), calls=%async_computation.2 | async-start | bytes 524288 | tf_op jit(solution)/shard_map/all_to_all | solution.py:67
  74.5 2.1 %copy-start.2 = (bf16[1,384,2048]{2,1,0:T(8,128)(2,1)S(1)}, bf16[1,384,2048]{2,1,0:T(8,128)(2,1)}, u32[]{:S(2)}) copy-start(bf16[1,384,2048]{2,1,0:T(8,128)(2,1)} %all-gather.8.cloned.1.call-done) | copy-start | bytes 4718596
  77.7 6.7 %copy-start.3 = (bf16[1,2048,384]{2,1,0:T(8,128)(2,1)S(1)}, bf16[1,2048,384]{2,1,0:T(8,128)(2,1)}, u32[]{:S(2)}) copy-start(bf16[1,2048,384]{2,1,0:T(8,128)(2,1)} %all-gather.6.cloned.1.call-done) | copy-start | bytes 4718596
  77.7 14.0 %all-to-all-start.1 = ((bf16[4,16,2048]{2,1,0:T(8,128)(2,1)}), bf16[4,16,2048]{2,1,0:T(8,128)(2,1)S(1)}, u32[]{:S(2)}, u32[]{:S(2)}) async-start(bf16[4,16,2048]{2,1,0:T(8,128)(2,1)} %bitcast.8), calls=%async_computation.1 | async-start | bytes 524288 | tf_op jit(solution)/shard_map/all_to_all | solution.py:75
  91.8 10.3 %all-to-all-start.3 = ((bf16[4,16,2048]{2,1,0:T(8,128)(2,1)}), bf16[4,16,2048]{2,1,0:T(8,128)(2,1)S(1)}, u32[]{:S(2)}, u32[]{:S(2)}) async-start(bf16[4,16,2048]{2,1,0:T(8,128)(2,1)} %bitcast.12), calls=%async_computation.3 | async-start | bytes 524288 | tf_op jit(solution)/shard_map/all_to_all | solution.py:82
  102.1 23.6 %all-to-all-start.4 = ((bf16[4,512,384]{2,1,0:T(8,128)(2,1)}), bf16[4,512,384]{2,1,0:T(8,128)(2,1)S(1)}, u32[]{:S(2)}, u32[]{:S(2)}) async-start(bf16[4,512,384]{2,1,0:T(8,128)(2,1)} %bitcast.67), calls=%async_computation.4 | async-start | bytes 3145728 | tf_op jit(solution)/shard_map/all_to_all | solution.py:112
  125.7 24.5 %all-to-all-start.6 = ((bf16[4,512,384]{2,1,0:T(8,128)(2,1)}), bf16[4,512,384]{2,1,0:T(8,128)(2,1)}, u32[]{:S(2)}, u32[]{:S(2)}) async-start(bf16[4,512,384]{2,1,0:T(8,128)(2,1)} %bitcast.66), calls=%async_computation.6 | async-start | bytes 3145728 | tf_op jit(solution)/shard_map/all_to_all | solution.py:126
  150.2 4.6 %copy-start.4 = (s32[128,8]{0,1:T(8,128)S(1)}, s32[128,8]{0,1:T(8,128)}, u32[]{:S(2)}) copy-start(s32[128,8]{0,1:T(8,128)} %param.11) | copy-start | bytes 12292
  150.2 5.0 %copy-start.5 = (f32[128,8]{0,1:T(8,128)S(1)}, f32[128,8]{0,1:T(8,128)}, u32[]{:S(2)}) copy-start(f32[128,8]{0,1:T(8,128)} %param.12) | copy-start | bytes 12292
  150.2 24.6 %all-to-all-start.5 = ((bf16[4,512,384]{2,1,0:T(8,128)(2,1)}), bf16[4,512,384]{2,1,0:T(8,128)(2,1)}, u32[]{:S(2)}, u32[]{:S(2)}) async-start(bf16[4,512,384]{2,1,0:T(8,128)(2,1)} %bitcast.65), calls=%async_computation.5 | async-start | bytes 3145728 | tf_op jit(solution)/shard_map/all_to_all | solution.py:119
Sparse Core Ops, SparseCore 0:
  9.6 22.3 all-gather.3
  33.5 19.6 all-gather.5
  54.8 19.6 all-gather.7
where the time goes:
time: 185 us; the launch traced here: 184 us
  waiting for transfers between devices  101 us (55%)
  starting transfers between devices  24 us (13%)
  matrix products  18.5 us (10%)
  blocking collectives  15 us (8%)
  between operations  14 us (8%)
  other arithmetic  7.8 us (4%)
  local copies, waits for them, and re-layouts  3.77 us (2%)
    all_gather x1, waiting for transfers between devices, on_device(): lax.all_gather(w_down, 'dp', axis=2, tiled=True)  19.5 us
    all_gather x1, waiting for transfers between devices, on_device(): lax.all_gather(w_up, 'dp', axis=1, tiled=True)  19.1 us
    all_to_all x1, waiting for transfers between devices, on_device(): lax.all_to_all(local_down.reshape(dp_count, slice_width, hidden_width), '...  18.4 us
    all_to_all x1, waiting for transfers between devices, on_device(): lax.all_to_all(local_gate.reshape(dp_count, slice_width, hidden_width), '...  18.3 us
    all_to_all x1, blocking collectives, on_device(): lax.all_to_all(send_x, 'expert', split_axis=0, concat_axis=0, tiled=True)  15 us
    all_to_all x1, waiting for transfers between devices, on_device(): lax.all_to_all(local_up.reshape(dp_count, slice_width, hidden_width), 'dp...  12.4 us
    all_to_all x1, waiting for transfers between devices, on_device(): lax.all_to_all(expert_out.reshape(expert_count, capacity, model_width), '...  5.98 us
    dot_general x4, matrix products, dot_last(): lax.dot_general(left, right, (((1,), (1,)), ((), ())), preferred_element_...  5.78 us
  transfers between devices with their start and end apart: 9, of which 7 were waited for; matrix products, arithmetic and copies ran while one was open for 13% of the time, Pallas kernels for 0%

commit v1 on v0

v1 whole, which is shorter than its diff:
```python
import jax
import jax.numpy as jnp
from jax import lax
from jax.sharding import PartitionSpec as P

EXPERTS = 128
CORES = 2


def dot_first(left, right):
    return lax.dot_general(
        left, right, (((0,), (0,)), ((), ())), preferred_element_type=jnp.float32
    )


def dot_last(left, right):
    return lax.dot_general(
        left, right, (((1,), (1,)), ((), ())), preferred_element_type=jnp.float32
    )


def dot(left, right):
    return jnp.dot(left, right, preferred_element_type=jnp.float32)


def on_device(tokens, cotangent, expert_ids, gate_probs, w_gate, w_up, w_down):
    expert_count = lax.axis_size("expert")
    dp_count = lax.axis_size("dp")
    chips = dp_count // CORES
    token_rows, model_width = tokens.shape
    top_count = expert_ids.shape[1]
    width = w_gate.shape[1]
    capacity = 2 * token_rows * top_count // EXPERTS
    slot_total = expert_count * capacity
    me_z = lax.axis_index("expert")
    me_d = lax.axis_index("dp")

    def to_dp(array, mask):
        return lax.ppermute(array, "dp", [(i, i ^ mask) for i in range(dp_count)])

    def to_expert(array, step):
        pairs = [(i, (i + step) % expert_count) for i in range(expert_count)]
        return lax.ppermute(array, "expert", pairs)

    own = (w_gate[0], w_up[0], w_down[0])
    pieces = [{0: w} for w in own]
    for mask in range(CORES, dp_count, CORES):
        for k in range(3):
            pieces[k][mask] = to_dp(own[k], mask)
    for mask in range(0, dp_count, CORES):
        for k in range(3):
            pieces[k][mask + 1] = to_dp(pieces[k][mask], 1)
    gate_p, up_p, down_p = pieces

    wanted = (me_z + jnp.arange(expert_count, dtype=jnp.int32)) % expert_count
    hit = expert_ids[:, :, None] == wanted[None, None, :]
    named = jnp.any(hit, axis=1)
    before = jnp.arange(token_rows)[:, None] > jnp.arange(token_rows)[None, :]
    slot = dot(before.astype(jnp.bfloat16), named.astype(jnp.bfloat16))
    chosen = named[:, :, None] & (
        slot[:, :, None] == jnp.arange(capacity, dtype=jnp.float32)[None, None, :]
    )
    select = chosen.reshape(token_rows, slot_total).astype(jnp.bfloat16)
    prob = jnp.sum(jnp.where(hit, gate_probs[:, :, None], 0.0), axis=1)

    def turned(array):
        return jnp.concatenate(
            [
                lax.dynamic_slice_in_dim(array, (me_d ^ j) * width, width, 1)
                for j in range(dp_count)
            ],
            axis=1,
        )

    tokens_t = turned(tokens)
    cot_t = turned(cotangent)
    send_x = dot_first(select, tokens_t).astype(jnp.bfloat16)
    send_dy = dot_first(select, cot_t).astype(jnp.bfloat16)
    send = jnp.concatenate(
        [
            send_x.reshape(expert_count, capacity, model_width),
            send_dy.reshape(expert_count, capacity, model_width),
        ],
        axis=1,
    )
    got = [send[0]] + [to_expert(send[j], j) for j in range(1, expert_count)]
    rows_x = jnp.concatenate([g[:capacity] for g in got], axis=0)
    rows_dy = jnp.concatenate([g[capacity:] for g in got], axis=0)

    def cols(array, j, n=1):
        return array[:, j * width : (j + n) * width]

    gate_part = sum(dot(cols(rows_x, j), gate_p[j]) for j in range(dp_count))
    up_part = sum(dot(cols(rows_x, j), up_p[j]) for j in range(dp_count))
    back_hidden = sum(dot_last(cols(rows_dy, j), down_p[j]) for j in range(dp_count))
    sigmoid_gate = jax.nn.sigmoid(gate_part)
    activated = gate_part * sigmoid_gate
    hidden = (activated * up_part).astype(jnp.bfloat16)
    d_gate = (
        back_hidden * up_part * sigmoid_gate * (1.0 + gate_part * (1.0 - sigmoid_gate))
    ).astype(jnp.bfloat16)
    d_up = (back_hidden * activated).astype(jnp.bfloat16)
    expert_out = jnp.concatenate(
        [dot(hidden, down_p[j]).astype(jnp.bfloat16) for j in range(dp_count)], axis=1
    )
    d_rows = jnp.concatenate(
        [
            (dot_last(d_gate, gate_p[j]) + dot_last(d_up, up_p[j])).astype(jnp.bfloat16)
            for j in range(dp_count)
        ],
        axis=1,
    )
    back = jnp.concatenate(
        [
            expert_out.reshape(expert_count, capacity, model_width),
            d_rows.reshape(expert_count, capacity, model_width),
        ],
        axis=1,
    )
    home = [back[0]] + [to_expert(back[j], -j) for j in range(1, expert_count)]
    back_out = jnp.concatenate([h[:capacity] for h in home], axis=0)
    back_rows = jnp.concatenate([h[capacity:] for h in home], axis=0)

    trio = jnp.concatenate([hidden, d_gate, d_up], axis=1)
    pair = jnp.concatenate([rows_x, rows_dy], axis=0)
    trios, pairs = [trio], [cols(pair, 0, CORES)]
    for mask in range(CORES, dp_count, CORES):
        pairs.append(to_dp(cols(pair, mask, CORES), mask))
        trios.append(to_dp(trio, mask))
    all_trio = jnp.concatenate(trios, axis=0)
    all_x = jnp.concatenate([p[:slot_total] for p in pairs], axis=0)
    all_dy = jnp.concatenate([p[slot_total:] for p in pairs], axis=0)
    ff = w_gate.shape[2]

    def reduced(part_own, part_other):
        return (part_own + to_dp(part_other.astype(jnp.bfloat16), 1).astype(jnp.float32)).astype(
            jnp.bfloat16
        )

    all_h, all_g, all_u = (all_trio[:, k * ff : (k + 1) * ff] for k in range(3))
    grad_w_gate = reduced(dot_first(cols(all_x, 0), all_g), dot_first(cols(all_x, 1), all_g))[None]
    grad_w_up = reduced(dot_first(cols(all_x, 0), all_u), dot_first(cols(all_x, 1), all_u))[None]
    grad_w_down = reduced(dot_first(all_h, cols(all_dy, 0)), dot_first(all_h, cols(all_dy, 1)))[
        None
    ]

    table = jnp.where(chosen, prob[:, :, None], 0.0).reshape(token_rows, slot_total)
    high = table.astype(jnp.bfloat16)
    rest = table - high.astype(jnp.float32)
    middle = rest.astype(jnp.bfloat16)
    low = (rest - middle.astype(jnp.float32)).astype(jnp.bfloat16)

    def weighted(rows):
        total = dot(high, rows) + (dot(middle, rows) + dot(low, rows))
        return turned(total.astype(jnp.bfloat16))

    mixed = weighted(back_out)
    grad_tokens = weighted(back_rows)
    inner = jnp.sum(
        jnp.where(
            chosen, dot_last(cot_t, back_out).reshape(token_rows, expert_count, capacity), 0.0
        ),
        axis=2,
    )
    grad_gates = jnp.sum(jnp.where(hit, inner[:, None, :], 0.0), axis=2)
    return (mixed, grad_tokens, grad_gates, grad_w_gate, grad_w_up, grad_w_down)


def solution(mesh):
    rows = P(("groups", "expert", "dp"), None)
    in_specs = (
        rows,
        rows,
        rows,
        rows,
        P("expert", "dp", None),
        P("expert", "dp", None),
        P("expert", None, "dp"),
    )
    out_specs = (
        rows,
        rows,
        rows,
        P(("groups", "expert"), "dp", None),
        P(("groups", "expert"), "dp", None),
        P(("groups", "expert"), None, "dp"),
    )
    return jax.shard_map(
        on_device, mesh=mesh, in_specs=in_specs, out_specs=out_specs, check_vma=False
    )
```

time: 185 us -> 76.1 us (0.41)
  waiting for transfers between devices: 101 us -> 36 us
  blocking collectives: 15 us -> 0 us
  between operations: 14 us -> 1.17 us
  matrix products: 18.5 us -> 12.1 us
  other arithmetic: 7.8 us -> 2.87 us
  starting transfers between devices: 24 us -> 19.4 us
    all_to_all x6 -> x0, waiting for transfers between devices: 60.2 us -> none  [the longest x1 18.4 us: on_device(): lax.all_to_all(local_down.reshape(dp_count, slice_width, hidden_width), '...]
    all_gather x3 -> x0, waiting for transfers between devices: 38.6 us -> none  [the longest x1 19.5 us: on_device(): lax.all_gather(w_down, 'dp', axis=2, tiled=True)]
    ppermute x0 -> x20, waiting for transfers between devices: none -> 36 us  [the longest x6 22.5 us: to_expert(): return lax.ppermute(array, 'expert', pairs)]
    all_to_all x6 -> x0, starting transfers between devices: 23.9 us -> none  [the longest x1 4.72 us: on_device(): lax.all_to_all(expert_out.reshape(expert_count, capacity, model_width), '...]
    ppermute x0 -> x20, starting transfers between devices: none -> 19.4 us  [the longest x6 9.98 us: to_expert(): return lax.ppermute(array, 'expert', pairs)]
    all_to_all x1 -> x0, blocking collectives: 15 us -> none  [on_device(): lax.all_to_all(send_x, 'expert', split_axis=0, concat_axis=0, tiled=True)]
    reduce_sum x6 -> x1, other arithmetic: 6.52 us -> 0.67 us  [on_device(): grad_gates = jnp.sum(jnp.where(hit, inner[:, None, :], 0.0), axis=2)]
    dot_general x8 -> x27, matrix products: 12.7 us -> 8.78 us  [the longest x19 4.41 us: dot(): return jnp.dot(left, right, preferred_element_type=jnp.float32)]
  transfers between devices with their start and end apart: 9 -> 20, of which waited for: 7 -> 8; matrix products, arithmetic and copies ran while one was open for 13% -> 16% of each run, Pallas kernels for 0% -> 0%
where the time goes in v1:
time: 76.1 us; the launch traced here: 75 us
  waiting for transfers between devices  36 us (47%)
  starting transfers between devices  19.4 us (25%)
  matrix products  12.1 us (16%)
  local copies, waits for them, and re-layouts  3.49 us (5%)
  other arithmetic  2.87 us (4%)
  between operations  1.17 us (2%)
    ppermute x6, waiting for transfers between devices, to_expert(): return lax.ppermute(array, 'expert', pairs)  22.5 us
    ppermute x14, waiting for transfers between devices, to_dp(): return lax.ppermute(array, 'dp', [(i, i ^ mask) for i in range(dp_count)])  13.4 us
    ppermute x6, starting transfers between devices, to_expert(): return lax.ppermute(array, 'expert', pairs)  9.98 us
    ppermute x14, starting transfers between devices, to_dp(): return lax.ppermute(array, 'dp', [(i, i ^ mask) for i in range(dp_count)])  9.39 us
    dot_general x19, matrix products, dot(): return jnp.dot(left, right, preferred_element_type=jnp.float32)  4.41 us
    dot_general x8, matrix products, dot_first(): lax.dot_general(left, right, (((0,), (0,)), ((), ())), preferred_element_...  4.38 us
    dot_general x13, matrix products, dot_last(): lax.dot_general(left, right, (((1,), (1,)), ((), ())), preferred_element_...  3.32 us
    unnamed x19, local copies, waits for them, and re-layouts  1.92 us
  transfers between devices with their start and end apart: 20, of which 8 were waited for; matrix products, arithmetic and copies ran while one was open for 16% of the time, Pallas kernels for 0%

profile of v1, /device:TPU:0, one launch (start us, length us, event | category | flops | bytes accessed | tf_op | source)
XLA Modules:
  0.0 75.0 jit_solution(14172654857100669596)
XLA Ops:
  0.6 0.5 collective-permute-start.3
  1.1 2.6 %collective-permute-start.4 = (bf16[512,384]{1,0:T(8,128)(2,1)}, bf16[512,384]{1,0:T(8,128)(2,1)S(1)}, u32[]{:S(2)}, u32[]{:S(2)}) collective-permute-start(bf16[512,384]{1,0:T(8,128)(2,1)} %bitcast.113), channel_id=1, source_target_pairs={{0,2},{1,3},{2,0},{3,1},{4,6},{5,7},{6,4},{7,5},{8,10},{9,11},{10,... | collective-permute-start | bytes 1179656 | tf_op jit(solution)/shard_map/ppermute | solution.py:39
  3.9 0.3 collective-permute-start.10
  4.2 0.7 copy-done.4
  5.2 1.2 %constant_dynamic-slice_fusion.15 = (bf16[128,512]{1,0:T(8,128)(2,1)S(1)}, bf16[128,512]{1,0:T(8,128)(2,1)S(1)}, bf16[128,512]{1,0:T(8,128)(2,1)S(1)}, bf16[128,512]{1,0:T(8,128)(2,1)S(1)}) fusion(bf16[128,2048]{1,0:T(8,128)(2,1)} %param.7, s32[]{:T(128)S(6)} %select_n.55, s32[]{:T(128)S(6)} %select_n.56, s32[]{:T(128)S(6)} %select_n.58, s32[]{:T(128)S(6)} %select_n.57), kind=kLoop, calls=%fused_computation.143 | loop fusion | bytes 1048592 | tf_op jit(solution)/shard_map/dynamic_slice | solution.py:69
  6.6 0.2 convolution_convert_fusion.1
  6.8 0.2 convolution_convert_fusion
  7.1 1.9 %collective-permute-start = (bf16[32,2048]{1,0:T(8,128)(2,1)S(1)}, bf16[32,2048]{1,0:T(8,128)(2,1)S(1)}, u32[]{:S(2)}, u32[]{:S(2)}) collective-permute-start(bf16[32,2048]{1,0:T(8,128)(2,1)S(1)} %get-tuple-element.19), channel_id=1, source_target_pairs={{0,4},{4,8},{8,12},{12,0},{1,5},{5,9},{9,13},{13,1},{2,6},{6,10},{... | collective-permute-start | bytes 393224 | tf_op jit(solution)/shard_map/ppermute | solution.py:43
  9.0 5.7 %collective-permute-done = bf16[32,2048]{1,0:T(8,128)(2,1)S(1)} collective-permute-done((bf16[32,2048]{1,0:T(8,128)(2,1)S(1)}, bf16[32,2048]{1,0:T(8,128)(2,1)S(1)}, u32[]{:S(2)}, u32[]{:S(2)}) %collective-permute-start) | collective-permute-done | bytes 131104 | tf_op jit(solution)/shard_map/ppermute | solution.py:43
  14.7 0.7 collective-permute-start.1
  15.5 6.8 %collective-permute-done.1 = bf16[32,2048]{1,0:T(8,128)(2,1)S(1)} collective-permute-done((bf16[32,2048]{1,0:T(8,128)(2,1)S(1)}, bf16[32,2048]{1,0:T(8,128)(2,1)S(1)}, u32[]{:S(2)}, u32[]{:S(2)}) %collective-permute-start.1) | collective-permute-done | bytes 131104 | tf_op jit(solution)/shard_map/ppermute | solution.py:43
  22.2 2.5 %collective-permute-start.2 = (bf16[32,2048]{1,0:T(8,128)(2,1)S(1)}, bf16[32,2048]{1,0:T(8,128)(2,1)S(1)}, u32[]{:S(2)}, u32[]{:S(2)}) collective-permute-start(bf16[32,2048]{1,0:T(8,128)(2,1)S(1)} %get-tuple-element.21), channel_id=1, source_target_pairs={{0,12},{4,0},{8,4},{12,8},{1,13},{5,1},{9,5},{13,9},{2,14},{6,2},{... | collective-permute-start | bytes 393224 | tf_op jit(solution)/shard_map/ppermute | solution.py:43
  24.7 2.7 %collective-permute-done.2 = bf16[32,2048]{1,0:T(8,128)(2,1)S(1)} collective-permute-done((bf16[32,2048]{1,0:T(8,128)(2,1)S(1)}, bf16[32,2048]{1,0:T(8,128)(2,1)S(1)}, u32[]{:S(2)}, u32[]{:S(2)}) %collective-permute-start.2) | collective-permute-done | bytes 131104 | tf_op jit(solution)/shard_map/ppermute | solution.py:43
  27.5 1.6 %collective-permute-start.15 = (bf16[128,1024]{1,0:T(8,128)(2,1)S(1)}, bf16[128,1024]{1,0:T(8,128)(2,1)S(1)}, u32[]{:S(2)}, u32[]{:S(2)}) collective-permute-start(bf16[128,1024]{1,0:T(8,128)(2,1)S(1)} %slice.222), channel_id=1, source_target_pairs={{0,2},{1,3},{2,0},{3,1},{4,6},{5,7},{6,4},{7,5},{8,10},{9,11},{10,... | collective-permute-start | bytes 786440 | tf_op jit(solution)/shard_map/ppermute | solution.py:39
  29.2 5.5 %collective-permute-done.15 = bf16[128,1024]{1,0:T(8,128)(2,1)S(1)} collective-permute-done((bf16[128,1024]{1,0:T(8,128)(2,1)S(1)}, bf16[128,1024]{1,0:T(8,128)(2,1)S(1)}, u32[]{:S(2)}, u32[]{:S(2)}) %collective-permute-start.15) | collective-permute-done | bytes 262176 | tf_op jit(solution)/shard_map/ppermute | solution.py:39
  34.7 1.6 %collective-permute-start.7 = (bf16[512,384]{1,0:T(8,128)(2,1)S(1)}, bf16[512,384]{1,0:T(8,128)(2,1)S(1)}, u32[]{:S(2)}, u32[]{:S(2)}) collective-permute-start(bf16[512,384]{1,0:T(8,128)(2,1)S(1)} %bitcast.115), channel_id=1, source_target_pairs={{0,2},{1,3},{2,0},{3,1},{4,6},{5,7},{6,4},{7,5},{8,10},{9,11},{10,... | collective-permute-start | bytes 1179656 | tf_op jit(solution)/shard_map/ppermute | solution.py:39
  36.3 0.2 collective-permute-start.5
  36.5 0.3 collective-permute-start.11
  36.8 0.2 fusion.45
  37.0 0.2 convolution_add_fusion.19
  37.3 0.3 fusion.35
  37.5 0.7 copy-done.2
  38.2 0.3 convolution_add_fusion.13
  38.5 0.2 fusion.43
  38.7 0.2 convolution_add_fusion.16
  38.9 0.2 convolution_add_fusion.18
  39.1 7.2 %collective-permute-done.7 = bf16[512,384]{1,0:T(8,128)(2,1)S(1)} collective-permute-done((bf16[512,384]{1,0:T(8,128)(2,1)S(1)}, bf16[512,384]{1,0:T(8,128)(2,1)S(1)}, u32[]{:S(2)}, u32[]{:S(2)}) %collective-permute-start.7) | collective-permute-done | bytes 393248 | tf_op jit(solution)/shard_map/ppermute | solution.py:39
  46.3 0.3 convolution_add_fusion.12
  46.6 0.2 convolution_add_fusion.15
  46.8 0.2 convolution_add_fusion.17
  47.0 0.3 convolution_add_fusion.11
  47.3 0.7 collective-permute-done.8
  48.0 0.2 multiply_convert_fusion.2
  48.3 0.2 fusion.68
  48.5 0.2 convolution_convert_fusion.8
  49.3 0.2 fusion.8
  49.6 0.2 fusion.81
  49.8 0.2 fusion.80
  50.1 0.2 fusion.79
  50.3 0.2 fusion.11
  50.6 0.2 fusion.10
  50.8 0.2 fusion.9
  51.2 4.8 %collective-permute-start.13 = (bf16[32,2048]{1,0:T(8,128)(2,1)S(1)}, bf16[32,2048]{1,0:T(8,128)(2,1)S(1)}, u32[]{:S(2)}, u32[]{:S(2)}) collective-permute-start(bf16[32,2048]{1,0:T(8,128)(2,1)S(1)} %get-tuple-element.17), channel_id=1, source_target_pairs={{0,8},{4,12},{8,0},{12,4},{1,9},{5,13},{9,1},{13,5},{2,10},{6,14},... | collective-permute-start | bytes 393224 | tf_op jit(solution)/shard_map/ppermute | solution.py:43
  56.1 1.5 %collective-permute-start.16 = (bf16[64,1152]{1,0:T(8,128)(2,1)S(1)}, bf16[64,1152]{1,0:T(8,128)(2,1)S(1)}, u32[]{:S(2)}, u32[]{:S(2)}) collective-permute-start(bf16[64,1152]{1,0:T(8,128)(2,1)S(1)} %pad_maximum_fusion.10), channel_id=1, source_target_pairs={{0,2},{1,3},{2,0},{3,1},{4,6},{5,7},{6,4},{7,5},{8,10},{9,11},{10,... | collective-permute-start | bytes 442376 | tf_op jit(solution)/shard_map/ppermute | solution.py:39
  57.6 2.3 %collective-permute-done.14 = bf16[32,2048]{1,0:T(8,128)(2,1)S(1)} collective-permute-done((bf16[32,2048]{1,0:T(8,128)(2,1)S(1)}, bf16[32,2048]{1,0:T(8,128)(2,1)S(1)}, u32[]{:S(2)}, u32[]{:S(2)}) %collective-permute-start.14) | collective-permute-done | bytes 131104 | tf_op jit(solution)/shard_map/ppermute | solution.py:43
  59.9 5.1 %collective-permute-done.13 = bf16[32,2048]{1,0:T(8,128)(2,1)S(1)} collective-permute-done((bf16[32,2048]{1,0:T(8,128)(2,1)S(1)}, bf16[32,2048]{1,0:T(8,128)(2,1)S(1)}, u32[]{:S(2)}, u32[]{:S(2)}) %collective-permute-start.13) | collective-permute-done | bytes 131104 | tf_op jit(solution)/shard_map/ppermute | solution.py:43
  65.0 0.3 select_reduce_fusion
  65.3 0.4 copy-done.5
  65.7 0.7 fusion.55
  66.5 0.3 fusion.74
  66.8 0.3 fusion.73
  67.2 0.3 convolution_add_fusion
  67.5 0.3 convolution_add_fusion.2
  67.8 0.3 fusion.1
  68.1 0.3 fusion
  68.6 0.8 %pad_maximum_fusion.1 = bf16[128,2048]{1,0:T(8,128)(2,1)} fusion(bf16[128,512]{1,0:T(8,128)(2,1)S(1)} %get-tuple-element.58, bf16[128,512]{1,0:T(8,128)(2,1)S(1)} %get-tuple-element.57, bf16[128,512]{1,0:T(8,128)(2,1)S(1)} %get-tuple-element.56, bf16[128,512]{1,0:T(8,128)(2,1)S(1)} %get-tuple-element.59), kind=kLoop, calls=%fused_computation.49 | loop fusion | flops 2097152 | bytes 1048576 | tf_op jit(solution)/shard_map/concatenate | solution.py:67
  69.5 0.3 convolution_convert_fusion.4
  69.8 0.3 convolution_convert_fusion.3
  70.1 0.5 collective-permute-start.18
  70.6 0.3 convolution_convert_fusion.2
  71.0 0.8 %pad_maximum_fusion.2 = bf16[128,2048]{1,0:T(8,128)(2,1)} fusion(bf16[128,512]{1,0:T(8,128)(2,1)S(1)} %get-tuple-element.9, bf16[128,512]{1,0:T(8,128)(2,1)S(1)} %get-tuple-element.10, bf16[128,512]{1,0:T(8,128)(2,1)S(1)} %get-tuple-element.11, bf16[128,512]{1,0:T(8,128)(2,1)S(1)} %get-tuple-element.8), kind=kLoop, calls=%fused_computation.50 | loop fusion | flops 2097152 | bytes 1048576 | tf_op jit(solution)/shard_map/concatenate | solution.py:67
  71.9 1.0 %fusion.7 = bf16[1,512,384]{2,1,0:T(8,128)(2,1)} fusion(bf16[512,384]{1,0:T(8,128)(2,1)S(1)} %collective-permute-done.17, bf16[128,1152]{1,0:T(8,128)(2,1)S(1)} %pad_maximum_fusion.3, bf16[64,1024]{1,0:T(8,128)(2,1)S(1)} %slice.221, bf16[64,1024]{1,0:T(8,128)(2,1)S(1)} %get-tuple-element.31), kind=kOutput, calls=%fused_computation.19 | convolution fusion | flops 51183616 | bytes 1146880 | tf_op jit(solution)/shard_map/dot_general | solution.py:11
  72.9 1.0 %fusion.6 = bf16[1,512,384]{2,1,0:T(8,128)(2,1)} fusion(bf16[512,384]{1,0:T(8,128)(2,1)S(1)} %collective-permute-done.18, bf16[128,1152]{1,0:T(8,128)(2,1)S(1)} %pad_maximum_fusion.3, bf16[64,1024]{1,0:T(8,128)(2,1)S(1)} %slice.221, bf16[64,1024]{1,0:T(8,128)(2,1)S(1)} %get-tuple-element.31), kind=kOutput, calls=%fused_computation.18 | convolution fusion | flops 51183616 | bytes 1146880 | tf_op jit(solution)/shard_map/dot_general | solution.py:11
  74.0 1.0 %fusion.5 = bf16[1,384,512]{2,1,0:T(8,128)(2,1)} fusion(bf16[384,512]{1,0:T(8,128)(2,1)S(1)} %collective-permute-done.19, bf16[64,1024]{1,0:T(8,128)(2,1)S(1)} %slice.229, bf16[64,1024]{1,0:T(8,128)(2,1)S(1)} %get-tuple-element.30, bf16[128,1152]{1,0:T(8,128)(2,1)S(1)} %pad_maximum_fusion.3), kind=kOutput, calls=%fused_computation.17 | convolution fusion | flops 51183616 | bytes 1146880 | tf_op jit(solution)/shard_map/dot_general | solution.py:11
  (66 shorter events, 2.2 us)
Async XLA Ops:
  0.6 34.1 %collective-permute-start.3 = (bf16[512,384]{1,0:T(8,128)(2,1)}, bf16[512,384]{1,0:T(8,128)(2,1)S(1)}, u32[]{:S(2)}, u32[]{:S(2)}) collective-permute-start(bf16[512,384]{1,0:T(8,128)(2,1)} %bitcast.112), channel_id=1, source_target_pairs={{0,1},{1,0},{2,3},{3,2},{4,5},{5,4},{6,7},{7,6},{8,9},{9,8},{10,11... | collective-permute-start | bytes 1179656 | tf_op jit(solution)/shard_map/ppermute | solution.py:39
  1.1 35.1 %collective-permute-start.4 = (bf16[512,384]{1,0:T(8,128)(2,1)}, bf16[512,384]{1,0:T(8,128)(2,1)S(1)}, u32[]{:S(2)}, u32[]{:S(2)}) collective-permute-start(bf16[512,384]{1,0:T(8,128)(2,1)} %bitcast.113), channel_id=1, source_target_pairs={{0,2},{1,3},{2,0},{3,1},{4,6},{5,7},{6,4},{7,5},{8,10},{9,11},{10,... | collective-permute-start | bytes 1179656 | tf_op jit(solution)/shard_map/ppermute | solution.py:39
  3.7 33.5 %collective-permute-start.9 = (bf16[384,512]{1,0:T(8,128)(2,1)}, bf16[384,512]{1,0:T(8,128)(2,1)S(1)}, u32[]{:S(2)}, u32[]{:S(2)}) collective-permute-start(bf16[384,512]{1,0:T(8,128)(2,1)} %bitcast.116), channel_id=1, source_target_pairs={{0,1},{1,0},{2,3},{3,2},{4,5},{5,4},{6,7},{7,6},{8,9},{9,8},{10,11... | collective-permute-start | bytes 1179656 | tf_op jit(solution)/shard_map/ppermute | solution.py:39
  3.9 32.6 %collective-permute-start.10 = (bf16[384,512]{1,0:T(8,128)(2,1)}, bf16[384,512]{1,0:T(8,128)(2,1)S(1)}, u32[]{:S(2)}, u32[]{:S(2)}) collective-permute-start(bf16[384,512]{1,0:T(8,128)(2,1)} %bitcast.117), channel_id=1, source_target_pairs={{0,2},{1,3},{2,0},{3,1},{4,6},{5,7},{6,4},{7,5},{8,10},{9,11},{10,... | collective-permute-start | bytes 1179656 | tf_op jit(solution)/shard_map/ppermute | solution.py:39
  4.1 0.7 copy-start.4
  5.2 1.3 %copy-start.3 = (bf16[128,2048]{1,0:T(8,128)(2,1)S(1)}, bf16[128,2048]{1,0:T(8,128)(2,1)}, u32[]{:S(2)}) copy-start(bf16[128,2048]{1,0:T(8,128)(2,1)} %param.8) | copy-start | bytes 1572868
  7.1 7.7 %collective-permute-start = (bf16[32,2048]{1,0:T(8,128)(2,1)S(1)}, bf16[32,2048]{1,0:T(8,128)(2,1)S(1)}, u32[]{:S(2)}, u32[]{:S(2)}) collective-permute-start(bf16[32,2048]{1,0:T(8,128)(2,1)S(1)} %get-tuple-element.19), channel_id=1, source_target_pairs={{0,4},{4,8},{8,12},{12,0},{1,5},{5,9},{9,13},{13,1},{2,6},{6,10},{... | collective-permute-start | bytes 393224 | tf_op jit(solution)/shard_map/ppermute | solution.py:43
  14.7 7.5 %collective-permute-start.1 = (bf16[32,2048]{1,0:T(8,128)(2,1)S(1)}, bf16[32,2048]{1,0:T(8,128)(2,1)S(1)}, u32[]{:S(2)}, u32[]{:S(2)}) collective-permute-start(bf16[32,2048]{1,0:T(8,128)(2,1)S(1)} %get-tuple-element.20), channel_id=1, source_target_pairs={{0,8},{4,12},{8,0},{12,4},{1,9},{5,13},{9,1},{13,5},{2,10},{6,14},... | collective-permute-start | bytes 393224 | tf_op jit(solution)/shard_map/ppermute | solution.py:43
  22.2 5.2 %collective-permute-start.2 = (bf16[32,2048]{1,0:T(8,128)(2,1)S(1)}, bf16[32,2048]{1,0:T(8,128)(2,1)S(1)}, u32[]{:S(2)}, u32[]{:S(2)}) collective-permute-start(bf16[32,2048]{1,0:T(8,128)(2,1)S(1)} %get-tuple-element.21), channel_id=1, source_target_pairs={{0,12},{4,0},{8,4},{12,8},{1,13},{5,1},{9,5},{13,9},{2,14},{6,2},{... | collective-permute-start | bytes 393224 | tf_op jit(solution)/shard_map/ppermute | solution.py:43
  27.5 7.2 %collective-permute-start.15 = (bf16[128,1024]{1,0:T(8,128)(2,1)S(1)}, bf16[128,1024]{1,0:T(8,128)(2,1)S(1)}, u32[]{:S(2)}, u32[]{:S(2)}) collective-permute-start(bf16[128,1024]{1,0:T(8,128)(2,1)S(1)} %slice.222), channel_id=1, source_target_pairs={{0,2},{1,3},{2,0},{3,1},{4,6},{5,7},{6,4},{7,5},{8,10},{9,11},{10,... | collective-permute-start | bytes 786440 | tf_op jit(solution)/shard_map/ppermute | solution.py:39
  29.1 5.6 %copy-start.1 = (bf16[1,512,384]{2,1,0:T(8,128)(2,1)S(1)}, bf16[1,512,384]{2,1,0:T(8,128)(2,1)}, u32[]{:S(2)}) copy-start(bf16[1,512,384]{2,1,0:T(8,128)(2,1)} %param.12) | copy-start | bytes 1179652
  34.7 3.8 %collective-permute-start.6 = (bf16[512,384]{1,0:T(8,128)(2,1)S(1)}, bf16[512,384]{1,0:T(8,128)(2,1)S(1)}, u32[]{:S(2)}, u32[]{:S(2)}) collective-permute-start(bf16[512,384]{1,0:T(8,128)(2,1)S(1)} %bitcast.114), channel_id=1, source_target_pairs={{0,1},{1,0},{2,3},{3,2},{4,5},{5,4},{6,7},{7,6},{8,9},{9,8},{10,11... | collective-permute-start | bytes 1179656 | tf_op jit(solution)/shard_map/ppermute | solution.py:39
  34.7 2.3 %copy-start = (bf16[1,512,384]{2,1,0:T(8,128)(2,1)S(1)}, bf16[1,512,384]{2,1,0:T(8,128)(2,1)}, u32[]{:S(2)}) copy-start(bf16[1,512,384]{2,1,0:T(8,128)(2,1)} %param.11) | copy-start | bytes 1179652
  34.7 11.6 %collective-permute-start.7 = (bf16[512,384]{1,0:T(8,128)(2,1)S(1)}, bf16[512,384]{1,0:T(8,128)(2,1)S(1)}, u32[]{:S(2)}, u32[]{:S(2)}) collective-permute-start(bf16[512,384]{1,0:T(8,128)(2,1)S(1)} %bitcast.115), channel_id=1, source_target_pairs={{0,2},{1,3},{2,0},{3,1},{4,6},{5,7},{6,4},{7,5},{8,10},{9,11},{10,... | collective-permute-start | bytes 1179656 | tf_op jit(solution)/shard_map/ppermute | solution.py:39
  36.3 10.5 %collective-permute-start.5 = (bf16[512,384]{1,0:T(8,128)(2,1)S(1)}, bf16[512,384]{1,0:T(8,128)(2,1)S(1)}, u32[]{:S(2)}, u32[]{:S(2)}) collective-permute-start(bf16[512,384]{1,0:T(8,128)(2,1)S(1)} %collective-permute-done.4), channel_id=1, source_target_pairs={{0,1},{1,0},{2,3},{3,2},{4,5},{5,4},{6,7},{7,6},{8,9},{9,8},{10,11... | collective-permute-start | bytes 1179656 | tf_op jit(solution)/shard_map/ppermute | solution.py:39
  36.5 10.5 %collective-permute-start.11 = (bf16[384,512]{1,0:T(8,128)(2,1)S(1)}, bf16[384,512]{1,0:T(8,128)(2,1)S(1)}, u32[]{:S(2)}, u32[]{:S(2)}) collective-permute-start(bf16[384,512]{1,0:T(8,128)(2,1)S(1)} %collective-permute-done.10), channel_id=1, source_target_pairs={{0,1},{1,0},{2,3},{3,2},{4,5},{5,4},{6,7},{7,6},{8,9},{9,8},{10,11... | collective-permute-start | bytes 1179656 | tf_op jit(solution)/shard_map/ppermute | solution.py:39
  37.2 1.0 %copy-start.2 = (bf16[1,384,512]{2,1,0:T(8,128)(2,1)S(1)}, bf16[1,384,512]{2,1,0:T(8,128)(2,1)}, u32[]{:S(2)}) copy-start(bf16[1,384,512]{2,1,0:T(8,128)(2,1)} %param.13) | copy-start | bytes 1179652
  46.3 1.7 %collective-permute-start.8 = (bf16[512,384]{1,0:T(8,128)(2,1)S(1)}, bf16[512,384]{1,0:T(8,128)(2,1)S(1)}, u32[]{:S(2)}, u32[]{:S(2)}) collective-permute-start(bf16[512,384]{1,0:T(8,128)(2,1)S(1)} %collective-permute-done.7), channel_id=1, source_target_pairs={{0,1},{1,0},{2,3},{3,2},{4,5},{5,4},{6,7},{7,6},{8,9},{9,8},{10,11... | collective-permute-start | bytes 1179656 | tf_op jit(solution)/shard_map/ppermute | solution.py:39
  51.1 8.7 %collective-permute-start.14 = (bf16[32,2048]{1,0:T(8,128)(2,1)S(1)}, bf16[32,2048]{1,0:T(8,128)(2,1)S(1)}, u32[]{:S(2)}, u32[]{:S(2)}) collective-permute-start(bf16[32,2048]{1,0:T(8,128)(2,1)S(1)} %get-tuple-element.18), channel_id=1, source_target_pairs={{0,4},{4,8},{8,12},{12,0},{1,5},{5,9},{9,13},{13,1},{2,6},{6,10},{... | collective-permute-start | bytes 393224 | tf_op jit(solution)/shard_map/ppermute | solution.py:43
  51.2 13.8 %collective-permute-start.13 = (bf16[32,2048]{1,0:T(8,128)(2,1)S(1)}, bf16[32,2048]{1,0:T(8,128)(2,1)S(1)}, u32[]{:S(2)}, u32[]{:S(2)}) collective-permute-start(bf16[32,2048]{1,0:T(8,128)(2,1)S(1)} %get-tuple-element.17), channel_id=1, source_target_pairs={{0,8},{4,12},{8,0},{12,4},{1,9},{5,13},{9,1},{13,5},{2,10},{6,14},... | collective-permute-start | bytes 393224 | tf_op jit(solution)/shard_map/ppermute | solution.py:43
  56.0 8.9 %collective-permute-start.12 = (bf16[32,2048]{1,0:T(8,128)(2,1)S(1)}, bf16[32,2048]{1,0:T(8,128)(2,1)S(1)}, u32[]{:S(2)}, u32[]{:S(2)}) collective-permute-start(bf16[32,2048]{1,0:T(8,128)(2,1)S(1)} %get-tuple-element.16), channel_id=1, source_target_pairs={{0,12},{4,0},{8,4},{12,8},{1,13},{5,1},{9,5},{13,9},{2,14},{6,2},{... | collective-permute-start | bytes 393224 | tf_op jit(solution)/shard_map/ppermute | solution.py:43
  56.1 13.4 %collective-permute-start.16 = (bf16[64,1152]{1,0:T(8,128)(2,1)S(1)}, bf16[64,1152]{1,0:T(8,128)(2,1)S(1)}, u32[]{:S(2)}, u32[]{:S(2)}) collective-permute-start(bf16[64,1152]{1,0:T(8,128)(2,1)S(1)} %pad_maximum_fusion.10), channel_id=1, source_target_pairs={{0,2},{1,3},{2,0},{3,1},{4,6},{5,7},{6,4},{7,5},{8,10},{9,11},{10,... | collective-permute-start | bytes 442376 | tf_op jit(solution)/shard_map/ppermute | solution.py:39
  65.0 0.7 copy-start.5
  70.0 1.9 %collective-permute-start.17 = (bf16[512,384]{1,0:T(8,128)(2,1)S(1)}, bf16[512,384]{1,0:T(8,128)(2,1)S(1)}, u32[]{:S(2)}, u32[]{:S(2)}) collective-permute-start(bf16[512,384]{1,0:T(8,128)(2,1)S(1)} %convolution_convert_fusion.4), channel_id=1, source_target_pairs={{0,1},{1,0},{2,3},{3,2},{4,5},{5,4},{6,7},{7,6},{8,9},{9,8},{10,11... | collective-permute-start | bytes 1179656 | tf_op jit(solution)/shard_map/ppermute | solution.py:39
  70.1 2.8 %collective-permute-start.18 = (bf16[512,384]{1,0:T(8,128)(2,1)S(1)}, bf16[512,384]{1,0:T(8,128)(2,1)S(1)}, u32[]{:S(2)}, u32[]{:S(2)}) collective-permute-start(bf16[512,384]{1,0:T(8,128)(2,1)S(1)} %convolution_convert_fusion.3), channel_id=1, source_target_pairs={{0,1},{1,0},{2,3},{3,2},{4,5},{5,4},{6,7},{7,6},{8,9},{9,8},{10,11... | collective-permute-start | bytes 1179656 | tf_op jit(solution)/shard_map/ppermute | solution.py:39
  70.9 3.1 %collective-permute-start.19 = (bf16[384,512]{1,0:T(8,128)(2,1)S(1)}, bf16[384,512]{1,0:T(8,128)(2,1)S(1)}, u32[]{:S(2)}, u32[]{:S(2)}) collective-permute-start(bf16[384,512]{1,0:T(8,128)(2,1)S(1)} %convolution_convert_fusion.2), channel_id=1, source_target_pairs={{0,1},{1,0},{2,3},{3,2},{4,5},{5,4},{6,7},{7,6},{8,9},{9,8},{10,11... | collective-permute-start | bytes 1179656 | tf_op jit(solution)/shard_map/ppermute | solution.py:39

commit v2 on v1

--- a/solution.py
+++ b/solution.py
@@ -26,7 +26,6 @@
 def on_device(tokens, cotangent, expert_ids, gate_probs, w_gate, w_up, w_down):
     expert_count = lax.axis_size("expert")
     dp_count = lax.axis_size("dp")
-    chips = dp_count // CORES
     token_rows, model_width = tokens.shape
     top_count = expert_ids.shape[1]
     width = w_gate.shape[1]
@@ -38,21 +37,42 @@
     def to_dp(array, mask):
         return lax.ppermute(array, "dp", [(i, i ^ mask) for i in range(dp_count)])
 
+    even = expert_count & (expert_count - 1) == 0
+
     def to_expert(array, step):
-        pairs = [(i, (i + step) % expert_count) for i in range(expert_count)]
+        if even:
+            pairs = [(i, i ^ step) for i in range(expert_count)]
+        else:
+            pairs = [(i, (i + step) % expert_count) for i in range(expert_count)]
         return lax.ppermute(array, "expert", pairs)
 
+    def after(values, *others):
+        return lax.optimization_barrier((values, others))[0]
+
     own = (w_gate[0], w_up[0], w_down[0])
-    pieces = [{0: w} for w in own]
-    for mask in range(CORES, dp_count, CORES):
-        for k in range(3):
-            pieces[k][mask] = to_dp(own[k], mask)
-    for mask in range(0, dp_count, CORES):
-        for k in range(3):
-            pieces[k][mask + 1] = to_dp(pieces[k][mask], 1)
-    gate_p, up_p, down_p = pieces
-
-    wanted = (me_z + jnp.arange(expert_count, dtype=jnp.int32)) % expert_count
+    paired = lax.axis_size("groups") == 2
+    first_group = lax.axis_index("groups") == 0
+
+    def to_group(array):
+        return lax.ppermute(array, "groups", [(0, 1), (1, 0)])
+
+    def near_far(first, second):
+        return (first, second) if not paired else pick(first_group, first, second)
+
+    def pick(flag, first, second):
+        return (jnp.where(flag, first, second), jnp.where(flag, second, first))
+
+    lead = near_far(own[0], own[1])[0]
+    masks = range(CORES, dp_count, CORES)
+    lead_got = {mask: to_dp(lead, mask) for mask in masks}
+    down_got = {mask: to_dp(own[2], mask) for mask in masks}
+    other_got = {
+        mask: to_group(lead_got[mask]) if paired else to_dp(own[1], mask) for mask in masks
+    }
+    pieces = {0: own, 1: tuple(to_dp(w, 1) for w in own)}
+
+    steps = jnp.arange(expert_count, dtype=jnp.int32)
+    wanted = me_z ^ steps if even else (me_z + steps) % expert_count
     hit = expert_ids[:, :, None] == wanted[None, None, :]
     named = jnp.any(hit, axis=1)
     before = jnp.arange(token_rows)[:, None] > jnp.arange(token_rows)[None, :]
@@ -83,16 +103,31 @@
         ],
         axis=1,
     )
-    got = [send[0]] + [to_expert(send[j], j) for j in range(1, expert_count)]
+    order = [1, *range(expert_count - 1, 1, -1)]
+    send = after(send, pieces[1])
+    got = [send[0]] + [None] * (expert_count - 1)
+    for j in order:
+        got[j] = to_expert(send[j], j)
+    for mask in masks:
+        pieces[mask] = (lead_got[mask], other_got[mask], down_got[mask])
+        sibling = [to_dp(after(w, got), 1) for w in (lead_got[mask], down_got[mask])]
+        pieces[mask + 1] = (sibling[0], to_dp(other_got[mask], 1), sibling[1])
     rows_x = jnp.concatenate([g[:capacity] for g in got], axis=0)
     rows_dy = jnp.concatenate([g[capacity:] for g in got], axis=0)
 
     def cols(array, j, n=1):
         return array[:, j * width : (j + n) * width]
 
-    gate_part = sum(dot(cols(rows_x, j), gate_p[j]) for j in range(dp_count))
-    up_part = sum(dot(cols(rows_x, j), up_p[j]) for j in range(dp_count))
-    back_hidden = sum(dot_last(cols(rows_dy, j), down_p[j]) for j in range(dp_count))
+    local = range(CORES)
+    remote = range(CORES, dp_count)
+
+    def side(rows, k, js):
+        return sum(dot(cols(rows, j), pieces[j][k]) for j in js)
+
+    far = near_far(side(rows_x, 0, remote), side(rows_x, 1, remote))
+    gate_part = side(rows_x, 0, local) + far[0]
+    up_part = side(rows_x, 1, local) + far[1]
+    back_hidden = sum(dot_last(cols(rows_dy, j), pieces[j][2]) for j in range(dp_count))
     sigmoid_gate = jax.nn.sigmoid(gate_part)
     activated = gate_part * sigmoid_gate
     hidden = (activated * up_part).astype(jnp.bfloat16)
@@ -101,11 +136,14 @@
     ).astype(jnp.bfloat16)
     d_up = (back_hidden * activated).astype(jnp.bfloat16)
     expert_out = jnp.concatenate(
-        [dot(hidden, down_p[j]).astype(jnp.bfloat16) for j in range(dp_count)], axis=1
-    )
+        [dot(hidden, pieces[j][2]).astype(jnp.bfloat16) for j in range(dp_count)], axis=1
+    )
+    d_pair = {j: (d_gate, d_up) if j < CORES else near_far(d_gate, d_up) for j in range(dp_count)}
     d_rows = jnp.concatenate(
         [
-            (dot_last(d_gate, gate_p[j]) + dot_last(d_up, up_p[j])).astype(jnp.bfloat16)
+            (dot_last(d_pair[j][0], pieces[j][0]) + dot_last(d_pair[j][1], pieces[j][1])).astype(
+                jnp.bfloat16
+            )
             for j in range(dp_count)
         ],
         axis=1,
@@ -117,33 +155,38 @@
         ],
         axis=1,
     )
-    home = [back[0]] + [to_expert(back[j], -j) for j in range(1, expert_count)]
-    back_out = jnp.concatenate([h[:capacity] for h in home], axis=0)
-    back_rows = jnp.concatenate([h[capacity:] for h in home], axis=0)
+    home = [back[0]] + [None] * (expert_count - 1)
+    for j in order:
+        home[j] = to_expert(back[j], j if even else -j)
 
     trio = jnp.concatenate([hidden, d_gate, d_up], axis=1)
     pair = jnp.concatenate([rows_x, rows_dy], axis=0)
+    pair_far = after(pair, pieces[dp_count - 1])
     trios, pairs = [trio], [cols(pair, 0, CORES)]
     for mask in range(CORES, dp_count, CORES):
-        pairs.append(to_dp(cols(pair, mask, CORES), mask))
+        pairs.append(to_dp(cols(pair_far, mask, CORES), mask))
         trios.append(to_dp(trio, mask))
+    trios, pairs = after((trios, pairs), home[order[0]])
     all_trio = jnp.concatenate(trios, axis=0)
     all_x = jnp.concatenate([p[:slot_total] for p in pairs], axis=0)
     all_dy = jnp.concatenate([p[slot_total:] for p in pairs], axis=0)
     ff = w_gate.shape[2]
 
-    def reduced(part_own, part_other):
-        return (part_own + to_dp(part_other.astype(jnp.bfloat16), 1).astype(jnp.float32)).astype(
+    all_h, all_gu = all_trio[:, :ff], all_trio[:, ff:]
+
+    def reduced(half):
+        mine, theirs = half(0), half(1)
+        return (mine + to_dp(theirs.astype(jnp.bfloat16), 1).astype(jnp.float32)).astype(
             jnp.bfloat16
         )
 
-    all_h, all_g, all_u = (all_trio[:, k * ff : (k + 1) * ff] for k in range(3))
-    grad_w_gate = reduced(dot_first(cols(all_x, 0), all_g), dot_first(cols(all_x, 1), all_g))[None]
-    grad_w_up = reduced(dot_first(cols(all_x, 0), all_u), dot_first(cols(all_x, 1), all_u))[None]
-    grad_w_down = reduced(dot_first(all_h, cols(all_dy, 0)), dot_first(all_h, cols(all_dy, 1)))[
-        None
-    ]
-
+    grad_gu = reduced(lambda c: dot_first(cols(all_x, c), all_gu))
+    grad_down = reduced(lambda c: dot_first(all_h, cols(all_dy, c)))
+    home, grad_gu, grad_down = lax.optimization_barrier((home, grad_gu, grad_down))
+    grad_w_gate, grad_w_up, grad_w_down = grad_gu[None, :, :ff], grad_gu[None, :, ff:], grad_down[None]
+
+    back_out = jnp.concatenate([h[:capacity] for h in home], axis=0)
+    back_rows = jnp.concatenate([h[capacity:] for h in home], axis=0)
     table = jnp.where(chosen, prob[:, :, None], 0.0).reshape(token_rows, slot_total)
     high = table.astype(jnp.bfloat16)
     rest = table - high.astype(jnp.float32)

time: 76.1 us -> 69.1 us (0.908)
  waiting for transfers between devices: 36 us -> 29.8 us
  other arithmetic: 2.87 us -> 4.83 us
  matrix products: 12.1 us -> 10.3 us
  local copies, waits for them, and re-layouts: 3.49 us -> 2.72 us
    ppermute x6, waiting for transfers between devices: 22.5 us -> 10.7 us  [to_expert(): return lax.ppermute(array, 'expert', pairs)]
    ppermute x0 -> x1, waiting for transfers between devices: none -> 7.2 us  [to_group(): return lax.ppermute(array, 'groups', [(0, 1), (1, 0)])]
    ppermute x14 -> x12, starting transfers between devices: 9.39 us -> 7.09 us  [to_dp(): return lax.ppermute(array, 'dp', [(i, i ^ mask) for i in range(dp_count)])]
    select_n x1, other arithmetic: 0.01 us -> 1.97 us  [pick(): return (jnp.where(flag, first, second), jnp.where(flag, second, first))]
    dot_general x8 -> x6, matrix products: 4.38 us -> 2.52 us  [dot_first(): lax.dot_general(left, right, (((0,), (0,)), ((), ())), preferred_element_...]
    ppermute x0 -> x1, starting transfers between devices: none -> 1.79 us  [to_group(): return lax.ppermute(array, 'groups', [(0, 1), (1, 0)])]
    unnamed x19 -> x20, local copies, waits for them, and re-layouts: 1.92 us -> 0.16 us
    ppermute x14 -> x12, waiting for transfers between devices: 13.4 us -> 11.8 us  [to_dp(): return lax.ppermute(array, 'dp', [(i, i ^ mask) for i in range(dp_count)])]
  transfers between devices with their start and end apart: 20 -> 19, of which waited for: 8 -> 6; matrix products, arithmetic and copies ran while one was open for 16% -> 14% of each run, Pallas kernels for 0% -> 0%
where the time goes in v2:
time: 69.1 us; the launch traced here: 68.1 us
  waiting for transfers between devices  29.8 us (43%)
  starting transfers between devices  19.3 us (28%)
  matrix products  10.3 us (15%)
  other arithmetic  4.83 us (7%)
  local copies, waits for them, and re-layouts  2.72 us (4%)
  between operations  1.23 us (2%)
    ppermute x12, waiting for transfers between devices, to_dp(): return lax.ppermute(array, 'dp', [(i, i ^ mask) for i in range(dp_count)])  11.8 us
    ppermute x6, waiting for transfers between devices, to_expert(): return lax.ppermute(array, 'expert', pairs)  10.7 us
    ppermute x6, starting transfers between devices, to_expert(): return lax.ppermute(array, 'expert', pairs)  10.4 us
    ppermute x1, waiting for transfers between devices, to_group(): return lax.ppermute(array, 'groups', [(0, 1), (1, 0)])  7.2 us
    ppermute x12, starting transfers between devices, to_dp(): return lax.ppermute(array, 'dp', [(i, i ^ mask) for i in range(dp_count)])  7.09 us
    dot_general x19, matrix products, dot(): return jnp.dot(left, right, preferred_element_type=jnp.float32)  4.42 us
    dot_general x13, matrix products, dot_last(): lax.dot_general(left, right, (((1,), (1,)), ((), ())), preferred_element_...  3.33 us
    dot_general x6, matrix products, dot_first(): lax.dot_general(left, right, (((0,), (0,)), ((), ())), preferred_element_...  2.52 us
  transfers between devices with their start and end apart: 19, of which 6 were waited for; matrix products, arithmetic and copies ran while one was open for 14% of the time, Pallas kernels for 0%

profile of v2, /device:TPU:0, one launch (start us, length us, event | category | flops | bytes accessed | tf_op | source)
XLA Modules:
  0.0 68.1 jit_solution(15659947174056124196)
XLA Ops:
  0.7 0.5 collective-permute-start.2
  1.2 2.6 %collective-permute-start.10 = (bf16[384,512]{1,0:T(8,128)(2,1)}, bf16[384,512]{1,0:T(8,128)(2,1)S(1)}, u32[]{:S(2)}, u32[]{:S(2)}) collective-permute-start(bf16[384,512]{1,0:T(8,128)(2,1)} %bitcast.124), channel_id=1, source_target_pairs={{0,2},{1,3},{2,0},{3,1},{4,6},{5,7},{6,4},{7,5},{8,10},{9,11},{10,... | collective-permute-start | bytes 1179656 | tf_op jit(solution)/shard_map/ppermute | solution.py:38
  3.7 2.0 %broadcast_select_fusion = bf16[512,384]{1,0:T(8,128)(2,1)} fusion(pred[]{:T(512)S(6)} %eq.50, bf16[1,512,384]{2,1,0:T(8,128)(2,1)} %param.12, bf16[1,512,384]{2,1,0:T(8,128)(2,1)} %param.11), kind=kLoop, calls=%fused_computation.51 | loop fusion | flops 196608 | bytes 1179649 | tf_op jit(solution)/shard_map/jit(_where)/select_n | solution.py:63
  5.9 0.4 collective-permute-start.1
  6.4 0.1 fusion.48
  6.6 1.1 %constant_dynamic-slice_fusion.11 = (bf16[128,512]{1,0:T(8,128)(2,1)S(1)}, bf16[128,512]{1,0:T(8,128)(2,1)S(1)}, bf16[128,512]{1,0:T(8,128)(2,1)S(1)}, bf16[128,512]{1,0:T(8,128)(2,1)S(1)}) fusion(bf16[128,2048]{1,0:T(8,128)(2,1)} %param.8, s32[]{:T(128)S(6)} %select_n.77, s32[]{:T(128)S(6)} %select_n.78, s32[]{:T(128)S(6)} %select_n.80, s32[]{:T(128)S(6)} %select_n.79), kind=kLoop, calls=%fused_computation.156 | loop fusion | bytes 1048592 | tf_op jit(solution)/shard_map/dynamic_slice | solution.py:89
  8.0 0.2 convolution_convert_fusion
  8.2 0.2 convolution_convert_fusion.1
  8.5 2.1 %collective-permute-start.3 = (bf16[32,2048]{1,0:T(8,128)(2,1)S(1)}, bf16[32,2048]{1,0:T(8,128)(2,1)S(1)}, u32[]{:S(2)}, u32[]{:S(2)}) collective-permute-start(bf16[32,2048]{1,0:T(8,128)(2,1)S(1)} %get-tuple-element.55), channel_id=1, source_target_pairs={{0,4},{4,0},{8,12},{12,8},{1,5},{5,1},{9,13},{13,9},{2,6},{6,2},{1... | collective-permute-start | bytes 393224 | tf_op jit(solution)/shard_map/ppermute | solution.py:47
  10.6 2.6 %collective-permute-start.4 = (bf16[32,2048]{1,0:T(8,128)(2,1)S(1)}, bf16[32,2048]{1,0:T(8,128)(2,1)S(1)}, u32[]{:S(2)}, u32[]{:S(2)}) collective-permute-start(bf16[32,2048]{1,0:T(8,128)(2,1)S(1)} %get-tuple-element.54), channel_id=1, source_target_pairs={{0,8},{4,12},{8,0},{12,4},{1,9},{5,13},{9,1},{13,5},{2,10},{6,14},... | collective-permute-start | bytes 393224 | tf_op jit(solution)/shard_map/ppermute | solution.py:47
  13.2 8.9 %collective-permute-done.6 = bf16[512,384]{1,0:T(8,128)(2,1)S(1)} collective-permute-done((bf16[512,384]{1,0:T(8,128)(2,1)}, bf16[512,384]{1,0:T(8,128)(2,1)S(1)}, u32[]{:S(2)}, u32[]{:S(2)}) %collective-permute-start.6) | collective-permute-done | bytes 393248 | tf_op jit(solution)/shard_map/ppermute | solution.py:38
  22.1 1.8 %collective-permute-start.8 = (bf16[512,384]{1,0:T(8,128)(2,1)S(1)}, bf16[512,384]{1,0:T(8,128)(2,1)S(1)}, u32[]{:S(2)}, u32[]{:S(2)}) collective-permute-start(bf16[512,384]{1,0:T(8,128)(2,1)S(1)} %collective-permute-done.6), channel_id=1, source_target_pairs={{0,16},{16,0},{1,17},{17,1},{2,18},{18,2},{3,19},{19,3},{4,20},{20... | collective-permute-start | bytes 1179656 | tf_op jit(solution)/shard_map/ppermute | solution.py:57
  24.0 0.5 collective-permute-start.11
  24.7 0.3 fusion.45
  25.0 0.3 convolution_add_fusion.7
  25.3 0.2 fusion.57
  25.5 0.2 fusion.55
  25.8 7.2 %collective-permute-done.8 = bf16[512,384]{1,0:T(8,128)(2,1)S(1)} collective-permute-done((bf16[512,384]{1,0:T(8,128)(2,1)S(1)}, bf16[512,384]{1,0:T(8,128)(2,1)S(1)}, u32[]{:S(2)}, u32[]{:S(2)}) %collective-permute-start.8) | collective-permute-done | bytes 393248 | tf_op jit(solution)/shard_map/ppermute | solution.py:57
  33.0 0.2 fusion.52
  33.2 0.2 fusion.50
  33.4 0.3 fusion.42
  33.7 0.2 convolution_add_fusion.10
  33.9 0.8 %collective-permute-done.9 = bf16[512,384]{1,0:T(8,128)(2,1)S(1)} collective-permute-done((bf16[512,384]{1,0:T(8,128)(2,1)S(1)}, bf16[512,384]{1,0:T(8,128)(2,1)S(1)}, u32[]{:S(2)}, u32[]{:S(2)}) %collective-permute-start.9) | collective-permute-done | bytes 393248 | tf_op jit(solution)/shard_map/ppermute | solution.py:38
  34.7 0.2 convolution_add_fusion.9
  34.9 0.2 fusion.8
  35.1 0.2 select_add_fusion
  35.3 0.3 multiply_convert_fusion
  35.6 0.2 fusion.83
  35.9 0.2 convolution_convert_fusion.7
  36.1 0.2 fusion.4
  36.3 1.6 %collective-permute-start.15 = (bf16[64,1152]{1,0:T(8,128)(2,1)S(1)}, bf16[64,1152]{1,0:T(8,128)(2,1)S(1)}, u32[]{:S(2)}, u32[]{:S(2)}) collective-permute-start(bf16[64,1152]{1,0:T(8,128)(2,1)S(1)} %pad_maximum_fusion.10), channel_id=1, source_target_pairs={{0,2},{1,3},{2,0},{3,1},{4,6},{5,7},{6,4},{7,5},{8,10},{9,11},{10,... | collective-permute-start | bytes 442376 | tf_op jit(solution)/shard_map/ppermute | solution.py:38
  38.0 0.5 collective-permute-start.16
  38.5 0.2 fusion.68
  38.7 0.2 fusion.69
  39.0 0.2 fusion.96
  39.2 0.2 fusion.7
  39.5 0.2 fusion.6
  39.7 0.2 fusion.5
  40.0 0.2 convolution_convert_fusion.4
  40.2 0.2 convolution_convert_fusion.5
  40.4 0.2 convolution_convert_fusion.6
  40.7 1.7 %collective-permute-start.12 = (bf16[32,2048]{1,0:T(8,128)(2,1)S(1)}, bf16[32,2048]{1,0:T(8,128)(2,1)S(1)}, u32[]{:S(2)}, u32[]{:S(2)}) collective-permute-start(bf16[32,2048]{1,0:T(8,128)(2,1)S(1)} %get-tuple-element.48), channel_id=1, source_target_pairs={{0,4},{4,0},{8,12},{12,8},{1,5},{5,1},{9,13},{13,9},{2,6},{6,2},{1... | collective-permute-start | bytes 393224 | tf_op jit(solution)/shard_map/ppermute | solution.py:47
  42.4 3.3 %collective-permute-done.12 = bf16[32,2048]{1,0:T(8,128)(2,1)S(1)} collective-permute-done((bf16[32,2048]{1,0:T(8,128)(2,1)S(1)}, bf16[32,2048]{1,0:T(8,128)(2,1)S(1)}, u32[]{:S(2)}, u32[]{:S(2)}) %collective-permute-start.12) | collective-permute-done | bytes 131104 | tf_op jit(solution)/shard_map/ppermute | solution.py:47
  45.7 2.1 %collective-permute-done.16 = bf16[128,1024]{1,0:T(8,128)(2,1)S(1)} collective-permute-done((bf16[128,1024]{1,0:T(8,128)(2,1)S(1)}, bf16[128,1024]{1,0:T(8,128)(2,1)S(1)}, u32[]{:S(2)}, u32[]{:S(2)}) %collective-permute-start.16) | collective-permute-done | bytes 262176 | tf_op jit(solution)/shard_map/ppermute | solution.py:38
  48.0 0.4 convolution_convert_fusion.2
  48.5 0.3 convolution_convert_fusion.3
  48.7 0.6 collective-permute-start.18
  49.3 2.7 %collective-permute-start.13 = (bf16[32,2048]{1,0:T(8,128)(2,1)S(1)}, bf16[32,2048]{1,0:T(8,128)(2,1)S(1)}, u32[]{:S(2)}, u32[]{:S(2)}) collective-permute-start(bf16[32,2048]{1,0:T(8,128)(2,1)S(1)} %get-tuple-element.49), channel_id=1, source_target_pairs={{0,8},{4,12},{8,0},{12,4},{1,9},{5,13},{9,1},{13,5},{2,10},{6,14},... | collective-permute-start | bytes 393224 | tf_op jit(solution)/shard_map/ppermute | solution.py:47
  52.0 1.3 %collective-permute-start.14 = (bf16[32,2048]{1,0:T(8,128)(2,1)S(1)}, bf16[32,2048]{1,0:T(8,128)(2,1)S(1)}, u32[]{:S(2)}, u32[]{:S(2)}) collective-permute-start(bf16[32,2048]{1,0:T(8,128)(2,1)S(1)} %get-tuple-element.46), channel_id=1, source_target_pairs={{0,12},{4,8},{8,4},{12,0},{1,13},{5,9},{9,5},{13,1},{2,14},{6,10},... | collective-permute-start | bytes 393224 | tf_op jit(solution)/shard_map/ppermute | solution.py:47
  53.3 1.0 %add_convert_fusion.1 = bf16[384,512]{1,0:T(8,128)(2,1)} fusion(bf16[384,512]{1,0:T(8,128)(2,1)S(1)} %collective-permute-done.18, bf16[64,1024]{1,0:T(8,128)(2,1)S(1)} %get-tuple-element.64, bf16[64,1024]{1,0:T(8,128)(2,1)S(1)} %get-tuple-element.66, bf16[128,1152]{1,0:T(8,128)(2,1)S(1)} %constant_dynamic-update-slice_fusion.8), kind=kOutput, calls=%fused_computation.31 | convolution fusion | flops 51183616 | bytes 1146880 | tf_op jit(solution)/shard_map/dot_general | solution.py:11
  54.4 0.4 add_convert_fusion
  54.8 7.4 %collective-permute-done.13 = bf16[32,2048]{1,0:T(8,128)(2,1)S(1)} collective-permute-done((bf16[32,2048]{1,0:T(8,128)(2,1)S(1)}, bf16[32,2048]{1,0:T(8,128)(2,1)S(1)}, u32[]{:S(2)}, u32[]{:S(2)}) %collective-permute-start.13) | collective-permute-done | bytes 131104 | tf_op jit(solution)/shard_map/ppermute | solution.py:47
  62.2 0.3 select_reduce_fusion
  62.6 0.7 fusion.71
  63.4 0.3 fusion.89
  63.7 0.3 fusion.87
  64.1 0.3 fusion.86
  64.4 0.3 fusion.88
  64.7 1.0 %slice_bitcast_fusion = (bf16[1,512,384]{2,1,0:T(8,128)(2,1)}, bf16[1,512,384]{2,1,0:T(8,128)(2,1)}) fusion(bf16[512,768]{1,0:T(8,128)(2,1)S(1)} %add_convert_fusion), kind=kLoop, calls=%fused_computation.49 | loop fusion | bytes 1572864 | tf_op jit(solution)/shard_map/broadcast_in_dim | solution.py:186
  65.7 0.3 fusion.3
  66.0 0.3 fusion.2
  66.3 0.1 constant_dynamic-slice_fusion.3
  66.4 0.8 %pad_maximum_fusion.2 = bf16[128,2048]{1,0:T(8,128)(2,1)} fusion(bf16[128,512]{1,0:T(8,128)(2,1)S(1)} %get-tuple-element.92, bf16[128,512]{1,0:T(8,128)(2,1)S(1)} %get-tuple-element.91, bf16[128,512]{1,0:T(8,128)(2,1)S(1)} %get-tuple-element.90, bf16[128,512]{1,0:T(8,128)(2,1)S(1)} %get-tuple-element.93), kind=kLoop, calls=%fused_computation.47 | loop fusion | flops 2097152 | bytes 1048576 | tf_op jit(solution)/shard_map/concatenate | solution.py:87
  67.3 0.8 %pad_maximum_fusion.3 = bf16[128,2048]{1,0:T(8,128)(2,1)} fusion(bf16[128,512]{1,0:T(8,128)(2,1)S(1)} %get-tuple-element.39, bf16[128,512]{1,0:T(8,128)(2,1)S(1)} %get-tuple-element.40, bf16[128,512]{1,0:T(8,128)(2,1)S(1)} %get-tuple-element.41, bf16[128,512]{1,0:T(8,128)(2,1)S(1)} %get-tuple-element.38), kind=kLoop, calls=%fused_computation.48 | loop fusion | flops 2097152 | bytes 1048576 | tf_op jit(solution)/shard_map/concatenate | solution.py:87
  (66 shorter events, 1.3 us)
Async XLA Ops:
  0.6 5.3 %copy-start.1 = (bf16[1,512,384]{2,1,0:T(8,128)(2,1)S(1)}, bf16[1,512,384]{2,1,0:T(8,128)(2,1)}, u32[]{:S(2)}) copy-start(bf16[1,512,384]{2,1,0:T(8,128)(2,1)} %param.12) | copy-start | bytes 1179652
  0.6 5.2 %copy-start = (bf16[1,512,384]{2,1,0:T(8,128)(2,1)S(1)}, bf16[1,512,384]{2,1,0:T(8,128)(2,1)}, u32[]{:S(2)}) copy-start(bf16[1,512,384]{2,1,0:T(8,128)(2,1)} %param.11) | copy-start | bytes 1179652
  0.7 5.7 %copy-start.4 = (s32[128,8]{0,1:T(8,128)S(1)}, s32[128,8]{0,1:T(8,128)}, u32[]{:S(2)}) copy-start(s32[128,8]{0,1:T(8,128)} %param.9) | copy-start | bytes 12292
  0.7 7.8 %collective-permute-start.2 = (bf16[384,512]{1,0:T(8,128)(2,1)}, bf16[384,512]{1,0:T(8,128)(2,1)S(1)}, u32[]{:S(2)}, u32[]{:S(2)}) collective-permute-start(bf16[384,512]{1,0:T(8,128)(2,1)} %bitcast.123), channel_id=1, source_target_pairs={{0,1},{1,0},{2,3},{3,2},{4,5},{5,4},{6,7},{7,6},{8,9},{9,8},{10,11... | collective-permute-start | bytes 1179656 | tf_op jit(solution)/shard_map/ppermute | solution.py:38
  1.2 22.9 %collective-permute-start.10 = (bf16[384,512]{1,0:T(8,128)(2,1)}, bf16[384,512]{1,0:T(8,128)(2,1)S(1)}, u32[]{:S(2)}, u32[]{:S(2)}) collective-permute-start(bf16[384,512]{1,0:T(8,128)(2,1)} %bitcast.124), channel_id=1, source_target_pairs={{0,2},{1,3},{2,0},{3,1},{4,6},{5,7},{6,4},{7,5},{8,10},{9,11},{10,... | collective-permute-start | bytes 1179656 | tf_op jit(solution)/shard_map/ppermute | solution.py:38
  3.7 4.1 %copy-start.3 = (bf16[128,2048]{1,0:T(8,128)(2,1)S(1)}, bf16[128,2048]{1,0:T(8,128)(2,1)}, u32[]{:S(2)}) copy-start(bf16[128,2048]{1,0:T(8,128)(2,1)} %param.7) | copy-start | bytes 1572868
  5.7 16.4 %collective-permute-start.6 = (bf16[512,384]{1,0:T(8,128)(2,1)}, bf16[512,384]{1,0:T(8,128)(2,1)S(1)}, u32[]{:S(2)}, u32[]{:S(2)}) collective-permute-start(bf16[512,384]{1,0:T(8,128)(2,1)} %broadcast_select_fusion), channel_id=1, source_target_pairs={{0,2},{1,3},{2,0},{3,1},{4,6},{5,7},{6,4},{7,5},{8,10},{9,11},{10,... | collective-permute-start | bytes 1179656 | tf_op jit(solution)/shard_map/ppermute | solution.py:38
  5.8 2.6 %collective-permute-start = (bf16[512,384]{1,0:T(8,128)(2,1)S(1)}, bf16[512,384]{1,0:T(8,128)(2,1)S(1)}, u32[]{:S(2)}, u32[]{:S(2)}) collective-permute-start(bf16[512,384]{1,0:T(8,128)(2,1)S(1)} %bitcast.121), channel_id=1, source_target_pairs={{0,1},{1,0},{2,3},{3,2},{4,5},{5,4},{6,7},{7,6},{8,9},{9,8},{10,11... | collective-permute-start | bytes 1179656 | tf_op jit(solution)/shard_map/ppermute | solution.py:38
  5.9 2.6 %collective-permute-start.1 = (bf16[512,384]{1,0:T(8,128)(2,1)S(1)}, bf16[512,384]{1,0:T(8,128)(2,1)S(1)}, u32[]{:S(2)}, u32[]{:S(2)}) collective-permute-start(bf16[512,384]{1,0:T(8,128)(2,1)S(1)} %bitcast.122), channel_id=1, source_target_pairs={{0,1},{1,0},{2,3},{3,2},{4,5},{5,4},{6,7},{7,6},{8,9},{9,8},{10,11... | collective-permute-start | bytes 1179656 | tf_op jit(solution)/shard_map/ppermute | solution.py:38
  8.5 15.4 %collective-permute-start.3 = (bf16[32,2048]{1,0:T(8,128)(2,1)S(1)}, bf16[32,2048]{1,0:T(8,128)(2,1)S(1)}, u32[]{:S(2)}, u32[]{:S(2)}) collective-permute-start(bf16[32,2048]{1,0:T(8,128)(2,1)S(1)} %get-tuple-element.55), channel_id=1, source_target_pairs={{0,4},{4,0},{8,12},{12,8},{1,5},{5,1},{9,13},{13,9},{2,6},{6,2},{1... | collective-permute-start | bytes 393224 | tf_op jit(solution)/shard_map/ppermute | solution.py:47
  10.6 13.3 %collective-permute-start.4 = (bf16[32,2048]{1,0:T(8,128)(2,1)S(1)}, bf16[32,2048]{1,0:T(8,128)(2,1)S(1)}, u32[]{:S(2)}, u32[]{:S(2)}) collective-permute-start(bf16[32,2048]{1,0:T(8,128)(2,1)S(1)} %get-tuple-element.54), channel_id=1, source_target_pairs={{0,8},{4,12},{8,0},{12,4},{1,9},{5,13},{9,1},{13,5},{2,10},{6,14},... | collective-permute-start | bytes 393224 | tf_op jit(solution)/shard_map/ppermute | solution.py:47
  13.2 10.7 %collective-permute-start.5 = (bf16[32,2048]{1,0:T(8,128)(2,1)S(1)}, bf16[32,2048]{1,0:T(8,128)(2,1)S(1)}, u32[]{:S(2)}, u32[]{:S(2)}) collective-permute-start(bf16[32,2048]{1,0:T(8,128)(2,1)S(1)} %get-tuple-element.53), channel_id=1, source_target_pairs={{0,12},{4,8},{8,4},{12,0},{1,13},{5,9},{9,5},{13,1},{2,14},{6,10},... | collective-permute-start | bytes 393224 | tf_op jit(solution)/shard_map/ppermute | solution.py:47
  22.1 10.9 %collective-permute-start.8 = (bf16[512,384]{1,0:T(8,128)(2,1)S(1)}, bf16[512,384]{1,0:T(8,128)(2,1)S(1)}, u32[]{:S(2)}, u32[]{:S(2)}) collective-permute-start(bf16[512,384]{1,0:T(8,128)(2,1)S(1)} %collective-permute-done.6), channel_id=1, source_target_pairs={{0,16},{16,0},{1,17},{17,1},{2,18},{18,2},{3,19},{19,3},{4,20},{20... | collective-permute-start | bytes 1179656 | tf_op jit(solution)/shard_map/ppermute | solution.py:57
  23.9 9.3 %collective-permute-start.7 = (bf16[512,384]{1,0:T(8,128)(2,1)S(1)}, bf16[512,384]{1,0:T(8,128)(2,1)S(1)}, u32[]{:S(2)}, u32[]{:S(2)}) collective-permute-start(bf16[512,384]{1,0:T(8,128)(2,1)S(1)} %collective-permute-done.6), channel_id=1, source_target_pairs={{0,1},{1,0},{2,3},{3,2},{4,5},{5,4},{6,7},{7,6},{8,9},{9,8},{10,11... | collective-permute-start | bytes 1179656 | tf_op jit(solution)/shard_map/ppermute | solution.py:38
  24.0 1.0 %copy-start.2 = (bf16[1,384,512]{2,1,0:T(8,128)(2,1)S(1)}, bf16[1,384,512]{2,1,0:T(8,128)(2,1)}, u32[]{:S(2)}) copy-start(bf16[1,384,512]{2,1,0:T(8,128)(2,1)} %param.13) | copy-start | bytes 1179652
  24.0 9.3 %collective-permute-start.11 = (bf16[384,512]{1,0:T(8,128)(2,1)S(1)}, bf16[384,512]{1,0:T(8,128)(2,1)S(1)}, u32[]{:S(2)}, u32[]{:S(2)}) collective-permute-start(bf16[384,512]{1,0:T(8,128)(2,1)S(1)} %collective-permute-done.10), channel_id=1, source_target_pairs={{0,1},{1,0},{2,3},{3,2},{4,5},{5,4},{6,7},{7,6},{8,9},{9,8},{10,11... | collective-permute-start | bytes 1179656 | tf_op jit(solution)/shard_map/ppermute | solution.py:38
  33.0 1.7 %collective-permute-start.9 = (bf16[512,384]{1,0:T(8,128)(2,1)S(1)}, bf16[512,384]{1,0:T(8,128)(2,1)S(1)}, u32[]{:S(2)}, u32[]{:S(2)}) collective-permute-start(bf16[512,384]{1,0:T(8,128)(2,1)S(1)} %collective-permute-done.8), channel_id=1, source_target_pairs={{0,1},{1,0},{2,3},{3,2},{4,5},{5,4},{6,7},{7,6},{8,9},{9,8},{10,11... | collective-permute-start | bytes 1179656 | tf_op jit(solution)/shard_map/ppermute | solution.py:38
  36.3 9.4 %collective-permute-start.15 = (bf16[64,1152]{1,0:T(8,128)(2,1)S(1)}, bf16[64,1152]{1,0:T(8,128)(2,1)S(1)}, u32[]{:S(2)}, u32[]{:S(2)}) collective-permute-start(bf16[64,1152]{1,0:T(8,128)(2,1)S(1)} %pad_maximum_fusion.10), channel_id=1, source_target_pairs={{0,2},{1,3},{2,0},{3,1},{4,6},{5,7},{6,4},{7,5},{8,10},{9,11},{10,... | collective-permute-start | bytes 442376 | tf_op jit(solution)/shard_map/ppermute | solution.py:38
  38.0 9.9 %collective-permute-start.16 = (bf16[128,1024]{1,0:T(8,128)(2,1)S(1)}, bf16[128,1024]{1,0:T(8,128)(2,1)S(1)}, u32[]{:S(2)}, u32[]{:S(2)}) collective-permute-start(bf16[128,1024]{1,0:T(8,128)(2,1)S(1)} %slice.177), channel_id=1, source_target_pairs={{0,2},{1,3},{2,0},{3,1},{4,6},{5,7},{6,4},{7,5},{8,10},{9,11},{10,... | collective-permute-start | bytes 786440 | tf_op jit(solution)/shard_map/ppermute | solution.py:38
  40.7 5.1 %collective-permute-start.12 = (bf16[32,2048]{1,0:T(8,128)(2,1)S(1)}, bf16[32,2048]{1,0:T(8,128)(2,1)S(1)}, u32[]{:S(2)}, u32[]{:S(2)}) collective-permute-start(bf16[32,2048]{1,0:T(8,128)(2,1)S(1)} %get-tuple-element.48), channel_id=1, source_target_pairs={{0,4},{4,0},{8,12},{12,8},{1,5},{5,1},{9,13},{13,9},{2,6},{6,2},{1... | collective-permute-start | bytes 393224 | tf_op jit(solution)/shard_map/ppermute | solution.py:47
  48.4 6.0 %collective-permute-start.17 = (bf16[512,768]{1,0:T(8,128)(2,1)S(1)}, bf16[512,768]{1,0:T(8,128)(2,1)S(1)}, u32[]{:S(2)}, u32[]{:S(2)}) collective-permute-start(bf16[512,768]{1,0:T(8,128)(2,1)S(1)} %convolution_convert_fusion.2), channel_id=1, source_target_pairs={{0,1},{1,0},{2,3},{3,2},{4,5},{5,4},{6,7},{7,6},{8,9},{9,8},{10,11... | collective-permute-start | bytes 2359304 | tf_op jit(solution)/shard_map/ppermute | solution.py:38
  48.7 4.6 %collective-permute-start.18 = (bf16[384,512]{1,0:T(8,128)(2,1)S(1)}, bf16[384,512]{1,0:T(8,128)(2,1)S(1)}, u32[]{:S(2)}, u32[]{:S(2)}) collective-permute-start(bf16[384,512]{1,0:T(8,128)(2,1)S(1)} %convolution_convert_fusion.3), channel_id=1, source_target_pairs={{0,1},{1,0},{2,3},{3,2},{4,5},{5,4},{6,7},{7,6},{8,9},{9,8},{10,11... | collective-permute-start | bytes 1179656 | tf_op jit(solution)/shard_map/ppermute | solution.py:38
  49.3 12.9 %collective-permute-start.13 = (bf16[32,2048]{1,0:T(8,128)(2,1)S(1)}, bf16[32,2048]{1,0:T(8,128)(2,1)S(1)}, u32[]{:S(2)}, u32[]{:S(2)}) collective-permute-start(bf16[32,2048]{1,0:T(8,128)(2,1)S(1)} %get-tuple-element.49), channel_id=1, source_target_pairs={{0,8},{4,12},{8,0},{12,4},{1,9},{5,13},{9,1},{13,5},{2,10},{6,14},... | collective-permute-start | bytes 393224 | tf_op jit(solution)/shard_map/ppermute | solution.py:47
  52.0 10.2 %collective-permute-start.14 = (bf16[32,2048]{1,0:T(8,128)(2,1)S(1)}, bf16[32,2048]{1,0:T(8,128)(2,1)S(1)}, u32[]{:S(2)}, u32[]{:S(2)}) collective-permute-start(bf16[32,2048]{1,0:T(8,128)(2,1)S(1)} %get-tuple-element.46), channel_id=1, source_target_pairs={{0,12},{4,8},{8,4},{12,0},{1,13},{5,9},{9,5},{13,1},{2,14},{6,10},... | collective-permute-start | bytes 393224 | tf_op jit(solution)/shard_map/ppermute | solution.py:47
  54.8 7.8 %copy-start.5 = (f32[128,8]{0,1:T(8,128)S(1)}, f32[128,8]{0,1:T(8,128)}, u32[]{:S(2)}) copy-start(f32[128,8]{0,1:T(8,128)} %param.10) | copy-start | bytes 12292

commit v3 on v2

--- a/solution.py
+++ b/solution.py
@@ -1,6 +1,8 @@
 import jax
 import jax.numpy as jnp
 from jax import lax
+from jax.experimental import pallas as pl
+from jax.experimental.pallas import tpu as pltpu
 from jax.sharding import PartitionSpec as P
 
 EXPERTS = 128
@@ -21,6 +23,31 @@
 
 def dot(left, right):
     return jnp.dot(left, right, preferred_element_type=jnp.float32)
+
+
+def choose_kernel(flag_ref, first_ref, second_ref, out_ref, sem):
+    @pl.when(flag_ref[0] == 0)
+    def _():
+        copy = pltpu.make_async_copy(first_ref, out_ref, sem)
+        copy.start()
+        copy.wait()
+
+    @pl.when(flag_ref[0] != 0)
+    def _():
+        copy = pltpu.make_async_copy(second_ref, out_ref, sem)
+        copy.start()
+        copy.wait()
+
+
+def choose(flag, first, second):
+    anywhere = pl.BlockSpec(memory_space=pl.ANY)
+    return pl.pallas_call(
+        choose_kernel,
+        out_shape=jax.ShapeDtypeStruct(first.shape, first.dtype),
+        in_specs=[pl.BlockSpec(memory_space=pltpu.SMEM), anywhere, anywhere],
+        out_specs=anywhere,
+        scratch_shapes=[pltpu.SemaphoreType.DMA],
+    )(flag.reshape(1), first, second)
 
 
 def on_device(tokens, cotangent, expert_ids, gate_probs, w_gate, w_up, w_down):
@@ -62,7 +89,8 @@
     def pick(flag, first, second):
         return (jnp.where(flag, first, second), jnp.where(flag, second, first))
 
-    lead = near_far(own[0], own[1])[0]
+    lead = choose(lax.axis_index("groups"), own[0], own[1]) if paired else own[0]
+    own = after(own, lead)
     masks = range(CORES, dp_count, CORES)
     lead_got = {mask: to_dp(lead, mask) for mask in masks}
     down_got = {mask: to_dp(own[2], mask) for mask in masks}
@@ -166,7 +194,7 @@
     for mask in range(CORES, dp_count, CORES):
         pairs.append(to_dp(cols(pair_far, mask, CORES), mask))
         trios.append(to_dp(trio, mask))
-    trios, pairs = after((trios, pairs), home[order[0]])
+    home, trios, pairs = lax.optimization_barrier((home, trios, pairs))
     all_trio = jnp.concatenate(trios, axis=0)
     all_x = jnp.concatenate([p[:slot_total] for p in pairs], axis=0)
     all_dy = jnp.concatenate([p[slot_total:] for p in pairs], axis=0)
@@ -182,7 +210,6 @@
 
     grad_gu = reduced(lambda c: dot_first(cols(all_x, c), all_gu))
     grad_down = reduced(lambda c: dot_first(all_h, cols(all_dy, c)))
-    home, grad_gu, grad_down = lax.optimization_barrier((home, grad_gu, grad_down))
     grad_w_gate, grad_w_up, grad_w_down = grad_gu[None, :, :ff], grad_gu[None, :, ff:], grad_down[None]
 
     back_out = jnp.concatenate([h[:capacity] for h in home], axis=0)

time: 69.1 us -> 73.3 us (1.061)
  Pallas kernels: 0 us -> 13 us
  waiting for transfers between devices: 29.8 us -> 19.5 us
  matrix products: 10.3 us -> 13.2 us
  other arithmetic: 4.83 us -> 2.86 us
  local copies, waits for them, and re-layouts: 2.72 us -> 4.68 us
  starting transfers between devices: 19.3 us -> 18.5 us
    pallas_call x0 -> x1, Pallas kernels: none -> 13 us  [choose(): pl.pallas_call(choose_kernel, out_shape=jax.ShapeDtypeStruct(first.shape,...]
    ppermute x12, waiting for transfers between devices: 11.8 us -> 0.83 us  [to_dp(): return lax.ppermute(array, 'dp', [(i, i ^ mask) for i in range(dp_count)])]
    ppermute x6, waiting for transfers between devices: 10.7 us -> 18.6 us  [to_expert(): return lax.ppermute(array, 'expert', pairs)]
    ppermute x1, waiting for transfers between devices: 7.2 us -> 0.01 us  [to_group(): return lax.ppermute(array, 'groups', [(0, 1), (1, 0)])]
    select_n x1 -> x0, other arithmetic: 1.97 us -> none  [pick(): return (jnp.where(flag, first, second), jnp.where(flag, second, first))]
    unnamed x20 -> x38, local copies, waits for them, and re-layouts: 0.16 us -> 1.32 us
    dot_general x13, matrix products: 3.33 us -> 4.32 us  [dot_last(): lax.dot_general(left, right, (((1,), (1,)), ((), ())), preferred_element_...]
    dot_general x6, matrix products: 2.52 us -> 3.51 us  [dot_first(): lax.dot_general(left, right, (((0,), (0,)), ((), ())), preferred_element_...]
  transfers between devices with their start and end apart: 19 -> 19, of which waited for: 6 -> 6; matrix products, arithmetic and copies ran while one was open for 14% -> 17% of each run, Pallas kernels for 0% -> 0%
where the time goes in v3:
time: 73.3 us; the launch traced here: 73 us
  waiting for transfers between devices  19.5 us (27%)
  starting transfers between devices  18.5 us (25%)
  matrix products  13.2 us (18%)
  Pallas kernels  13 us (18%)
  local copies, waits for them, and re-layouts  4.68 us (6%)
  other arithmetic  2.86 us (4%)
  between operations  1.34 us (2%)
    ppermute x6, waiting for transfers between devices, to_expert(): return lax.ppermute(array, 'expert', pairs)  18.6 us
    pallas_call x1, Pallas kernels, choose(): pl.pallas_call(choose_kernel, out_shape=jax.ShapeDtypeStruct(first.shape,...  13 us
    ppermute x6, starting transfers between devices, to_expert(): return lax.ppermute(array, 'expert', pairs)  9.54 us
    ppermute x12, starting transfers between devices, to_dp(): return lax.ppermute(array, 'dp', [(i, i ^ mask) for i in range(dp_count)])  7.11 us
    dot_general x19, matrix products, dot(): return jnp.dot(left, right, preferred_element_type=jnp.float32)  5.4 us
    dot_general x13, matrix products, dot_last(): lax.dot_general(left, right, (((1,), (1,)), ((), ())), preferred_element_...  4.32 us
    dot_general x6, matrix products, dot_first(): lax.dot_general(left, right, (((0,), (0,)), ((), ())), preferred_element_...  3.51 us
    dynamic_slice x3, local copies, waits for them, and re-layouts, turned(): lax.dynamic_slice_in_dim(array, (me_d ^ j) * width, width, 1)  2.12 us
  transfers between devices with their start and end apart: 19, of which 6 were waited for; matrix products, arithmetic and copies ran while one was open for 17% of the time, Pallas kernels for 0%

profile of v3, /device:TPU:0, one launch (start us, length us, event | category | flops | bytes accessed | tf_op | source)
XLA Modules:
  0.0 73.0 jit_solution(16596032813538894945)
XLA Ops:
  0.7 13.0 %shard_map.118 = bf16[512,384]{1,0:T(8,128)(2,1)} custom-call(s32[1]{0:T(128)} %bitcast.8.flag_ref, bf16[512,384]{1,0:T(8,128)(2,1)} %bitcast.115, bf16[512,384]{1,0:T(8,128)(2,1)} %bitcast.119), custom_call_target="tpu_custom_call" | custom-call | tf_op jit(solution)/shard_map/pallas_call | solution.py:44
  13.7 3.0 %collective-permute-start.6 = (bf16[512,384]{1,0:T(8,128)(2,1)}, bf16[512,384]{1,0:T(8,128)(2,1)S(1)}, u32[]{:S(2)}, u32[]{:S(2)}) collective-permute-start(bf16[512,384]{1,0:T(8,128)(2,1)} %shard_map.118), channel_id=1, source_target_pairs={{0,2},{1,3},{2,0},{3,1},{4,6},{5,7},{6,4},{7,5},{8,10},{9,11},{10,... | collective-permute-start | bytes 1179656 | tf_op jit(solution)/shard_map/ppermute | solution.py:65
  16.9 0.3 collective-permute-start
  17.4 0.6 copy-done.13
  18.3 1.1 %constant_dynamic-slice_fusion.11 = (bf16[128,512]{1,0:T(8,128)(2,1)S(1)}, bf16[128,512]{1,0:T(8,128)(2,1)S(1)}, bf16[128,512]{1,0:T(8,128)(2,1)S(1)}, bf16[128,512]{1,0:T(8,128)(2,1)S(1)}) fusion(bf16[128,2048]{1,0:T(8,128)(2,1)} %param.8, s32[]{:T(128)S(6)} %select_n.69, s32[]{:T(128)S(6)} %select_n.70, s32[]{:T(128)S(6)} %select_n.72, s32[]{:T(128)S(6)} %select_n.71), kind=kLoop, calls=%fused_computation.156 | loop fusion | bytes 1048592 | tf_op jit(solution)/shard_map/dynamic_slice | solution.py:117
  19.5 0.8 %constant_dynamic-slice_fusion.15 = (bf16[128,512]{1,0:T(8,128)(2,1)}, bf16[128,512]{1,0:T(8,128)(2,1)}, bf16[128,512]{1,0:T(8,128)(2,1)}, bf16[128,512]{1,0:T(8,128)(2,1)}) fusion(bf16[128,2048]{1,0:T(8,128)(2,1)S(1)} %copy-done.3, s32[]{:T(128)S(6)} %select_n.69, s32[]{:T(128)S(6)} %select_n.70, s32[]{:T(128)S(6)} %select_n.72, s32[]{:T(128)S(6)} %select_n.71), kind=kLoop, calls=%fused_computation.160 | loop fusion | bytes 1048592 | tf_op jit(solution)/shard_map/dynamic_slice | solution.py:117
  20.5 0.6 copy-done.11
  21.0 0.2 convolution_convert_fusion
  21.3 1.2 %convolution_convert_fusion.1 = bf16[64,2048]{1,0:T(8,128)(2,1)S(1)} fusion(pred[128,64]{0,1:T(32,128)(4,1)} %copy-done.11, bf16[128,512]{1,0:T(8,128)(2,1)} %get-tuple-element.60, bf16[128,512]{1,0:T(8,128)(2,1)} %get-tuple-element.61, bf16[128,512]{1,0:T(8,128)(2,1)S(1)} %copy-done.9, bf16[128,512]{1,0:T(8,128)(2,1)S(1)} %copy-done.8), kind=kOutput, calls=%fused_computation.7 | convolution fusion | flops 35782656 | bytes 794624 | tf_op jit(solution)/shard_map/dot_general | solution.py:13
  22.7 2.0 %collective-permute-start.3 = (bf16[32,2048]{1,0:T(8,128)(2,1)S(1)}, bf16[32,2048]{1,0:T(8,128)(2,1)S(1)}, u32[]{:S(2)}, u32[]{:S(2)}) collective-permute-start(bf16[32,2048]{1,0:T(8,128)(2,1)S(1)} %get-tuple-element.57), channel_id=1, source_target_pairs={{0,4},{4,0},{8,12},{12,8},{1,5},{5,1},{9,13},{13,9},{2,6},{6,2},{1... | collective-permute-start | bytes 393224 | tf_op jit(solution)/shard_map/ppermute | solution.py:74
  24.7 2.6 %collective-permute-start.4 = (bf16[32,2048]{1,0:T(8,128)(2,1)S(1)}, bf16[32,2048]{1,0:T(8,128)(2,1)S(1)}, u32[]{:S(2)}, u32[]{:S(2)}) collective-permute-start(bf16[32,2048]{1,0:T(8,128)(2,1)S(1)} %get-tuple-element.56), channel_id=1, source_target_pairs={{0,8},{4,12},{8,0},{12,4},{1,9},{5,13},{9,1},{13,5},{2,10},{6,14},... | collective-permute-start | bytes 393224 | tf_op jit(solution)/shard_map/ppermute | solution.py:74
  27.3 1.8 %collective-permute-start.8 = (bf16[512,384]{1,0:T(8,128)(2,1)S(1)}, bf16[512,384]{1,0:T(8,128)(2,1)S(1)}, u32[]{:S(2)}, u32[]{:S(2)}) collective-permute-start(bf16[512,384]{1,0:T(8,128)(2,1)S(1)} %collective-permute-done.6), channel_id=1, source_target_pairs={{0,16},{16,0},{1,17},{17,1},{2,18},{18,2},{3,19},{19,3},{4,20},{20... | collective-permute-start | bytes 1179656 | tf_op jit(solution)/shard_map/ppermute | solution.py:84
  29.1 1.5 %collective-permute-done.3 = bf16[32,2048]{1,0:T(8,128)(2,1)S(1)} collective-permute-done((bf16[32,2048]{1,0:T(8,128)(2,1)S(1)}, bf16[32,2048]{1,0:T(8,128)(2,1)S(1)}, u32[]{:S(2)}, u32[]{:S(2)}) %collective-permute-start.3) | collective-permute-done | bytes 131104 | tf_op jit(solution)/shard_map/ppermute | solution.py:74
  30.5 7.0 %collective-permute-done.4 = bf16[32,2048]{1,0:T(8,128)(2,1)S(1)} collective-permute-done((bf16[32,2048]{1,0:T(8,128)(2,1)S(1)}, bf16[32,2048]{1,0:T(8,128)(2,1)S(1)}, u32[]{:S(2)}, u32[]{:S(2)}) %collective-permute-start.4) | collective-permute-done | bytes 131104 | tf_op jit(solution)/shard_map/ppermute | solution.py:74
  37.6 0.6 collective-permute-start.11
  38.3 0.3 fusion.46
  38.6 0.3 convolution_add_fusion.7
  38.9 0.2 fusion.58
  39.1 0.2 fusion.56
  39.4 0.2 fusion.53
  39.6 0.2 fusion.51
  39.8 0.3 collective-permute-done.11
  40.1 0.3 fusion.43
  40.3 0.2 convolution_add_fusion.10
  40.5 0.5 collective-permute-done.9
  41.1 0.2 convolution_add_fusion.9
  41.3 0.2 fusion.8
  41.5 0.2 select_add_fusion
  41.7 1.3 %multiply_convert_fusion = (bf16[64,384]{1,0:T(8,128)(2,1)S(1)}, bf16[64,384]{1,0:T(8,128)(2,1)S(1)}, bf16[64,384]{1,0:T(8,128)(2,1)S(1)}) fusion(f32[64,384]{1,0:T(8,128)S(1)} %fusion.8, f32[64,384]{1,0:T(8,128)S(1)} %select_add_fusion, f32[64,384]{1,0:T(8,128)S(1)} %fusion.43, f32[64,384]{1,0:T(8,128)S(1)} %convolution_add_fusion.7, ...), kind=kOutput, calls=%fused_computation.85 | convolution fusion | flops 25583616 | bytes 999424 | tf_op jit(solution)/shard_map/dot_general | solution.py:19
  43.0 0.2 fusion.90
  43.3 0.2 convolution_convert_fusion.7
  43.5 0.2 fusion.4
  43.7 1.6 %collective-permute-start.15 = (bf16[64,1152]{1,0:T(8,128)(2,1)S(1)}, bf16[64,1152]{1,0:T(8,128)(2,1)S(1)}, u32[]{:S(2)}, u32[]{:S(2)}) collective-permute-start(bf16[64,1152]{1,0:T(8,128)(2,1)S(1)} %pad_maximum_fusion.10), channel_id=1, source_target_pairs={{0,2},{1,3},{2,0},{3,1},{4,6},{5,7},{6,4},{7,5},{8,10},{9,11},{10,... | collective-permute-start | bytes 442376 | tf_op jit(solution)/shard_map/ppermute | solution.py:65
  45.3 0.6 collective-permute-start.16
  45.9 0.2 fusion.69
  46.1 0.2 fusion.70
  46.4 0.2 fusion.91
  46.6 0.2 fusion.7
  46.9 0.2 fusion.6
  47.1 0.2 fusion.5
  47.4 0.2 convolution_convert_fusion.4
  47.6 1.2 %convolution_convert_fusion.5 = bf16[64,512]{1,0:T(8,128)(2,1)S(1)} fusion(bf16[64,384]{1,0:T(8,128)(2,1)S(1)} %get-tuple-element.72, bf16[384,512]{1,0:T(8,128)(2,1)} %collective-permute-done.10), kind=kOutput, calls=%fused_computation.20 | convolution fusion | flops 25198592 | bytes 507904 | tf_op jit(solution)/shard_map/dot_general | solution.py:25
  48.8 0.2 convolution_convert_fusion.6
  49.1 2.5 %collective-permute-start.12 = (bf16[32,2048]{1,0:T(8,128)(2,1)S(1)}, bf16[32,2048]{1,0:T(8,128)(2,1)S(1)}, u32[]{:S(2)}, u32[]{:S(2)}) collective-permute-start(bf16[32,2048]{1,0:T(8,128)(2,1)S(1)} %get-tuple-element.50), channel_id=1, source_target_pairs={{0,4},{4,0},{8,12},{12,8},{1,5},{5,1},{9,13},{13,9},{2,6},{6,2},{1... | collective-permute-start | bytes 393224 | tf_op jit(solution)/shard_map/ppermute | solution.py:74
  51.6 1.1 %collective-permute-start.13 = (bf16[32,2048]{1,0:T(8,128)(2,1)S(1)}, bf16[32,2048]{1,0:T(8,128)(2,1)S(1)}, u32[]{:S(2)}, u32[]{:S(2)}) collective-permute-start(bf16[32,2048]{1,0:T(8,128)(2,1)S(1)} %get-tuple-element.51), channel_id=1, source_target_pairs={{0,8},{4,12},{8,0},{12,4},{1,9},{5,13},{9,1},{13,5},{2,10},{6,14},... | collective-permute-start | bytes 393224 | tf_op jit(solution)/shard_map/ppermute | solution.py:74
  52.6 1.4 %collective-permute-start.14 = (bf16[32,2048]{1,0:T(8,128)(2,1)S(1)}, bf16[32,2048]{1,0:T(8,128)(2,1)S(1)}, u32[]{:S(2)}, u32[]{:S(2)}) collective-permute-start(bf16[32,2048]{1,0:T(8,128)(2,1)S(1)} %get-tuple-element.48), channel_id=1, source_target_pairs={{0,12},{4,8},{8,4},{12,0},{1,13},{5,9},{9,5},{13,1},{2,14},{6,10},... | collective-permute-start | bytes 393224 | tf_op jit(solution)/shard_map/ppermute | solution.py:74
  54.1 2.1 %collective-permute-done.12 = bf16[32,2048]{1,0:T(8,128)(2,1)S(1)} collective-permute-done((bf16[32,2048]{1,0:T(8,128)(2,1)S(1)}, bf16[32,2048]{1,0:T(8,128)(2,1)S(1)}, u32[]{:S(2)}, u32[]{:S(2)}) %collective-permute-start.12) | collective-permute-done | bytes 131104 | tf_op jit(solution)/shard_map/ppermute | solution.py:74
  56.2 8.0 %collective-permute-done.13 = bf16[32,2048]{1,0:T(8,128)(2,1)S(1)} collective-permute-done((bf16[32,2048]{1,0:T(8,128)(2,1)S(1)}, bf16[32,2048]{1,0:T(8,128)(2,1)S(1)}, u32[]{:S(2)}, u32[]{:S(2)}) %collective-permute-start.13) | collective-permute-done | bytes 131104 | tf_op jit(solution)/shard_map/ppermute | solution.py:74
  64.3 0.3 select_reduce_fusion
  64.7 0.7 fusion.72
  65.5 0.3 fusion.83
  65.8 0.3 fusion.81
  66.1 0.3 fusion.80
  66.5 0.3 fusion.82
  66.9 0.4 convolution_convert_fusion.2
  67.3 0.3 convolution_convert_fusion.3
  67.6 0.6 collective-permute-start.18
  68.2 0.3 fusion.3
  68.5 0.3 fusion.2
  69.0 0.8 %pad_maximum_fusion.2 = bf16[128,2048]{1,0:T(8,128)(2,1)} fusion(bf16[128,512]{1,0:T(8,128)(2,1)S(1)} %get-tuple-element.94, bf16[128,512]{1,0:T(8,128)(2,1)S(1)} %get-tuple-element.93, bf16[128,512]{1,0:T(8,128)(2,1)S(1)} %get-tuple-element.92, bf16[128,512]{1,0:T(8,128)(2,1)S(1)} %get-tuple-element.95), kind=kLoop, calls=%fused_computation.47 | loop fusion | flops 2097152 | bytes 1048576 | tf_op jit(solution)/shard_map/concatenate | solution.py:115
  69.8 0.8 %pad_maximum_fusion.3 = bf16[128,2048]{1,0:T(8,128)(2,1)} fusion(bf16[128,512]{1,0:T(8,128)(2,1)S(1)} %get-tuple-element.41, bf16[128,512]{1,0:T(8,128)(2,1)S(1)} %get-tuple-element.42, bf16[128,512]{1,0:T(8,128)(2,1)S(1)} %get-tuple-element.43, bf16[128,512]{1,0:T(8,128)(2,1)S(1)} %get-tuple-element.40), kind=kLoop, calls=%fused_computation.48 | loop fusion | flops 2097152 | bytes 1048576 | tf_op jit(solution)/shard_map/concatenate | solution.py:115
  70.7 1.0 %fusion.17 = bf16[1,384,512]{2,1,0:T(8,128)(2,1)} fusion(bf16[384,512]{1,0:T(8,128)(2,1)S(1)} %collective-permute-done.18, bf16[64,1024]{1,0:T(8,128)(2,1)S(1)} %get-tuple-element.66, bf16[64,1024]{1,0:T(8,128)(2,1)S(1)} %get-tuple-element.97, bf16[128,1152]{1,0:T(8,128)(2,1)S(1)} %constant_dynamic-update-slice_fusion.8), kind=kOutput, calls=%fused_computation.49 | convolution fusion | flops 51183616 | bytes 1146880 | tf_op jit(solution)/shard_map/dot_general | solution.py:13
  71.7 0.4 add_convert_fusion
  72.1 1.0 %slice_bitcast_fusion = (bf16[1,512,384]{2,1,0:T(8,128)(2,1)}, bf16[1,512,384]{2,1,0:T(8,128)(2,1)}) fusion(bf16[512,768]{1,0:T(8,128)(2,1)S(1)} %add_convert_fusion), kind=kLoop, calls=%fused_computation.50 | loop fusion | bytes 1572864 | tf_op jit(solution)/shard_map/broadcast_in_dim | solution.py:213
  (83 shorter events, 1.7 us)
Async XLA Ops:
  0.6 16.3 %copy-start = (bf16[1,512,384]{2,1,0:T(8,128)(2,1)S(1)}, bf16[1,512,384]{2,1,0:T(8,128)(2,1)}, u32[]{:S(2)}) copy-start(bf16[1,512,384]{2,1,0:T(8,128)(2,1)} %param.11) | copy-start | bytes 1179652
  0.6 16.6 %copy-start.1 = (bf16[1,512,384]{2,1,0:T(8,128)(2,1)S(1)}, bf16[1,512,384]{2,1,0:T(8,128)(2,1)}, u32[]{:S(2)}) copy-start(bf16[1,512,384]{2,1,0:T(8,128)(2,1)} %param.12) | copy-start | bytes 1179652
  0.7 16.1 %copy-start.2 = (bf16[1,384,512]{2,1,0:T(8,128)(2,1)S(1)}, bf16[1,384,512]{2,1,0:T(8,128)(2,1)}, u32[]{:S(2)}) copy-start(bf16[1,384,512]{2,1,0:T(8,128)(2,1)} %param.13) | copy-start | bytes 1179652
  0.7 17.3 %copy-start.10 = (s32[128,8]{0,1:T(8,128)S(1)}, s32[128,8]{0,1:T(8,128)}, u32[]{:S(2)}) copy-start(s32[128,8]{0,1:T(8,128)} %param.9) | copy-start | bytes 12292
  0.7 18.8 %copy-start.3 = (bf16[128,2048]{1,0:T(8,128)(2,1)S(1)}, bf16[128,2048]{1,0:T(8,128)(2,1)}, u32[]{:S(2)}) copy-start(bf16[128,2048]{1,0:T(8,128)(2,1)} %param.7) | copy-start | bytes 1572868
  13.7 13.6 %collective-permute-start.6 = (bf16[512,384]{1,0:T(8,128)(2,1)}, bf16[512,384]{1,0:T(8,128)(2,1)S(1)}, u32[]{:S(2)}, u32[]{:S(2)}) collective-permute-start(bf16[512,384]{1,0:T(8,128)(2,1)} %shard_map.118), channel_id=1, source_target_pairs={{0,2},{1,3},{2,0},{3,1},{4,6},{5,7},{6,4},{7,5},{8,10},{9,11},{10,... | collective-permute-start | bytes 1179656 | tf_op jit(solution)/shard_map/ppermute | solution.py:65
  16.7 5.9 %collective-permute-start.2 = (bf16[384,512]{1,0:T(8,128)(2,1)S(1)}, bf16[384,512]{1,0:T(8,128)(2,1)S(1)}, u32[]{:S(2)}, u32[]{:S(2)}) collective-permute-start(bf16[384,512]{1,0:T(8,128)(2,1)S(1)} %bitcast.123), channel_id=1, source_target_pairs={{0,1},{1,0},{2,3},{3,2},{4,5},{5,4},{6,7},{7,6},{8,9},{9,8},{10,11... | collective-permute-start | bytes 1179656 | tf_op jit(solution)/shard_map/ppermute | solution.py:65
  16.7 20.9 %collective-permute-start.10 = (bf16[384,512]{1,0:T(8,128)(2,1)S(1)}, bf16[384,512]{1,0:T(8,128)(2,1)}, u32[]{:S(2)}, u32[]{:S(2)}) collective-permute-start(bf16[384,512]{1,0:T(8,128)(2,1)S(1)} %bitcast.124), channel_id=1, source_target_pairs={{0,2},{1,3},{2,0},{3,1},{4,6},{5,7},{6,4},{7,5},{8,10},{9,11},{10,... | collective-permute-start | bytes 1179656 | tf_op jit(solution)/shard_map/ppermute | solution.py:65
  16.9 5.7 %collective-permute-start = (bf16[512,384]{1,0:T(8,128)(2,1)S(1)}, bf16[512,384]{1,0:T(8,128)(2,1)S(1)}, u32[]{:S(2)}, u32[]{:S(2)}) collective-permute-start(bf16[512,384]{1,0:T(8,128)(2,1)S(1)} %bitcast.116), channel_id=1, source_target_pairs={{0,1},{1,0},{2,3},{3,2},{4,5},{5,4},{6,7},{7,6},{8,9},{9,8},{10,11... | collective-permute-start | bytes 1179656 | tf_op jit(solution)/shard_map/ppermute | solution.py:65
  17.2 5.3 %collective-permute-start.1 = (bf16[512,384]{1,0:T(8,128)(2,1)S(1)}, bf16[512,384]{1,0:T(8,128)(2,1)S(1)}, u32[]{:S(2)}, u32[]{:S(2)}) collective-permute-start(bf16[512,384]{1,0:T(8,128)(2,1)S(1)} %bitcast.120), channel_id=1, source_target_pairs={{0,1},{1,0},{2,3},{3,2},{4,5},{5,4},{6,7},{7,6},{8,9},{9,8},{10,11... | collective-permute-start | bytes 1179656 | tf_op jit(solution)/shard_map/ppermute | solution.py:65
  17.4 0.6 copy-start.13
  19.5 1.0 %copy-start.4 = (bf16[128,512]{1,0:T(8,128)(2,1)}, bf16[128,512]{1,0:T(8,128)(2,1)S(1)}, u32[]{:S(2)}) copy-start(bf16[128,512]{1,0:T(8,128)(2,1)S(1)} %get-tuple-element.64) | copy-start | bytes 393220
  19.5 1.0 %copy-start.6 = (bf16[128,512]{1,0:T(8,128)(2,1)}, bf16[128,512]{1,0:T(8,128)(2,1)S(1)}, u32[]{:S(2)}) copy-start(bf16[128,512]{1,0:T(8,128)(2,1)S(1)} %get-tuple-element.65) | copy-start | bytes 393220
  20.3 0.9 %copy-start.8 = (bf16[128,512]{1,0:T(8,128)(2,1)S(1)}, bf16[128,512]{1,0:T(8,128)(2,1)}, u32[]{:S(2)}) copy-start(bf16[128,512]{1,0:T(8,128)(2,1)} %get-tuple-element.58) | copy-start | bytes 393220
  20.3 1.0 %copy-start.9 = (bf16[128,512]{1,0:T(8,128)(2,1)S(1)}, bf16[128,512]{1,0:T(8,128)(2,1)}, u32[]{:S(2)}) copy-start(bf16[128,512]{1,0:T(8,128)(2,1)} %get-tuple-element.59) | copy-start | bytes 393220
  20.4 0.6 copy-start.11
  22.7 7.9 %collective-permute-start.3 = (bf16[32,2048]{1,0:T(8,128)(2,1)S(1)}, bf16[32,2048]{1,0:T(8,128)(2,1)S(1)}, u32[]{:S(2)}, u32[]{:S(2)}) collective-permute-start(bf16[32,2048]{1,0:T(8,128)(2,1)S(1)} %get-tuple-element.57), channel_id=1, source_target_pairs={{0,4},{4,0},{8,12},{12,8},{1,5},{5,1},{9,13},{13,9},{2,6},{6,2},{1... | collective-permute-start | bytes 393224 | tf_op jit(solution)/shard_map/ppermute | solution.py:74
  24.7 12.9 %collective-permute-start.4 = (bf16[32,2048]{1,0:T(8,128)(2,1)S(1)}, bf16[32,2048]{1,0:T(8,128)(2,1)S(1)}, u32[]{:S(2)}, u32[]{:S(2)}) collective-permute-start(bf16[32,2048]{1,0:T(8,128)(2,1)S(1)} %get-tuple-element.56), channel_id=1, source_target_pairs={{0,8},{4,12},{8,0},{12,4},{1,9},{5,13},{9,1},{13,5},{2,10},{6,14},... | collective-permute-start | bytes 393224 | tf_op jit(solution)/shard_map/ppermute | solution.py:74
  27.3 10.3 %collective-permute-start.5 = (bf16[32,2048]{1,0:T(8,128)(2,1)S(1)}, bf16[32,2048]{1,0:T(8,128)(2,1)S(1)}, u32[]{:S(2)}, u32[]{:S(2)}) collective-permute-start(bf16[32,2048]{1,0:T(8,128)(2,1)S(1)} %get-tuple-element.55), channel_id=1, source_target_pairs={{0,12},{4,8},{8,4},{12,0},{1,13},{5,9},{9,5},{13,1},{2,14},{6,10},... | collective-permute-start | bytes 393224 | tf_op jit(solution)/shard_map/ppermute | solution.py:74
  27.3 12.0 %collective-permute-start.8 = (bf16[512,384]{1,0:T(8,128)(2,1)S(1)}, bf16[512,384]{1,0:T(8,128)(2,1)S(1)}, u32[]{:S(2)}, u32[]{:S(2)}) collective-permute-start(bf16[512,384]{1,0:T(8,128)(2,1)S(1)} %collective-permute-done.6), channel_id=1, source_target_pairs={{0,16},{16,0},{1,17},{17,1},{2,18},{18,2},{3,19},{19,3},{4,20},{20... | collective-permute-start | bytes 1179656 | tf_op jit(solution)/shard_map/ppermute | solution.py:84
  37.6 2.0 %collective-permute-start.7 = (bf16[512,384]{1,0:T(8,128)(2,1)S(1)}, bf16[512,384]{1,0:T(8,128)(2,1)S(1)}, u32[]{:S(2)}, u32[]{:S(2)}) collective-permute-start(bf16[512,384]{1,0:T(8,128)(2,1)S(1)} %collective-permute-done.6), channel_id=1, source_target_pairs={{0,1},{1,0},{2,3},{3,2},{4,5},{5,4},{6,7},{7,6},{8,9},{9,8},{10,11... | collective-permute-start | bytes 1179656 | tf_op jit(solution)/shard_map/ppermute | solution.py:65
  37.6 2.4 %collective-permute-start.11 = (bf16[384,512]{1,0:T(8,128)(2,1)}, bf16[384,512]{1,0:T(8,128)(2,1)S(1)}, u32[]{:S(2)}, u32[]{:S(2)}) collective-permute-start(bf16[384,512]{1,0:T(8,128)(2,1)} %collective-permute-done.10), channel_id=1, source_target_pairs={{0,1},{1,0},{2,3},{3,2},{4,5},{5,4},{6,7},{7,6},{8,9},{9,8},{10,11... | collective-permute-start | bytes 1179656 | tf_op jit(solution)/shard_map/ppermute | solution.py:65
  39.3 1.8 %collective-permute-start.9 = (bf16[512,384]{1,0:T(8,128)(2,1)S(1)}, bf16[512,384]{1,0:T(8,128)(2,1)S(1)}, u32[]{:S(2)}, u32[]{:S(2)}) collective-permute-start(bf16[512,384]{1,0:T(8,128)(2,1)S(1)} %collective-permute-done.8), channel_id=1, source_target_pairs={{0,1},{1,0},{2,3},{3,2},{4,5},{5,4},{6,7},{7,6},{8,9},{9,8},{10,11... | collective-permute-start | bytes 1179656 | tf_op jit(solution)/shard_map/ppermute | solution.py:65
  43.7 20.5 %collective-permute-start.15 = (bf16[64,1152]{1,0:T(8,128)(2,1)S(1)}, bf16[64,1152]{1,0:T(8,128)(2,1)S(1)}, u32[]{:S(2)}, u32[]{:S(2)}) collective-permute-start(bf16[64,1152]{1,0:T(8,128)(2,1)S(1)} %pad_maximum_fusion.10), channel_id=1, source_target_pairs={{0,2},{1,3},{2,0},{3,1},{4,6},{5,7},{6,4},{7,5},{8,10},{9,11},{10,... | collective-permute-start | bytes 442376 | tf_op jit(solution)/shard_map/ppermute | solution.py:65
  45.3 18.9 %collective-permute-start.16 = (bf16[128,1024]{1,0:T(8,128)(2,1)S(1)}, bf16[128,1024]{1,0:T(8,128)(2,1)S(1)}, u32[]{:S(2)}, u32[]{:S(2)}) collective-permute-start(bf16[128,1024]{1,0:T(8,128)(2,1)S(1)} %slice.177), channel_id=1, source_target_pairs={{0,2},{1,3},{2,0},{3,1},{4,6},{5,7},{6,4},{7,5},{8,10},{9,11},{10,... | collective-permute-start | bytes 786440 | tf_op jit(solution)/shard_map/ppermute | solution.py:65
  49.1 15.2 %copy-start.5 = (bf16[128,512]{1,0:T(8,128)(2,1)S(1)}, bf16[128,512]{1,0:T(8,128)(2,1)}, u32[]{:S(2)}) copy-start(bf16[128,512]{1,0:T(8,128)(2,1)} %copy-done.4) | copy-start | bytes 393220
  49.1 15.2 %copy-start.7 = (bf16[128,512]{1,0:T(8,128)(2,1)S(1)}, bf16[128,512]{1,0:T(8,128)(2,1)}, u32[]{:S(2)}) copy-start(bf16[128,512]{1,0:T(8,128)(2,1)} %copy-done.6) | copy-start | bytes 393220
  49.1 7.1 %collective-permute-start.12 = (bf16[32,2048]{1,0:T(8,128)(2,1)S(1)}, bf16[32,2048]{1,0:T(8,128)(2,1)S(1)}, u32[]{:S(2)}, u32[]{:S(2)}) collective-permute-start(bf16[32,2048]{1,0:T(8,128)(2,1)S(1)} %get-tuple-element.50), channel_id=1, source_target_pairs={{0,4},{4,0},{8,12},{12,8},{1,5},{5,1},{9,13},{13,9},{2,6},{6,2},{1... | collective-permute-start | bytes 393224 | tf_op jit(solution)/shard_map/ppermute | solution.py:74
  51.6 12.7 %collective-permute-start.13 = (bf16[32,2048]{1,0:T(8,128)(2,1)S(1)}, bf16[32,2048]{1,0:T(8,128)(2,1)S(1)}, u32[]{:S(2)}, u32[]{:S(2)}) collective-permute-start(bf16[32,2048]{1,0:T(8,128)(2,1)S(1)} %get-tuple-element.51), channel_id=1, source_target_pairs={{0,8},{4,12},{8,0},{12,4},{1,9},{5,13},{9,1},{13,5},{2,10},{6,14},... | collective-permute-start | bytes 393224 | tf_op jit(solution)/shard_map/ppermute | solution.py:74
  52.6 11.6 %collective-permute-start.14 = (bf16[32,2048]{1,0:T(8,128)(2,1)S(1)}, bf16[32,2048]{1,0:T(8,128)(2,1)S(1)}, u32[]{:S(2)}, u32[]{:S(2)}) collective-permute-start(bf16[32,2048]{1,0:T(8,128)(2,1)S(1)} %get-tuple-element.48), channel_id=1, source_target_pairs={{0,12},{4,8},{8,4},{12,0},{1,13},{5,9},{9,5},{13,1},{2,14},{6,10},... | collective-permute-start | bytes 393224 | tf_op jit(solution)/shard_map/ppermute | solution.py:74
  54.1 10.6 %copy-start.12 = (f32[128,8]{0,1:T(8,128)S(1)}, f32[128,8]{0,1:T(8,128)}, u32[]{:S(2)}) copy-start(f32[128,8]{0,1:T(8,128)} %param.10) | copy-start | bytes 12292
  54.1 10.6 %copy-start.14 = (s32[4]{0:T(128)S(1)}, s32[4]{0:T(128)}, u32[]{:S(2)}) copy-start(s32[4]{0:T(128)} %copy-done.13) | copy-start | bytes 52
  67.3 4.4 %collective-permute-start.17 = (bf16[512,768]{1,0:T(8,128)(2,1)S(1)}, bf16[512,768]{1,0:T(8,128)(2,1)S(1)}, u32[]{:S(2)}, u32[]{:S(2)}) collective-permute-start(bf16[512,768]{1,0:T(8,128)(2,1)S(1)} %convolution_convert_fusion.2), channel_id=1, source_target_pairs={{0,1},{1,0},{2,3},{3,2},{4,5},{5,4},{6,7},{7,6},{8,9},{9,8},{10,11... | collective-permute-start | bytes 2359304 | tf_op jit(solution)/shard_map/ppermute | solution.py:65
  67.6 3.0 %collective-permute-start.18 = (bf16[384,512]{1,0:T(8,128)(2,1)S(1)}, bf16[384,512]{1,0:T(8,128)(2,1)S(1)}, u32[]{:S(2)}, u32[]{:S(2)}) collective-permute-start(bf16[384,512]{1,0:T(8,128)(2,1)S(1)} %convolution_convert_fusion.3), channel_id=1, source_target_pairs={{0,1},{1,0},{2,3},{3,2},{4,5},{5,4},{6,7},{7,6},{8,9},{9,8},{10,11... | collective-permute-start | bytes 1179656 | tf_op jit(solution)/shard_map/ppermute | solution.py:65

commit v4 on v2

v4 whole, which is shorter than its diff:
```python
import jax
import jax.numpy as jnp
from jax import lax
from jax.experimental import pallas as pl
from jax.experimental.pallas import tpu as pltpu
from jax.sharding import PartitionSpec as P

EXPERTS = 128
CORES = 2
BF16 = jnp.bfloat16
F32 = jnp.float32
VMEM_LIMIT = 16 << 20


def dot(left, right):
    return jnp.dot(left, right, preferred_element_type=F32)


def dot_first(left, right):
    return lax.dot_general(left, right, (((0,), (0,)), ((), ())), preferred_element_type=F32)


def dot_last(left, right):
    return lax.dot_general(left, right, (((1,), (1,)), ((), ())), preferred_element_type=F32)


def shape(dims, dtype=BF16):
    return jax.ShapeDtypeStruct(dims, dtype)


def call(kernel, out_shape, *args, smem=0, scratch=(), flops=0, anywhere=()):
    vmem = pl.BlockSpec(memory_space=pltpu.VMEM)
    specs = [
        pl.BlockSpec(memory_space=pltpu.SMEM)
        if i < smem
        else pl.BlockSpec(memory_space=pl.ANY)
        if i in anywhere
        else vmem
        for i in range(len(args))
    ]
    return pl.pallas_call(
        kernel,
        out_shape=out_shape,
        in_specs=specs,
        out_specs=jax.tree.map(lambda _: vmem, out_shape),
        scratch_shapes=list(scratch),
        compiler_params=pltpu.CompilerParams(vmem_limit_bytes=VMEM_LIMIT),
        cost_estimate=pl.CostEstimate(flops=flops, bytes_accessed=1, transcendentals=0),
    )(*args)


def choose(flag, first, second):
    def kernel(flag_ref, first_ref, second_ref, out_ref, sem):
        @pl.when(flag_ref[0] == 0)
        def _():
            copy = pltpu.make_async_copy(first_ref, out_ref, sem)
            copy.start()
            copy.wait()

        @pl.when(flag_ref[0] != 0)
        def _():
            copy = pltpu.make_async_copy(second_ref, out_ref, sem)
            copy.start()
            copy.wait()

    return call(
        kernel,
        shape(first.shape),
        flag.reshape(1),
        first,
        second,
        smem=1,
        anywhere=(1, 2),
        scratch=[pltpu.SemaphoreType.DMA],
    )


def slots(place, ids, probs, tokens, cotangent, expert_count, capacity, dp_count, even):
    top_count, token_rows = ids.shape
    width = tokens.shape[1] // dp_count
    total = expert_count * capacity

    def kernel(place_ref, ids_ref, probs_ref, x_ref, dy_ref, *outs):
        chunks, (select_ref, table_ref) = outs[:expert_count], outs[expert_count:]
        row = lax.broadcasted_iota(jnp.int32, (total, token_rows), 0)
        step = row // capacity
        far = step + place_ref[0]
        wanted = step ^ place_ref[0] if even else jnp.where(far >= expert_count, far - expert_count, far)
        named = jnp.zeros((total, token_rows), F32)
        prob = jnp.zeros((total, token_rows), F32)
        for k in range(top_count):
            hit = ids_ref[k : k + 1, :] == wanted
            named = jnp.where(hit, 1.0, named)
            prob = jnp.where(hit, probs_ref[k : k + 1, :], prob)
        earlier = lax.broadcasted_iota(jnp.int32, (token_rows, token_rows), 0)
        later = lax.broadcasted_iota(jnp.int32, (token_rows, token_rows), 1)
        before = jnp.where(earlier < later, 1.0, 0.0).astype(BF16)
        slot = dot(named.astype(BF16), before)
        own_slot = (row - step * capacity).astype(F32)
        select = jnp.where((named > 0.5) & (slot == own_slot), 1.0, 0.0)
        pick = select.astype(BF16)
        select_ref[...] = pick
        for j in range(dp_count):
            source = pl.ds(pl.multiple_of((place_ref[1] ^ j) * width, width), width)
            target = slice(j * width, (j + 1) * width)
            rows_x = dot(pick, x_ref[:, source]).astype(BF16)
            rows_dy = dot(pick, dy_ref[:, source]).astype(BF16)
            for e in range(expert_count):
                part = slice(e * capacity, (e + 1) * capacity)
                chunks[e][0:capacity, target] = rows_x[part]
                chunks[e][capacity:, target] = rows_dy[part]
        table = (select * prob).T
        high = table.astype(BF16)
        rest = table - high.astype(F32)
        middle = rest.astype(BF16)
        table_ref[:, 0:total] = high
        table_ref[:, total : 2 * total] = middle
        table_ref[:, 2 * total :] = (rest - middle.astype(F32)).astype(BF16)

    outs = [shape((2 * capacity, tokens.shape[1]))] * expert_count
    outs += [shape((total, token_rows)), shape((token_rows, 3 * total))]
    got = call(kernel, outs, place, ids, probs, tokens, cotangent, smem=1)
    return got[:expert_count], got[expert_count], got[expert_count + 1]


def first_half(chunks, pieces, near, width):
    count, dp_count = len(chunks), len(pieces)
    capacity = chunks[0].shape[0] // 2
    total = count * capacity
    model_width = chunks[0].shape[1]
    ff = pieces[0][2].shape[0]
    weights = [w for p in pieces for w in p if w is not None]

    def kernel(*refs):
        chunk_refs, refs = refs[:count], refs[count:]
        weight_refs, (rows_ref, keep_ref, send_ref, sums_ref) = refs[: len(weights)], refs[len(weights) :]
        for e in range(count):
            rows_ref[e * capacity : (e + 1) * capacity, :] = chunk_refs[e][0:capacity, :]
            rows_ref[total + e * capacity : total + (e + 1) * capacity, :] = chunk_refs[e][capacity:, :]
        keep_ref[...] = rows_ref[:, 0 : near * width]
        send_ref[...] = rows_ref[:, near * width :]
        sums = [0.0, 0.0, 0.0, 0.0]
        at = 0
        for j, piece in enumerate(pieces):
            column = slice(j * width, (j + 1) * width)
            x, dy = rows_ref[0:total, column], rows_ref[total:, column]
            if j < near:
                sums[0] += dot(x, weight_refs[at][...])
                sums[1] += dot(x, weight_refs[at + 1][...])
                sums[3] += dot_last(dy, weight_refs[at + 2][...])
                at += 3
            else:
                sums[2] += dot(x, weight_refs[at][...])
                sums[3] += dot_last(dy, weight_refs[at + 1][...])
                at += 2
        for k in range(4):
            sums_ref[:, k * ff : (k + 1) * ff] = sums[k]

    outs = [
        shape((2 * total, model_width)),
        shape((2 * total, near * width)),
        shape((2 * total, model_width - near * width)),
        shape((total, 4 * ff), F32),
    ]
    return call(kernel, outs, *chunks, *weights)


def second_half(flag, rows, sums, pieces, near, width, count):
    total = rows.shape[0] // 2
    capacity = total // count
    model_width = rows.shape[1]
    ff = sums.shape[1] // 4
    weights = [w for p in pieces for w in p]
    far = [j for j in range(len(pieces)) if j >= near]

    def kernel(flag_ref, rows_ref, sums_ref, *refs):
        weight_refs, outs = refs[: len(weights)], refs[len(weights) :]
        chunk_refs, trio_ref = outs[:count], outs[count]
        last = 0.0
        for j in far:
            last += dot(rows_ref[0:total, j * width : (j + 1) * width], weight_refs[3 * j + 1][...])
        lead = sums_ref[:, 2 * ff : 3 * ff]
        swapped = flag_ref[0] != 0
        gate_part = sums_ref[:, 0:ff] + jnp.where(swapped, last, lead)
        up_part = sums_ref[:, ff : 2 * ff] + jnp.where(swapped, lead, last)
        back_hidden = sums_ref[:, 3 * ff :]
        sigmoid_gate = jax.nn.sigmoid(gate_part)
        activated = gate_part * sigmoid_gate
        hidden = (activated * up_part).astype(BF16)
        d_gate = back_hidden * up_part * sigmoid_gate * (1.0 + gate_part * (1.0 - sigmoid_gate))
        d_up = back_hidden * activated
        far_first = jnp.where(swapped, d_up, d_gate).astype(BF16)
        far_second = jnp.where(swapped, d_gate, d_up).astype(BF16)
        d_gate, d_up = d_gate.astype(BF16), d_up.astype(BF16)
        trio_ref[:, 0:ff] = hidden
        trio_ref[:, ff : 2 * ff] = d_gate
        trio_ref[:, 2 * ff :] = d_up
        for j in range(len(pieces)):
            column = slice(j * width, (j + 1) * width)
            one, two = (d_gate, d_up) if j < near else (far_first, far_second)
            out = dot(hidden, weight_refs[3 * j + 2][...]).astype(BF16)
            back = dot_last(one, weight_refs[3 * j][...]) + dot_last(two, weight_refs[3 * j + 1][...])
            back = back.astype(BF16)
            for e in range(count):
                part = slice(e * capacity, (e + 1) * capacity)
                chunk_refs[e][0:capacity, column] = out[part]
                chunk_refs[e][capacity:, column] = back[part]

    outs = [shape((2 * capacity, model_width))] * count + [shape((total, 3 * ff))]
    got = call(kernel, outs, flag, rows, sums, *weights, smem=1)
    return got[:count], got[count]


def gradients(keeps, trios, width, ff):
    count = len(keeps)

    def kernel(*refs):
        keep_refs, trio_refs = refs[:count], refs[count : 2 * count]
        gate_ref, up_ref, down_ref = refs[2 * count :]
        half = keep_refs[0].shape[0] // 2
        x = jnp.concatenate([r[0:half, 0:width] for r in keep_refs], axis=0)
        dy = jnp.concatenate([r[half:, 0:width] for r in keep_refs], axis=0)
        trio = jnp.concatenate([r[...] for r in trio_refs], axis=0)
        gate_ref[...] = dot_first(x, trio[:, ff : 2 * ff]).astype(BF16)
        up_ref[...] = dot_first(x, trio[:, 2 * ff :]).astype(BF16)
        down_ref[...] = dot_first(trio[:, 0:ff], dy).astype(BF16)

    outs = [shape((width, ff)), shape((width, ff)), shape((ff, width))]
    return call(kernel, outs, *keeps, *trios)


def collect(place, ids, select, table, cotangent, chunks, dp_count, even):
    count = len(chunks)
    capacity = chunks[0].shape[0] // 2
    total = count * capacity
    token_rows, model_width = cotangent.shape
    width = model_width // dp_count

    def kernel(place_ref, ids_ref, select_ref, table_ref, dy_ref, *refs):
        chunk_refs, (mixed_ref, grad_ref, gates_ref) = refs[:count], refs[count:]
        inner = 0.0
        for j in range(dp_count):
            column = slice(j * width, (j + 1) * width)
            home = pl.ds(pl.multiple_of((place_ref[1] ^ j) * width, width), width)
            out = jnp.concatenate([r[0:capacity, column] for r in chunk_refs], axis=0)
            back = jnp.concatenate([r[capacity:, column] for r in chunk_refs], axis=0)
            mixed_ref[:, home] = dot(table_ref[...], jnp.concatenate([out] * 3, axis=0)).astype(BF16)
            grad_ref[:, home] = dot(table_ref[...], jnp.concatenate([back] * 3, axis=0)).astype(BF16)
            inner += dot_last(out, dy_ref[:, home])
        inner = jnp.where(select_ref[...] > 0, inner, 0.0)
        step = lax.broadcasted_iota(jnp.int32, (total, token_rows), 0) // capacity
        far = step + place_ref[0]
        wanted = step ^ place_ref[0] if even else jnp.where(far >= count, far - count, far)
        for k in range(ids_ref.shape[0]):
            hit = ids_ref[k : k + 1, :] == wanted
            gates_ref[k : k + 1, :] = jnp.sum(jnp.where(hit, inner, 0.0), axis=0, keepdims=True)

    outs = [
        shape((token_rows, model_width)),
        shape((token_rows, model_width)),
        shape(ids.shape, F32),
    ]
    return call(kernel, outs, place, ids, select, table, cotangent, *chunks, smem=1)


def on_device(tokens, cotangent, expert_ids, gate_probs, w_gate, w_up, w_down):
    expert_count = lax.axis_size("expert")
    dp_count = lax.axis_size("dp")
    token_rows = tokens.shape[0]
    width, ff = w_gate.shape[1:]
    capacity = 2 * token_rows * expert_ids.shape[1] // EXPERTS
    group = lax.axis_index("groups").astype(jnp.int32)
    place = jnp.stack([lax.axis_index("expert"), lax.axis_index("dp")]).astype(jnp.int32)
    even = expert_count & (expert_count - 1) == 0
    paired = lax.axis_size("groups") == 2
    flag = (group if paired else jnp.zeros_like(group)).reshape(1)

    def to_dp(array, mask):
        return lax.ppermute(array, "dp", [(i, i ^ mask) for i in range(dp_count)])

    def to_group(array):
        return lax.ppermute(array, "groups", [(0, 1), (1, 0)])

    def to_expert(array, step):
        if even:
            pairs = [(i, i ^ step) for i in range(expert_count)]
        else:
            pairs = [(i, (i + step) % expert_count) for i in range(expert_count)]
        return lax.ppermute(array, "expert", pairs)

    def after(values, *others):
        return lax.optimization_barrier((values, others))[0]

    own = (w_gate[0], w_up[0], w_down[0])
    lead = choose(group, own[0], own[1]) if paired else own[0]
    own = after(own, lead)
    masks = range(CORES, dp_count, CORES)
    lead_got = {mask: to_dp(lead, mask) for mask in masks}
    other_got = {
        mask: to_group(lead_got[mask]) if paired else to_dp(own[1], mask) for mask in masks
    }
    sibling = tuple(to_dp(w, 1) for w in own)

    ids, probs = expert_ids.T, gate_probs.T
    send, select, table = slots(
        place, ids, probs, tokens, cotangent, expert_count, capacity, dp_count, even
    )
    order = [1, *range(expert_count - 1, 1, -1)]
    send = after(send, sibling)
    down = after(own[2], send)
    down_got = {mask: to_dp(down, mask) for mask in masks}
    got = [send[0]] + [None] * (expert_count - 1)
    for j in order:
        got[j] = to_expert(send[j], j)

    early = [(own[0], own[1], own[2]), (sibling[0], sibling[1], sibling[2])]
    full = list(early)
    for mask in masks:
        lead_sib, down_sib = (to_dp(after(w, got), 1) for w in (lead_got[mask], down_got[mask]))
        early += [(lead_got[mask], None, down_got[mask]), (lead_sib, None, down_sib)]
        other_sib = to_dp(other_got[mask], 1)
        full += [
            (lead_got[mask], other_got[mask], down_got[mask]),
            (lead_sib, other_sib, down_sib),
        ]
    rows, keep, far_rows, sums = first_half(got, early, CORES, width)
    back, trio = second_half(flag, rows, sums, full, CORES, width, expert_count)

    home = [back[0]] + [None] * (expert_count - 1)
    for j in order:
        home[j] = to_expert(back[j], j if even else -j)

    kept = [keep]
    for i, mask in enumerate(masks):
        part = far_rows[:, i * CORES * width : (i + 1) * CORES * width]
        kept.append(to_dp(part, mask))
    trios = [trio] + [to_dp(trio, mask) for mask in masks]
    trios, kept = lax.optimization_barrier((trios, kept))
    theirs = to_dp(jnp.concatenate([k[:, width:] for k in kept], axis=0), 1)
    size = keep.shape[0]
    kept += [theirs[i * size : (i + 1) * size] for i in range(len(kept))]
    trios += [to_dp(t, 1) for t in trios]

    home, kept, trios = lax.optimization_barrier((home, kept, trios))
    mixed, grad_tokens, grad_gates = collect(
        place, ids, select, table, cotangent, home, dp_count, even
    )
    grad_w_gate, grad_w_up, grad_w_down = gradients(kept, trios, width, ff)
    return (
        mixed,
        grad_tokens,
        grad_gates.T,
        grad_w_gate[None],
        grad_w_up[None],
        grad_w_down[None],
    )


def solution(mesh):
    rows = P(("groups", "expert", "dp"), None)
    in_specs = (
        rows,
        rows,
        rows,
        rows,
        P("expert", "dp", None),
        P("expert", "dp", None),
        P("expert", None, "dp"),
    )
    out_specs = (
        rows,
        rows,
        rows,
        P(("groups", "expert"), "dp", None),
        P(("groups", "expert"), "dp", None),
        P(("groups", "expert"), None, "dp"),
    )
    return jax.shard_map(
        on_device, mesh=mesh, in_specs=in_specs, out_specs=out_specs, check_vma=False
    )
```

time: 69.1 us -> 65.6 us (0.949); the launches traced: 68.1 us -> 65.3 us
  matrix products: 10.3 us -> 0 us
  Pallas kernels: 0 us -> 10.2 us
  waiting for transfers between devices: 29.8 us -> 34.7 us
  other arithmetic: 4.83 us -> 0.09 us
  starting transfers between devices: 19.3 us -> 17.9 us
  local copies, waits for them, and re-layouts: 2.72 us -> 1.71 us
    dot_general x38 -> x0, matrix products: 10.3 us -> none  [the longest x19 4.42 us: dot(): return jnp.dot(left, right, preferred_element_type=jnp.float32)]
    pallas_call x0 -> x6, Pallas kernels: none -> 10.2 us  [call(): pl.pallas_call(kernel, out_shape=out_shape, in_specs=specs, out_specs=jax...]
    ppermute x6, waiting for transfers between devices: 10.7 us -> 19.1 us  [to_expert(): return lax.ppermute(array, 'expert', pairs)]
    ppermute x1, waiting for transfers between devices: 7.2 us -> 0.01 us  [to_group(): return lax.ppermute(array, 'groups', [(0, 1), (1, 0)])]
    ppermute x12 -> x13, waiting for transfers between devices: 11.8 us -> 15.6 us  [to_dp(): return lax.ppermute(array, 'dp', [(i, i ^ mask) for i in range(dp_count)])]
    select_n x1 -> x0, other arithmetic: 1.97 us -> none  [pick(): return (jnp.where(flag, first, second), jnp.where(flag, second, first))]
    concatenate x8 -> x1, other arithmetic: 1.83 us -> 0.02 us  [on_device(): theirs = to_dp(jnp.concatenate([k[:, width:] for k in kept], axis=0), 1)]
    ppermute x6, starting transfers between devices: 10.4 us -> 8.89 us  [to_expert(): return lax.ppermute(array, 'expert', pairs)]
  transfers between devices with their start and end apart: 19 -> 20, of which waited for: 6 -> 8; matrix products, arithmetic and copies ran while one was open for 14% -> 0% of each run, Pallas kernels for 0% -> 9%
where the time goes in v4:
time: 65.6 us; the launch traced here: 65.3 us
  waiting for transfers between devices  34.7 us (53%)
  starting transfers between devices  17.9 us (27%)
  Pallas kernels  10.2 us (16%)
  local copies, waits for them, and re-layouts  1.71 us (3%)
  between operations  0.77 us (1%)
    ppermute x6, waiting for transfers between devices, to_expert(): return lax.ppermute(array, 'expert', pairs)  19.1 us
    ppermute x13, waiting for transfers between devices, to_dp(): return lax.ppermute(array, 'dp', [(i, i ^ mask) for i in range(dp_count)])  15.6 us
    pallas_call x6, Pallas kernels, call(): pl.pallas_call(kernel, out_shape=out_shape, in_specs=specs, out_specs=jax...  10.2 us
    ppermute x6, starting transfers between devices, to_expert(): return lax.ppermute(array, 'expert', pairs)  8.89 us
    ppermute x13, starting transfers between devices, to_dp(): return lax.ppermute(array, 'dp', [(i, i ^ mask) for i in range(dp_count)])  6.98 us
    ppermute x1, starting transfers between devices, to_group(): return lax.ppermute(array, 'groups', [(0, 1), (1, 0)])  1.98 us
    unnamed x10, local copies, waits for them, and re-layouts  1.67 us
  transfers between devices with their start and end apart: 20, of which 8 were waited for; matrix products, arithmetic and copies ran while one was open for 0% of the time, Pallas kernels for 9%

profile of v4, /device:TPU:0, one launch (start us, length us, event | category | flops | bytes accessed | tf_op | source)
XLA Modules:
  0.0 65.3 jit_solution(16625035662977128395)
XLA Ops:
  0.6 0.0 copy-start.1
  0.6 0.0 copy-start
  0.7 1.1 %shard_map.119 = bf16[512,384]{1,0:T(8,128)(2,1)S(1)} custom-call(s32[1]{0:T(128)} %bitcast.4.flag_ref, bf16[512,384]{1,0:T(8,128)(2,1)} %bitcast.5.first_ref.refs_4_.refs_0_, bf16[512,384]{1,0:T(8,128)(2,1)} %bitcast.6.second_ref.refs_5_.refs_1_), custom_call_target="tpu_custom_call" | custom-call | bytes 1 | tf_op jit(solution)/shard_map/pallas_call | solution.py:41
  1.8 0.5 collective-permute-start
  2.3 0.1 collective-permute-start.1
  2.4 0.0 copy-done.1
  2.4 0.4 collective-permute-start.2
  2.8 2.6 %collective-permute-start.6 = (bf16[512,384]{1,0:T(8,128)(2,1)S(1)}, bf16[512,384]{1,0:T(8,128)(2,1)S(1)}, u32[]{:S(2)}, u32[]{:S(2)}) collective-permute-start(bf16[512,384]{1,0:T(8,128)(2,1)S(1)} %shard_map.119), channel_id=1, source_target_pairs={{0,2},{1,3},{2,0},{3,1},{4,6},{5,7},{6,4},{7,5},{8,10},{9,11},{10,... | collective-permute-start | bytes 1179656 | tf_op jit(solution)/shard_map/ppermute | solution.py:279
  5.3 0.0 copy-start.4
  5.4 0.0 copy-start.3
  5.4 0.1 pad_add_fusion.place_ref
  5.4 0.0 copy-done
  5.4 0.6 copy-done.4
  6.0 0.0 copy-done.3
  6.1 0.0 copy-start.2
  6.1 1.0 %copy-done.2 = bf16[128,2048]{1,0:T(8,128)(2,1)S(1)} copy-done((bf16[128,2048]{1,0:T(8,128)(2,1)S(1)}, bf16[128,2048]{1,0:T(8,128)(2,1)}, u32[]{:S(2)}) %copy-start.2) | copy-done | bytes 524312
  7.1 1.0 %shard_map.118 = (bf16[32,2048]{1,0:T(8,128)(2,1)S(1)}, bf16[32,2048]{1,0:T(8,128)(2,1)S(1)}, bf16[32,2048]{1,0:T(8,128)(2,1)S(1)}, bf16[32,2048]{1,0:T(8,128)(2...) custom-call(s32[2]{0:T(128)S(1)} %pad_add_fusion.place_ref, s32[8,128]{1,0:T(8,128)S(1)} %bitcast.16, ...), custom_call_target="tpu_custom_call" | custom-call | bytes 1 | tf_op jit(solution)/shard_map/pallas_call | solution.py:41
  8.1 0.0 collective-permute-done.refs_7_.refs_3_
  8.1 0.0 collective-permute-done.1.refs_8_.refs_4_
  8.1 0.0 collective-permute-done.2.refs_9_.refs_5_
  8.1 0.1 collective-permute-start.7
  8.2 7.1 %collective-permute-done.6.refs_10_.refs_6_ = bf16[512,384]{1,0:T(8,128)(2,1)S(1)} collective-permute-done((bf16[512,384]{1,0:T(8,128)(2,1)S(1)}, bf16[512,384]{1,0:T(8,128)(2,1)S(1)}, u32[]{:S(2)}, u32[]{:S(2)}) %collective-permute-start.6) | collective-permute-done | bytes 393248 | tf_op jit(solution)/shard_map/ppermute | solution.py:279
  15.3 2.0 %collective-permute-start.10 = (bf16[512,384]{1,0:T(8,128)(2,1)S(1)}, bf16[512,384]{1,0:T(8,128)(2,1)S(1)}, u32[]{:S(2)}, u32[]{:S(2)}) collective-permute-start(bf16[512,384]{1,0:T(8,128)(2,1)S(1)} %collective-permute-done.6.refs_10_.refs_6_), channel_id=1, source_target_pairs={{0,16},{16,0},{1,17},{17,1},{2,18},{18,2},{3,19},{19,3},{4,20},{20... | collective-permute-start | bytes 1179656 | tf_op jit(solution)/shard_map/ppermute | solution.py:282
  17.3 1.6 %collective-permute-start.3 = (bf16[32,2048]{1,0:T(8,128)(2,1)S(1)}, bf16[32,2048]{1,0:T(8,128)(2,1)S(1)}, u32[]{:S(2)}, u32[]{:S(2)}) collective-permute-start(bf16[32,2048]{1,0:T(8,128)(2,1)S(1)} %get-tuple-element.63), channel_id=1, source_target_pairs={{0,4},{4,0},{8,12},{12,8},{1,5},{5,1},{9,13},{13,9},{2,6},{6,2},{1... | collective-permute-start | bytes 393224 | tf_op jit(solution)/shard_map/ppermute | solution.py:289
  18.9 2.6 %collective-permute-start.4 = (bf16[32,2048]{1,0:T(8,128)(2,1)S(1)}, bf16[32,2048]{1,0:T(8,128)(2,1)S(1)}, u32[]{:S(2)}, u32[]{:S(2)}) collective-permute-start(bf16[32,2048]{1,0:T(8,128)(2,1)S(1)} %get-tuple-element.64), channel_id=1, source_target_pairs={{0,8},{4,12},{8,0},{12,4},{1,9},{5,13},{9,1},{13,5},{2,10},{6,14},... | collective-permute-start | bytes 393224 | tf_op jit(solution)/shard_map/ppermute | solution.py:289
  21.5 0.2 collective-permute-start.5
  21.7 2.0 %collective-permute-done.3.refs_1_ = bf16[32,2048]{1,0:T(8,128)(2,1)S(1)} collective-permute-done((bf16[32,2048]{1,0:T(8,128)(2,1)S(1)}, bf16[32,2048]{1,0:T(8,128)(2,1)S(1)}, u32[]{:S(2)}, u32[]{:S(2)}) %collective-permute-start.3) | collective-permute-done | bytes 131104 | tf_op jit(solution)/shard_map/ppermute | solution.py:289
  23.7 7.2 %collective-permute-done.4.refs_2_ = bf16[32,2048]{1,0:T(8,128)(2,1)S(1)} collective-permute-done((bf16[32,2048]{1,0:T(8,128)(2,1)S(1)}, bf16[32,2048]{1,0:T(8,128)(2,1)S(1)}, u32[]{:S(2)}, u32[]{:S(2)}) %collective-permute-start.4) | collective-permute-done | bytes 131104 | tf_op jit(solution)/shard_map/ppermute | solution.py:289
  30.9 0.0 collective-permute-done.5.refs_3_
  30.9 0.0 collective-permute-start.8
  30.9 0.0 collective-permute-done.7.refs_11_.refs_8_
  30.9 0.5 collective-permute-start.9
  31.4 0.0 collective-permute-done.10.refs_7_
  31.4 0.1 collective-permute-start.11
  31.5 1.1 %collective-permute-done.8.refs_12_.refs_9_ = bf16[512,384]{1,0:T(8,128)(2,1)S(1)} collective-permute-done((bf16[512,384]{1,0:T(8,128)(2,1)S(1)}, bf16[512,384]{1,0:T(8,128)(2,1)S(1)}, u32[]{:S(2)}, u32[]{:S(2)}) %collective-permute-start.8) | collective-permute-done | bytes 393248 | tf_op jit(solution)/shard_map/ppermute | solution.py:279
  32.6 0.6 collective-permute-done.9.refs_13_.refs_11_
  33.2 2.1 %shard_map.120 = (bf16[128,2048]{1,0:T(8,128)(2,1)S(1)}, bf16[128,1024]{1,0:T(8,128)(2,1)S(1)}, bf16[128,1024]{1,0:T(8,128)(2,1)S(1)}, f32[64,1536]{1,0:T(8,128)S(1)}) custom-call(bf16[32,2048]{1,0:T(8,128)(2,1)S(1)} %get-tuple-element.62.refs_0_, bf16[32,2048]{1,0:T(8,128)(2,1)S(1)} %collective-permute-done.3.refs_1_, ...), custom_call_target="tpu_custom_call" | custom-call | bytes 1 | tf_op jit(solution)/shard_map/pallas_call | solution.py:41
  35.3 1.6 %collective-permute-start.16 = (bf16[128,1024]{1,0:T(8,128)(2,1)S(1)}, bf16[128,1024]{1,0:T(8,128)(2,1)S(1)}, u32[]{:S(2)}, u32[]{:S(2)}) collective-permute-start(bf16[128,1024]{1,0:T(8,128)(2,1)S(1)} %get-tuple-element.77), channel_id=1, source_target_pairs={{0,2},{1,3},{2,0},{3,1},{4,6},{5,7},{6,4},{7,5},{8,10},{9,11},{10,... | collective-permute-start | bytes 786440 | tf_op jit(solution)/shard_map/ppermute | solution.py:279
  36.8 0.0 collective-permute-done.11.refs_10_
  36.8 2.7 %shard_map.121 = (bf16[32,2048]{1,0:T(8,128)(2,1)S(1)}, bf16[32,2048]{1,0:T(8,128)(2,1)S(1)}, bf16[32,2048]{1,0:T(8,128)(2,1)S(1)}, bf16[32,2048]{1,0:T(8,128)(2,1)S(1)}, bf16[64,1152]{1,0:T(8,128)(2,1)S(1)}) custom-call(s32[1]{0:T(128)} %bitcast.4.flag_ref, bf16[128,2048]{1,0:T(8,128)(2,1)S(1)} %get-tuple-element.69.rows_ref, ...), custom_call_target="tpu_custom_call" | custom-call | bytes 1 | tf_op jit(solution)/shard_map/pallas_call | solution.py:41
  39.5 0.6 collective-permute-start.15
  40.1 6.7 %collective-permute-done.15.refs_5_ = bf16[64,1152]{1,0:T(8,128)(2,1)S(1)} collective-permute-done((bf16[64,1152]{1,0:T(8,128)(2,1)S(1)}, bf16[64,1152]{1,0:T(8,128)(2,1)S(1)}, u32[]{:S(2)}, u32[]{:S(2)}) %collective-permute-start.15) | collective-permute-done | bytes 147488 | tf_op jit(solution)/shard_map/ppermute | solution.py:279
  46.8 0.0 collective-permute-done.16.refs_1_
  46.9 0.1 collective-permute-start.17
  47.0 2.0 %collective-permute-start.12 = (bf16[32,2048]{1,0:T(8,128)(2,1)S(1)}, bf16[32,2048]{1,0:T(8,128)(2,1)S(1)}, u32[]{:S(2)}, u32[]{:S(2)}) collective-permute-start(bf16[32,2048]{1,0:T(8,128)(2,1)S(1)} %get-tuple-element.72), channel_id=1, source_target_pairs={{0,4},{4,0},{8,12},{12,8},{1,5},{5,1},{9,13},{13,9},{2,6},{6,2},{1... | collective-permute-start | bytes 393224 | tf_op jit(solution)/shard_map/ppermute | solution.py:289
  49.0 1.1 %collective-permute-start.13 = (bf16[32,2048]{1,0:T(8,128)(2,1)S(1)}, bf16[32,2048]{1,0:T(8,128)(2,1)S(1)}, u32[]{:S(2)}, u32[]{:S(2)}) collective-permute-start(bf16[32,2048]{1,0:T(8,128)(2,1)S(1)} %get-tuple-element.73), channel_id=1, source_target_pairs={{0,8},{4,12},{8,0},{12,4},{1,9},{5,13},{9,1},{13,5},{2,10},{6,14},... | collective-permute-start | bytes 393224 | tf_op jit(solution)/shard_map/ppermute | solution.py:289
  50.1 1.4 %collective-permute-start.14 = (bf16[32,2048]{1,0:T(8,128)(2,1)S(1)}, bf16[32,2048]{1,0:T(8,128)(2,1)S(1)}, u32[]{:S(2)}, u32[]{:S(2)}) collective-permute-start(bf16[32,2048]{1,0:T(8,128)(2,1)S(1)} %get-tuple-element.74), channel_id=1, source_target_pairs={{0,12},{4,8},{8,4},{12,0},{1,13},{5,9},{9,5},{13,1},{2,14},{6,10},... | collective-permute-start | bytes 393224 | tf_op jit(solution)/shard_map/ppermute | solution.py:289
  51.5 0.0 collective-permute-start.18
  51.5 0.0 collective-permute-done.17
  51.5 0.5 collective-permute-start.19
  52.0 3.3 %collective-permute-done.12.refs_1_ = bf16[32,2048]{1,0:T(8,128)(2,1)S(1)} collective-permute-done((bf16[32,2048]{1,0:T(8,128)(2,1)S(1)}, bf16[32,2048]{1,0:T(8,128)(2,1)S(1)}, u32[]{:S(2)}, u32[]{:S(2)}) %collective-permute-start.12) | collective-permute-done | bytes 131104 | tf_op jit(solution)/shard_map/ppermute | solution.py:289
  55.3 6.6 %collective-permute-done.13.refs_2_ = bf16[32,2048]{1,0:T(8,128)(2,1)S(1)} collective-permute-done((bf16[32,2048]{1,0:T(8,128)(2,1)S(1)}, bf16[32,2048]{1,0:T(8,128)(2,1)S(1)}, u32[]{:S(2)}, u32[]{:S(2)}) %collective-permute-start.13) | collective-permute-done | bytes 131104 | tf_op jit(solution)/shard_map/ppermute | solution.py:289
  61.9 0.0 collective-permute-done.14.refs_3_
  61.9 0.0 collective-permute-done.18.refs_6_
  61.9 0.0 collective-permute-done.19.refs_7_
  61.9 2.0 %shard_map.122 = (bf16[128,2048]{1,0:T(8,128)(2,1)}, bf16[128,2048]{1,0:T(8,128)(2,1)}, f32[8,128]{1,0:T(8,128)}) custom-call(s32[2]{0:T(128)S(1)} %pad_add_fusion.place_ref, s32[8,128]{1,0:T(8,128)S(1)} %bitcast.17, bf16[64,128]{1,0:T(8,128)(2,1)S(1)} %get-tuple-element.53.select_ref, bf16[128,192]{1,0:T(8,128)(2,1)S(1)} %get-tuple-element.54.table_ref, ...), custom_call_target="tpu_custom_call" | custom-call | bytes 1 | tf_op jit(solution)/shard_map/pallas_call | solution.py:41
  64.0 1.4 %shard_map.123 = (bf16[512,384]{1,0:T(8,128)(2,1)}, bf16[512,384]{1,0:T(8,128)(2,1)}, bf16[384,512]{1,0:T(8,128)(2,1)}) custom-call(bf16[128,1024]{1,0:T(8,128)(2,1)S(1)} %get-tuple-element.89.refs_0_, bf16[128,1024]{1,0:T(8,128)(2,1)S(1)} %collective-permute-done.16.refs_1_, bf16[128,512]{1,0:T(8,128)(2,1)S(1)} %get-tuple-element.91.refs_2_, ...), custom_call_target="tpu_custom_call" | custom-call | bytes 1 | tf_op jit(solution)/shard_map/pallas_call | solution.py:41
  (4 shorter events, 0.1 us)
Async XLA Ops:
  0.6 1.7 %copy-start.1 = (bf16[1,384,512]{2,1,0:T(8,128)(2,1)S(1)}, bf16[1,384,512]{2,1,0:T(8,128)(2,1)}, u32[]{:S(2)}) copy-start(bf16[1,384,512]{2,1,0:T(8,128)(2,1)} %param.13) | copy-start | bytes 1179652
  0.6 4.8 %copy-start = (bf16[128,2048]{1,0:T(8,128)(2,1)S(1)}, bf16[128,2048]{1,0:T(8,128)(2,1)}, u32[]{:S(2)}) copy-start(bf16[128,2048]{1,0:T(8,128)(2,1)} %dy_ref.3) | copy-start | bytes 1572868
  1.8 6.3 %collective-permute-start = (bf16[512,384]{1,0:T(8,128)(2,1)}, bf16[512,384]{1,0:T(8,128)(2,1)S(1)}, u32[]{:S(2)}, u32[]{:S(2)}) collective-permute-start(bf16[512,384]{1,0:T(8,128)(2,1)} %bitcast.5.first_ref.refs_4_.refs_0_), channel_id=1, source_target_pairs={{0,1},{1,0},{2,3},{3,2},{4,5},{5,4},{6,7},{7,6},{8,9},{9,8},{10,11... | collective-permute-start | bytes 1179656 | tf_op jit(solution)/shard_map/ppermute | solution.py:279
  2.3 5.8 %collective-permute-start.1 = (bf16[512,384]{1,0:T(8,128)(2,1)}, bf16[512,384]{1,0:T(8,128)(2,1)S(1)}, u32[]{:S(2)}, u32[]{:S(2)}) collective-permute-start(bf16[512,384]{1,0:T(8,128)(2,1)} %bitcast.6.second_ref.refs_5_.refs_1_), channel_id=1, source_target_pairs={{0,1},{1,0},{2,3},{3,2},{4,5},{5,4},{6,7},{7,6},{8,9},{9,8},{10,11... | collective-permute-start | bytes 1179656 | tf_op jit(solution)/shard_map/ppermute | solution.py:279
  2.4 5.7 %collective-permute-start.2 = (bf16[384,512]{1,0:T(8,128)(2,1)S(1)}, bf16[384,512]{1,0:T(8,128)(2,1)S(1)}, u32[]{:S(2)}, u32[]{:S(2)}) collective-permute-start(bf16[384,512]{1,0:T(8,128)(2,1)S(1)} %bitcast.12), channel_id=1, source_target_pairs={{0,1},{1,0},{2,3},{3,2},{4,5},{5,4},{6,7},{7,6},{8,9},{9,8},{10,11... | collective-permute-start | bytes 1179656 | tf_op jit(solution)/shard_map/ppermute | solution.py:279
  2.8 12.5 %collective-permute-start.6 = (bf16[512,384]{1,0:T(8,128)(2,1)S(1)}, bf16[512,384]{1,0:T(8,128)(2,1)S(1)}, u32[]{:S(2)}, u32[]{:S(2)}) collective-permute-start(bf16[512,384]{1,0:T(8,128)(2,1)S(1)} %shard_map.119), channel_id=1, source_target_pairs={{0,2},{1,3},{2,0},{3,1},{4,6},{5,7},{6,4},{7,5},{8,10},{9,11},{10,... | collective-permute-start | bytes 1179656 | tf_op jit(solution)/shard_map/ppermute | solution.py:279
  5.3 0.7 %copy-start.4 = (f32[128,8]{0,1:T(8,128)S(1)}, f32[128,8]{0,1:T(8,128)}, u32[]{:S(2)}) copy-start(f32[128,8]{0,1:T(8,128)} %param.10) | copy-start | bytes 12292
  5.4 0.7 %copy-start.3 = (s32[128,8]{0,1:T(8,128)S(1)}, s32[128,8]{0,1:T(8,128)}, u32[]{:S(2)}) copy-start(s32[128,8]{0,1:T(8,128)} %param.9) | copy-start | bytes 12292
  6.1 1.0 %copy-start.2 = (bf16[128,2048]{1,0:T(8,128)(2,1)S(1)}, bf16[128,2048]{1,0:T(8,128)(2,1)}, u32[]{:S(2)}) copy-start(bf16[128,2048]{1,0:T(8,128)(2,1)} %x_ref.1) | copy-start | bytes 1572868
  8.1 22.8 %collective-permute-start.7 = (bf16[384,512]{1,0:T(8,128)(2,1)S(1)}, bf16[384,512]{1,0:T(8,128)(2,1)S(1)}, u32[]{:S(2)}, u32[]{:S(2)}) collective-permute-start(bf16[384,512]{1,0:T(8,128)(2,1)S(1)} %bitcast.13), channel_id=1, source_target_pairs={{0,2},{1,3},{2,0},{3,1},{4,6},{5,7},{6,4},{7,5},{8,10},{9,11},{10,... | collective-permute-start | bytes 1179656 | tf_op jit(solution)/shard_map/ppermute | solution.py:279
  15.3 16.1 %collective-permute-start.10 = (bf16[512,384]{1,0:T(8,128)(2,1)S(1)}, bf16[512,384]{1,0:T(8,128)(2,1)S(1)}, u32[]{:S(2)}, u32[]{:S(2)}) collective-permute-start(bf16[512,384]{1,0:T(8,128)(2,1)S(1)} %collective-permute-done.6.refs_10_.refs_6_), channel_id=1, source_target_pairs={{0,16},{16,0},{1,17},{17,1},{2,18},{18,2},{3,19},{19,3},{4,20},{20... | collective-permute-start | bytes 1179656 | tf_op jit(solution)/shard_map/ppermute | solution.py:282
  17.3 6.4 %collective-permute-start.3 = (bf16[32,2048]{1,0:T(8,128)(2,1)S(1)}, bf16[32,2048]{1,0:T(8,128)(2,1)S(1)}, u32[]{:S(2)}, u32[]{:S(2)}) collective-permute-start(bf16[32,2048]{1,0:T(8,128)(2,1)S(1)} %get-tuple-element.63), channel_id=1, source_target_pairs={{0,4},{4,0},{8,12},{12,8},{1,5},{5,1},{9,13},{13,9},{2,6},{6,2},{1... | collective-permute-start | bytes 393224 | tf_op jit(solution)/shard_map/ppermute | solution.py:289
  18.9 12.0 %collective-permute-start.4 = (bf16[32,2048]{1,0:T(8,128)(2,1)S(1)}, bf16[32,2048]{1,0:T(8,128)(2,1)S(1)}, u32[]{:S(2)}, u32[]{:S(2)}) collective-permute-start(bf16[32,2048]{1,0:T(8,128)(2,1)S(1)} %get-tuple-element.64), channel_id=1, source_target_pairs={{0,8},{4,12},{8,0},{12,4},{1,9},{5,13},{9,1},{13,5},{2,10},{6,14},... | collective-permute-start | bytes 393224 | tf_op jit(solution)/shard_map/ppermute | solution.py:289
  21.5 9.4 %collective-permute-start.5 = (bf16[32,2048]{1,0:T(8,128)(2,1)S(1)}, bf16[32,2048]{1,0:T(8,128)(2,1)S(1)}, u32[]{:S(2)}, u32[]{:S(2)}) collective-permute-start(bf16[32,2048]{1,0:T(8,128)(2,1)S(1)} %get-tuple-element.65), channel_id=1, source_target_pairs={{0,12},{4,8},{8,4},{12,0},{1,13},{5,9},{9,5},{13,1},{2,14},{6,10},... | collective-permute-start | bytes 393224 | tf_op jit(solution)/shard_map/ppermute | solution.py:289
  30.9 1.7 %collective-permute-start.8 = (bf16[512,384]{1,0:T(8,128)(2,1)S(1)}, bf16[512,384]{1,0:T(8,128)(2,1)S(1)}, u32[]{:S(2)}, u32[]{:S(2)}) collective-permute-start(bf16[512,384]{1,0:T(8,128)(2,1)S(1)} %collective-permute-done.6.refs_10_.refs_6_), channel_id=1, source_target_pairs={{0,1},{1,0},{2,3},{3,2},{4,5},{5,4},{6,7},{7,6},{8,9},{9,8},{10,11... | collective-permute-start | bytes 1179656 | tf_op jit(solution)/shard_map/ppermute | solution.py:279
  30.9 2.3 %collective-permute-start.9 = (bf16[384,512]{1,0:T(8,128)(2,1)S(1)}, bf16[384,512]{1,0:T(8,128)(2,1)S(1)}, u32[]{:S(2)}, u32[]{:S(2)}) collective-permute-start(bf16[384,512]{1,0:T(8,128)(2,1)S(1)} %collective-permute-done.7.refs_11_.refs_8_), channel_id=1, source_target_pairs={{0,1},{1,0},{2,3},{3,2},{4,5},{5,4},{6,7},{7,6},{8,9},{9,8},{10,11... | collective-permute-start | bytes 1179656 | tf_op jit(solution)/shard_map/ppermute | solution.py:279
  31.4 5.4 %collective-permute-start.11 = (bf16[512,384]{1,0:T(8,128)(2,1)S(1)}, bf16[512,384]{1,0:T(8,128)(2,1)S(1)}, u32[]{:S(2)}, u32[]{:S(2)}) collective-permute-start(bf16[512,384]{1,0:T(8,128)(2,1)S(1)} %collective-permute-done.10.refs_7_), channel_id=1, source_target_pairs={{0,1},{1,0},{2,3},{3,2},{4,5},{5,4},{6,7},{7,6},{8,9},{9,8},{10,11... | collective-permute-start | bytes 1179656 | tf_op jit(solution)/shard_map/ppermute | solution.py:279
  35.3 11.6 %collective-permute-start.16 = (bf16[128,1024]{1,0:T(8,128)(2,1)S(1)}, bf16[128,1024]{1,0:T(8,128)(2,1)S(1)}, u32[]{:S(2)}, u32[]{:S(2)}) collective-permute-start(bf16[128,1024]{1,0:T(8,128)(2,1)S(1)} %get-tuple-element.77), channel_id=1, source_target_pairs={{0,2},{1,3},{2,0},{3,1},{4,6},{5,7},{6,4},{7,5},{8,10},{9,11},{10,... | collective-permute-start | bytes 786440 | tf_op jit(solution)/shard_map/ppermute | solution.py:279
  39.5 7.3 %collective-permute-start.15 = (bf16[64,1152]{1,0:T(8,128)(2,1)S(1)}, bf16[64,1152]{1,0:T(8,128)(2,1)S(1)}, u32[]{:S(2)}, u32[]{:S(2)}) collective-permute-start(bf16[64,1152]{1,0:T(8,128)(2,1)S(1)} %get-tuple-element.93.refs_4_), channel_id=1, source_target_pairs={{0,2},{1,3},{2,0},{3,1},{4,6},{5,7},{6,4},{7,5},{8,10},{9,11},{10,... | collective-permute-start | bytes 442376 | tf_op jit(solution)/shard_map/ppermute | solution.py:279
  46.9 4.6 %collective-permute-start.17 = (bf16[256,512]{1,0:T(8,128)(2,1)S(1)}, bf16[256,512]{1,0:T(8,128)(2,1)S(1)}, u32[]{:S(2)}, u32[]{:S(2)}) collective-permute-start(bf16[256,512]{1,0:T(8,128)(2,1)S(1)} %pad_maximum_fusion), channel_id=1, source_target_pairs={{0,1},{1,0},{2,3},{3,2},{4,5},{5,4},{6,7},{7,6},{8,9},{9,8},{10,11... | collective-permute-start | bytes 786440 | tf_op jit(solution)/shard_map/ppermute | solution.py:279
  47.0 8.3 %collective-permute-start.12 = (bf16[32,2048]{1,0:T(8,128)(2,1)S(1)}, bf16[32,2048]{1,0:T(8,128)(2,1)S(1)}, u32[]{:S(2)}, u32[]{:S(2)}) collective-permute-start(bf16[32,2048]{1,0:T(8,128)(2,1)S(1)} %get-tuple-element.72), channel_id=1, source_target_pairs={{0,4},{4,0},{8,12},{12,8},{1,5},{5,1},{9,13},{13,9},{2,6},{6,2},{1... | collective-permute-start | bytes 393224 | tf_op jit(solution)/shard_map/ppermute | solution.py:289
  49.0 12.9 %collective-permute-start.13 = (bf16[32,2048]{1,0:T(8,128)(2,1)S(1)}, bf16[32,2048]{1,0:T(8,128)(2,1)S(1)}, u32[]{:S(2)}, u32[]{:S(2)}) collective-permute-start(bf16[32,2048]{1,0:T(8,128)(2,1)S(1)} %get-tuple-element.73), channel_id=1, source_target_pairs={{0,8},{4,12},{8,0},{12,4},{1,9},{5,13},{9,1},{13,5},{2,10},{6,14},... | collective-permute-start | bytes 393224 | tf_op jit(solution)/shard_map/ppermute | solution.py:289
  50.1 11.8 %collective-permute-start.14 = (bf16[32,2048]{1,0:T(8,128)(2,1)S(1)}, bf16[32,2048]{1,0:T(8,128)(2,1)S(1)}, u32[]{:S(2)}, u32[]{:S(2)}) collective-permute-start(bf16[32,2048]{1,0:T(8,128)(2,1)S(1)} %get-tuple-element.74), channel_id=1, source_target_pairs={{0,12},{4,8},{8,4},{12,0},{1,13},{5,9},{9,5},{13,1},{2,14},{6,10},... | collective-permute-start | bytes 393224 | tf_op jit(solution)/shard_map/ppermute | solution.py:289
  51.5 10.4 %collective-permute-start.18 = (bf16[64,1152]{1,0:T(8,128)(2,1)S(1)}, bf16[64,1152]{1,0:T(8,128)(2,1)S(1)}, u32[]{:S(2)}, u32[]{:S(2)}) collective-permute-start(bf16[64,1152]{1,0:T(8,128)(2,1)S(1)} %get-tuple-element.93.refs_4_), channel_id=1, source_target_pairs={{0,1},{1,0},{2,3},{3,2},{4,5},{5,4},{6,7},{7,6},{8,9},{9,8},{10,11... | collective-permute-start | bytes 442376 | tf_op jit(solution)/shard_map/ppermute | solution.py:279
  51.5 10.4 %collective-permute-start.19 = (bf16[64,1152]{1,0:T(8,128)(2,1)S(1)}, bf16[64,1152]{1,0:T(8,128)(2,1)S(1)}, u32[]{:S(2)}, u32[]{:S(2)}) collective-permute-start(bf16[64,1152]{1,0:T(8,128)(2,1)S(1)} %collective-permute-done.15.refs_5_), channel_id=1, source_target_pairs={{0,1},{1,0},{2,3},{3,2},{4,5},{5,4},{6,7},{7,6},{8,9},{9,8},{10,11... | collective-permute-start | bytes 442376 | tf_op jit(solution)/shard_map/ppermute | solution.py:279

commit v5 on v4

--- a/solution.py
+++ b/solution.py
@@ -10,6 +10,8 @@
 BF16 = jnp.bfloat16
 F32 = jnp.float32
 VMEM_LIMIT = 16 << 20
+FIRST_WEIGHT = 1 << 36
+COLLECT_WEIGHT = 1 << 33
 
 
 def dot(left, right):
@@ -28,7 +30,7 @@
     return jax.ShapeDtypeStruct(dims, dtype)
 
 
-def call(kernel, out_shape, *args, smem=0, scratch=(), flops=0, anywhere=()):
+def call(kernel, out_shape, *args, smem=0, scratch=(), flops=0, anywhere=(), weight=1):
     vmem = pl.BlockSpec(memory_space=pltpu.VMEM)
     specs = [
         pl.BlockSpec(memory_space=pltpu.SMEM)
@@ -45,7 +47,7 @@
         out_specs=jax.tree.map(lambda _: vmem, out_shape),
         scratch_shapes=list(scratch),
         compiler_params=pltpu.CompilerParams(vmem_limit_bytes=VMEM_LIMIT),
-        cost_estimate=pl.CostEstimate(flops=flops, bytes_accessed=1, transcendentals=0),
+        cost_estimate=pl.CostEstimate(flops=weight, bytes_accessed=1, transcendentals=0),
     )(*args)
 
 
@@ -162,7 +164,7 @@
         shape((2 * total, model_width - near * width)),
         shape((total, 4 * ff), F32),
     ]
-    return call(kernel, outs, *chunks, *weights)
+    return call(kernel, outs, *chunks, *weights, weight=FIRST_WEIGHT)
 
 
 def second_half(flag, rows, sums, pieces, near, width, count):
@@ -260,7 +262,9 @@
         shape((token_rows, model_width)),
         shape(ids.shape, F32),
     ]
-    return call(kernel, outs, place, ids, select, table, cotangent, *chunks, smem=1)
+    return call(
+        kernel, outs, place, ids, select, table, cotangent, *chunks, smem=1, weight=COLLECT_WEIGHT
+    )
 
 
 def on_device(tokens, cotangent, expert_ids, gate_probs, w_gate, w_up, w_down):
@@ -341,10 +345,10 @@
     kept += [theirs[i * size : (i + 1) * size] for i in range(len(kept))]
     trios += [to_dp(t, 1) for t in trios]
 
-    home, kept, trios = lax.optimization_barrier((home, kept, trios))
     mixed, grad_tokens, grad_gates = collect(
         place, ids, select, table, cotangent, home, dp_count, even
     )
+    mixed, kept, trios = lax.optimization_barrier((mixed, kept, trios))
     grad_w_gate, grad_w_up, grad_w_down = gradients(kept, trios, width, ff)
     return (
         mixed,

time: 65.6 us -> 52.7 us (0.80)
  waiting for transfers between devices: 34.7 us -> 22.8 us
  local copies, waits for them, and re-layouts: 1.71 us -> 0.67 us
    ppermute x13, waiting for transfers between devices: 15.6 us -> 7.99 us  [to_dp(): return lax.ppermute(array, 'dp', [(i, i ^ mask) for i in range(dp_count)])]
    ppermute x6, waiting for transfers between devices: 19.1 us -> 12.4 us  [to_expert(): return lax.ppermute(array, 'expert', pairs)]
    ppermute x1, waiting for transfers between devices: 0.01 us -> 2.44 us  [to_group(): return lax.ppermute(array, 'groups', [(0, 1), (1, 0)])]
    unnamed x10, local copies, waits for them, and re-layouts: 1.67 us -> 0.63 us
  transfers between devices with their start and end apart: 20 -> 20, of which waited for: 8 -> 8; matrix products, arithmetic and copies ran while one was open for 0% -> 0% of each run, Pallas kernels for 9% -> 15%
where the time goes in v5:
time: 52.7 us; the launch traced here: 52.4 us
  waiting for transfers between devices  22.8 us (43%)
  starting transfers between devices  17.8 us (34%)
  Pallas kernels  10.2 us (19%)
  between operations  0.78 us (1%)
  local copies, waits for them, and re-layouts  0.67 us (1%)
    ppermute x6, waiting for transfers between devices, to_expert(): return lax.ppermute(array, 'expert', pairs)  12.4 us
    pallas_call x6, Pallas kernels, call(): pl.pallas_call(kernel, out_shape=out_shape, in_specs=specs, out_specs=jax...  10.2 us
    ppermute x6, starting transfers between devices, to_expert(): return lax.ppermute(array, 'expert', pairs)  8.77 us
    ppermute x13, waiting for transfers between devices, to_dp(): return lax.ppermute(array, 'dp', [(i, i ^ mask) for i in range(dp_count)])  7.99 us
    ppermute x13, starting transfers between devices, to_dp(): return lax.ppermute(array, 'dp', [(i, i ^ mask) for i in range(dp_count)])  7.08 us
    ppermute x1, waiting for transfers between devices, to_group(): return lax.ppermute(array, 'groups', [(0, 1), (1, 0)])  2.44 us
    ppermute x1, starting transfers between devices, to_group(): return lax.ppermute(array, 'groups', [(0, 1), (1, 0)])  1.98 us
  transfers between devices with their start and end apart: 20, of which 8 were waited for; matrix products, arithmetic and copies ran while one was open for 0% of the time, Pallas kernels for 15%

profile of v5, /device:TPU:0, one launch (start us, length us, event | category | flops | bytes accessed | tf_op | source)
XLA Modules:
  0.0 52.4 jit_solution(14561844066039877213)
XLA Ops:
  0.6 0.0 copy-start
  0.6 0.0 copy-start.1
  0.7 1.1 %shard_map.119 = bf16[512,384]{1,0:T(8,128)(2,1)S(1)} custom-call(s32[1]{0:T(128)} %bitcast.4.flag_ref, bf16[512,384]{1,0:T(8,128)(2,1)} %bitcast.5.first_ref.refs_4_.refs_0_, bf16[512,384]{1,0:T(8,128)(2,1)} %bitcast.6.second_ref.refs_5_.refs_1_), custom_call_target="tpu_custom_call" | custom-call | flops 1 | bytes 1 | tf_op jit(solution)/shard_map/pallas_call | solution.py:43
  1.8 0.5 collective-permute-start
  2.3 0.1 collective-permute-start.1
  2.4 0.4 collective-permute-start.2
  2.8 2.6 %collective-permute-start.6 = (bf16[512,384]{1,0:T(8,128)(2,1)S(1)}, bf16[512,384]{1,0:T(8,128)(2,1)S(1)}, u32[]{:S(2)}, u32[]{:S(2)}) collective-permute-start(bf16[512,384]{1,0:T(8,128)(2,1)S(1)} %shard_map.119), channel_id=1, source_target_pairs={{0,2},{1,3},{2,0},{3,1},{4,6},{5,7},{6,4},{7,5},{8,10},{9,11},{10,... | collective-permute-start | bytes 1179656 | tf_op jit(solution)/shard_map/ppermute | solution.py:283
  5.4 0.0 copy-start.4
  5.4 0.0 copy-start.3
  5.4 0.1 pad_add_fusion.place_ref
  5.4 0.0 copy-done
  5.4 0.0 copy-done.1
  5.4 0.6 %copy-done.4 = s32[128,8]{0,1:T(8,128)S(1)} copy-done((s32[128,8]{0,1:T(8,128)S(1)}, s32[128,8]{0,1:T(8,128)}, u32[]{:S(2)}) %copy-start.4) | copy-done | bytes 4120
  6.0 0.0 copy-done.3
  6.1 0.0 copy-start.2
  6.1 1.0 %shard_map.118 = (bf16[32,2048]{1,0:T(8,128)(2,1)S(1)}, bf16[32,2048]{1,0:T(8,128)(2,1)S(1)}, bf16[32,2048]{1,0:T(8,128)(2,1)S(1)}, bf16[32,2048]{1,0:T(8,128)(2...) custom-call(s32[2]{0:T(128)S(1)} %pad_add_fusion.place_ref, s32[8,128]{1,0:T(8,128)S(1)} %bitcast.17, ...), custom_call_target="tpu_custom_call" | custom-call | flops 1 | bytes 1 | tf_op jit(solution)/shard_map/pallas_call | solution.py:43
  7.0 0.0 collective-permute-done.refs_7_.refs_3_
  7.0 0.0 collective-permute-done.1.refs_8_.refs_4_
  7.1 0.0 collective-permute-done.2.refs_9_.refs_5_
  7.1 0.0 copy-done.2
  7.1 0.7 %collective-permute-start.7 = (bf16[384,512]{1,0:T(8,128)(2,1)S(1)}, bf16[384,512]{1,0:T(8,128)(2,1)S(1)}, u32[]{:S(2)}, u32[]{:S(2)}) collective-permute-start(bf16[384,512]{1,0:T(8,128)(2,1)S(1)} %bitcast.13), channel_id=1, source_target_pairs={{0,2},{1,3},{2,0},{3,1},{4,6},{5,7},{6,4},{7,5},{8,10},{9,11},{10,... | collective-permute-start | bytes 1179656 | tf_op jit(solution)/shard_map/ppermute | solution.py:283
  7.8 1.6 %collective-permute-start.3 = (bf16[32,2048]{1,0:T(8,128)(2,1)S(1)}, bf16[32,2048]{1,0:T(8,128)(2,1)S(1)}, u32[]{:S(2)}, u32[]{:S(2)}) collective-permute-start(bf16[32,2048]{1,0:T(8,128)(2,1)S(1)} %get-tuple-element.60), channel_id=1, source_target_pairs={{0,4},{4,0},{8,12},{12,8},{1,5},{5,1},{9,13},{13,9},{2,6},{6,2},{1... | collective-permute-start | bytes 393224 | tf_op jit(solution)/shard_map/ppermute | solution.py:293
  9.4 2.6 %collective-permute-start.4 = (bf16[32,2048]{1,0:T(8,128)(2,1)S(1)}, bf16[32,2048]{1,0:T(8,128)(2,1)S(1)}, u32[]{:S(2)}, u32[]{:S(2)}) collective-permute-start(bf16[32,2048]{1,0:T(8,128)(2,1)S(1)} %get-tuple-element.61), channel_id=1, source_target_pairs={{0,8},{4,12},{8,0},{12,4},{1,9},{5,13},{9,1},{13,5},{2,10},{6,14},... | collective-permute-start | bytes 393224 | tf_op jit(solution)/shard_map/ppermute | solution.py:293
  12.0 0.2 collective-permute-start.5
  12.2 3.1 %collective-permute-done.6.refs_10_.refs_6_ = bf16[512,384]{1,0:T(8,128)(2,1)S(1)} collective-permute-done((bf16[512,384]{1,0:T(8,128)(2,1)S(1)}, bf16[512,384]{1,0:T(8,128)(2,1)S(1)}, u32[]{:S(2)}, u32[]{:S(2)}) %collective-permute-start.6) | collective-permute-done | bytes 393248 | tf_op jit(solution)/shard_map/ppermute | solution.py:283
  15.3 2.0 %collective-permute-start.10 = (bf16[512,384]{1,0:T(8,128)(2,1)S(1)}, bf16[512,384]{1,0:T(8,128)(2,1)S(1)}, u32[]{:S(2)}, u32[]{:S(2)}) collective-permute-start(bf16[512,384]{1,0:T(8,128)(2,1)S(1)} %collective-permute-done.6.refs_10_.refs_6_), channel_id=1, source_target_pairs={{0,16},{16,0},{1,17},{17,1},{2,18},{18,2},{3,19},{19,3},{4,20},{20... | collective-permute-start | bytes 1179656 | tf_op jit(solution)/shard_map/ppermute | solution.py:286
  17.3 0.0 collective-permute-done.3.refs_1_
  17.3 5.0 %collective-permute-done.4.refs_2_ = bf16[32,2048]{1,0:T(8,128)(2,1)S(1)} collective-permute-done((bf16[32,2048]{1,0:T(8,128)(2,1)S(1)}, bf16[32,2048]{1,0:T(8,128)(2,1)S(1)}, u32[]{:S(2)}, u32[]{:S(2)}) %collective-permute-start.4) | collective-permute-done | bytes 131104 | tf_op jit(solution)/shard_map/ppermute | solution.py:293
  22.3 0.0 collective-permute-done.5.refs_3_
  22.3 0.0 collective-permute-start.8
  22.3 1.1 %collective-permute-done.7.refs_11_.refs_8_ = bf16[384,512]{1,0:T(8,128)(2,1)S(1)} collective-permute-done((bf16[384,512]{1,0:T(8,128)(2,1)S(1)}, bf16[384,512]{1,0:T(8,128)(2,1)S(1)}, u32[]{:S(2)}, u32[]{:S(2)}) %collective-permute-start.7) | collective-permute-done | bytes 393248 | tf_op jit(solution)/shard_map/ppermute | solution.py:283
  23.5 0.0 collective-permute-start.9
  23.5 2.4 %collective-permute-done.10.refs_7_ = bf16[512,384]{1,0:T(8,128)(2,1)S(1)} collective-permute-done((bf16[512,384]{1,0:T(8,128)(2,1)S(1)}, bf16[512,384]{1,0:T(8,128)(2,1)S(1)}, u32[]{:S(2)}, u32[]{:S(2)}) %collective-permute-start.10) | collective-permute-done | bytes 393248 | tf_op jit(solution)/shard_map/ppermute | solution.py:286
  25.9 0.0 collective-permute-start.11
  25.9 0.0 collective-permute-done.8.refs_12_.refs_9_
  25.9 0.0 collective-permute-done.9.refs_13_.refs_11_
  25.9 2.1 %shard_map.120 = (bf16[128,2048]{1,0:T(8,128)(2,1)S(1)}, bf16[128,1024]{1,0:T(8,128)(2,1)S(1)}, bf16[128,1024]{1,0:T(8,128)(2,1)S(1)}, f32[64,1536]{1,0:T(8,128)S(1)}) custom-call(bf16[32,2048]{1,0:T(8,128)(2,1)S(1)} %get-tuple-element.59.refs_0_, bf16[32,2048]{1,0:T(8,128)(2,1)S(1)} %collective-permute-done.3.refs_1_, ...), custom_call_target="tpu_custom_call" | custom-call | flops 68719476736 | bytes 1 | tf_op jit(solution)/shard_map/pallas_call | solution.py:43
  28.0 1.6 %collective-permute-start.16 = (bf16[128,1024]{1,0:T(8,128)(2,1)S(1)}, bf16[128,1024]{1,0:T(8,128)(2,1)S(1)}, u32[]{:S(2)}, u32[]{:S(2)}) collective-permute-start(bf16[128,1024]{1,0:T(8,128)(2,1)S(1)} %get-tuple-element.75), channel_id=1, source_target_pairs={{0,2},{1,3},{2,0},{3,1},{4,6},{5,7},{6,4},{7,5},{8,10},{9,11},{10,... | collective-permute-start | bytes 786440 | tf_op jit(solution)/shard_map/ppermute | solution.py:283
  29.7 0.0 collective-permute-done.11.refs_10_
  29.7 2.7 %shard_map.121 = (bf16[32,2048]{1,0:T(8,128)(2,1)S(1)}, bf16[32,2048]{1,0:T(8,128)(2,1)S(1)}, bf16[32,2048]{1,0:T(8,128)(2,1)S(1)}, bf16[32,2048]{1,0:T(8,128)(2,1)S(1)}, bf16[64,1152]{1,0:T(8,128)(2,1)S(1)}) custom-call(s32[1]{0:T(128)} %bitcast.4.flag_ref, bf16[128,2048]{1,0:T(8,128)(2,1)S(1)} %get-tuple-element.66.rows_ref, ...), custom_call_target="tpu_custom_call" | custom-call | flops 1 | bytes 1 | tf_op jit(solution)/shard_map/pallas_call | solution.py:43
  32.4 0.5 %collective-permute-start.15 = (bf16[64,1152]{1,0:T(8,128)(2,1)S(1)}, bf16[64,1152]{1,0:T(8,128)(2,1)S(1)}, u32[]{:S(2)}, u32[]{:S(2)}) collective-permute-start(bf16[64,1152]{1,0:T(8,128)(2,1)S(1)} %get-tuple-element.87.refs_4_), channel_id=1, source_target_pairs={{0,2},{1,3},{2,0},{3,1},{4,6},{5,7},{6,4},{7,5},{8,10},{9,11},{10,... | collective-permute-start | bytes 442376 | tf_op jit(solution)/shard_map/ppermute | solution.py:283
  32.9 1.6 %collective-permute-start.12 = (bf16[32,2048]{1,0:T(8,128)(2,1)S(1)}, bf16[32,2048]{1,0:T(8,128)(2,1)S(1)}, u32[]{:S(2)}, u32[]{:S(2)}) collective-permute-start(bf16[32,2048]{1,0:T(8,128)(2,1)S(1)} %get-tuple-element.69), channel_id=1, source_target_pairs={{0,4},{4,0},{8,12},{12,8},{1,5},{5,1},{9,13},{13,9},{2,6},{6,2},{1... | collective-permute-start | bytes 393224 | tf_op jit(solution)/shard_map/ppermute | solution.py:293
  34.5 2.6 %collective-permute-start.13 = (bf16[32,2048]{1,0:T(8,128)(2,1)S(1)}, bf16[32,2048]{1,0:T(8,128)(2,1)S(1)}, u32[]{:S(2)}, u32[]{:S(2)}) collective-permute-start(bf16[32,2048]{1,0:T(8,128)(2,1)S(1)} %get-tuple-element.70), channel_id=1, source_target_pairs={{0,8},{4,12},{8,0},{12,4},{1,9},{5,13},{9,1},{13,5},{2,10},{6,14},... | collective-permute-start | bytes 393224 | tf_op jit(solution)/shard_map/ppermute | solution.py:293
  37.1 0.1 collective-permute-start.14
  37.3 2.7 %collective-permute-done.15.refs_5_ = bf16[64,1152]{1,0:T(8,128)(2,1)S(1)} collective-permute-done((bf16[64,1152]{1,0:T(8,128)(2,1)S(1)}, bf16[64,1152]{1,0:T(8,128)(2,1)S(1)}, u32[]{:S(2)}, u32[]{:S(2)}) %collective-permute-start.15) | collective-permute-done | bytes 147488 | tf_op jit(solution)/shard_map/ppermute | solution.py:283
  40.0 0.0 collective-permute-done.16.refs_1_
  40.0 0.1 collective-permute-start.17
  40.1 0.0 collective-permute-done.12.refs_1_
  40.1 7.4 %collective-permute-done.13.refs_2_ = bf16[32,2048]{1,0:T(8,128)(2,1)S(1)} collective-permute-done((bf16[32,2048]{1,0:T(8,128)(2,1)S(1)}, bf16[32,2048]{1,0:T(8,128)(2,1)S(1)}, u32[]{:S(2)}, u32[]{:S(2)}) %collective-permute-start.13) | collective-permute-done | bytes 131104 | tf_op jit(solution)/shard_map/ppermute | solution.py:293
  47.5 0.0 collective-permute-done.14.refs_3_
  47.5 2.0 %shard_map.122 = (bf16[128,2048]{1,0:T(8,128)(2,1)}, bf16[128,2048]{1,0:T(8,128)(2,1)}, f32[8,128]{1,0:T(8,128)}) custom-call(s32[2]{0:T(128)S(1)} %pad_add_fusion.place_ref, s32[8,128]{1,0:T(8,128)S(1)} %bitcast.18, bf16[64,128]{1,0:T(8,128)(2,1)S(1)} %get-tuple-element.50.select_ref, bf16[128,192]{1,0:T(8,128)(2,1)S(1)} %get-tuple-element.51.table_ref, ...), custom_call_target="tpu_custom_call" | custom-call | flops 8589934592 | bytes 1 | tf_op jit(solution)/shard_map/pallas_call | solution.py:43
  49.5 0.0 collective-permute-start.18
  49.5 0.5 collective-permute-start.19
  50.0 0.0 collective-permute-done.17
  50.1 0.8 %collective-permute-done.18.refs_6_ = bf16[64,1152]{1,0:T(8,128)(2,1)S(1)} collective-permute-done((bf16[64,1152]{1,0:T(8,128)(2,1)S(1)}, bf16[64,1152]{1,0:T(8,128)(2,1)S(1)}, u32[]{:S(2)}, u32[]{:S(2)}) %collective-permute-start.18) | collective-permute-done | bytes 147488 | tf_op jit(solution)/shard_map/ppermute | solution.py:283
  50.9 0.2 collective-permute-done.19.refs_7_
  51.1 1.3 %shard_map.123 = (bf16[512,384]{1,0:T(8,128)(2,1)}, bf16[512,384]{1,0:T(8,128)(2,1)}, bf16[384,512]{1,0:T(8,128)(2,1)}) custom-call(bf16[128,1024]{1,0:T(8,128)(2,1)S(1)} %get-tuple-element.83.refs_0_, bf16[128,1024]{1,0:T(8,128)(2,1)S(1)} %collective-permute-done.16.refs_1_, bf16[128,512]{1,0:T(8,128)(2,1)S(1)} %get-tuple-element.85.refs_2_, ...), custom_call_target="tpu_custom_call" | custom-call | flops 1 | bytes 1 | tf_op jit(solution)/shard_map/pallas_call | solution.py:43
  (4 shorter events, 0.1 us)
Async XLA Ops:
  0.6 4.8 %copy-start = (bf16[128,2048]{1,0:T(8,128)(2,1)S(1)}, bf16[128,2048]{1,0:T(8,128)(2,1)}, u32[]{:S(2)}) copy-start(bf16[128,2048]{1,0:T(8,128)(2,1)} %x_ref.1) | copy-start | bytes 1572868
  0.6 4.8 %copy-start.1 = (bf16[128,2048]{1,0:T(8,128)(2,1)S(1)}, bf16[128,2048]{1,0:T(8,128)(2,1)}, u32[]{:S(2)}) copy-start(bf16[128,2048]{1,0:T(8,128)(2,1)} %dy_ref.3) | copy-start | bytes 1572868
  1.8 5.3 %collective-permute-start = (bf16[512,384]{1,0:T(8,128)(2,1)}, bf16[512,384]{1,0:T(8,128)(2,1)S(1)}, u32[]{:S(2)}, u32[]{:S(2)}) collective-permute-start(bf16[512,384]{1,0:T(8,128)(2,1)} %bitcast.5.first_ref.refs_4_.refs_0_), channel_id=1, source_target_pairs={{0,1},{1,0},{2,3},{3,2},{4,5},{5,4},{6,7},{7,6},{8,9},{9,8},{10,11... | collective-permute-start | bytes 1179656 | tf_op jit(solution)/shard_map/ppermute | solution.py:283
  2.3 4.8 %collective-permute-start.1 = (bf16[512,384]{1,0:T(8,128)(2,1)}, bf16[512,384]{1,0:T(8,128)(2,1)S(1)}, u32[]{:S(2)}, u32[]{:S(2)}) collective-permute-start(bf16[512,384]{1,0:T(8,128)(2,1)} %bitcast.6.second_ref.refs_5_.refs_1_), channel_id=1, source_target_pairs={{0,1},{1,0},{2,3},{3,2},{4,5},{5,4},{6,7},{7,6},{8,9},{9,8},{10,11... | collective-permute-start | bytes 1179656 | tf_op jit(solution)/shard_map/ppermute | solution.py:283
  2.4 4.7 %collective-permute-start.2 = (bf16[384,512]{1,0:T(8,128)(2,1)}, bf16[384,512]{1,0:T(8,128)(2,1)S(1)}, u32[]{:S(2)}, u32[]{:S(2)}) collective-permute-start(bf16[384,512]{1,0:T(8,128)(2,1)} %bitcast.12), channel_id=1, source_target_pairs={{0,1},{1,0},{2,3},{3,2},{4,5},{5,4},{6,7},{7,6},{8,9},{9,8},{10,11... | collective-permute-start | bytes 1179656 | tf_op jit(solution)/shard_map/ppermute | solution.py:283
  2.8 12.5 %collective-permute-start.6 = (bf16[512,384]{1,0:T(8,128)(2,1)S(1)}, bf16[512,384]{1,0:T(8,128)(2,1)S(1)}, u32[]{:S(2)}, u32[]{:S(2)}) collective-permute-start(bf16[512,384]{1,0:T(8,128)(2,1)S(1)} %shard_map.119), channel_id=1, source_target_pairs={{0,2},{1,3},{2,0},{3,1},{4,6},{5,7},{6,4},{7,5},{8,10},{9,11},{10,... | collective-permute-start | bytes 1179656 | tf_op jit(solution)/shard_map/ppermute | solution.py:283
  5.4 0.7 %copy-start.4 = (s32[128,8]{0,1:T(8,128)S(1)}, s32[128,8]{0,1:T(8,128)}, u32[]{:S(2)}) copy-start(s32[128,8]{0,1:T(8,128)} %param.9) | copy-start | bytes 12292
  5.4 0.7 %copy-start.3 = (f32[128,8]{0,1:T(8,128)S(1)}, f32[128,8]{0,1:T(8,128)}, u32[]{:S(2)}) copy-start(f32[128,8]{0,1:T(8,128)} %param.10) | copy-start | bytes 12292
  6.1 1.0 %copy-start.2 = (bf16[1,384,512]{2,1,0:T(8,128)(2,1)S(1)}, bf16[1,384,512]{2,1,0:T(8,128)(2,1)}, u32[]{:S(2)}) copy-start(bf16[1,384,512]{2,1,0:T(8,128)(2,1)} %param.13) | copy-start | bytes 1179652
  7.1 16.4 %collective-permute-start.7 = (bf16[384,512]{1,0:T(8,128)(2,1)S(1)}, bf16[384,512]{1,0:T(8,128)(2,1)S(1)}, u32[]{:S(2)}, u32[]{:S(2)}) collective-permute-start(bf16[384,512]{1,0:T(8,128)(2,1)S(1)} %bitcast.13), channel_id=1, source_target_pairs={{0,2},{1,3},{2,0},{3,1},{4,6},{5,7},{6,4},{7,5},{8,10},{9,11},{10,... | collective-permute-start | bytes 1179656 | tf_op jit(solution)/shard_map/ppermute | solution.py:283
  7.8 9.5 %collective-permute-start.3 = (bf16[32,2048]{1,0:T(8,128)(2,1)S(1)}, bf16[32,2048]{1,0:T(8,128)(2,1)S(1)}, u32[]{:S(2)}, u32[]{:S(2)}) collective-permute-start(bf16[32,2048]{1,0:T(8,128)(2,1)S(1)} %get-tuple-element.60), channel_id=1, source_target_pairs={{0,4},{4,0},{8,12},{12,8},{1,5},{5,1},{9,13},{13,9},{2,6},{6,2},{1... | collective-permute-start | bytes 393224 | tf_op jit(solution)/shard_map/ppermute | solution.py:293
  9.4 12.9 %collective-permute-start.4 = (bf16[32,2048]{1,0:T(8,128)(2,1)S(1)}, bf16[32,2048]{1,0:T(8,128)(2,1)S(1)}, u32[]{:S(2)}, u32[]{:S(2)}) collective-permute-start(bf16[32,2048]{1,0:T(8,128)(2,1)S(1)} %get-tuple-element.61), channel_id=1, source_target_pairs={{0,8},{4,12},{8,0},{12,4},{1,9},{5,13},{9,1},{13,5},{2,10},{6,14},... | collective-permute-start | bytes 393224 | tf_op jit(solution)/shard_map/ppermute | solution.py:293
  12.0 10.4 %collective-permute-start.5 = (bf16[32,2048]{1,0:T(8,128)(2,1)S(1)}, bf16[32,2048]{1,0:T(8,128)(2,1)S(1)}, u32[]{:S(2)}, u32[]{:S(2)}) collective-permute-start(bf16[32,2048]{1,0:T(8,128)(2,1)S(1)} %get-tuple-element.62), channel_id=1, source_target_pairs={{0,12},{4,8},{8,4},{12,0},{1,13},{5,9},{9,5},{13,1},{2,14},{6,10},... | collective-permute-start | bytes 393224 | tf_op jit(solution)/shard_map/ppermute | solution.py:293
  15.3 10.6 %collective-permute-start.10 = (bf16[512,384]{1,0:T(8,128)(2,1)S(1)}, bf16[512,384]{1,0:T(8,128)(2,1)S(1)}, u32[]{:S(2)}, u32[]{:S(2)}) collective-permute-start(bf16[512,384]{1,0:T(8,128)(2,1)S(1)} %collective-permute-done.6.refs_10_.refs_6_), channel_id=1, source_target_pairs={{0,16},{16,0},{1,17},{17,1},{2,18},{18,2},{3,19},{19,3},{4,20},{20... | collective-permute-start | bytes 1179656 | tf_op jit(solution)/shard_map/ppermute | solution.py:286
  22.3 3.6 %collective-permute-start.8 = (bf16[512,384]{1,0:T(8,128)(2,1)S(1)}, bf16[512,384]{1,0:T(8,128)(2,1)S(1)}, u32[]{:S(2)}, u32[]{:S(2)}) collective-permute-start(bf16[512,384]{1,0:T(8,128)(2,1)S(1)} %collective-permute-done.6.refs_10_.refs_6_), channel_id=1, source_target_pairs={{0,1},{1,0},{2,3},{3,2},{4,5},{5,4},{6,7},{7,6},{8,9},{9,8},{10,11... | collective-permute-start | bytes 1179656 | tf_op jit(solution)/shard_map/ppermute | solution.py:283
  23.5 2.5 %collective-permute-start.9 = (bf16[384,512]{1,0:T(8,128)(2,1)S(1)}, bf16[384,512]{1,0:T(8,128)(2,1)S(1)}, u32[]{:S(2)}, u32[]{:S(2)}) collective-permute-start(bf16[384,512]{1,0:T(8,128)(2,1)S(1)} %collective-permute-done.7.refs_11_.refs_8_), channel_id=1, source_target_pairs={{0,1},{1,0},{2,3},{3,2},{4,5},{5,4},{6,7},{7,6},{8,9},{9,8},{10,11... | collective-permute-start | bytes 1179656 | tf_op jit(solution)/shard_map/ppermute | solution.py:283
  25.9 3.7 %collective-permute-start.11 = (bf16[512,384]{1,0:T(8,128)(2,1)S(1)}, bf16[512,384]{1,0:T(8,128)(2,1)S(1)}, u32[]{:S(2)}, u32[]{:S(2)}) collective-permute-start(bf16[512,384]{1,0:T(8,128)(2,1)S(1)} %collective-permute-done.10.refs_7_), channel_id=1, source_target_pairs={{0,1},{1,0},{2,3},{3,2},{4,5},{5,4},{6,7},{7,6},{8,9},{9,8},{10,11... | collective-permute-start | bytes 1179656 | tf_op jit(solution)/shard_map/ppermute | solution.py:283
  28.0 11.9 %collective-permute-start.16 = (bf16[128,1024]{1,0:T(8,128)(2,1)S(1)}, bf16[128,1024]{1,0:T(8,128)(2,1)S(1)}, u32[]{:S(2)}, u32[]{:S(2)}) collective-permute-start(bf16[128,1024]{1,0:T(8,128)(2,1)S(1)} %get-tuple-element.75), channel_id=1, source_target_pairs={{0,2},{1,3},{2,0},{3,1},{4,6},{5,7},{6,4},{7,5},{8,10},{9,11},{10,... | collective-permute-start | bytes 786440 | tf_op jit(solution)/shard_map/ppermute | solution.py:283
  32.4 7.6 %collective-permute-start.15 = (bf16[64,1152]{1,0:T(8,128)(2,1)S(1)}, bf16[64,1152]{1,0:T(8,128)(2,1)S(1)}, u32[]{:S(2)}, u32[]{:S(2)}) collective-permute-start(bf16[64,1152]{1,0:T(8,128)(2,1)S(1)} %get-tuple-element.87.refs_4_), channel_id=1, source_target_pairs={{0,2},{1,3},{2,0},{3,1},{4,6},{5,7},{6,4},{7,5},{8,10},{9,11},{10,... | collective-permute-start | bytes 442376 | tf_op jit(solution)/shard_map/ppermute | solution.py:283
  32.9 7.2 %collective-permute-start.12 = (bf16[32,2048]{1,0:T(8,128)(2,1)S(1)}, bf16[32,2048]{1,0:T(8,128)(2,1)S(1)}, u32[]{:S(2)}, u32[]{:S(2)}) collective-permute-start(bf16[32,2048]{1,0:T(8,128)(2,1)S(1)} %get-tuple-element.69), channel_id=1, source_target_pairs={{0,4},{4,0},{8,12},{12,8},{1,5},{5,1},{9,13},{13,9},{2,6},{6,2},{1... | collective-permute-start | bytes 393224 | tf_op jit(solution)/shard_map/ppermute | solution.py:293
  34.5 12.9 %collective-permute-start.13 = (bf16[32,2048]{1,0:T(8,128)(2,1)S(1)}, bf16[32,2048]{1,0:T(8,128)(2,1)S(1)}, u32[]{:S(2)}, u32[]{:S(2)}) collective-permute-start(bf16[32,2048]{1,0:T(8,128)(2,1)S(1)} %get-tuple-element.70), channel_id=1, source_target_pairs={{0,8},{4,12},{8,0},{12,4},{1,9},{5,13},{9,1},{13,5},{2,10},{6,14},... | collective-permute-start | bytes 393224 | tf_op jit(solution)/shard_map/ppermute | solution.py:293
  37.1 10.3 %collective-permute-start.14 = (bf16[32,2048]{1,0:T(8,128)(2,1)S(1)}, bf16[32,2048]{1,0:T(8,128)(2,1)S(1)}, u32[]{:S(2)}, u32[]{:S(2)}) collective-permute-start(bf16[32,2048]{1,0:T(8,128)(2,1)S(1)} %get-tuple-element.71), channel_id=1, source_target_pairs={{0,12},{4,8},{8,4},{12,0},{1,13},{5,9},{9,5},{13,1},{2,14},{6,10},... | collective-permute-start | bytes 393224 | tf_op jit(solution)/shard_map/ppermute | solution.py:293
  40.0 10.0 %collective-permute-start.17 = (bf16[256,512]{1,0:T(8,128)(2,1)S(1)}, bf16[256,512]{1,0:T(8,128)(2,1)S(1)}, u32[]{:S(2)}, u32[]{:S(2)}) collective-permute-start(bf16[256,512]{1,0:T(8,128)(2,1)S(1)} %pad_maximum_fusion), channel_id=1, source_target_pairs={{0,1},{1,0},{2,3},{3,2},{4,5},{5,4},{6,7},{7,6},{8,9},{9,8},{10,11... | collective-permute-start | bytes 786440 | tf_op jit(solution)/shard_map/ppermute | solution.py:283
  49.5 1.4 %collective-permute-start.18 = (bf16[64,1152]{1,0:T(8,128)(2,1)S(1)}, bf16[64,1152]{1,0:T(8,128)(2,1)S(1)}, u32[]{:S(2)}, u32[]{:S(2)}) collective-permute-start(bf16[64,1152]{1,0:T(8,128)(2,1)S(1)} %get-tuple-element.87.refs_4_), channel_id=1, source_target_pairs={{0,1},{1,0},{2,3},{3,2},{4,5},{5,4},{6,7},{7,6},{8,9},{9,8},{10,11... | collective-permute-start | bytes 442376 | tf_op jit(solution)/shard_map/ppermute | solution.py:283
  49.5 1.6 %collective-permute-start.19 = (bf16[64,1152]{1,0:T(8,128)(2,1)S(1)}, bf16[64,1152]{1,0:T(8,128)(2,1)S(1)}, u32[]{:S(2)}, u32[]{:S(2)}) collective-permute-start(bf16[64,1152]{1,0:T(8,128)(2,1)S(1)} %collective-permute-done.15.refs_5_), channel_id=1, source_target_pairs={{0,1},{1,0},{2,3},{3,2},{4,5},{5,4},{6,7},{7,6},{8,9},{9,8},{10,11... | collective-permute-start | bytes 442376 | tf_op jit(solution)/shard_map/ppermute | solution.py:283

commit v6 on v5

--- a/solution.py
+++ b/solution.py
@@ -10,8 +10,9 @@
 BF16 = jnp.bfloat16
 F32 = jnp.float32
 VMEM_LIMIT = 16 << 20
-FIRST_WEIGHT = 1 << 36
+FIRST_WEIGHT = 9 * 10**9
 COLLECT_WEIGHT = 1 << 33
+BACK_WEIGHT = 1 << 33
 
 
 def dot(left, right):
@@ -32,6 +33,10 @@
 
 def call(kernel, out_shape, *args, smem=0, scratch=(), flops=0, anywhere=(), weight=1):
     vmem = pl.BlockSpec(memory_space=pltpu.VMEM)
+    args = [
+        pltpu.with_memory_space_constraint(a, pltpu.HBM) if i in anywhere else a
+        for i, a in enumerate(args)
+    ]
     specs = [
         pl.BlockSpec(memory_space=pltpu.SMEM)
         if i < smem
@@ -51,29 +56,43 @@
     )(*args)
 
 
+def step_of(index, count):
+    return jnp.where(index == 0, 0, count - index) if isinstance(index, jax.Array) else -index % count
+
+
 def choose(flag, first, second):
-    def kernel(flag_ref, first_ref, second_ref, out_ref, sem):
+    rows, columns = first.shape
+
+    def kernel(flag_ref, first_ref, second_ref, one_ref, both_ref, sems):
+        top = pltpu.make_async_copy(first_ref, both_ref.at[0:rows], sems.at[0])
+        bottom = pltpu.make_async_copy(second_ref, both_ref.at[rows:], sems.at[1])
+        top.start()
+        bottom.start()
+
         @pl.when(flag_ref[0] == 0)
         def _():
-            copy = pltpu.make_async_copy(first_ref, out_ref, sem)
+            copy = pltpu.make_async_copy(first_ref, one_ref, sems.at[2])
             copy.start()
             copy.wait()
 
         @pl.when(flag_ref[0] != 0)
         def _():
-            copy = pltpu.make_async_copy(second_ref, out_ref, sem)
+            copy = pltpu.make_async_copy(second_ref, one_ref, sems.at[2])
             copy.start()
             copy.wait()
 
+        top.wait()
+        bottom.wait()
+
     return call(
         kernel,
-        shape(first.shape),
-        flag.reshape(1),
+        [shape((rows, columns)), shape((2 * rows, columns))],
+        flag,
         first,
         second,
         smem=1,
         anywhere=(1, 2),
-        scratch=[pltpu.SemaphoreType.DMA],
+        scratch=[pltpu.SemaphoreType.DMA((3,))],
     )
 
 
@@ -82,10 +101,19 @@
     width = tokens.shape[1] // dp_count
     total = expert_count * capacity
 
-    def kernel(place_ref, ids_ref, probs_ref, x_ref, dy_ref, *outs):
-        chunks, (select_ref, table_ref) = outs[:expert_count], outs[expert_count:]
+    def kernel(place_ref, ids_ref, probs_ref, x_hbm, dy_hbm, *outs):
+        chunks, outs = outs[:expert_count], outs[expert_count:]
+        select_ref, table_ref, x_ref, dy_ref, sems = outs
+        copies = []
+        for j in range(dp_count):
+            source = pl.ds(pl.multiple_of((place_ref[1] ^ j) * width, width), width)
+            target = pl.ds(j * width, width)
+            for i, (hbm, ref) in enumerate(((x_hbm, x_ref), (dy_hbm, dy_ref))):
+                copy = pltpu.make_async_copy(hbm.at[:, source], ref.at[:, target], sems.at[2 * j + i])
+                copy.start()
+                copies.append(copy)
         row = lax.broadcasted_iota(jnp.int32, (total, token_rows), 0)
-        step = row // capacity
+        step = step_of(row // capacity, expert_count)
         far = step + place_ref[0]
         wanted = step ^ place_ref[0] if even else jnp.where(far >= expert_count, far - expert_count, far)
         named = jnp.zeros((total, token_rows), F32)
@@ -98,15 +126,16 @@
         later = lax.broadcasted_iota(jnp.int32, (token_rows, token_rows), 1)
         before = jnp.where(earlier < later, 1.0, 0.0).astype(BF16)
         slot = dot(named.astype(BF16), before)
-        own_slot = (row - step * capacity).astype(F32)
+        own_slot = (row % capacity).astype(F32)
         select = jnp.where((named > 0.5) & (slot == own_slot), 1.0, 0.0)
         pick = select.astype(BF16)
         select_ref[...] = pick
         for j in range(dp_count):
-            source = pl.ds(pl.multiple_of((place_ref[1] ^ j) * width, width), width)
             target = slice(j * width, (j + 1) * width)
-            rows_x = dot(pick, x_ref[:, source]).astype(BF16)
-            rows_dy = dot(pick, dy_ref[:, source]).astype(BF16)
+            copies[2 * j].wait()
+            copies[2 * j + 1].wait()
+            rows_x = dot(pick, x_ref[:, target]).astype(BF16)
+            rows_dy = dot(pick, dy_ref[:, target]).astype(BF16)
             for e in range(expert_count):
                 part = slice(e * capacity, (e + 1) * capacity)
                 chunks[e][0:capacity, target] = rows_x[part]
@@ -121,71 +150,121 @@
 
     outs = [shape((2 * capacity, tokens.shape[1]))] * expert_count
     outs += [shape((total, token_rows)), shape((token_rows, 3 * total))]
-    got = call(kernel, outs, place, ids, probs, tokens, cotangent, smem=1)
+    got = call(
+        kernel,
+        outs,
+        place,
+        ids,
+        probs,
+        tokens,
+        cotangent,
+        smem=1,
+        anywhere=(3, 4),
+        scratch=[
+            pltpu.VMEM(tokens.shape, BF16),
+            pltpu.VMEM(tokens.shape, BF16),
+            pltpu.SemaphoreType.DMA((2 * dp_count,)),
+        ],
+    )
     return got[:expert_count], got[expert_count], got[expert_count + 1]
 
 
-def first_half(chunks, pieces, near, width):
-    count, dp_count = len(chunks), len(pieces)
-    capacity = chunks[0].shape[0] // 2
+def arrange(chunks, dp_count, near):
+    count = len(chunks)
+    capacity, model_width = chunks[0].shape[0] // 2, chunks[0].shape[1]
     total = count * capacity
-    model_width = chunks[0].shape[1]
-    ff = pieces[0][2].shape[0]
-    weights = [w for p in pieces for w in p if w is not None]
+    width = model_width // dp_count * near
+    dp_count //= near
 
     def kernel(*refs):
-        chunk_refs, refs = refs[:count], refs[count:]
-        weight_refs, (rows_ref, keep_ref, send_ref, sums_ref) = refs[: len(weights)], refs[len(weights) :]
+        chunk_refs, rows_ref, part_refs = refs[:count], refs[count], refs[count + 1 :]
         for e in range(count):
-            rows_ref[e * capacity : (e + 1) * capacity, :] = chunk_refs[e][0:capacity, :]
-            rows_ref[total + e * capacity : total + (e + 1) * capacity, :] = chunk_refs[e][capacity:, :]
-        keep_ref[...] = rows_ref[:, 0 : near * width]
-        send_ref[...] = rows_ref[:, near * width :]
+            x, dy = slice(e * capacity, (e + 1) * capacity), slice(total + e * capacity, total + (e + 1) * capacity)
+            rows_ref[x, :] = chunk_refs[e][0:capacity, :]
+            rows_ref[dy, :] = chunk_refs[e][capacity:, :]
+            for j in range(dp_count):
+                column = slice(j * width, (j + 1) * width)
+                part_refs[j][x, :] = chunk_refs[e][0:capacity, column]
+                part_refs[j][dy, :] = chunk_refs[e][capacity:, column]
+
+    outs = [shape((2 * total, model_width))] + [shape((2 * total, width))] * dp_count
+    got = call(kernel, outs, *chunks)
+    return got[0], got[1:]
+
+
+def first_half(rows, near_pieces, far_leads, width):
+    total = rows.shape[0] // 2
+    ff = near_pieces[0][1].shape[0]
+    near = len(near_pieces)
+    given = [(j, w) for j, w in enumerate(far_leads) if w is not None]
+    weights = [w for p in near_pieces for w in p] + [w for _, w in given]
+
+    def kernel(rows_ref, *refs):
+        weight_refs, sums_ref = refs[:-1], refs[-1]
         sums = [0.0, 0.0, 0.0, 0.0]
-        at = 0
-        for j, piece in enumerate(pieces):
+        for j in range(near):
             column = slice(j * width, (j + 1) * width)
             x, dy = rows_ref[0:total, column], rows_ref[total:, column]
-            if j < near:
-                sums[0] += dot(x, weight_refs[at][...])
-                sums[1] += dot(x, weight_refs[at + 1][...])
-                sums[3] += dot_last(dy, weight_refs[at + 2][...])
-                at += 3
-            else:
-                sums[2] += dot(x, weight_refs[at][...])
-                sums[3] += dot_last(dy, weight_refs[at + 1][...])
-                at += 2
+            sums[0] += dot(x, weight_refs[2 * j][0:width, :])
+            sums[1] += dot(x, weight_refs[2 * j][width:, :])
+            sums[3] += dot_last(dy, weight_refs[2 * j + 1][...])
+        for i, (j, _) in enumerate(given):
+            x = rows_ref[0:total, (near + j) * width : (near + j + 1) * width]
+            sums[2] += dot(x, weight_refs[2 * near + i][...])
         for k in range(4):
             sums_ref[:, k * ff : (k + 1) * ff] = sums[k]
 
-    outs = [
-        shape((2 * total, model_width)),
-        shape((2 * total, near * width)),
-        shape((2 * total, model_width - near * width)),
-        shape((total, 4 * ff), F32),
-    ]
-    return call(kernel, outs, *chunks, *weights, weight=FIRST_WEIGHT)
-
-
-def second_half(flag, rows, sums, pieces, near, width, count):
+    return call(kernel, shape((total, 4 * ff), F32), rows, *weights, weight=FIRST_WEIGHT)
+
+
+def far_sums(rows, sums, leads, downs, near, width):
+    total = rows.shape[0] // 2
+    ff = sums.shape[1] // 4
+    given = [(j, w) for j, w in enumerate(leads) if w is not None]
+
+    def kernel(rows_ref, sums_ref, *refs):
+        lead_refs, down_refs, out_ref = refs[: len(given)], refs[len(given) : -1], refs[-1]
+        lead = sums_ref[:, 2 * ff : 3 * ff]
+        back_hidden = sums_ref[:, 3 * ff :]
+        for (j, _), ref in zip(given, lead_refs):
+            lead += dot(rows_ref[0:total, (near + j) * width : (near + j + 1) * width], ref[...])
+        for j, ref in enumerate(down_refs):
+            column = slice((near + j) * width, (near + j + 1) * width)
+            back_hidden += dot_last(rows_ref[total:, column], ref[...])
+        out_ref[:, 0:ff] = lead
+        out_ref[:, ff:] = back_hidden
+
+    return call(
+        kernel,
+        shape((total, 2 * ff), F32),
+        rows,
+        sums,
+        *(w for _, w in given),
+        *downs,
+        weight=BACK_WEIGHT,
+    )
+
+
+def second_half(flag, rows, sums, far, near_pieces, far_pieces, width, count):
     total = rows.shape[0] // 2
     capacity = total // count
     model_width = rows.shape[1]
     ff = sums.shape[1] // 4
-    weights = [w for p in pieces for w in p]
-    far = [j for j in range(len(pieces)) if j >= near]
-
-    def kernel(flag_ref, rows_ref, sums_ref, *refs):
+    near = len(near_pieces)
+    weights = [w for p in (*near_pieces, *far_pieces) for w in p]
+
+    def kernel(flag_ref, rows_ref, sums_ref, back_ref, *refs):
         weight_refs, outs = refs[: len(weights)], refs[len(weights) :]
         chunk_refs, trio_ref = outs[:count], outs[count]
-        last = 0.0
-        for j in far:
-            last += dot(rows_ref[0:total, j * width : (j + 1) * width], weight_refs[3 * j + 1][...])
-        lead = sums_ref[:, 2 * ff : 3 * ff]
+        far_refs = [weight_refs[2 * near + 3 * j : 2 * near + 3 * j + 3] for j in range(len(far_pieces))]
+        last, back_hidden = 0.0, back_ref[:, ff:]
+        for j, (_, late, _) in enumerate(far_refs):
+            column = slice((near + j) * width, (near + j + 1) * width)
+            last += dot(rows_ref[0:total, column], late[...])
+        lead = back_ref[:, 0:ff]
         swapped = flag_ref[0] != 0
         gate_part = sums_ref[:, 0:ff] + jnp.where(swapped, last, lead)
         up_part = sums_ref[:, ff : 2 * ff] + jnp.where(swapped, lead, last)
-        back_hidden = sums_ref[:, 3 * ff :]
         sigmoid_gate = jax.nn.sigmoid(gate_part)
         activated = gate_part * sigmoid_gate
         hidden = (activated * up_part).astype(BF16)
@@ -197,11 +276,16 @@
         trio_ref[:, 0:ff] = hidden
         trio_ref[:, ff : 2 * ff] = d_gate
         trio_ref[:, 2 * ff :] = d_up
-        for j in range(len(pieces)):
+        for j in range(near + len(far_pieces)):
             column = slice(j * width, (j + 1) * width)
-            one, two = (d_gate, d_up) if j < near else (far_first, far_second)
-            out = dot(hidden, weight_refs[3 * j + 2][...]).astype(BF16)
-            back = dot_last(one, weight_refs[3 * j][...]) + dot_last(two, weight_refs[3 * j + 1][...])
+            if j < near:
+                down = weight_refs[2 * j + 1]
+                back = dot_last(d_gate, weight_refs[2 * j][0:width, :])
+                back += dot_last(d_up, weight_refs[2 * j][width:, :])
+            else:
+                one, two, down = far_refs[j - near]
+                back = dot_last(far_first, one[...]) + dot_last(far_second, two[...])
+            out = dot(hidden, down[...]).astype(BF16)
             back = back.astype(BF16)
             for e in range(count):
                 part = slice(e * capacity, (e + 1) * capacity)
@@ -209,7 +293,7 @@
                 chunk_refs[e][capacity:, column] = back[part]
 
     outs = [shape((2 * capacity, model_width))] * count + [shape((total, 3 * ff))]
-    got = call(kernel, outs, flag, rows, sums, *weights, smem=1)
+    got = call(kernel, outs, flag, rows, sums, far, *weights, smem=1)
     return got[:count], got[count]
 
 
@@ -250,7 +334,7 @@
             grad_ref[:, home] = dot(table_ref[...], jnp.concatenate([back] * 3, axis=0)).astype(BF16)
             inner += dot_last(out, dy_ref[:, home])
         inner = jnp.where(select_ref[...] > 0, inner, 0.0)
-        step = lax.broadcasted_iota(jnp.int32, (total, token_rows), 0) // capacity
+        step = step_of(lax.broadcasted_iota(jnp.int32, (total, token_rows), 0) // capacity, count)
         far = step + place_ref[0]
         wanted = step ^ place_ref[0] if even else jnp.where(far >= count, far - count, far)
         for k in range(ids_ref.shape[0]):
@@ -295,56 +379,59 @@
     def after(values, *others):
         return lax.optimization_barrier((values, others))[0]
 
-    own = (w_gate[0], w_up[0], w_down[0])
-    lead = choose(group, own[0], own[1]) if paired else own[0]
-    own = after(own, lead)
+    lead, both = choose(flag, w_gate[0], w_up[0])
+    down = after(w_down[0], lead)
     masks = range(CORES, dp_count, CORES)
     lead_got = {mask: to_dp(lead, mask) for mask in masks}
-    other_got = {
-        mask: to_group(lead_got[mask]) if paired else to_dp(own[1], mask) for mask in masks
-    }
-    sibling = tuple(to_dp(w, 1) for w in own)
+    near_pieces = [(both, down), (to_dp(both, 1), to_dp(down, 1))]
 
     ids, probs = expert_ids.T, gate_probs.T
     send, select, table = slots(
         place, ids, probs, tokens, cotangent, expert_count, capacity, dp_count, even
     )
-    order = [1, *range(expert_count - 1, 1, -1)]
-    send = after(send, sibling)
-    down = after(own[2], send)
-    down_got = {mask: to_dp(down, mask) for mask in masks}
-    got = [send[0]] + [None] * (expert_count - 1)
-    for j in order:
-        got[j] = to_expert(send[j], j)
-
-    early = [(own[0], own[1], own[2]), (sibling[0], sibling[1], sibling[2])]
-    full = list(early)
+    send, down_far = after((send, down), near_pieces[1])
+    down_got = {mask: to_dp(down_far, mask) for mask in masks}
+    lead_got = after(lead_got, send)
+    if paired:
+        late_got = {mask: to_group(lead_got[mask]) for mask in masks}
+    else:
+        late_got = {mask: to_dp(w_up[0], mask) for mask in masks}
+    ways = [step_of(i, expert_count) for i in range(expert_count)]
+    got = [send[0]] + [to_expert(c, j) for c, j in zip(send[1:], ways[1:])]
+
+    rows, parts = arrange(got, dp_count, CORES)
+    lead_sib = {mask: to_dp(lead_got[mask], 1) for mask in masks}
+    far_leads = [w for mask in masks for w in (lead_got[mask], None)]
+    sums = first_half(rows, near_pieces, far_leads, width)
+    late_got = after(late_got, sums)
+    far_pieces = []
     for mask in masks:
-        lead_sib, down_sib = (to_dp(after(w, got), 1) for w in (lead_got[mask], down_got[mask]))
-        early += [(lead_got[mask], None, down_got[mask]), (lead_sib, None, down_sib)]
-        other_sib = to_dp(other_got[mask], 1)
-        full += [
-            (lead_got[mask], other_got[mask], down_got[mask]),
-            (lead_sib, other_sib, down_sib),
+        late_sib, down_sib = to_dp(late_got[mask], 1), to_dp(down_got[mask], 1)
+        far_pieces += [
+            (lead_got[mask], late_got[mask], down_got[mask]),
+            (lead_sib[mask], late_sib, down_sib),
         ]
-    rows, keep, far_rows, sums = first_half(got, early, CORES, width)
-    back, trio = second_half(flag, rows, sums, full, CORES, width, expert_count)
-
-    home = [back[0]] + [None] * (expert_count - 1)
-    for j in order:
-        home[j] = to_expert(back[j], j if even else -j)
-
-    kept = [keep]
-    for i, mask in enumerate(masks):
-        part = far_rows[:, i * CORES * width : (i + 1) * CORES * width]
-        kept.append(to_dp(part, mask))
-    trios = [trio] + [to_dp(trio, mask) for mask in masks]
-    trios, kept = lax.optimization_barrier((trios, kept))
+    far = far_sums(
+        rows,
+        sums,
+        [w for mask in masks for w in (None, lead_sib[mask])],
+        [p[2] for p in far_pieces],
+        CORES,
+        width,
+    )
+    back, trio = second_half(
+        flag, rows, sums, far, near_pieces, far_pieces, width, expert_count
+    )
+
+    home = [back[0]]
+    home += [to_expert(c, j if even else -j) for c, j in zip(back[1:], ways[1:])]
+    peers = [*masks, 1, *(mask + 1 for mask in masks)]
+    trios = [trio] + [to_dp(trio, j) for j in peers]
+    parts = after(parts, trio)
+    kept = [parts[0]] + [to_dp(parts[i + 1], mask) for i, mask in enumerate(masks)]
     theirs = to_dp(jnp.concatenate([k[:, width:] for k in kept], axis=0), 1)
-    size = keep.shape[0]
+    size = rows.shape[0]
     kept += [theirs[i * size : (i + 1) * size] for i in range(len(kept))]
-    trios += [to_dp(t, 1) for t in trios]
-
     mixed, grad_tokens, grad_gates = collect(
         place, ids, select, table, cotangent, home, dp_count, even
     )

time: 52.7 us -> 48.7 us (0.924)
  waiting for transfers between devices: 22.8 us -> 20.1 us
  starting transfers between devices: 17.8 us -> 16.9 us
    ppermute x13 -> x12, waiting for transfers between devices: 7.99 us -> 5.91 us  [to_dp(): return lax.ppermute(array, 'dp', [(i, i ^ mask) for i in range(dp_count)])]
    ppermute x1, waiting for transfers between devices: 2.44 us -> 1.05 us  [to_group(): return lax.ppermute(array, 'groups', [(0, 1), (1, 0)])]
    ppermute x13 -> x12, starting transfers between devices: 7.08 us -> 5.77 us  [to_dp(): return lax.ppermute(array, 'dp', [(i, i ^ mask) for i in range(dp_count)])]
    ppermute x6, waiting for transfers between devices: 12.4 us -> 13.1 us  [to_expert(): return lax.ppermute(array, 'expert', pairs)]
    pallas_call x6 -> x8, Pallas kernels: 10.2 us -> 9.83 us  [call(): pl.pallas_call(kernel, out_shape=out_shape, in_specs=specs, out_specs=jax...]
  transfers between devices with their start and end apart: 20 -> 19, of which waited for: 8 -> 7; matrix products, arithmetic and copies ran while one was open for 0% -> 0% of each run, Pallas kernels for 15% -> 12%
where the time goes in v6:
time: 48.7 us; the launch traced here: 48.4 us
  waiting for transfers between devices  20.1 us (41%)
  starting transfers between devices  16.9 us (35%)
  Pallas kernels  9.83 us (20%)
  between operations  0.79 us (2%)
  local copies, waits for them, and re-layouts  0.67 us (1%)
    ppermute x6, waiting for transfers between devices, to_expert(): return lax.ppermute(array, 'expert', pairs)  13.1 us
    pallas_call x8, Pallas kernels, call(): pl.pallas_call(kernel, out_shape=out_shape, in_specs=specs, out_specs=jax...  9.83 us
    ppermute x6, starting transfers between devices, to_expert(): return lax.ppermute(array, 'expert', pairs)  9.08 us
    ppermute x12, waiting for transfers between devices, to_dp(): return lax.ppermute(array, 'dp', [(i, i ^ mask) for i in range(dp_count)])  5.91 us
    ppermute x12, starting transfers between devices, to_dp(): return lax.ppermute(array, 'dp', [(i, i ^ mask) for i in range(dp_count)])  5.77 us
    ppermute x1, starting transfers between devices, to_group(): return lax.ppermute(array, 'groups', [(0, 1), (1, 0)])  2.1 us
    ppermute x1, waiting for transfers between devices, to_group(): return lax.ppermute(array, 'groups', [(0, 1), (1, 0)])  1.05 us
  transfers between devices with their start and end apart: 19, of which 7 were waited for; matrix products, arithmetic and copies ran while one was open for 0% of the time, Pallas kernels for 12%

profile of v6, /device:TPU:0, one launch (start us, length us, event | category | flops | bytes accessed | tf_op | source)
XLA Modules:
  0.0 48.4 jit_solution(7142062075774447648)
XLA Ops:
  0.6 0.0 copy-start.1
  0.6 1.3 %shard_map.119 = (bf16[512,384]{1,0:T(8,128)(2,1)S(1)}, bf16[1024,384]{1,0:T(8,128)(2,1)S(1)}) custom-call(s32[1]{0:T(128)} %bitcast.4.flag_ref, bf16[512,384]{1,0:T(8,128)(2,1)} %bitcast.19, bf16[512,384]{1,0:T(8,128)(2,1)} %bitcast.20), custom_call_target="tpu_custom_call" | custom-call | flops 1 | bytes 1 | tf_op jit(solution)/shard_map/pallas_call | solution.py:48
  2.0 0.5 %collective-permute-start = (bf16[1024,384]{1,0:T(8,128)(2,1)S(1)}, bf16[1024,384]{1,0:T(8,128)(2,1)S(1)}, u32[]{:S(2)}, u32[]{:S(2)}) collective-permute-start(bf16[1024,384]{1,0:T(8,128)(2,1)S(1)} %get-tuple-element.55.refs_0_), channel_id=1, source_target_pairs={{0,1},{1,0},{2,3},{3,2},{4,5},{5,4},{6,7},{7,6},{8,9},{9,8},{10,11... | collective-permute-start | bytes 2359304 | tf_op jit(solution)/shard_map/ppermute | solution.py:367
  2.5 0.0 copy-done.1
  2.5 0.1 collective-permute-start.1
  2.6 2.9 %collective-permute-start.5 = (bf16[512,384]{1,0:T(8,128)(2,1)S(1)}, bf16[512,384]{1,0:T(8,128)(2,1)S(1)}, u32[]{:S(2)}, u32[]{:S(2)}) collective-permute-start(bf16[512,384]{1,0:T(8,128)(2,1)S(1)} %get-tuple-element.53), channel_id=1, source_target_pairs={{0,2},{1,3},{2,0},{3,1},{4,6},{5,7},{6,4},{7,5},{8,10},{9,11},{10,... | collective-permute-start | bytes 1179656 | tf_op jit(solution)/shard_map/ppermute | solution.py:367
  5.5 0.0 copy-start.3
  5.5 0.0 copy-start.2
  5.5 0.1 pad_add_fusion.place_ref
  5.6 0.6 %copy-done.3 = s32[128,8]{0,1:T(8,128)S(1)} copy-done((s32[128,8]{0,1:T(8,128)S(1)}, s32[128,8]{0,1:T(8,128)}, u32[]{:S(2)}) %copy-start.3) | copy-done | bytes 4120
  6.2 0.0 copy-done.2
  6.2 2.3 %shard_map.118 = (bf16[32,2048]{1,0:T(8,128)(2,1)S(1)}, bf16[32,2048]{1,0:T(8,128)(2,1)S(1)}, bf16[32,2048]{1,0:T(8,128)(2,1)S(1)}, bf16[32,2048]{1,0:T(8,128)(2...) custom-call(s32[2]{0:T(128)S(1)} %pad_add_fusion.place_ref, s32[8,128]{1,0:T(8,128)S(1)} %bitcast.17, ...), custom_call_target="tpu_custom_call" | custom-call | flops 1 | bytes 1 | tf_op jit(solution)/shard_map/pallas_call | solution.py:48
  8.5 0.0 collective-permute-done.1.refs_3_
  8.5 0.0 collective-permute-done.refs_2_
  8.5 0.1 collective-permute-start.7
  8.6 4.1 %collective-permute-start.2 = (bf16[32,2048]{1,0:T(8,128)(2,1)S(1)}, bf16[32,2048]{1,0:T(8,128)(2,1)S(1)}, u32[]{:S(2)}, u32[]{:S(2)}) collective-permute-start(bf16[32,2048]{1,0:T(8,128)(2,1)S(1)} %get-tuple-element.57), channel_id=1, source_target_pairs={{0,12},{4,8},{8,4},{12,0},{1,13},{5,9},{9,5},{13,1},{2,14},{6,10},... | collective-permute-start | bytes 393224 | tf_op jit(solution)/shard_map/ppermute | solution.py:377
  12.7 0.0 collective-permute-start.3
  12.7 0.6 %collective-permute-start.4 = (bf16[32,2048]{1,0:T(8,128)(2,1)S(1)}, bf16[32,2048]{1,0:T(8,128)(2,1)S(1)}, u32[]{:S(2)}, u32[]{:S(2)}) collective-permute-start(bf16[32,2048]{1,0:T(8,128)(2,1)S(1)} %get-tuple-element.59), channel_id=1, source_target_pairs={{0,4},{4,0},{8,12},{12,8},{1,5},{5,1},{9,13},{13,9},{2,6},{6,2},{1... | collective-permute-start | bytes 393224 | tf_op jit(solution)/shard_map/ppermute | solution.py:377
  13.3 2.1 %collective-permute-done.5.refs_4_ = bf16[512,384]{1,0:T(8,128)(2,1)S(1)} collective-permute-done((bf16[512,384]{1,0:T(8,128)(2,1)S(1)}, bf16[512,384]{1,0:T(8,128)(2,1)S(1)}, u32[]{:S(2)}, u32[]{:S(2)}) %collective-permute-start.5) | collective-permute-done | bytes 393248 | tf_op jit(solution)/shard_map/ppermute | solution.py:367
  15.4 2.1 %collective-permute-start.9 = (bf16[512,384]{1,0:T(8,128)(2,1)S(1)}, bf16[512,384]{1,0:T(8,128)(2,1)S(1)}, u32[]{:S(2)}, u32[]{:S(2)}) collective-permute-start(bf16[512,384]{1,0:T(8,128)(2,1)S(1)} %collective-permute-done.5.refs_4_), channel_id=1, source_target_pairs={{0,16},{16,0},{1,17},{17,1},{2,18},{18,2},{3,19},{19,3},{4,20},{20... | collective-permute-start | bytes 1179656 | tf_op jit(solution)/shard_map/ppermute | solution.py:370
  17.5 0.0 collective-permute-done.2.refs_1_
  17.5 0.0 collective-permute-start.6
  17.5 6.0 %collective-permute-done.3.refs_2_ = bf16[32,2048]{1,0:T(8,128)(2,1)S(1)} collective-permute-done((bf16[32,2048]{1,0:T(8,128)(2,1)S(1)}, bf16[32,2048]{1,0:T(8,128)(2,1)S(1)}, u32[]{:S(2)}, u32[]{:S(2)}) %collective-permute-start.3) | collective-permute-done | bytes 131104 | tf_op jit(solution)/shard_map/ppermute | solution.py:377
  23.5 0.0 collective-permute-done.4.refs_3_
  23.5 0.1 shard_map.120
  23.6 0.0 collective-permute-done.7.refs_1_.refs_6_
  23.6 0.1 collective-permute-start.8
  23.7 0.7 %shard_map.121.sums_ref = f32[64,1536]{1,0:T(8,128)S(1)} custom-call(bf16[128,2048]{1,0:T(8,128)(2,1)S(1)} %get-tuple-element.60.rows_ref, bf16[1024,384]{1,0:T(8,128)(2,1)S(1)} %get-tuple-element.55.refs_0_, bf16[384,512]{1,0:T(8,128)(2,1)S(1)} %bitcast.14, bf16[1024,384]{1,0:T(8,128)(2,1)S(1)} %collective-permute-done.refs_2_, ...), custom_call_target="tpu_custom_call" | custom-call | flops 8999999488 | bytes 1 | tf_op jit(solution)/shard_map/pallas_call | solution.py:48
  24.4 1.1 %collective-permute-done.9.refs_5_ = bf16[512,384]{1,0:T(8,128)(2,1)S(1)} collective-permute-done((bf16[512,384]{1,0:T(8,128)(2,1)S(1)}, bf16[512,384]{1,0:T(8,128)(2,1)S(1)}, u32[]{:S(2)}, u32[]{:S(2)}) %collective-permute-start.9) | collective-permute-done | bytes 393248 | tf_op jit(solution)/shard_map/ppermute | solution.py:370
  25.4 0.0 collective-permute-start.10
  25.4 0.0 collective-permute-done.6.refs_0_.refs_7_
  25.4 0.0 collective-permute-done.8.refs_2_.refs_9_
  25.4 0.4 shard_map.122.back_ref
  25.9 1.3 %collective-permute-done.10.refs_8_ = bf16[512,384]{1,0:T(8,128)(2,1)S(1)} collective-permute-done((bf16[512,384]{1,0:T(8,128)(2,1)S(1)}, bf16[512,384]{1,0:T(8,128)(2,1)S(1)}, u32[]{:S(2)}, u32[]{:S(2)}) %collective-permute-start.10) | collective-permute-done | bytes 393248 | tf_op jit(solution)/shard_map/ppermute | solution.py:367
  27.2 1.6 %shard_map.123 = (bf16[32,2048]{1,0:T(8,128)(2,1)S(1)}, bf16[32,2048]{1,0:T(8,128)(2,1)S(1)}, bf16[32,2048]{1,0:T(8,128)(2,1)S(1)}, bf16[32,2048]{1,0:T(8,128)(2,1)S(1)}, bf16[64,1152]{1,0:T(8,128)(2,1)S(1)}) custom-call(s32[1]{0:T(128)} %bitcast.4.flag_ref, bf16[128,2048]{1,0:T(8,128)(2,1)S(1)} %get-tuple-element.60.rows_ref, ...), custom_call_target="tpu_custom_call" | custom-call | flops 1 | bytes 1 | tf_op jit(solution)/shard_map/pallas_call | solution.py:48
  28.8 1.5 %collective-permute-start.14 = (bf16[128,1024]{1,0:T(8,128)(2,1)S(1)}, bf16[128,1024]{1,0:T(8,128)(2,1)S(1)}, u32[]{:S(2)}, u32[]{:S(2)}) collective-permute-start(bf16[128,1024]{1,0:T(8,128)(2,1)S(1)} %get-tuple-element.73), channel_id=1, source_target_pairs={{0,2},{1,3},{2,0},{3,1},{4,6},{5,7},{6,4},{7,5},{8,10},{9,11},{10,... | collective-permute-start | bytes 786440 | tf_op jit(solution)/shard_map/ppermute | solution.py:367
  30.2 3.6 %collective-permute-start.11 = (bf16[32,2048]{1,0:T(8,128)(2,1)S(1)}, bf16[32,2048]{1,0:T(8,128)(2,1)S(1)}, u32[]{:S(2)}, u32[]{:S(2)}) collective-permute-start(bf16[32,2048]{1,0:T(8,128)(2,1)S(1)} %get-tuple-element.65), channel_id=1, source_target_pairs={{0,12},{4,8},{8,4},{12,0},{1,13},{5,9},{9,5},{13,1},{2,14},{6,10},... | collective-permute-start | bytes 393224 | tf_op jit(solution)/shard_map/ppermute | solution.py:377
  33.8 0.0 collective-permute-start.12
  33.9 0.0 copy-start
  33.9 0.8 %collective-permute-start.13 = (bf16[32,2048]{1,0:T(8,128)(2,1)S(1)}, bf16[32,2048]{1,0:T(8,128)(2,1)S(1)}, u32[]{:S(2)}, u32[]{:S(2)}) collective-permute-start(bf16[32,2048]{1,0:T(8,128)(2,1)S(1)} %get-tuple-element.67), channel_id=1, source_target_pairs={{0,4},{4,0},{8,12},{12,8},{1,5},{5,1},{9,13},{13,9},{2,6},{6,2},{1... | collective-permute-start | bytes 393224 | tf_op jit(solution)/shard_map/ppermute | solution.py:377
  34.6 0.0 collective-permute-start.18
  34.6 2.5 %collective-permute-done.14.refs_1_ = bf16[128,1024]{1,0:T(8,128)(2,1)S(1)} collective-permute-done((bf16[128,1024]{1,0:T(8,128)(2,1)S(1)}, bf16[128,1024]{1,0:T(8,128)(2,1)S(1)}, u32[]{:S(2)}, u32[]{:S(2)}) %collective-permute-start.14) | collective-permute-done | bytes 262176 | tf_op jit(solution)/shard_map/ppermute | solution.py:367
  37.2 0.0 collective-permute-start.17
  37.2 1.3 %collective-permute-done.11.refs_1_ = bf16[32,2048]{1,0:T(8,128)(2,1)S(1)} collective-permute-done((bf16[32,2048]{1,0:T(8,128)(2,1)S(1)}, bf16[32,2048]{1,0:T(8,128)(2,1)S(1)}, u32[]{:S(2)}, u32[]{:S(2)}) %collective-permute-start.11) | collective-permute-done | bytes 131104 | tf_op jit(solution)/shard_map/ppermute | solution.py:377
  38.5 0.6 %collective-permute-start.16 = (bf16[64,1152]{1,0:T(8,128)(2,1)S(1)}, bf16[64,1152]{1,0:T(8,128)(2,1)S(1)}, u32[]{:S(2)}, u32[]{:S(2)}) collective-permute-start(bf16[64,1152]{1,0:T(8,128)(2,1)S(1)} %get-tuple-element.81.refs_4_), channel_id=1, source_target_pairs={{0,2},{1,3},{2,0},{3,1},{4,6},{5,7},{6,4},{7,5},{8,10},{9,11},{10,... | collective-permute-start | bytes 442376 | tf_op jit(solution)/shard_map/ppermute | solution.py:367
  39.1 5.9 %collective-permute-done.12.refs_2_ = bf16[32,2048]{1,0:T(8,128)(2,1)S(1)} collective-permute-done((bf16[32,2048]{1,0:T(8,128)(2,1)S(1)}, bf16[32,2048]{1,0:T(8,128)(2,1)S(1)}, u32[]{:S(2)}, u32[]{:S(2)}) %collective-permute-start.12) | collective-permute-done | bytes 131104 | tf_op jit(solution)/shard_map/ppermute | solution.py:377
  44.9 0.0 collective-permute-start.15
  44.9 0.0 collective-permute-done.13.refs_3_
  45.0 0.0 copy-done
  45.0 2.0 %shard_map.124 = (bf16[128,2048]{1,0:T(8,128)(2,1)}, bf16[128,2048]{1,0:T(8,128)(2,1)}, f32[8,128]{1,0:T(8,128)}) custom-call(s32[2]{0:T(128)S(1)} %pad_add_fusion.place_ref, s32[8,128]{1,0:T(8,128)S(1)} %bitcast.18, bf16[64,128]{1,0:T(8,128)(2,1)S(1)} %get-tuple-element.47.select_ref, bf16[128,192]{1,0:T(8,128)(2,1)S(1)} %get-tuple-element.48.table_ref, ...), custom_call_target="tpu_custom_call" | custom-call | flops 8589934592 | bytes 1 | tf_op jit(solution)/shard_map/pallas_call | solution.py:48
  47.0 0.0 collective-permute-done.15
  47.0 0.0 collective-permute-done.18.refs_7_
  47.0 0.0 collective-permute-done.17.refs_6_
  47.1 0.0 collective-permute-done.16.refs_5_
  47.1 1.4 %shard_map.125 = (bf16[512,384]{1,0:T(8,128)(2,1)}, bf16[512,384]{1,0:T(8,128)(2,1)}, bf16[384,512]{1,0:T(8,128)(2,1)}) custom-call(bf16[128,1024]{1,0:T(8,128)(2,1)S(1)} %get-tuple-element.77.refs_0_, bf16[128,1024]{1,0:T(8,128)(2,1)S(1)} %collective-permute-done.14.refs_1_, bf16[128,512]{1,0:T(8,128)(2,1)S(1)} %get-tuple-element.79.refs_2_, ...), custom_call_target="tpu_custom_call" | custom-call | flops 1 | bytes 1 | tf_op jit(solution)/shard_map/pallas_call | solution.py:48
  (4 shorter events, 0.1 us)
Async XLA Ops:
  0.6 1.9 %copy-start.1 = (bf16[1,384,512]{2,1,0:T(8,128)(2,1)S(1)}, bf16[1,384,512]{2,1,0:T(8,128)(2,1)}, u32[]{:S(2)}) copy-start(bf16[1,384,512]{2,1,0:T(8,128)(2,1)} %param.13) | copy-start | bytes 1179652
  2.0 6.6 %collective-permute-start = (bf16[1024,384]{1,0:T(8,128)(2,1)S(1)}, bf16[1024,384]{1,0:T(8,128)(2,1)S(1)}, u32[]{:S(2)}, u32[]{:S(2)}) collective-permute-start(bf16[1024,384]{1,0:T(8,128)(2,1)S(1)} %get-tuple-element.55.refs_0_), channel_id=1, source_target_pairs={{0,1},{1,0},{2,3},{3,2},{4,5},{5,4},{6,7},{7,6},{8,9},{9,8},{10,11... | collective-permute-start | bytes 2359304 | tf_op jit(solution)/shard_map/ppermute | solution.py:367
  2.5 6.0 %collective-permute-start.1 = (bf16[384,512]{1,0:T(8,128)(2,1)S(1)}, bf16[384,512]{1,0:T(8,128)(2,1)S(1)}, u32[]{:S(2)}, u32[]{:S(2)}) collective-permute-start(bf16[384,512]{1,0:T(8,128)(2,1)S(1)} %bitcast.12), channel_id=1, source_target_pairs={{0,1},{1,0},{2,3},{3,2},{4,5},{5,4},{6,7},{7,6},{8,9},{9,8},{10,11... | collective-permute-start | bytes 1179656 | tf_op jit(solution)/shard_map/ppermute | solution.py:367
  2.6 12.8 %collective-permute-start.5 = (bf16[512,384]{1,0:T(8,128)(2,1)S(1)}, bf16[512,384]{1,0:T(8,128)(2,1)S(1)}, u32[]{:S(2)}, u32[]{:S(2)}) collective-permute-start(bf16[512,384]{1,0:T(8,128)(2,1)S(1)} %get-tuple-element.53), channel_id=1, source_target_pairs={{0,2},{1,3},{2,0},{3,1},{4,6},{5,7},{6,4},{7,5},{8,10},{9,11},{10,... | collective-permute-start | bytes 1179656 | tf_op jit(solution)/shard_map/ppermute | solution.py:367
  5.5 0.7 %copy-start.3 = (s32[128,8]{0,1:T(8,128)S(1)}, s32[128,8]{0,1:T(8,128)}, u32[]{:S(2)}) copy-start(s32[128,8]{0,1:T(8,128)} %param.9) | copy-start | bytes 12292
  5.5 0.7 %copy-start.2 = (f32[128,8]{0,1:T(8,128)S(1)}, f32[128,8]{0,1:T(8,128)}, u32[]{:S(2)}) copy-start(f32[128,8]{0,1:T(8,128)} %param.10) | copy-start | bytes 12292
  8.5 15.0 %collective-permute-start.7 = (bf16[384,512]{1,0:T(8,128)(2,1)S(1)}, bf16[384,512]{1,0:T(8,128)(2,1)S(1)}, u32[]{:S(2)}, u32[]{:S(2)}) collective-permute-start(bf16[384,512]{1,0:T(8,128)(2,1)S(1)} %bitcast.13), channel_id=1, source_target_pairs={{0,2},{1,3},{2,0},{3,1},{4,6},{5,7},{6,4},{7,5},{8,10},{9,11},{10,... | collective-permute-start | bytes 1179656 | tf_op jit(solution)/shard_map/ppermute | solution.py:367
  8.6 8.9 %collective-permute-start.2 = (bf16[32,2048]{1,0:T(8,128)(2,1)S(1)}, bf16[32,2048]{1,0:T(8,128)(2,1)S(1)}, u32[]{:S(2)}, u32[]{:S(2)}) collective-permute-start(bf16[32,2048]{1,0:T(8,128)(2,1)S(1)} %get-tuple-element.57), channel_id=1, source_target_pairs={{0,12},{4,8},{8,4},{12,0},{1,13},{5,9},{9,5},{13,1},{2,14},{6,10},... | collective-permute-start | bytes 393224 | tf_op jit(solution)/shard_map/ppermute | solution.py:377
  12.7 10.8 %collective-permute-start.3 = (bf16[32,2048]{1,0:T(8,128)(2,1)S(1)}, bf16[32,2048]{1,0:T(8,128)(2,1)S(1)}, u32[]{:S(2)}, u32[]{:S(2)}) collective-permute-start(bf16[32,2048]{1,0:T(8,128)(2,1)S(1)} %get-tuple-element.58), channel_id=1, source_target_pairs={{0,8},{4,12},{8,0},{12,4},{1,9},{5,13},{9,1},{13,5},{2,10},{6,14},... | collective-permute-start | bytes 393224 | tf_op jit(solution)/shard_map/ppermute | solution.py:377
  12.7 10.8 %collective-permute-start.4 = (bf16[32,2048]{1,0:T(8,128)(2,1)S(1)}, bf16[32,2048]{1,0:T(8,128)(2,1)S(1)}, u32[]{:S(2)}, u32[]{:S(2)}) collective-permute-start(bf16[32,2048]{1,0:T(8,128)(2,1)S(1)} %get-tuple-element.59), channel_id=1, source_target_pairs={{0,4},{4,0},{8,12},{12,8},{1,5},{5,1},{9,13},{13,9},{2,6},{6,2},{1... | collective-permute-start | bytes 393224 | tf_op jit(solution)/shard_map/ppermute | solution.py:377
  15.4 10.0 %collective-permute-start.9 = (bf16[512,384]{1,0:T(8,128)(2,1)S(1)}, bf16[512,384]{1,0:T(8,128)(2,1)S(1)}, u32[]{:S(2)}, u32[]{:S(2)}) collective-permute-start(bf16[512,384]{1,0:T(8,128)(2,1)S(1)} %collective-permute-done.5.refs_4_), channel_id=1, source_target_pairs={{0,16},{16,0},{1,17},{17,1},{2,18},{18,2},{3,19},{19,3},{4,20},{20... | collective-permute-start | bytes 1179656 | tf_op jit(solution)/shard_map/ppermute | solution.py:370
  17.5 8.0 %collective-permute-start.6 = (bf16[512,384]{1,0:T(8,128)(2,1)S(1)}, bf16[512,384]{1,0:T(8,128)(2,1)S(1)}, u32[]{:S(2)}, u32[]{:S(2)}) collective-permute-start(bf16[512,384]{1,0:T(8,128)(2,1)S(1)} %collective-permute-done.5.refs_4_), channel_id=1, source_target_pairs={{0,1},{1,0},{2,3},{3,2},{4,5},{5,4},{6,7},{7,6},{8,9},{9,8},{10,11... | collective-permute-start | bytes 1179656 | tf_op jit(solution)/shard_map/ppermute | solution.py:367
  23.6 1.9 %collective-permute-start.8 = (bf16[384,512]{1,0:T(8,128)(2,1)S(1)}, bf16[384,512]{1,0:T(8,128)(2,1)S(1)}, u32[]{:S(2)}, u32[]{:S(2)}) collective-permute-start(bf16[384,512]{1,0:T(8,128)(2,1)S(1)} %collective-permute-done.7.refs_1_.refs_6_), channel_id=1, source_target_pairs={{0,1},{1,0},{2,3},{3,2},{4,5},{5,4},{6,7},{7,6},{8,9},{9,8},{10,11... | collective-permute-start | bytes 1179656 | tf_op jit(solution)/shard_map/ppermute | solution.py:367
  25.4 1.7 %collective-permute-start.10 = (bf16[512,384]{1,0:T(8,128)(2,1)S(1)}, bf16[512,384]{1,0:T(8,128)(2,1)S(1)}, u32[]{:S(2)}, u32[]{:S(2)}) collective-permute-start(bf16[512,384]{1,0:T(8,128)(2,1)S(1)} %collective-permute-done.9.refs_5_), channel_id=1, source_target_pairs={{0,1},{1,0},{2,3},{3,2},{4,5},{5,4},{6,7},{7,6},{8,9},{9,8},{10,11... | collective-permute-start | bytes 1179656 | tf_op jit(solution)/shard_map/ppermute | solution.py:367
  28.8 8.4 %collective-permute-start.14 = (bf16[128,1024]{1,0:T(8,128)(2,1)S(1)}, bf16[128,1024]{1,0:T(8,128)(2,1)S(1)}, u32[]{:S(2)}, u32[]{:S(2)}) collective-permute-start(bf16[128,1024]{1,0:T(8,128)(2,1)S(1)} %get-tuple-element.73), channel_id=1, source_target_pairs={{0,2},{1,3},{2,0},{3,1},{4,6},{5,7},{6,4},{7,5},{8,10},{9,11},{10,... | collective-permute-start | bytes 786440 | tf_op jit(solution)/shard_map/ppermute | solution.py:367
  30.2 8.2 %collective-permute-start.11 = (bf16[32,2048]{1,0:T(8,128)(2,1)S(1)}, bf16[32,2048]{1,0:T(8,128)(2,1)S(1)}, u32[]{:S(2)}, u32[]{:S(2)}) collective-permute-start(bf16[32,2048]{1,0:T(8,128)(2,1)S(1)} %get-tuple-element.65), channel_id=1, source_target_pairs={{0,12},{4,8},{8,4},{12,0},{1,13},{5,9},{9,5},{13,1},{2,14},{6,10},... | collective-permute-start | bytes 393224 | tf_op jit(solution)/shard_map/ppermute | solution.py:377
  33.8 11.1 %collective-permute-start.12 = (bf16[32,2048]{1,0:T(8,128)(2,1)S(1)}, bf16[32,2048]{1,0:T(8,128)(2,1)S(1)}, u32[]{:S(2)}, u32[]{:S(2)}) collective-permute-start(bf16[32,2048]{1,0:T(8,128)(2,1)S(1)} %get-tuple-element.66), channel_id=1, source_target_pairs={{0,8},{4,12},{8,0},{12,4},{1,9},{5,13},{9,1},{13,5},{2,10},{6,14},... | collective-permute-start | bytes 393224 | tf_op jit(solution)/shard_map/ppermute | solution.py:377
  33.9 11.1 %copy-start = (bf16[128,2048]{1,0:T(8,128)(2,1)S(1)}, bf16[128,2048]{1,0:T(8,128)(2,1)}, u32[]{:S(2)}) copy-start(bf16[128,2048]{1,0:T(8,128)(2,1)} %dy_ref.1) | copy-start | bytes 1572868
  33.9 11.1 %collective-permute-start.13 = (bf16[32,2048]{1,0:T(8,128)(2,1)S(1)}, bf16[32,2048]{1,0:T(8,128)(2,1)S(1)}, u32[]{:S(2)}, u32[]{:S(2)}) collective-permute-start(bf16[32,2048]{1,0:T(8,128)(2,1)S(1)} %get-tuple-element.67), channel_id=1, source_target_pairs={{0,4},{4,0},{8,12},{12,8},{1,5},{5,1},{9,13},{13,9},{2,6},{6,2},{1... | collective-permute-start | bytes 393224 | tf_op jit(solution)/shard_map/ppermute | solution.py:377
  34.6 12.4 %collective-permute-start.18 = (bf16[64,1152]{1,0:T(8,128)(2,1)S(1)}, bf16[64,1152]{1,0:T(8,128)(2,1)S(1)}, u32[]{:S(2)}, u32[]{:S(2)}) collective-permute-start(bf16[64,1152]{1,0:T(8,128)(2,1)S(1)} %get-tuple-element.81.refs_4_), channel_id=1, source_target_pairs={{0,3},{1,2},{2,1},{3,0},{4,7},{5,6},{6,5},{7,4},{8,11},{9,10},{10,... | collective-permute-start | bytes 442376 | tf_op jit(solution)/shard_map/ppermute | solution.py:367
  37.2 9.9 %collective-permute-start.17 = (bf16[64,1152]{1,0:T(8,128)(2,1)S(1)}, bf16[64,1152]{1,0:T(8,128)(2,1)S(1)}, u32[]{:S(2)}, u32[]{:S(2)}) collective-permute-start(bf16[64,1152]{1,0:T(8,128)(2,1)S(1)} %get-tuple-element.81.refs_4_), channel_id=1, source_target_pairs={{0,1},{1,0},{2,3},{3,2},{4,5},{5,4},{6,7},{7,6},{8,9},{9,8},{10,11... | collective-permute-start | bytes 442376 | tf_op jit(solution)/shard_map/ppermute | solution.py:367
  38.5 8.6 %collective-permute-start.16 = (bf16[64,1152]{1,0:T(8,128)(2,1)S(1)}, bf16[64,1152]{1,0:T(8,128)(2,1)S(1)}, u32[]{:S(2)}, u32[]{:S(2)}) collective-permute-start(bf16[64,1152]{1,0:T(8,128)(2,1)S(1)} %get-tuple-element.81.refs_4_), channel_id=1, source_target_pairs={{0,2},{1,3},{2,0},{3,1},{4,6},{5,7},{6,4},{7,5},{8,10},{9,11},{10,... | collective-permute-start | bytes 442376 | tf_op jit(solution)/shard_map/ppermute | solution.py:367
  44.9 2.1 %collective-permute-start.15 = (bf16[256,512]{1,0:T(8,128)(2,1)S(1)}, bf16[256,512]{1,0:T(8,128)(2,1)S(1)}, u32[]{:S(2)}, u32[]{:S(2)}) collective-permute-start(bf16[256,512]{1,0:T(8,128)(2,1)S(1)} %pad_maximum_fusion), channel_id=1, source_target_pairs={{0,1},{1,0},{2,3},{3,2},{4,5},{5,4},{6,7},{7,6},{8,9},{9,8},{10,11... | collective-permute-start | bytes 786440 | tf_op jit(solution)/shard_map/ppermute | solution.py:367

commit v7 on v6

--- a/solution.py
+++ b/solution.py
@@ -31,7 +31,7 @@
     return jax.ShapeDtypeStruct(dims, dtype)
 
 
-def call(kernel, out_shape, *args, smem=0, scratch=(), flops=0, anywhere=(), weight=1):
+def call(kernel, out_shape, *args, smem=0, scratch=(), anywhere=(), weight=1):
     vmem = pl.BlockSpec(memory_space=pltpu.VMEM)
     args = [
         pltpu.with_memory_space_constraint(a, pltpu.HBM) if i in anywhere else a
@@ -57,7 +57,8 @@
 
 
 def step_of(index, count):
-    return jnp.where(index == 0, 0, count - index) if isinstance(index, jax.Array) else -index % count
+    step = 1 + (index + count // 2 - 2) % max(count - 1, 1)
+    return jnp.where(index == 0, 0, step) if isinstance(index, jax.Array) else step * (index > 0)
 
 
 def choose(flag, first, second):
@@ -101,17 +102,10 @@
     width = tokens.shape[1] // dp_count
     total = expert_count * capacity
 
-    def kernel(place_ref, ids_ref, probs_ref, x_hbm, dy_hbm, *outs):
-        chunks, outs = outs[:expert_count], outs[expert_count:]
-        select_ref, table_ref, x_ref, dy_ref, sems = outs
-        copies = []
-        for j in range(dp_count):
-            source = pl.ds(pl.multiple_of((place_ref[1] ^ j) * width, width), width)
-            target = pl.ds(j * width, width)
-            for i, (hbm, ref) in enumerate(((x_hbm, x_ref), (dy_hbm, dy_ref))):
-                copy = pltpu.make_async_copy(hbm.at[:, source], ref.at[:, target], sems.at[2 * j + i])
-                copy.start()
-                copies.append(copy)
+    def kernel(place_ref, ids_ref, probs_ref, x_ref, dy_hbm, *outs):
+        chunks, (select_ref, table_ref, dy_ref, sem) = outs[:expert_count], outs[expert_count:]
+        fetch = pltpu.make_async_copy(dy_hbm, dy_ref, sem)
+        fetch.start()
         row = lax.broadcasted_iota(jnp.int32, (total, token_rows), 0)
         step = step_of(row // capacity, expert_count)
         far = step + place_ref[0]
@@ -130,26 +124,25 @@
         select = jnp.where((named > 0.5) & (slot == own_slot), 1.0, 0.0)
         pick = select.astype(BF16)
         select_ref[...] = pick
-        for j in range(dp_count):
-            target = slice(j * width, (j + 1) * width)
-            copies[2 * j].wait()
-            copies[2 * j + 1].wait()
-            rows_x = dot(pick, x_ref[:, target]).astype(BF16)
-            rows_dy = dot(pick, dy_ref[:, target]).astype(BF16)
-            for e in range(expert_count):
-                part = slice(e * capacity, (e + 1) * capacity)
-                chunks[e][0:capacity, target] = rows_x[part]
-                chunks[e][capacity:, target] = rows_dy[part]
+        def gather(ref, first):
+            for j in range(dp_count):
+                source = pl.ds(pl.multiple_of((place_ref[1] ^ j) * width, width), width)
+                got = dot(pick, ref[:, source]).astype(BF16)
+                for e in range(expert_count):
+                    chunks[e][first : first + capacity, j * width : (j + 1) * width] = got[
+                        e * capacity : (e + 1) * capacity
+                    ]
+
+        gather(x_ref, 0)
         table = (select * prob).T
         high = table.astype(BF16)
-        rest = table - high.astype(F32)
-        middle = rest.astype(BF16)
         table_ref[:, 0:total] = high
-        table_ref[:, total : 2 * total] = middle
-        table_ref[:, 2 * total :] = (rest - middle.astype(F32)).astype(BF16)
+        table_ref[:, total:] = (table - high.astype(F32)).astype(BF16)
+        fetch.wait()
+        gather(dy_ref, capacity)
 
     outs = [shape((2 * capacity, tokens.shape[1]))] * expert_count
-    outs += [shape((total, token_rows)), shape((token_rows, 3 * total))]
+    outs += [shape((total, token_rows)), shape((token_rows, 2 * total))]
     got = call(
         kernel,
         outs,
@@ -159,12 +152,8 @@
         tokens,
         cotangent,
         smem=1,
-        anywhere=(3, 4),
-        scratch=[
-            pltpu.VMEM(tokens.shape, BF16),
-            pltpu.VMEM(tokens.shape, BF16),
-            pltpu.SemaphoreType.DMA((2 * dp_count,)),
-        ],
+        anywhere=(4,),
+        scratch=[pltpu.VMEM(cotangent.shape, BF16), pltpu.SemaphoreType.DMA],
     )
     return got[:expert_count], got[expert_count], got[expert_count + 1]
 
@@ -330,8 +319,8 @@
             home = pl.ds(pl.multiple_of((place_ref[1] ^ j) * width, width), width)
             out = jnp.concatenate([r[0:capacity, column] for r in chunk_refs], axis=0)
             back = jnp.concatenate([r[capacity:, column] for r in chunk_refs], axis=0)
-            mixed_ref[:, home] = dot(table_ref[...], jnp.concatenate([out] * 3, axis=0)).astype(BF16)
-            grad_ref[:, home] = dot(table_ref[...], jnp.concatenate([back] * 3, axis=0)).astype(BF16)
+            mixed_ref[:, home] = dot(table_ref[...], jnp.concatenate([out] * 2, axis=0)).astype(BF16)
+            grad_ref[:, home] = dot(table_ref[...], jnp.concatenate([back] * 2, axis=0)).astype(BF16)
             inner += dot_last(out, dy_ref[:, home])
         inner = jnp.where(select_ref[...] > 0, inner, 0.0)
         step = step_of(lax.broadcasted_iota(jnp.int32, (total, token_rows), 0) // capacity, count)
@@ -404,6 +393,7 @@
     far_leads = [w for mask in masks for w in (lead_got[mask], None)]
     sums = first_half(rows, near_pieces, far_leads, width)
     late_got = after(late_got, sums)
+    kept = [parts[0]] + [to_dp(parts[i + 1], mask) for i, mask in enumerate(masks)]
     far_pieces = []
     for mask in masks:
         late_sib, down_sib = to_dp(late_got[mask], 1), to_dp(down_got[mask], 1)
@@ -427,8 +417,7 @@
     home += [to_expert(c, j if even else -j) for c, j in zip(back[1:], ways[1:])]
     peers = [*masks, 1, *(mask + 1 for mask in masks)]
     trios = [trio] + [to_dp(trio, j) for j in peers]
-    parts = after(parts, trio)
-    kept = [parts[0]] + [to_dp(parts[i + 1], mask) for i, mask in enumerate(masks)]
+    kept = after(kept, trios[2])
     theirs = to_dp(jnp.concatenate([k[:, width:] for k in kept], axis=0), 1)
     size = rows.shape[0]
     kept += [theirs[i * size : (i + 1) * size] for i in range(len(kept))]

time: 48.7 us -> 46.6 us (0.957)
  waiting for transfers between devices: 20.1 us -> 17.3 us
  starting transfers between devices: 16.9 us -> 17.9 us
    ppermute x12, waiting for transfers between devices: 5.91 us -> 4.05 us  [to_dp(): return lax.ppermute(array, 'dp', [(i, i ^ mask) for i in range(dp_count)])]
    ppermute x6, waiting for transfers between devices: 13.1 us -> 11.8 us  [to_expert(): return lax.ppermute(array, 'expert', pairs)]
    ppermute x12, starting transfers between devices: 5.77 us -> 6.96 us  [to_dp(): return lax.ppermute(array, 'dp', [(i, i ^ mask) for i in range(dp_count)])]
  transfers between devices with their start and end apart: 19 -> 19, of which waited for: 7 -> 8; matrix products, arithmetic and copies ran while one was open for 0% -> 0% of each run, Pallas kernels for 12% -> 15%
where the time goes in v7:
time: 46.6 us; the launch traced here: 46.1 us
  starting transfers between devices  17.9 us (38%)
  waiting for transfers between devices  17.3 us (37%)
  Pallas kernels  9.37 us (20%)
  between operations  0.78 us (2%)
  local copies, waits for them, and re-layouts  0.67 us (1%)
    ppermute x6, waiting for transfers between devices, to_expert(): return lax.ppermute(array, 'expert', pairs)  11.8 us
    pallas_call x8, Pallas kernels, call(): pl.pallas_call(kernel, out_shape=out_shape, in_specs=specs, out_specs=jax...  9.37 us
    ppermute x6, starting transfers between devices, to_expert(): return lax.ppermute(array, 'expert', pairs)  8.8 us
    ppermute x12, starting transfers between devices, to_dp(): return lax.ppermute(array, 'dp', [(i, i ^ mask) for i in range(dp_count)])  6.96 us
    ppermute x12, waiting for transfers between devices, to_dp(): return lax.ppermute(array, 'dp', [(i, i ^ mask) for i in range(dp_count)])  4.05 us
    ppermute x1, starting transfers between devices, to_group(): return lax.ppermute(array, 'groups', [(0, 1), (1, 0)])  2.09 us
    ppermute x1, waiting for transfers between devices, to_group(): return lax.ppermute(array, 'groups', [(0, 1), (1, 0)])  1.44 us
  transfers between devices with their start and end apart: 19, of which 8 were waited for; matrix products, arithmetic and copies ran while one was open for 0% of the time, Pallas kernels for 15%

profile of v7, /device:TPU:0, one launch (start us, length us, event | category | flops | bytes accessed | tf_op | source)
XLA Modules:
  0.0 46.1 jit_solution(8103206898773784475)
XLA Ops:
  0.6 0.0 copy-start
  0.6 1.3 %shard_map.119 = (bf16[512,384]{1,0:T(8,128)(2,1)S(1)}, bf16[1024,384]{1,0:T(8,128)(2,1)S(1)}) custom-call(s32[1]{0:T(128)} %bitcast.4.flag_ref, bf16[512,384]{1,0:T(8,128)(2,1)} %bitcast.19, bf16[512,384]{1,0:T(8,128)(2,1)} %bitcast.20), custom_call_target="tpu_custom_call" | custom-call | flops 1 | bytes 1 | tf_op jit(solution)/shard_map/pallas_call | solution.py:48
  2.0 0.5 %collective-permute-start = (bf16[1024,384]{1,0:T(8,128)(2,1)S(1)}, bf16[1024,384]{1,0:T(8,128)(2,1)S(1)}, u32[]{:S(2)}, u32[]{:S(2)}) collective-permute-start(bf16[1024,384]{1,0:T(8,128)(2,1)S(1)} %get-tuple-element.55.refs_0_), channel_id=1, source_target_pairs={{0,1},{1,0},{2,3},{3,2},{4,5},{5,4},{6,7},{7,6},{8,9},{9,8},{10,11... | collective-permute-start | bytes 2359304 | tf_op jit(solution)/shard_map/ppermute | solution.py:356
  2.5 0.1 collective-permute-start.1
  2.6 2.9 %collective-permute-start.5 = (bf16[512,384]{1,0:T(8,128)(2,1)S(1)}, bf16[512,384]{1,0:T(8,128)(2,1)S(1)}, u32[]{:S(2)}, u32[]{:S(2)}) collective-permute-start(bf16[512,384]{1,0:T(8,128)(2,1)S(1)} %get-tuple-element.53), channel_id=1, source_target_pairs={{0,2},{1,3},{2,0},{3,1},{4,6},{5,7},{6,4},{7,5},{8,10},{9,11},{10,... | collective-permute-start | bytes 1179656 | tf_op jit(solution)/shard_map/ppermute | solution.py:356
  5.5 0.0 copy-start.4
  5.5 0.0 copy-start.3
  5.5 0.1 pad_add_fusion.place_ref
  5.6 0.0 copy-done
  5.6 0.6 %copy-done.4 = s32[128,8]{0,1:T(8,128)S(1)} copy-done((s32[128,8]{0,1:T(8,128)S(1)}, s32[128,8]{0,1:T(8,128)}, u32[]{:S(2)}) %copy-start.4) | copy-done | bytes 4120
  6.2 0.0 copy-done.3
  6.2 0.0 copy-start.2
  6.2 1.8 %shard_map.118 = (bf16[32,2048]{1,0:T(8,128)(2,1)S(1)}, bf16[32,2048]{1,0:T(8,128)(2,1)S(1)}, bf16[32,2048]{1,0:T(8,128)(2,1)S(1)}, bf16[32,2048]{1,0:T(8,128)(2...) custom-call(s32[2]{0:T(128)S(1)} %pad_add_fusion.place_ref, s32[8,128]{1,0:T(8,128)S(1)} %bitcast.17, ...), custom_call_target="tpu_custom_call" | custom-call | flops 1 | bytes 1 | tf_op jit(solution)/shard_map/pallas_call | solution.py:48
  8.0 0.0 collective-permute-done.1.refs_3_
  8.0 0.0 collective-permute-done.refs_2_
  8.1 0.0 copy-done.2
  8.1 0.1 collective-permute-start.7
  8.1 3.1 %collective-permute-start.2 = (bf16[32,2048]{1,0:T(8,128)(2,1)S(1)}, bf16[32,2048]{1,0:T(8,128)(2,1)S(1)}, u32[]{:S(2)}, u32[]{:S(2)}) collective-permute-start(bf16[32,2048]{1,0:T(8,128)(2,1)S(1)} %get-tuple-element.57), channel_id=1, source_target_pairs={{0,8},{4,12},{8,0},{12,4},{1,9},{5,13},{9,1},{13,5},{2,10},{6,14},... | collective-permute-start | bytes 393224 | tf_op jit(solution)/shard_map/ppermute | solution.py:366
  11.2 1.3 %collective-permute-start.3 = (bf16[32,2048]{1,0:T(8,128)(2,1)S(1)}, bf16[32,2048]{1,0:T(8,128)(2,1)S(1)}, u32[]{:S(2)}, u32[]{:S(2)}) collective-permute-start(bf16[32,2048]{1,0:T(8,128)(2,1)S(1)} %get-tuple-element.58), channel_id=1, source_target_pairs={{0,12},{4,8},{8,4},{12,0},{1,13},{5,9},{9,5},{13,1},{2,14},{6,10},... | collective-permute-start | bytes 393224 | tf_op jit(solution)/shard_map/ppermute | solution.py:366
  12.6 0.2 collective-permute-start.4
  12.8 2.6 %collective-permute-done.5.refs_4_ = bf16[512,384]{1,0:T(8,128)(2,1)S(1)} collective-permute-done((bf16[512,384]{1,0:T(8,128)(2,1)S(1)}, bf16[512,384]{1,0:T(8,128)(2,1)S(1)}, u32[]{:S(2)}, u32[]{:S(2)}) %collective-permute-start.5) | collective-permute-done | bytes 393248 | tf_op jit(solution)/shard_map/ppermute | solution.py:356
  15.4 2.1 %collective-permute-start.9 = (bf16[512,384]{1,0:T(8,128)(2,1)S(1)}, bf16[512,384]{1,0:T(8,128)(2,1)S(1)}, u32[]{:S(2)}, u32[]{:S(2)}) collective-permute-start(bf16[512,384]{1,0:T(8,128)(2,1)S(1)} %collective-permute-done.5.refs_4_), channel_id=1, source_target_pairs={{0,16},{16,0},{1,17},{17,1},{2,18},{18,2},{3,19},{19,3},{4,20},{20... | collective-permute-start | bytes 1179656 | tf_op jit(solution)/shard_map/ppermute | solution.py:359
  17.5 3.7 %collective-permute-done.2.refs_1_ = bf16[32,2048]{1,0:T(8,128)(2,1)S(1)} collective-permute-done((bf16[32,2048]{1,0:T(8,128)(2,1)S(1)}, bf16[32,2048]{1,0:T(8,128)(2,1)S(1)}, u32[]{:S(2)}, u32[]{:S(2)}) %collective-permute-start.2) | collective-permute-done | bytes 131104 | tf_op jit(solution)/shard_map/ppermute | solution.py:366
  21.2 0.0 collective-permute-start.6
  21.2 0.0 collective-permute-done.3.refs_2_
  21.2 0.2 collective-permute-done.4.refs_3_
  21.4 0.1 shard_map.120
  21.5 1.6 %collective-permute-start.14 = (bf16[128,1024]{1,0:T(8,128)(2,1)S(1)}, bf16[128,1024]{1,0:T(8,128)(2,1)S(1)}, u32[]{:S(2)}, u32[]{:S(2)}) collective-permute-start(bf16[128,1024]{1,0:T(8,128)(2,1)S(1)} %get-tuple-element.70), channel_id=1, source_target_pairs={{0,2},{1,3},{2,0},{3,1},{4,6},{5,7},{6,4},{7,5},{8,10},{9,11},{10,... | collective-permute-start | bytes 786440 | tf_op jit(solution)/shard_map/ppermute | solution.py:356
  23.1 0.2 collective-permute-done.7.refs_1_.refs_6_
  23.3 0.0 collective-permute-start.8
  23.3 0.7 %shard_map.121.sums_ref = f32[64,1536]{1,0:T(8,128)S(1)} custom-call(bf16[128,2048]{1,0:T(8,128)(2,1)S(1)} %get-tuple-element.60.rows_ref, bf16[1024,384]{1,0:T(8,128)(2,1)S(1)} %get-tuple-element.55.refs_0_, bf16[384,512]{1,0:T(8,128)(2,1)S(1)} %bitcast.14, bf16[1024,384]{1,0:T(8,128)(2,1)S(1)} %collective-permute-done.refs_2_, ...), custom_call_target="tpu_custom_call" | custom-call | flops 8999999488 | bytes 1 | tf_op jit(solution)/shard_map/pallas_call | solution.py:48
  24.0 1.4 %collective-permute-done.9.refs_5_ = bf16[512,384]{1,0:T(8,128)(2,1)S(1)} collective-permute-done((bf16[512,384]{1,0:T(8,128)(2,1)S(1)}, bf16[512,384]{1,0:T(8,128)(2,1)S(1)}, u32[]{:S(2)}, u32[]{:S(2)}) %collective-permute-start.9) | collective-permute-done | bytes 393248 | tf_op jit(solution)/shard_map/ppermute | solution.py:359
  25.4 0.0 collective-permute-start.10
  25.4 0.0 collective-permute-done.6.refs_0_.refs_7_
  25.4 0.0 collective-permute-done.8.refs_2_.refs_9_
  25.4 0.4 shard_map.122.back_ref
  25.9 1.3 %collective-permute-done.10.refs_8_ = bf16[512,384]{1,0:T(8,128)(2,1)S(1)} collective-permute-done((bf16[512,384]{1,0:T(8,128)(2,1)S(1)}, bf16[512,384]{1,0:T(8,128)(2,1)S(1)}, u32[]{:S(2)}, u32[]{:S(2)}) %collective-permute-start.10) | collective-permute-done | bytes 393248 | tf_op jit(solution)/shard_map/ppermute | solution.py:356
  27.1 1.6 %shard_map.123 = (bf16[32,2048]{1,0:T(8,128)(2,1)S(1)}, bf16[32,2048]{1,0:T(8,128)(2,1)S(1)}, bf16[32,2048]{1,0:T(8,128)(2,1)S(1)}, bf16[32,2048]{1,0:T(8,128)(2,1)S(1)}, bf16[64,1152]{1,0:T(8,128)(2,1)S(1)}) custom-call(s32[1]{0:T(128)} %bitcast.4.flag_ref, bf16[128,2048]{1,0:T(8,128)(2,1)S(1)} %get-tuple-element.60.rows_ref, ...), custom_call_target="tpu_custom_call" | custom-call | flops 1 | bytes 1 | tf_op jit(solution)/shard_map/pallas_call | solution.py:48
  28.7 0.2 collective-permute-start.15
  28.9 2.9 %collective-permute-start.11 = (bf16[32,2048]{1,0:T(8,128)(2,1)S(1)}, bf16[32,2048]{1,0:T(8,128)(2,1)S(1)}, u32[]{:S(2)}, u32[]{:S(2)}) collective-permute-start(bf16[32,2048]{1,0:T(8,128)(2,1)S(1)} %get-tuple-element.65), channel_id=1, source_target_pairs={{0,8},{4,12},{8,0},{12,4},{1,9},{5,13},{9,1},{13,5},{2,10},{6,14},... | collective-permute-start | bytes 393224 | tf_op jit(solution)/shard_map/ppermute | solution.py:366
  31.8 1.0 %collective-permute-start.12 = (bf16[32,2048]{1,0:T(8,128)(2,1)S(1)}, bf16[32,2048]{1,0:T(8,128)(2,1)S(1)}, u32[]{:S(2)}, u32[]{:S(2)}) collective-permute-start(bf16[32,2048]{1,0:T(8,128)(2,1)S(1)} %get-tuple-element.66), channel_id=1, source_target_pairs={{0,12},{4,8},{8,4},{12,0},{1,13},{5,9},{9,5},{13,1},{2,14},{6,10},... | collective-permute-start | bytes 393224 | tf_op jit(solution)/shard_map/ppermute | solution.py:366
  32.8 0.2 collective-permute-start.13
  33.1 0.0 collective-permute-done.14.refs_1_
  33.1 0.9 %collective-permute-start.18 = (bf16[64,1152]{1,0:T(8,128)(2,1)S(1)}, bf16[64,1152]{1,0:T(8,128)(2,1)S(1)}, u32[]{:S(2)}, u32[]{:S(2)}) collective-permute-start(bf16[64,1152]{1,0:T(8,128)(2,1)S(1)} %get-tuple-element.81.refs_4_), channel_id=1, source_target_pairs={{0,3},{1,2},{2,1},{3,0},{4,7},{5,6},{6,5},{7,4},{8,11},{9,10},{10,... | collective-permute-start | bytes 442376 | tf_op jit(solution)/shard_map/ppermute | solution.py:356
  34.0 0.0 collective-permute-done.15.refs_6_
  34.0 0.7 %collective-permute-start.17 = (bf16[64,1152]{1,0:T(8,128)(2,1)S(1)}, bf16[64,1152]{1,0:T(8,128)(2,1)S(1)}, u32[]{:S(2)}, u32[]{:S(2)}) collective-permute-start(bf16[64,1152]{1,0:T(8,128)(2,1)S(1)} %get-tuple-element.81.refs_4_), channel_id=1, source_target_pairs={{0,2},{1,3},{2,0},{3,1},{4,6},{5,7},{6,4},{7,5},{8,10},{9,11},{10,... | collective-permute-start | bytes 442376 | tf_op jit(solution)/shard_map/ppermute | solution.py:356
  34.6 0.0 copy-start.1
  34.7 7.1 %collective-permute-done.11.refs_1_ = bf16[32,2048]{1,0:T(8,128)(2,1)S(1)} collective-permute-done((bf16[32,2048]{1,0:T(8,128)(2,1)S(1)}, bf16[32,2048]{1,0:T(8,128)(2,1)S(1)}, u32[]{:S(2)}, u32[]{:S(2)}) %collective-permute-start.11) | collective-permute-done | bytes 131104 | tf_op jit(solution)/shard_map/ppermute | solution.py:366
  41.8 0.0 collective-permute-start.16
  41.8 0.0 collective-permute-done.12.refs_2_
  41.8 0.8 %collective-permute-done.13.refs_3_ = bf16[32,2048]{1,0:T(8,128)(2,1)S(1)} collective-permute-done((bf16[32,2048]{1,0:T(8,128)(2,1)S(1)}, bf16[32,2048]{1,0:T(8,128)(2,1)S(1)}, u32[]{:S(2)}, u32[]{:S(2)}) %collective-permute-start.13) | collective-permute-done | bytes 131104 | tf_op jit(solution)/shard_map/ppermute | solution.py:366
  42.6 0.0 copy-done.1
  42.6 2.1 %shard_map.124 = (bf16[128,2048]{1,0:T(8,128)(2,1)}, bf16[128,2048]{1,0:T(8,128)(2,1)}, f32[8,128]{1,0:T(8,128)}) custom-call(s32[2]{0:T(128)S(1)} %pad_add_fusion.place_ref, s32[8,128]{1,0:T(8,128)S(1)} %bitcast.18, bf16[64,128]{1,0:T(8,128)(2,1)S(1)} %get-tuple-element.47.select_ref, bf16[128,128]{1,0:T(8,128)(2,1)S(1)} %get-tuple-element.48.table_ref, ...), custom_call_target="tpu_custom_call" | custom-call | flops 8589934592 | bytes 1 | tf_op jit(solution)/shard_map/pallas_call | solution.py:48
  44.7 0.0 collective-permute-done.16
  44.7 0.0 collective-permute-done.18.refs_7_
  44.7 0.0 collective-permute-done.17.refs_5_
  44.7 1.4 %shard_map.125 = (bf16[512,384]{1,0:T(8,128)(2,1)}, bf16[512,384]{1,0:T(8,128)(2,1)}, bf16[384,512]{1,0:T(8,128)(2,1)}) custom-call(bf16[128,1024]{1,0:T(8,128)(2,1)S(1)} %get-tuple-element.77.refs_0_, bf16[128,1024]{1,0:T(8,128)(2,1)S(1)} %collective-permute-done.14.refs_1_, bf16[128,512]{1,0:T(8,128)(2,1)S(1)} %get-tuple-element.79.refs_2_, ...), custom_call_target="tpu_custom_call" | custom-call | flops 1 | bytes 1 | tf_op jit(solution)/shard_map/pallas_call | solution.py:48
  (4 shorter events, 0.1 us)
Async XLA Ops:
  0.6 4.9 %copy-start = (bf16[128,2048]{1,0:T(8,128)(2,1)S(1)}, bf16[128,2048]{1,0:T(8,128)(2,1)}, u32[]{:S(2)}) copy-start(bf16[128,2048]{1,0:T(8,128)(2,1)} %x_ref.1) | copy-start | bytes 1572868
  2.0 6.1 %collective-permute-start = (bf16[1024,384]{1,0:T(8,128)(2,1)S(1)}, bf16[1024,384]{1,0:T(8,128)(2,1)S(1)}, u32[]{:S(2)}, u32[]{:S(2)}) collective-permute-start(bf16[1024,384]{1,0:T(8,128)(2,1)S(1)} %get-tuple-element.55.refs_0_), channel_id=1, source_target_pairs={{0,1},{1,0},{2,3},{3,2},{4,5},{5,4},{6,7},{7,6},{8,9},{9,8},{10,11... | collective-permute-start | bytes 2359304 | tf_op jit(solution)/shard_map/ppermute | solution.py:356
  2.5 5.5 %collective-permute-start.1 = (bf16[384,512]{1,0:T(8,128)(2,1)}, bf16[384,512]{1,0:T(8,128)(2,1)S(1)}, u32[]{:S(2)}, u32[]{:S(2)}) collective-permute-start(bf16[384,512]{1,0:T(8,128)(2,1)} %bitcast.12), channel_id=1, source_target_pairs={{0,1},{1,0},{2,3},{3,2},{4,5},{5,4},{6,7},{7,6},{8,9},{9,8},{10,11... | collective-permute-start | bytes 1179656 | tf_op jit(solution)/shard_map/ppermute | solution.py:356
  2.6 12.8 %collective-permute-start.5 = (bf16[512,384]{1,0:T(8,128)(2,1)S(1)}, bf16[512,384]{1,0:T(8,128)(2,1)S(1)}, u32[]{:S(2)}, u32[]{:S(2)}) collective-permute-start(bf16[512,384]{1,0:T(8,128)(2,1)S(1)} %get-tuple-element.53), channel_id=1, source_target_pairs={{0,2},{1,3},{2,0},{3,1},{4,6},{5,7},{6,4},{7,5},{8,10},{9,11},{10,... | collective-permute-start | bytes 1179656 | tf_op jit(solution)/shard_map/ppermute | solution.py:356
  5.5 0.7 %copy-start.4 = (s32[128,8]{0,1:T(8,128)S(1)}, s32[128,8]{0,1:T(8,128)}, u32[]{:S(2)}) copy-start(s32[128,8]{0,1:T(8,128)} %param.9) | copy-start | bytes 12292
  5.5 0.7 %copy-start.3 = (f32[128,8]{0,1:T(8,128)S(1)}, f32[128,8]{0,1:T(8,128)}, u32[]{:S(2)}) copy-start(f32[128,8]{0,1:T(8,128)} %param.10) | copy-start | bytes 12292
  6.2 1.9 %copy-start.2 = (bf16[1,384,512]{2,1,0:T(8,128)(2,1)S(1)}, bf16[1,384,512]{2,1,0:T(8,128)(2,1)}, u32[]{:S(2)}) copy-start(bf16[1,384,512]{2,1,0:T(8,128)(2,1)} %param.13) | copy-start | bytes 1179652
  8.1 15.2 %collective-permute-start.7 = (bf16[384,512]{1,0:T(8,128)(2,1)S(1)}, bf16[384,512]{1,0:T(8,128)(2,1)S(1)}, u32[]{:S(2)}, u32[]{:S(2)}) collective-permute-start(bf16[384,512]{1,0:T(8,128)(2,1)S(1)} %bitcast.13), channel_id=1, source_target_pairs={{0,2},{1,3},{2,0},{3,1},{4,6},{5,7},{6,4},{7,5},{8,10},{9,11},{10,... | collective-permute-start | bytes 1179656 | tf_op jit(solution)/shard_map/ppermute | solution.py:356
  8.1 13.1 %collective-permute-start.2 = (bf16[32,2048]{1,0:T(8,128)(2,1)S(1)}, bf16[32,2048]{1,0:T(8,128)(2,1)S(1)}, u32[]{:S(2)}, u32[]{:S(2)}) collective-permute-start(bf16[32,2048]{1,0:T(8,128)(2,1)S(1)} %get-tuple-element.57), channel_id=1, source_target_pairs={{0,8},{4,12},{8,0},{12,4},{1,9},{5,13},{9,1},{13,5},{2,10},{6,14},... | collective-permute-start | bytes 393224 | tf_op jit(solution)/shard_map/ppermute | solution.py:366
  11.2 10.0 %collective-permute-start.3 = (bf16[32,2048]{1,0:T(8,128)(2,1)S(1)}, bf16[32,2048]{1,0:T(8,128)(2,1)S(1)}, u32[]{:S(2)}, u32[]{:S(2)}) collective-permute-start(bf16[32,2048]{1,0:T(8,128)(2,1)S(1)} %get-tuple-element.58), channel_id=1, source_target_pairs={{0,12},{4,8},{8,4},{12,0},{1,13},{5,9},{9,5},{13,1},{2,14},{6,10},... | collective-permute-start | bytes 393224 | tf_op jit(solution)/shard_map/ppermute | solution.py:366
  12.6 8.8 %collective-permute-start.4 = (bf16[32,2048]{1,0:T(8,128)(2,1)S(1)}, bf16[32,2048]{1,0:T(8,128)(2,1)S(1)}, u32[]{:S(2)}, u32[]{:S(2)}) collective-permute-start(bf16[32,2048]{1,0:T(8,128)(2,1)S(1)} %get-tuple-element.59), channel_id=1, source_target_pairs={{0,4},{4,0},{8,12},{12,8},{1,5},{5,1},{9,13},{13,9},{2,6},{6,2},{1... | collective-permute-start | bytes 393224 | tf_op jit(solution)/shard_map/ppermute | solution.py:366
  15.4 10.0 %collective-permute-start.9 = (bf16[512,384]{1,0:T(8,128)(2,1)S(1)}, bf16[512,384]{1,0:T(8,128)(2,1)S(1)}, u32[]{:S(2)}, u32[]{:S(2)}) collective-permute-start(bf16[512,384]{1,0:T(8,128)(2,1)S(1)} %collective-permute-done.5.refs_4_), channel_id=1, source_target_pairs={{0,16},{16,0},{1,17},{17,1},{2,18},{18,2},{3,19},{19,3},{4,20},{20... | collective-permute-start | bytes 1179656 | tf_op jit(solution)/shard_map/ppermute | solution.py:359
  21.2 4.2 %collective-permute-start.6 = (bf16[512,384]{1,0:T(8,128)(2,1)S(1)}, bf16[512,384]{1,0:T(8,128)(2,1)S(1)}, u32[]{:S(2)}, u32[]{:S(2)}) collective-permute-start(bf16[512,384]{1,0:T(8,128)(2,1)S(1)} %collective-permute-done.5.refs_4_), channel_id=1, source_target_pairs={{0,1},{1,0},{2,3},{3,2},{4,5},{5,4},{6,7},{7,6},{8,9},{9,8},{10,11... | collective-permute-start | bytes 1179656 | tf_op jit(solution)/shard_map/ppermute | solution.py:356
  21.5 11.6 %collective-permute-start.14 = (bf16[128,1024]{1,0:T(8,128)(2,1)S(1)}, bf16[128,1024]{1,0:T(8,128)(2,1)S(1)}, u32[]{:S(2)}, u32[]{:S(2)}) collective-permute-start(bf16[128,1024]{1,0:T(8,128)(2,1)S(1)} %get-tuple-element.70), channel_id=1, source_target_pairs={{0,2},{1,3},{2,0},{3,1},{4,6},{5,7},{6,4},{7,5},{8,10},{9,11},{10,... | collective-permute-start | bytes 786440 | tf_op jit(solution)/shard_map/ppermute | solution.py:356
  23.3 2.2 %collective-permute-start.8 = (bf16[384,512]{1,0:T(8,128)(2,1)S(1)}, bf16[384,512]{1,0:T(8,128)(2,1)S(1)}, u32[]{:S(2)}, u32[]{:S(2)}) collective-permute-start(bf16[384,512]{1,0:T(8,128)(2,1)S(1)} %collective-permute-done.7.refs_1_.refs_6_), channel_id=1, source_target_pairs={{0,1},{1,0},{2,3},{3,2},{4,5},{5,4},{6,7},{7,6},{8,9},{9,8},{10,11... | collective-permute-start | bytes 1179656 | tf_op jit(solution)/shard_map/ppermute | solution.py:356
  25.4 1.7 %collective-permute-start.10 = (bf16[512,384]{1,0:T(8,128)(2,1)S(1)}, bf16[512,384]{1,0:T(8,128)(2,1)S(1)}, u32[]{:S(2)}, u32[]{:S(2)}) collective-permute-start(bf16[512,384]{1,0:T(8,128)(2,1)S(1)} %collective-permute-done.9.refs_5_), channel_id=1, source_target_pairs={{0,1},{1,0},{2,3},{3,2},{4,5},{5,4},{6,7},{7,6},{8,9},{9,8},{10,11... | collective-permute-start | bytes 1179656 | tf_op jit(solution)/shard_map/ppermute | solution.py:356
  28.7 5.2 %collective-permute-start.15 = (bf16[64,1152]{1,0:T(8,128)(2,1)S(1)}, bf16[64,1152]{1,0:T(8,128)(2,1)S(1)}, u32[]{:S(2)}, u32[]{:S(2)}) collective-permute-start(bf16[64,1152]{1,0:T(8,128)(2,1)S(1)} %get-tuple-element.81.refs_4_), channel_id=1, source_target_pairs={{0,1},{1,0},{2,3},{3,2},{4,5},{5,4},{6,7},{7,6},{8,9},{9,8},{10,11... | collective-permute-start | bytes 442376 | tf_op jit(solution)/shard_map/ppermute | solution.py:356
  28.9 12.9 %collective-permute-start.11 = (bf16[32,2048]{1,0:T(8,128)(2,1)S(1)}, bf16[32,2048]{1,0:T(8,128)(2,1)S(1)}, u32[]{:S(2)}, u32[]{:S(2)}) collective-permute-start(bf16[32,2048]{1,0:T(8,128)(2,1)S(1)} %get-tuple-element.65), channel_id=1, source_target_pairs={{0,8},{4,12},{8,0},{12,4},{1,9},{5,13},{9,1},{13,5},{2,10},{6,14},... | collective-permute-start | bytes 393224 | tf_op jit(solution)/shard_map/ppermute | solution.py:366
  31.8 10.0 %collective-permute-start.12 = (bf16[32,2048]{1,0:T(8,128)(2,1)S(1)}, bf16[32,2048]{1,0:T(8,128)(2,1)S(1)}, u32[]{:S(2)}, u32[]{:S(2)}) collective-permute-start(bf16[32,2048]{1,0:T(8,128)(2,1)S(1)} %get-tuple-element.66), channel_id=1, source_target_pairs={{0,12},{4,8},{8,4},{12,0},{1,13},{5,9},{9,5},{13,1},{2,14},{6,10},... | collective-permute-start | bytes 393224 | tf_op jit(solution)/shard_map/ppermute | solution.py:366
  32.8 9.8 %collective-permute-start.13 = (bf16[32,2048]{1,0:T(8,128)(2,1)S(1)}, bf16[32,2048]{1,0:T(8,128)(2,1)S(1)}, u32[]{:S(2)}, u32[]{:S(2)}) collective-permute-start(bf16[32,2048]{1,0:T(8,128)(2,1)S(1)} %get-tuple-element.67), channel_id=1, source_target_pairs={{0,4},{4,0},{8,12},{12,8},{1,5},{5,1},{9,13},{13,9},{2,6},{6,2},{1... | collective-permute-start | bytes 393224 | tf_op jit(solution)/shard_map/ppermute | solution.py:366
  33.1 11.6 %collective-permute-start.18 = (bf16[64,1152]{1,0:T(8,128)(2,1)S(1)}, bf16[64,1152]{1,0:T(8,128)(2,1)S(1)}, u32[]{:S(2)}, u32[]{:S(2)}) collective-permute-start(bf16[64,1152]{1,0:T(8,128)(2,1)S(1)} %get-tuple-element.81.refs_4_), channel_id=1, source_target_pairs={{0,3},{1,2},{2,1},{3,0},{4,7},{5,6},{6,5},{7,4},{8,11},{9,10},{10,... | collective-permute-start | bytes 442376 | tf_op jit(solution)/shard_map/ppermute | solution.py:356
  34.0 10.7 %collective-permute-start.17 = (bf16[64,1152]{1,0:T(8,128)(2,1)S(1)}, bf16[64,1152]{1,0:T(8,128)(2,1)S(1)}, u32[]{:S(2)}, u32[]{:S(2)}) collective-permute-start(bf16[64,1152]{1,0:T(8,128)(2,1)S(1)} %get-tuple-element.81.refs_4_), channel_id=1, source_target_pairs={{0,2},{1,3},{2,0},{3,1},{4,6},{5,7},{6,4},{7,5},{8,10},{9,11},{10,... | collective-permute-start | bytes 442376 | tf_op jit(solution)/shard_map/ppermute | solution.py:356
  34.6 8.0 %copy-start.1 = (bf16[128,2048]{1,0:T(8,128)(2,1)S(1)}, bf16[128,2048]{1,0:T(8,128)(2,1)}, u32[]{:S(2)}) copy-start(bf16[128,2048]{1,0:T(8,128)(2,1)} %dy_ref.1) | copy-start | bytes 1572868
  41.8 2.8 %collective-permute-start.16 = (bf16[256,512]{1,0:T(8,128)(2,1)S(1)}, bf16[256,512]{1,0:T(8,128)(2,1)S(1)}, u32[]{:S(2)}, u32[]{:S(2)}) collective-permute-start(bf16[256,512]{1,0:T(8,128)(2,1)S(1)} %pad_maximum_fusion), channel_id=1, source_target_pairs={{0,1},{1,0},{2,3},{3,2},{4,5},{5,4},{6,7},{7,6},{8,9},{9,8},{10,11... | collective-permute-start | bytes 786440 | tf_op jit(solution)/shard_map/ppermute | solution.py:356

commit v8 on v7

--- a/solution.py
+++ b/solution.py
@@ -13,6 +13,7 @@
 FIRST_WEIGHT = 9 * 10**9
 COLLECT_WEIGHT = 1 << 33
 BACK_WEIGHT = 1 << 33
+ARRANGE_WEIGHT = 3500 * 10**6
 
 
 def dot(left, right):
@@ -177,7 +178,7 @@
                 part_refs[j][dy, :] = chunk_refs[e][capacity:, column]
 
     outs = [shape((2 * total, model_width))] + [shape((2 * total, width))] * dp_count
-    got = call(kernel, outs, *chunks)
+    got = call(kernel, outs, *chunks, weight=ARRANGE_WEIGHT)
     return got[0], got[1:]
 
 
@@ -313,15 +314,17 @@
 
     def kernel(place_ref, ids_ref, select_ref, table_ref, dy_ref, *refs):
         chunk_refs, (mixed_ref, grad_ref, gates_ref) = refs[:count], refs[count:]
+        out = jnp.concatenate([r[0:capacity, :] for r in chunk_refs], axis=0)
+        back = jnp.concatenate([r[capacity:, :] for r in chunk_refs], axis=0)
+        mixed = dot(table_ref[...], jnp.concatenate([out] * 2, axis=0)).astype(BF16)
+        grad = dot(table_ref[...], jnp.concatenate([back] * 2, axis=0)).astype(BF16)
         inner = 0.0
         for j in range(dp_count):
             column = slice(j * width, (j + 1) * width)
             home = pl.ds(pl.multiple_of((place_ref[1] ^ j) * width, width), width)
-            out = jnp.concatenate([r[0:capacity, column] for r in chunk_refs], axis=0)
-            back = jnp.concatenate([r[capacity:, column] for r in chunk_refs], axis=0)
-            mixed_ref[:, home] = dot(table_ref[...], jnp.concatenate([out] * 2, axis=0)).astype(BF16)
-            grad_ref[:, home] = dot(table_ref[...], jnp.concatenate([back] * 2, axis=0)).astype(BF16)
-            inner += dot_last(out, dy_ref[:, home])
+            mixed_ref[:, home] = mixed[:, column]
+            grad_ref[:, home] = grad[:, column]
+            inner += dot_last(out[:, column], dy_ref[:, home])
         inner = jnp.where(select_ref[...] > 0, inner, 0.0)
         step = step_of(lax.broadcasted_iota(jnp.int32, (total, token_rows), 0) // capacity, count)
         far = step + place_ref[0]

time: 46.6 us -> 46.4 us (level)
  starting transfers between devices: 17.9 us -> 17 us
  waiting for transfers between devices: 17.3 us -> 18.2 us
    ppermute x12, waiting for transfers between devices: 4.05 us -> 5.3 us  [to_dp(): return lax.ppermute(array, 'dp', [(i, i ^ mask) for i in range(dp_count)])]
  transfers between devices with their start and end apart: 19 -> 19, of which waited for: 8 -> 8; matrix products, arithmetic and copies ran while one was open for 0% -> 0% of each run, Pallas kernels for 15% -> 14%
where the time goes in v8:
time: 46.4 us; the launch traced here: 46 us
  waiting for transfers between devices  18.2 us (39%)
  starting transfers between devices  17 us (37%)
  Pallas kernels  9.25 us (20%)
  between operations  0.76 us (2%)
  local copies, waits for them, and re-layouts  0.67 us (1%)
    ppermute x6, waiting for transfers between devices, to_expert(): return lax.ppermute(array, 'expert', pairs)  11.5 us
    pallas_call x8, Pallas kernels, call(): pl.pallas_call(kernel, out_shape=out_shape, in_specs=specs, out_specs=jax...  9.25 us
    ppermute x6, starting transfers between devices, to_expert(): return lax.ppermute(array, 'expert', pairs)  8.35 us
    ppermute x12, starting transfers between devices, to_dp(): return lax.ppermute(array, 'dp', [(i, i ^ mask) for i in range(dp_count)])  6.55 us
    ppermute x12, waiting for transfers between devices, to_dp(): return lax.ppermute(array, 'dp', [(i, i ^ mask) for i in range(dp_count)])  5.3 us
    ppermute x1, starting transfers between devices, to_group(): return lax.ppermute(array, 'groups', [(0, 1), (1, 0)])  2.09 us
    ppermute x1, waiting for transfers between devices, to_group(): return lax.ppermute(array, 'groups', [(0, 1), (1, 0)])  1.44 us
  transfers between devices with their start and end apart: 19, of which 8 were waited for; matrix products, arithmetic and copies ran while one was open for 0% of the time, Pallas kernels for 14%

profile of v8, /device:TPU:0, one launch (start us, length us, event | category | flops | bytes accessed | tf_op | source)
XLA Modules:
  0.0 46.0 jit_solution(7604865329545139011)
XLA Ops:
  0.6 0.0 copy-start
  0.6 1.3 %shard_map.119 = (bf16[512,384]{1,0:T(8,128)(2,1)S(1)}, bf16[1024,384]{1,0:T(8,128)(2,1)S(1)}) custom-call(s32[1]{0:T(128)} %bitcast.4.flag_ref, bf16[512,384]{1,0:T(8,128)(2,1)} %bitcast.19, bf16[512,384]{1,0:T(8,128)(2,1)} %bitcast.20), custom_call_target="tpu_custom_call" | custom-call | flops 1 | bytes 1 | tf_op jit(solution)/shard_map/pallas_call | solution.py:49
  2.0 0.5 %collective-permute-start = (bf16[1024,384]{1,0:T(8,128)(2,1)S(1)}, bf16[1024,384]{1,0:T(8,128)(2,1)S(1)}, u32[]{:S(2)}, u32[]{:S(2)}) collective-permute-start(bf16[1024,384]{1,0:T(8,128)(2,1)S(1)} %get-tuple-element.55.refs_0_), channel_id=1, source_target_pairs={{0,1},{1,0},{2,3},{3,2},{4,5},{5,4},{6,7},{7,6},{8,9},{9,8},{10,11... | collective-permute-start | bytes 2359304 | tf_op jit(solution)/shard_map/ppermute | solution.py:359
  2.5 0.1 collective-permute-start.1
  2.6 2.9 %collective-permute-start.5 = (bf16[512,384]{1,0:T(8,128)(2,1)S(1)}, bf16[512,384]{1,0:T(8,128)(2,1)S(1)}, u32[]{:S(2)}, u32[]{:S(2)}) collective-permute-start(bf16[512,384]{1,0:T(8,128)(2,1)S(1)} %get-tuple-element.53), channel_id=1, source_target_pairs={{0,2},{1,3},{2,0},{3,1},{4,6},{5,7},{6,4},{7,5},{8,10},{9,11},{10,... | collective-permute-start | bytes 1179656 | tf_op jit(solution)/shard_map/ppermute | solution.py:359
  5.5 0.0 copy-start.4
  5.5 0.0 copy-start.3
  5.5 0.1 pad_add_fusion.place_ref
  5.6 0.0 copy-done
  5.6 0.6 %copy-done.4 = s32[128,8]{0,1:T(8,128)S(1)} copy-done((s32[128,8]{0,1:T(8,128)S(1)}, s32[128,8]{0,1:T(8,128)}, u32[]{:S(2)}) %copy-start.4) | copy-done | bytes 4120
  6.2 0.0 copy-done.3
  6.2 0.0 copy-start.2
  6.2 1.8 %shard_map.118 = (bf16[32,2048]{1,0:T(8,128)(2,1)S(1)}, bf16[32,2048]{1,0:T(8,128)(2,1)S(1)}, bf16[32,2048]{1,0:T(8,128)(2,1)S(1)}, bf16[32,2048]{1,0:T(8,128)(2...) custom-call(s32[2]{0:T(128)S(1)} %pad_add_fusion.place_ref, s32[8,128]{1,0:T(8,128)S(1)} %bitcast.17, ...), custom_call_target="tpu_custom_call" | custom-call | flops 1 | bytes 1 | tf_op jit(solution)/shard_map/pallas_call | solution.py:49
  8.0 0.0 collective-permute-done.1.refs_3_
  8.0 0.0 collective-permute-done.refs_2_
  8.1 2.7 %collective-permute-start.2 = (bf16[32,2048]{1,0:T(8,128)(2,1)S(1)}, bf16[32,2048]{1,0:T(8,128)(2,1)S(1)}, u32[]{:S(2)}, u32[]{:S(2)}) collective-permute-start(bf16[32,2048]{1,0:T(8,128)(2,1)S(1)} %get-tuple-element.57), channel_id=1, source_target_pairs={{0,8},{4,12},{8,0},{12,4},{1,9},{5,13},{9,1},{13,5},{2,10},{6,14},... | collective-permute-start | bytes 393224 | tf_op jit(solution)/shard_map/ppermute | solution.py:369
  10.7 1.3 %collective-permute-start.3 = (bf16[32,2048]{1,0:T(8,128)(2,1)S(1)}, bf16[32,2048]{1,0:T(8,128)(2,1)S(1)}, u32[]{:S(2)}, u32[]{:S(2)}) collective-permute-start(bf16[32,2048]{1,0:T(8,128)(2,1)S(1)} %get-tuple-element.58), channel_id=1, source_target_pairs={{0,12},{4,8},{8,4},{12,0},{1,13},{5,9},{9,5},{13,1},{2,14},{6,10},... | collective-permute-start | bytes 393224 | tf_op jit(solution)/shard_map/ppermute | solution.py:369
  12.1 0.2 collective-permute-start.4
  12.3 0.0 copy-done.2
  12.3 0.5 %collective-permute-start.7 = (bf16[384,512]{1,0:T(8,128)(2,1)S(1)}, bf16[384,512]{1,0:T(8,128)(2,1)S(1)}, u32[]{:S(2)}, u32[]{:S(2)}) collective-permute-start(bf16[384,512]{1,0:T(8,128)(2,1)S(1)} %bitcast.13), channel_id=1, source_target_pairs={{0,2},{1,3},{2,0},{3,1},{4,6},{5,7},{6,4},{7,5},{8,10},{9,11},{10,... | collective-permute-start | bytes 1179656 | tf_op jit(solution)/shard_map/ppermute | solution.py:359
  12.8 2.6 %collective-permute-done.5.refs_4_ = bf16[512,384]{1,0:T(8,128)(2,1)S(1)} collective-permute-done((bf16[512,384]{1,0:T(8,128)(2,1)S(1)}, bf16[512,384]{1,0:T(8,128)(2,1)S(1)}, u32[]{:S(2)}, u32[]{:S(2)}) %collective-permute-start.5) | collective-permute-done | bytes 393248 | tf_op jit(solution)/shard_map/ppermute | solution.py:359
  15.4 2.1 %collective-permute-start.9 = (bf16[512,384]{1,0:T(8,128)(2,1)S(1)}, bf16[512,384]{1,0:T(8,128)(2,1)S(1)}, u32[]{:S(2)}, u32[]{:S(2)}) collective-permute-start(bf16[512,384]{1,0:T(8,128)(2,1)S(1)} %collective-permute-done.5.refs_4_), channel_id=1, source_target_pairs={{0,16},{16,0},{1,17},{17,1},{2,18},{18,2},{3,19},{19,3},{4,20},{20... | collective-permute-start | bytes 1179656 | tf_op jit(solution)/shard_map/ppermute | solution.py:362
  17.5 3.5 %collective-permute-done.2.refs_1_ = bf16[32,2048]{1,0:T(8,128)(2,1)S(1)} collective-permute-done((bf16[32,2048]{1,0:T(8,128)(2,1)S(1)}, bf16[32,2048]{1,0:T(8,128)(2,1)S(1)}, u32[]{:S(2)}, u32[]{:S(2)}) %collective-permute-start.2) | collective-permute-done | bytes 131104 | tf_op jit(solution)/shard_map/ppermute | solution.py:369
  21.0 0.0 collective-permute-start.6
  21.0 0.0 collective-permute-done.3.refs_2_
  21.0 0.2 collective-permute-done.4.refs_3_
  21.2 0.1 shard_map.120
  21.3 0.6 %collective-permute-start.14 = (bf16[128,1024]{1,0:T(8,128)(2,1)S(1)}, bf16[128,1024]{1,0:T(8,128)(2,1)S(1)}, u32[]{:S(2)}, u32[]{:S(2)}) collective-permute-start(bf16[128,1024]{1,0:T(8,128)(2,1)S(1)} %get-tuple-element.70), channel_id=1, source_target_pairs={{0,2},{1,3},{2,0},{3,1},{4,6},{5,7},{6,4},{7,5},{8,10},{9,11},{10,... | collective-permute-start | bytes 786440 | tf_op jit(solution)/shard_map/ppermute | solution.py:359
  21.8 1.4 %collective-permute-done.7.refs_1_.refs_6_ = bf16[384,512]{1,0:T(8,128)(2,1)S(1)} collective-permute-done((bf16[384,512]{1,0:T(8,128)(2,1)S(1)}, bf16[384,512]{1,0:T(8,128)(2,1)S(1)}, u32[]{:S(2)}, u32[]{:S(2)}) %collective-permute-start.7) | collective-permute-done | bytes 393248 | tf_op jit(solution)/shard_map/ppermute | solution.py:359
  23.3 0.0 collective-permute-start.8
  23.3 0.7 %shard_map.121.sums_ref = f32[64,1536]{1,0:T(8,128)S(1)} custom-call(bf16[128,2048]{1,0:T(8,128)(2,1)S(1)} %get-tuple-element.60.rows_ref, bf16[1024,384]{1,0:T(8,128)(2,1)S(1)} %get-tuple-element.55.refs_0_, bf16[384,512]{1,0:T(8,128)(2,1)S(1)} %bitcast.14, bf16[1024,384]{1,0:T(8,128)(2,1)S(1)} %collective-permute-done.refs_2_, ...), custom_call_target="tpu_custom_call" | custom-call | flops 8999999488 | bytes 1 | tf_op jit(solution)/shard_map/pallas_call | solution.py:49
  24.0 1.4 %collective-permute-done.9.refs_5_ = bf16[512,384]{1,0:T(8,128)(2,1)S(1)} collective-permute-done((bf16[512,384]{1,0:T(8,128)(2,1)S(1)}, bf16[512,384]{1,0:T(8,128)(2,1)S(1)}, u32[]{:S(2)}, u32[]{:S(2)}) %collective-permute-start.9) | collective-permute-done | bytes 393248 | tf_op jit(solution)/shard_map/ppermute | solution.py:362
  25.4 0.0 collective-permute-start.10
  25.4 0.0 collective-permute-done.6.refs_0_.refs_7_
  25.4 0.0 collective-permute-done.8.refs_2_.refs_9_
  25.4 0.4 shard_map.122.back_ref
  25.9 1.3 %collective-permute-done.10.refs_8_ = bf16[512,384]{1,0:T(8,128)(2,1)S(1)} collective-permute-done((bf16[512,384]{1,0:T(8,128)(2,1)S(1)}, bf16[512,384]{1,0:T(8,128)(2,1)S(1)}, u32[]{:S(2)}, u32[]{:S(2)}) %collective-permute-start.10) | collective-permute-done | bytes 393248 | tf_op jit(solution)/shard_map/ppermute | solution.py:359
  27.1 1.6 %shard_map.123 = (bf16[32,2048]{1,0:T(8,128)(2,1)S(1)}, bf16[32,2048]{1,0:T(8,128)(2,1)S(1)}, bf16[32,2048]{1,0:T(8,128)(2,1)S(1)}, bf16[32,2048]{1,0:T(8,128)(2,1)S(1)}, bf16[64,1152]{1,0:T(8,128)(2,1)S(1)}) custom-call(s32[1]{0:T(128)} %bitcast.4.flag_ref, bf16[128,2048]{1,0:T(8,128)(2,1)S(1)} %get-tuple-element.60.rows_ref, ...), custom_call_target="tpu_custom_call" | custom-call | flops 1 | bytes 1 | tf_op jit(solution)/shard_map/pallas_call | solution.py:49
  28.7 0.2 collective-permute-start.15
  28.9 2.5 %collective-permute-start.11 = (bf16[32,2048]{1,0:T(8,128)(2,1)S(1)}, bf16[32,2048]{1,0:T(8,128)(2,1)S(1)}, u32[]{:S(2)}, u32[]{:S(2)}) collective-permute-start(bf16[32,2048]{1,0:T(8,128)(2,1)S(1)} %get-tuple-element.65), channel_id=1, source_target_pairs={{0,8},{4,12},{8,0},{12,4},{1,9},{5,13},{9,1},{13,5},{2,10},{6,14},... | collective-permute-start | bytes 393224 | tf_op jit(solution)/shard_map/ppermute | solution.py:369
  31.5 1.4 %collective-permute-start.12 = (bf16[32,2048]{1,0:T(8,128)(2,1)S(1)}, bf16[32,2048]{1,0:T(8,128)(2,1)S(1)}, u32[]{:S(2)}, u32[]{:S(2)}) collective-permute-start(bf16[32,2048]{1,0:T(8,128)(2,1)S(1)} %get-tuple-element.66), channel_id=1, source_target_pairs={{0,12},{4,8},{8,4},{12,0},{1,13},{5,9},{9,5},{13,1},{2,14},{6,10},... | collective-permute-start | bytes 393224 | tf_op jit(solution)/shard_map/ppermute | solution.py:369
  32.8 0.2 collective-permute-start.13
  33.1 0.0 collective-permute-done.14.refs_1_
  33.1 0.9 %collective-permute-start.18 = (bf16[64,1152]{1,0:T(8,128)(2,1)S(1)}, bf16[64,1152]{1,0:T(8,128)(2,1)S(1)}, u32[]{:S(2)}, u32[]{:S(2)}) collective-permute-start(bf16[64,1152]{1,0:T(8,128)(2,1)S(1)} %get-tuple-element.81.refs_4_), channel_id=1, source_target_pairs={{0,3},{1,2},{2,1},{3,0},{4,7},{5,6},{6,5},{7,4},{8,11},{9,10},{10,... | collective-permute-start | bytes 442376 | tf_op jit(solution)/shard_map/ppermute | solution.py:359
  34.0 0.0 collective-permute-done.15.refs_6_
  34.0 0.8 %collective-permute-start.17 = (bf16[64,1152]{1,0:T(8,128)(2,1)S(1)}, bf16[64,1152]{1,0:T(8,128)(2,1)S(1)}, u32[]{:S(2)}, u32[]{:S(2)}) collective-permute-start(bf16[64,1152]{1,0:T(8,128)(2,1)S(1)} %get-tuple-element.81.refs_4_), channel_id=1, source_target_pairs={{0,2},{1,3},{2,0},{3,1},{4,6},{5,7},{6,4},{7,5},{8,10},{9,11},{10,... | collective-permute-start | bytes 442376 | tf_op jit(solution)/shard_map/ppermute | solution.py:359
  34.8 0.0 copy-start.1
  34.9 7.0 %collective-permute-done.11.refs_1_ = bf16[32,2048]{1,0:T(8,128)(2,1)S(1)} collective-permute-done((bf16[32,2048]{1,0:T(8,128)(2,1)S(1)}, bf16[32,2048]{1,0:T(8,128)(2,1)S(1)}, u32[]{:S(2)}, u32[]{:S(2)}) %collective-permute-start.11) | collective-permute-done | bytes 131104 | tf_op jit(solution)/shard_map/ppermute | solution.py:369
  41.8 0.0 collective-permute-start.16
  41.8 0.0 collective-permute-done.12.refs_2_
  41.8 0.8 %collective-permute-done.13.refs_3_ = bf16[32,2048]{1,0:T(8,128)(2,1)S(1)} collective-permute-done((bf16[32,2048]{1,0:T(8,128)(2,1)S(1)}, bf16[32,2048]{1,0:T(8,128)(2,1)S(1)}, u32[]{:S(2)}, u32[]{:S(2)}) %collective-permute-start.13) | collective-permute-done | bytes 131104 | tf_op jit(solution)/shard_map/ppermute | solution.py:369
  42.6 0.0 copy-done.1
  42.6 2.0 %shard_map.124 = (bf16[128,2048]{1,0:T(8,128)(2,1)}, bf16[128,2048]{1,0:T(8,128)(2,1)}, f32[8,128]{1,0:T(8,128)}) custom-call(s32[2]{0:T(128)S(1)} %pad_add_fusion.place_ref, s32[8,128]{1,0:T(8,128)S(1)} %bitcast.18, bf16[64,128]{1,0:T(8,128)(2,1)S(1)} %get-tuple-element.47.select_ref, bf16[128,128]{1,0:T(8,128)(2,1)S(1)} %get-tuple-element.48.table_ref, ...), custom_call_target="tpu_custom_call" | custom-call | flops 8589934592 | bytes 1 | tf_op jit(solution)/shard_map/pallas_call | solution.py:49
  44.6 0.0 collective-permute-done.16
  44.6 0.0 collective-permute-done.18.refs_7_
  44.6 0.0 collective-permute-done.17.refs_5_
  44.6 1.4 %shard_map.125 = (bf16[512,384]{1,0:T(8,128)(2,1)}, bf16[512,384]{1,0:T(8,128)(2,1)}, bf16[384,512]{1,0:T(8,128)(2,1)}) custom-call(bf16[128,1024]{1,0:T(8,128)(2,1)S(1)} %get-tuple-element.77.refs_0_, bf16[128,1024]{1,0:T(8,128)(2,1)S(1)} %collective-permute-done.14.refs_1_, bf16[128,512]{1,0:T(8,128)(2,1)S(1)} %get-tuple-element.79.refs_2_, ...), custom_call_target="tpu_custom_call" | custom-call | flops 1 | bytes 1 | tf_op jit(solution)/shard_map/pallas_call | solution.py:49
  (4 shorter events, 0.1 us)
Async XLA Ops:
  0.6 4.9 %copy-start = (bf16[128,2048]{1,0:T(8,128)(2,1)S(1)}, bf16[128,2048]{1,0:T(8,128)(2,1)}, u32[]{:S(2)}) copy-start(bf16[128,2048]{1,0:T(8,128)(2,1)} %x_ref.1) | copy-start | bytes 1572868
  2.0 6.1 %collective-permute-start = (bf16[1024,384]{1,0:T(8,128)(2,1)S(1)}, bf16[1024,384]{1,0:T(8,128)(2,1)S(1)}, u32[]{:S(2)}, u32[]{:S(2)}) collective-permute-start(bf16[1024,384]{1,0:T(8,128)(2,1)S(1)} %get-tuple-element.55.refs_0_), channel_id=1, source_target_pairs={{0,1},{1,0},{2,3},{3,2},{4,5},{5,4},{6,7},{7,6},{8,9},{9,8},{10,11... | collective-permute-start | bytes 2359304 | tf_op jit(solution)/shard_map/ppermute | solution.py:359
  2.5 5.5 %collective-permute-start.1 = (bf16[384,512]{1,0:T(8,128)(2,1)}, bf16[384,512]{1,0:T(8,128)(2,1)S(1)}, u32[]{:S(2)}, u32[]{:S(2)}) collective-permute-start(bf16[384,512]{1,0:T(8,128)(2,1)} %bitcast.12), channel_id=1, source_target_pairs={{0,1},{1,0},{2,3},{3,2},{4,5},{5,4},{6,7},{7,6},{8,9},{9,8},{10,11... | collective-permute-start | bytes 1179656 | tf_op jit(solution)/shard_map/ppermute | solution.py:359
  2.6 12.8 %collective-permute-start.5 = (bf16[512,384]{1,0:T(8,128)(2,1)S(1)}, bf16[512,384]{1,0:T(8,128)(2,1)S(1)}, u32[]{:S(2)}, u32[]{:S(2)}) collective-permute-start(bf16[512,384]{1,0:T(8,128)(2,1)S(1)} %get-tuple-element.53), channel_id=1, source_target_pairs={{0,2},{1,3},{2,0},{3,1},{4,6},{5,7},{6,4},{7,5},{8,10},{9,11},{10,... | collective-permute-start | bytes 1179656 | tf_op jit(solution)/shard_map/ppermute | solution.py:359
  5.5 0.7 %copy-start.4 = (s32[128,8]{0,1:T(8,128)S(1)}, s32[128,8]{0,1:T(8,128)}, u32[]{:S(2)}) copy-start(s32[128,8]{0,1:T(8,128)} %param.9) | copy-start | bytes 12292
  5.5 0.7 %copy-start.3 = (f32[128,8]{0,1:T(8,128)S(1)}, f32[128,8]{0,1:T(8,128)}, u32[]{:S(2)}) copy-start(f32[128,8]{0,1:T(8,128)} %param.10) | copy-start | bytes 12292
  6.2 6.1 %copy-start.2 = (bf16[1,384,512]{2,1,0:T(8,128)(2,1)S(1)}, bf16[1,384,512]{2,1,0:T(8,128)(2,1)}, u32[]{:S(2)}) copy-start(bf16[1,384,512]{2,1,0:T(8,128)(2,1)} %param.13) | copy-start | bytes 1179652
  8.1 13.0 %collective-permute-start.2 = (bf16[32,2048]{1,0:T(8,128)(2,1)S(1)}, bf16[32,2048]{1,0:T(8,128)(2,1)S(1)}, u32[]{:S(2)}, u32[]{:S(2)}) collective-permute-start(bf16[32,2048]{1,0:T(8,128)(2,1)S(1)} %get-tuple-element.57), channel_id=1, source_target_pairs={{0,8},{4,12},{8,0},{12,4},{1,9},{5,13},{9,1},{13,5},{2,10},{6,14},... | collective-permute-start | bytes 393224 | tf_op jit(solution)/shard_map/ppermute | solution.py:369
  10.7 10.3 %collective-permute-start.3 = (bf16[32,2048]{1,0:T(8,128)(2,1)S(1)}, bf16[32,2048]{1,0:T(8,128)(2,1)S(1)}, u32[]{:S(2)}, u32[]{:S(2)}) collective-permute-start(bf16[32,2048]{1,0:T(8,128)(2,1)S(1)} %get-tuple-element.58), channel_id=1, source_target_pairs={{0,12},{4,8},{8,4},{12,0},{1,13},{5,9},{9,5},{13,1},{2,14},{6,10},... | collective-permute-start | bytes 393224 | tf_op jit(solution)/shard_map/ppermute | solution.py:369
  12.1 9.2 %collective-permute-start.4 = (bf16[32,2048]{1,0:T(8,128)(2,1)S(1)}, bf16[32,2048]{1,0:T(8,128)(2,1)S(1)}, u32[]{:S(2)}, u32[]{:S(2)}) collective-permute-start(bf16[32,2048]{1,0:T(8,128)(2,1)S(1)} %get-tuple-element.59), channel_id=1, source_target_pairs={{0,4},{4,0},{8,12},{12,8},{1,5},{5,1},{9,13},{13,9},{2,6},{6,2},{1... | collective-permute-start | bytes 393224 | tf_op jit(solution)/shard_map/ppermute | solution.py:369
  12.3 11.0 %collective-permute-start.7 = (bf16[384,512]{1,0:T(8,128)(2,1)S(1)}, bf16[384,512]{1,0:T(8,128)(2,1)S(1)}, u32[]{:S(2)}, u32[]{:S(2)}) collective-permute-start(bf16[384,512]{1,0:T(8,128)(2,1)S(1)} %bitcast.13), channel_id=1, source_target_pairs={{0,2},{1,3},{2,0},{3,1},{4,6},{5,7},{6,4},{7,5},{8,10},{9,11},{10,... | collective-permute-start | bytes 1179656 | tf_op jit(solution)/shard_map/ppermute | solution.py:359
  15.4 10.0 %collective-permute-start.9 = (bf16[512,384]{1,0:T(8,128)(2,1)S(1)}, bf16[512,384]{1,0:T(8,128)(2,1)S(1)}, u32[]{:S(2)}, u32[]{:S(2)}) collective-permute-start(bf16[512,384]{1,0:T(8,128)(2,1)S(1)} %collective-permute-done.5.refs_4_), channel_id=1, source_target_pairs={{0,16},{16,0},{1,17},{17,1},{2,18},{18,2},{3,19},{19,3},{4,20},{20... | collective-permute-start | bytes 1179656 | tf_op jit(solution)/shard_map/ppermute | solution.py:362
  21.0 4.4 %collective-permute-start.6 = (bf16[512,384]{1,0:T(8,128)(2,1)S(1)}, bf16[512,384]{1,0:T(8,128)(2,1)S(1)}, u32[]{:S(2)}, u32[]{:S(2)}) collective-permute-start(bf16[512,384]{1,0:T(8,128)(2,1)S(1)} %collective-permute-done.5.refs_4_), channel_id=1, source_target_pairs={{0,1},{1,0},{2,3},{3,2},{4,5},{5,4},{6,7},{7,6},{8,9},{9,8},{10,11... | collective-permute-start | bytes 1179656 | tf_op jit(solution)/shard_map/ppermute | solution.py:359
  21.3 11.8 %collective-permute-start.14 = (bf16[128,1024]{1,0:T(8,128)(2,1)S(1)}, bf16[128,1024]{1,0:T(8,128)(2,1)S(1)}, u32[]{:S(2)}, u32[]{:S(2)}) collective-permute-start(bf16[128,1024]{1,0:T(8,128)(2,1)S(1)} %get-tuple-element.70), channel_id=1, source_target_pairs={{0,2},{1,3},{2,0},{3,1},{4,6},{5,7},{6,4},{7,5},{8,10},{9,11},{10,... | collective-permute-start | bytes 786440 | tf_op jit(solution)/shard_map/ppermute | solution.py:359
  23.3 2.2 %collective-permute-start.8 = (bf16[384,512]{1,0:T(8,128)(2,1)S(1)}, bf16[384,512]{1,0:T(8,128)(2,1)S(1)}, u32[]{:S(2)}, u32[]{:S(2)}) collective-permute-start(bf16[384,512]{1,0:T(8,128)(2,1)S(1)} %collective-permute-done.7.refs_1_.refs_6_), channel_id=1, source_target_pairs={{0,1},{1,0},{2,3},{3,2},{4,5},{5,4},{6,7},{7,6},{8,9},{9,8},{10,11... | collective-permute-start | bytes 1179656 | tf_op jit(solution)/shard_map/ppermute | solution.py:359
  25.4 1.7 %collective-permute-start.10 = (bf16[512,384]{1,0:T(8,128)(2,1)S(1)}, bf16[512,384]{1,0:T(8,128)(2,1)S(1)}, u32[]{:S(2)}, u32[]{:S(2)}) collective-permute-start(bf16[512,384]{1,0:T(8,128)(2,1)S(1)} %collective-permute-done.9.refs_5_), channel_id=1, source_target_pairs={{0,1},{1,0},{2,3},{3,2},{4,5},{5,4},{6,7},{7,6},{8,9},{9,8},{10,11... | collective-permute-start | bytes 1179656 | tf_op jit(solution)/shard_map/ppermute | solution.py:359
  28.7 5.2 %collective-permute-start.15 = (bf16[64,1152]{1,0:T(8,128)(2,1)S(1)}, bf16[64,1152]{1,0:T(8,128)(2,1)S(1)}, u32[]{:S(2)}, u32[]{:S(2)}) collective-permute-start(bf16[64,1152]{1,0:T(8,128)(2,1)S(1)} %get-tuple-element.81.refs_4_), channel_id=1, source_target_pairs={{0,1},{1,0},{2,3},{3,2},{4,5},{5,4},{6,7},{7,6},{8,9},{9,8},{10,11... | collective-permute-start | bytes 442376 | tf_op jit(solution)/shard_map/ppermute | solution.py:359
  28.9 12.9 %collective-permute-start.11 = (bf16[32,2048]{1,0:T(8,128)(2,1)S(1)}, bf16[32,2048]{1,0:T(8,128)(2,1)S(1)}, u32[]{:S(2)}, u32[]{:S(2)}) collective-permute-start(bf16[32,2048]{1,0:T(8,128)(2,1)S(1)} %get-tuple-element.65), channel_id=1, source_target_pairs={{0,8},{4,12},{8,0},{12,4},{1,9},{5,13},{9,1},{13,5},{2,10},{6,14},... | collective-permute-start | bytes 393224 | tf_op jit(solution)/shard_map/ppermute | solution.py:369
  31.5 10.4 %collective-permute-start.12 = (bf16[32,2048]{1,0:T(8,128)(2,1)S(1)}, bf16[32,2048]{1,0:T(8,128)(2,1)S(1)}, u32[]{:S(2)}, u32[]{:S(2)}) collective-permute-start(bf16[32,2048]{1,0:T(8,128)(2,1)S(1)} %get-tuple-element.66), channel_id=1, source_target_pairs={{0,12},{4,8},{8,4},{12,0},{1,13},{5,9},{9,5},{13,1},{2,14},{6,10},... | collective-permute-start | bytes 393224 | tf_op jit(solution)/shard_map/ppermute | solution.py:369
  32.8 9.8 %collective-permute-start.13 = (bf16[32,2048]{1,0:T(8,128)(2,1)S(1)}, bf16[32,2048]{1,0:T(8,128)(2,1)S(1)}, u32[]{:S(2)}, u32[]{:S(2)}) collective-permute-start(bf16[32,2048]{1,0:T(8,128)(2,1)S(1)} %get-tuple-element.67), channel_id=1, source_target_pairs={{0,4},{4,0},{8,12},{12,8},{1,5},{5,1},{9,13},{13,9},{2,6},{6,2},{1... | collective-permute-start | bytes 393224 | tf_op jit(solution)/shard_map/ppermute | solution.py:369
  33.1 11.5 %collective-permute-start.18 = (bf16[64,1152]{1,0:T(8,128)(2,1)S(1)}, bf16[64,1152]{1,0:T(8,128)(2,1)S(1)}, u32[]{:S(2)}, u32[]{:S(2)}) collective-permute-start(bf16[64,1152]{1,0:T(8,128)(2,1)S(1)} %get-tuple-element.81.refs_4_), channel_id=1, source_target_pairs={{0,3},{1,2},{2,1},{3,0},{4,7},{5,6},{6,5},{7,4},{8,11},{9,10},{10,... | collective-permute-start | bytes 442376 | tf_op jit(solution)/shard_map/ppermute | solution.py:359
  34.0 10.6 %collective-permute-start.17 = (bf16[64,1152]{1,0:T(8,128)(2,1)S(1)}, bf16[64,1152]{1,0:T(8,128)(2,1)S(1)}, u32[]{:S(2)}, u32[]{:S(2)}) collective-permute-start(bf16[64,1152]{1,0:T(8,128)(2,1)S(1)} %get-tuple-element.81.refs_4_), channel_id=1, source_target_pairs={{0,2},{1,3},{2,0},{3,1},{4,6},{5,7},{6,4},{7,5},{8,10},{9,11},{10,... | collective-permute-start | bytes 442376 | tf_op jit(solution)/shard_map/ppermute | solution.py:359
  34.8 7.8 %copy-start.1 = (bf16[128,2048]{1,0:T(8,128)(2,1)S(1)}, bf16[128,2048]{1,0:T(8,128)(2,1)}, u32[]{:S(2)}) copy-start(bf16[128,2048]{1,0:T(8,128)(2,1)} %dy_ref.1) | copy-start | bytes 1572868
  41.8 2.7 %collective-permute-start.16 = (bf16[256,512]{1,0:T(8,128)(2,1)S(1)}, bf16[256,512]{1,0:T(8,128)(2,1)S(1)}, u32[]{:S(2)}, u32[]{:S(2)}) collective-permute-start(bf16[256,512]{1,0:T(8,128)(2,1)S(1)} %pad_maximum_fusion), channel_id=1, source_target_pairs={{0,1},{1,0},{2,3},{3,2},{4,5},{5,4},{6,7},{7,6},{8,9},{9,8},{10,11... | collective-permute-start | bytes 786440 | tf_op jit(solution)/shard_map/ppermute | solution.py:359

commit v9 on v8

--- a/solution.py
+++ b/solution.py
@@ -62,10 +62,15 @@
     return jnp.where(index == 0, 0, step) if isinstance(index, jax.Array) else step * (index > 0)
 
 
-def choose(flag, first, second):
+def choose(flag, first, second, *small):
     rows, columns = first.shape
 
-    def kernel(flag_ref, first_ref, second_ref, one_ref, both_ref, sems):
+    def kernel(flag_ref, first_ref, second_ref, *refs):
+        given, (one_ref, both_ref), rest = refs[: len(small)], refs[len(small) : len(small) + 2], refs[len(small) + 2 :]
+        held, sems = rest[:-1], rest[-1]
+        extra = [pltpu.make_async_copy(g, h, sems.at[3 + i]) for i, (g, h) in enumerate(zip(given, held))]
+        for copy in extra:
+            copy.start()
         top = pltpu.make_async_copy(first_ref, both_ref.at[0:rows], sems.at[0])
         bottom = pltpu.make_async_copy(second_ref, both_ref.at[rows:], sems.at[1])
         top.start()
@@ -85,16 +90,19 @@
 
         top.wait()
         bottom.wait()
+        for copy in extra:
+            copy.wait()
 
     return call(
         kernel,
-        [shape((rows, columns)), shape((2 * rows, columns))],
+        [shape((rows, columns)), shape((2 * rows, columns)), *(shape(a.shape, a.dtype) for a in small)],
         flag,
         first,
         second,
+        *small,
         smem=1,
-        anywhere=(1, 2),
-        scratch=[pltpu.SemaphoreType.DMA((3,))],
+        anywhere=range(1, 3 + len(small)),
+        scratch=[pltpu.SemaphoreType.DMA((3 + len(small),))],
     )
 
 
@@ -371,13 +379,12 @@
     def after(values, *others):
         return lax.optimization_barrier((values, others))[0]
 
-    lead, both = choose(flag, w_gate[0], w_up[0])
+    lead, both, ids, probs = choose(flag, w_gate[0], w_up[0], expert_ids.T, gate_probs.T)
     down = after(w_down[0], lead)
     masks = range(CORES, dp_count, CORES)
     lead_got = {mask: to_dp(lead, mask) for mask in masks}
     near_pieces = [(both, down), (to_dp(both, 1), to_dp(down, 1))]
 
-    ids, probs = expert_ids.T, gate_probs.T
     send, select, table = slots(
         place, ids, probs, tokens, cotangent, expert_count, capacity, dp_count, even
     )

time: 46.4 us -> 46.4 us (level)
  local copies, waits for them, and re-layouts: 0.67 us -> 0.05 us
    ppermute x12, waiting for transfers between devices: 5.3 us -> 6.17 us  [to_dp(): return lax.ppermute(array, 'dp', [(i, i ^ mask) for i in range(dp_count)])]
    ppermute x6, waiting for transfers between devices: 11.5 us -> 10.8 us  [to_expert(): return lax.ppermute(array, 'expert', pairs)]
    unnamed x10 -> x6, local copies, waits for them, and re-layouts: 0.63 us -> 0.01 us
where the time goes in v9:
time: 46.4 us; the launch traced here: 46 us
  waiting for transfers between devices  18.4 us (40%)
  starting transfers between devices  17.4 us (37%)
  Pallas kernels  9.3 us (20%)
  between operations  0.76 us (2%)
    ppermute x6, waiting for transfers between devices, to_expert(): return lax.ppermute(array, 'expert', pairs)  10.8 us
    pallas_call x8, Pallas kernels, call(): pl.pallas_call(kernel, out_shape=out_shape, in_specs=specs, out_specs=jax...  9.3 us
    ppermute x6, starting transfers between devices, to_expert(): return lax.ppermute(array, 'expert', pairs)  8.53 us
    ppermute x12, starting transfers between devices, to_dp(): return lax.ppermute(array, 'dp', [(i, i ^ mask) for i in range(dp_count)])  6.77 us
    ppermute x12, waiting for transfers between devices, to_dp(): return lax.ppermute(array, 'dp', [(i, i ^ mask) for i in range(dp_count)])  6.17 us
    ppermute x1, starting transfers between devices, to_group(): return lax.ppermute(array, 'groups', [(0, 1), (1, 0)])  2.09 us
    ppermute x1, waiting for transfers between devices, to_group(): return lax.ppermute(array, 'groups', [(0, 1), (1, 0)])  1.43 us
  transfers between devices with their start and end apart: 19, of which 8 were waited for; matrix products, arithmetic and copies ran while one was open for 0% of the time, Pallas kernels for 14%

profile of v9, /device:TPU:0, one launch (start us, length us, event | category | flops | bytes accessed | tf_op | source)
XLA Modules:
  0.0 46.0 jit_solution(4530450166324758542)
XLA Ops:
  0.6 0.0 copy-start
  0.6 1.4 %shard_map.118 = (bf16[512,384]{1,0:T(8,128)(2,1)S(1)}, bf16[1024,384]{1,0:T(8,128)(2,1)S(1)}, s32[8,128]{1,0:T(8,128)S(1)}, f32[8,128]{1,0:T(8,128)S(1)}) custom-call(s32[1]{0:T(128)} %bitcast.2.flag_ref, bf16[512,384]{1,0:T(8,128)(2,1)} %bitcast.16, bf16[512,384]{1,0:T(8,128)(2,1)} %bitcast.17, s32[8,128]{1,0:T(8,128)} %bitcast.18, f32[8,128]{1,0:T(8,128)} %bitcast.19), custom_call_target="tpu_custom_call" | custom-call | flops 1 | bytes 1 | tf_op jit(solution)/shard_map/pallas_call | solution.py:49
  2.0 0.5 %collective-permute-start = (bf16[1024,384]{1,0:T(8,128)(2,1)S(1)}, bf16[1024,384]{1,0:T(8,128)(2,1)S(1)}, u32[]{:S(2)}, u32[]{:S(2)}) collective-permute-start(bf16[1024,384]{1,0:T(8,128)(2,1)S(1)} %get-tuple-element.59.refs_0_), channel_id=1, source_target_pairs={{0,1},{1,0},{2,3},{3,2},{4,5},{5,4},{6,7},{7,6},{8,9},{9,8},{10,11... | collective-permute-start | bytes 2359304 | tf_op jit(solution)/shard_map/ppermute | solution.py:367
  2.5 0.1 collective-permute-start.1
  2.6 2.9 %collective-permute-start.5 = (bf16[512,384]{1,0:T(8,128)(2,1)S(1)}, bf16[512,384]{1,0:T(8,128)(2,1)S(1)}, u32[]{:S(2)}, u32[]{:S(2)}) collective-permute-start(bf16[512,384]{1,0:T(8,128)(2,1)S(1)} %get-tuple-element.57), channel_id=1, source_target_pairs={{0,2},{1,3},{2,0},{3,1},{4,6},{5,7},{6,4},{7,5},{8,10},{9,11},{10,... | collective-permute-start | bytes 1179656 | tf_op jit(solution)/shard_map/ppermute | solution.py:367
  5.5 0.1 pad_add_fusion.place_ref
  5.6 0.0 copy-done
  5.6 0.0 copy-start.2
  5.6 1.8 %shard_map.119 = (bf16[32,2048]{1,0:T(8,128)(2,1)S(1)}, bf16[32,2048]{1,0:T(8,128)(2,1)S(1)}, bf16[32,2048]{1,0:T(8,128)(2,1)S(1)}, bf16[32,2048]{1,0:T(8,128)(2...) custom-call(s32[2]{0:T(128)S(1)} %pad_add_fusion.place_ref, s32[8,128]{1,0:T(8,128)S(1)} %get-tuple-element.49.ids_ref, ...), custom_call_target="tpu_custom_call" | custom-call | flops 1 | bytes 1 | tf_op jit(solution)/shard_map/pallas_call | solution.py:49
  7.5 0.0 collective-permute-done.1.refs_3_
  7.5 0.0 collective-permute-done.refs_2_
  7.5 2.7 %collective-permute-start.2 = (bf16[32,2048]{1,0:T(8,128)(2,1)S(1)}, bf16[32,2048]{1,0:T(8,128)(2,1)S(1)}, u32[]{:S(2)}, u32[]{:S(2)}) collective-permute-start(bf16[32,2048]{1,0:T(8,128)(2,1)S(1)} %get-tuple-element.61), channel_id=1, source_target_pairs={{0,8},{4,12},{8,0},{12,4},{1,9},{5,13},{9,1},{13,5},{2,10},{6,14},... | collective-permute-start | bytes 393224 | tf_op jit(solution)/shard_map/ppermute | solution.py:377
  10.1 1.3 %collective-permute-start.3 = (bf16[32,2048]{1,0:T(8,128)(2,1)S(1)}, bf16[32,2048]{1,0:T(8,128)(2,1)S(1)}, u32[]{:S(2)}, u32[]{:S(2)}) collective-permute-start(bf16[32,2048]{1,0:T(8,128)(2,1)S(1)} %get-tuple-element.62), channel_id=1, source_target_pairs={{0,12},{4,8},{8,4},{12,0},{1,13},{5,9},{9,5},{13,1},{2,14},{6,10},... | collective-permute-start | bytes 393224 | tf_op jit(solution)/shard_map/ppermute | solution.py:377
  11.5 0.2 collective-permute-start.4
  11.7 0.0 copy-done.2
  11.7 0.5 %collective-permute-start.7 = (bf16[384,512]{1,0:T(8,128)(2,1)S(1)}, bf16[384,512]{1,0:T(8,128)(2,1)S(1)}, u32[]{:S(2)}, u32[]{:S(2)}) collective-permute-start(bf16[384,512]{1,0:T(8,128)(2,1)S(1)} %bitcast.13), channel_id=1, source_target_pairs={{0,2},{1,3},{2,0},{3,1},{4,6},{5,7},{6,4},{7,5},{8,10},{9,11},{10,... | collective-permute-start | bytes 1179656 | tf_op jit(solution)/shard_map/ppermute | solution.py:367
  12.3 3.2 %collective-permute-done.5.refs_4_ = bf16[512,384]{1,0:T(8,128)(2,1)S(1)} collective-permute-done((bf16[512,384]{1,0:T(8,128)(2,1)S(1)}, bf16[512,384]{1,0:T(8,128)(2,1)S(1)}, u32[]{:S(2)}, u32[]{:S(2)}) %collective-permute-start.5) | collective-permute-done | bytes 393248 | tf_op jit(solution)/shard_map/ppermute | solution.py:367
  15.5 2.1 %collective-permute-start.9 = (bf16[512,384]{1,0:T(8,128)(2,1)S(1)}, bf16[512,384]{1,0:T(8,128)(2,1)S(1)}, u32[]{:S(2)}, u32[]{:S(2)}) collective-permute-start(bf16[512,384]{1,0:T(8,128)(2,1)S(1)} %collective-permute-done.5.refs_4_), channel_id=1, source_target_pairs={{0,16},{16,0},{1,17},{17,1},{2,18},{18,2},{3,19},{19,3},{4,20},{20... | collective-permute-start | bytes 1179656 | tf_op jit(solution)/shard_map/ppermute | solution.py:370
  17.5 2.9 %collective-permute-done.2.refs_1_ = bf16[32,2048]{1,0:T(8,128)(2,1)S(1)} collective-permute-done((bf16[32,2048]{1,0:T(8,128)(2,1)S(1)}, bf16[32,2048]{1,0:T(8,128)(2,1)S(1)}, u32[]{:S(2)}, u32[]{:S(2)}) %collective-permute-start.2) | collective-permute-done | bytes 131104 | tf_op jit(solution)/shard_map/ppermute | solution.py:377
  20.4 0.0 collective-permute-start.6
  20.4 0.0 collective-permute-done.3.refs_2_
  20.4 0.2 collective-permute-done.4.refs_3_
  20.6 0.1 shard_map.120
  20.7 0.9 %collective-permute-start.14 = (bf16[128,1024]{1,0:T(8,128)(2,1)S(1)}, bf16[128,1024]{1,0:T(8,128)(2,1)S(1)}, u32[]{:S(2)}, u32[]{:S(2)}) collective-permute-start(bf16[128,1024]{1,0:T(8,128)(2,1)S(1)} %get-tuple-element.74), channel_id=1, source_target_pairs={{0,2},{1,3},{2,0},{3,1},{4,6},{5,7},{6,4},{7,5},{8,10},{9,11},{10,... | collective-permute-start | bytes 786440 | tf_op jit(solution)/shard_map/ppermute | solution.py:367
  21.7 1.7 %collective-permute-done.7.refs_1_.refs_6_ = bf16[384,512]{1,0:T(8,128)(2,1)S(1)} collective-permute-done((bf16[384,512]{1,0:T(8,128)(2,1)S(1)}, bf16[384,512]{1,0:T(8,128)(2,1)S(1)}, u32[]{:S(2)}, u32[]{:S(2)}) %collective-permute-start.7) | collective-permute-done | bytes 393248 | tf_op jit(solution)/shard_map/ppermute | solution.py:367
  23.3 0.0 collective-permute-start.8
  23.3 0.7 %shard_map.121.sums_ref = f32[64,1536]{1,0:T(8,128)S(1)} custom-call(bf16[128,2048]{1,0:T(8,128)(2,1)S(1)} %get-tuple-element.64.rows_ref, bf16[1024,384]{1,0:T(8,128)(2,1)S(1)} %get-tuple-element.59.refs_0_, bf16[384,512]{1,0:T(8,128)(2,1)S(1)} %bitcast.14, bf16[1024,384]{1,0:T(8,128)(2,1)S(1)} %collective-permute-done.refs_2_, ...), custom_call_target="tpu_custom_call" | custom-call | flops 8999999488 | bytes 1 | tf_op jit(solution)/shard_map/pallas_call | solution.py:49
  24.0 1.4 %collective-permute-done.9.refs_5_ = bf16[512,384]{1,0:T(8,128)(2,1)S(1)} collective-permute-done((bf16[512,384]{1,0:T(8,128)(2,1)S(1)}, bf16[512,384]{1,0:T(8,128)(2,1)S(1)}, u32[]{:S(2)}, u32[]{:S(2)}) %collective-permute-start.9) | collective-permute-done | bytes 393248 | tf_op jit(solution)/shard_map/ppermute | solution.py:370
  25.5 0.0 collective-permute-start.10
  25.5 0.0 collective-permute-done.6.refs_0_.refs_7_
  25.5 0.0 collective-permute-done.8.refs_2_.refs_9_
  25.5 0.4 shard_map.122.back_ref
  25.9 1.3 %collective-permute-done.10.refs_8_ = bf16[512,384]{1,0:T(8,128)(2,1)S(1)} collective-permute-done((bf16[512,384]{1,0:T(8,128)(2,1)S(1)}, bf16[512,384]{1,0:T(8,128)(2,1)S(1)}, u32[]{:S(2)}, u32[]{:S(2)}) %collective-permute-start.10) | collective-permute-done | bytes 393248 | tf_op jit(solution)/shard_map/ppermute | solution.py:367
  27.2 1.6 %shard_map.123 = (bf16[32,2048]{1,0:T(8,128)(2,1)S(1)}, bf16[32,2048]{1,0:T(8,128)(2,1)S(1)}, bf16[32,2048]{1,0:T(8,128)(2,1)S(1)}, bf16[32,2048]{1,0:T(8,128)(2,1)S(1)}, bf16[64,1152]{1,0:T(8,128)(2,1)S(1)}) custom-call(s32[1]{0:T(128)} %bitcast.2.flag_ref, bf16[128,2048]{1,0:T(8,128)(2,1)S(1)} %get-tuple-element.64.rows_ref, ...), custom_call_target="tpu_custom_call" | custom-call | flops 1 | bytes 1 | tf_op jit(solution)/shard_map/pallas_call | solution.py:49
  28.8 0.2 collective-permute-start.15
  29.0 2.5 %collective-permute-start.11 = (bf16[32,2048]{1,0:T(8,128)(2,1)S(1)}, bf16[32,2048]{1,0:T(8,128)(2,1)S(1)}, u32[]{:S(2)}, u32[]{:S(2)}) collective-permute-start(bf16[32,2048]{1,0:T(8,128)(2,1)S(1)} %get-tuple-element.69), channel_id=1, source_target_pairs={{0,8},{4,12},{8,0},{12,4},{1,9},{5,13},{9,1},{13,5},{2,10},{6,14},... | collective-permute-start | bytes 393224 | tf_op jit(solution)/shard_map/ppermute | solution.py:377
  31.5 1.3 %collective-permute-start.12 = (bf16[32,2048]{1,0:T(8,128)(2,1)S(1)}, bf16[32,2048]{1,0:T(8,128)(2,1)S(1)}, u32[]{:S(2)}, u32[]{:S(2)}) collective-permute-start(bf16[32,2048]{1,0:T(8,128)(2,1)S(1)} %get-tuple-element.70), channel_id=1, source_target_pairs={{0,12},{4,8},{8,4},{12,0},{1,13},{5,9},{9,5},{13,1},{2,14},{6,10},... | collective-permute-start | bytes 393224 | tf_op jit(solution)/shard_map/ppermute | solution.py:377
  32.9 0.4 collective-permute-start.13
  33.3 0.0 collective-permute-done.14.refs_1_
  33.3 0.7 %collective-permute-start.18 = (bf16[64,1152]{1,0:T(8,128)(2,1)S(1)}, bf16[64,1152]{1,0:T(8,128)(2,1)S(1)}, u32[]{:S(2)}, u32[]{:S(2)}) collective-permute-start(bf16[64,1152]{1,0:T(8,128)(2,1)S(1)} %get-tuple-element.85.refs_4_), channel_id=1, source_target_pairs={{0,3},{1,2},{2,1},{3,0},{4,7},{5,6},{6,5},{7,4},{8,11},{9,10},{10,... | collective-permute-start | bytes 442376 | tf_op jit(solution)/shard_map/ppermute | solution.py:367
  34.0 0.0 collective-permute-done.15.refs_6_
  34.0 0.8 %collective-permute-start.17 = (bf16[64,1152]{1,0:T(8,128)(2,1)S(1)}, bf16[64,1152]{1,0:T(8,128)(2,1)S(1)}, u32[]{:S(2)}, u32[]{:S(2)}) collective-permute-start(bf16[64,1152]{1,0:T(8,128)(2,1)S(1)} %get-tuple-element.85.refs_4_), channel_id=1, source_target_pairs={{0,2},{1,3},{2,0},{3,1},{4,6},{5,7},{6,4},{7,5},{8,10},{9,11},{10,... | collective-permute-start | bytes 442376 | tf_op jit(solution)/shard_map/ppermute | solution.py:367
  34.9 0.0 copy-start.1
  34.9 7.0 %collective-permute-done.11.refs_1_ = bf16[32,2048]{1,0:T(8,128)(2,1)S(1)} collective-permute-done((bf16[32,2048]{1,0:T(8,128)(2,1)S(1)}, bf16[32,2048]{1,0:T(8,128)(2,1)S(1)}, u32[]{:S(2)}, u32[]{:S(2)}) %collective-permute-start.11) | collective-permute-done | bytes 131104 | tf_op jit(solution)/shard_map/ppermute | solution.py:377
  41.9 0.0 collective-permute-start.16
  41.9 0.0 collective-permute-done.12.refs_2_
  41.9 0.8 %collective-permute-done.13.refs_3_ = bf16[32,2048]{1,0:T(8,128)(2,1)S(1)} collective-permute-done((bf16[32,2048]{1,0:T(8,128)(2,1)S(1)}, bf16[32,2048]{1,0:T(8,128)(2,1)S(1)}, u32[]{:S(2)}, u32[]{:S(2)}) %collective-permute-start.13) | collective-permute-done | bytes 131104 | tf_op jit(solution)/shard_map/ppermute | solution.py:377
  42.7 0.0 copy-done.1
  42.7 2.0 %shard_map.124 = (bf16[128,2048]{1,0:T(8,128)(2,1)}, bf16[128,2048]{1,0:T(8,128)(2,1)}, f32[8,128]{1,0:T(8,128)}) custom-call(s32[2]{0:T(128)S(1)} %pad_add_fusion.place_ref, s32[8,128]{1,0:T(8,128)S(1)} %get-tuple-element.49.ids_ref, bf16[64,128]{1,0:T(8,128)(2,1)S(1)} %get-tuple-element.51.select_ref, bf16[128,128]{1,0:T(8,128)(2,1)S(1)} %get-tuple-element.52.table_ref, ...), custom_call_target="tpu_custom_call" | custom-call | flops 8589934592 | bytes 1 | tf_op jit(solution)/shard_map/pallas_call | solution.py:49
  44.6 0.0 collective-permute-done.16
  44.6 0.0 collective-permute-done.18.refs_7_
  44.7 0.0 collective-permute-done.17.refs_5_
  44.7 1.4 %shard_map.125 = (bf16[512,384]{1,0:T(8,128)(2,1)}, bf16[512,384]{1,0:T(8,128)(2,1)}, bf16[384,512]{1,0:T(8,128)(2,1)}) custom-call(bf16[128,1024]{1,0:T(8,128)(2,1)S(1)} %get-tuple-element.81.refs_0_, bf16[128,1024]{1,0:T(8,128)(2,1)S(1)} %collective-permute-done.14.refs_1_, bf16[128,512]{1,0:T(8,128)(2,1)S(1)} %get-tuple-element.83.refs_2_, ...), custom_call_target="tpu_custom_call" | custom-call | flops 1 | bytes 1 | tf_op jit(solution)/shard_map/pallas_call | solution.py:49
  (4 shorter events, 0.1 us)
Async XLA Ops:
  0.6 5.0 %copy-start = (bf16[128,2048]{1,0:T(8,128)(2,1)S(1)}, bf16[128,2048]{1,0:T(8,128)(2,1)}, u32[]{:S(2)}) copy-start(bf16[128,2048]{1,0:T(8,128)(2,1)} %x_ref.1) | copy-start | bytes 1572868
  2.0 5.4 %collective-permute-start = (bf16[1024,384]{1,0:T(8,128)(2,1)S(1)}, bf16[1024,384]{1,0:T(8,128)(2,1)S(1)}, u32[]{:S(2)}, u32[]{:S(2)}) collective-permute-start(bf16[1024,384]{1,0:T(8,128)(2,1)S(1)} %get-tuple-element.59.refs_0_), channel_id=1, source_target_pairs={{0,1},{1,0},{2,3},{3,2},{4,5},{5,4},{6,7},{7,6},{8,9},{9,8},{10,11... | collective-permute-start | bytes 2359304 | tf_op jit(solution)/shard_map/ppermute | solution.py:367
  2.5 4.9 %collective-permute-start.1 = (bf16[384,512]{1,0:T(8,128)(2,1)}, bf16[384,512]{1,0:T(8,128)(2,1)S(1)}, u32[]{:S(2)}, u32[]{:S(2)}) collective-permute-start(bf16[384,512]{1,0:T(8,128)(2,1)} %bitcast.12), channel_id=1, source_target_pairs={{0,1},{1,0},{2,3},{3,2},{4,5},{5,4},{6,7},{7,6},{8,9},{9,8},{10,11... | collective-permute-start | bytes 1179656 | tf_op jit(solution)/shard_map/ppermute | solution.py:367
  2.6 12.8 %collective-permute-start.5 = (bf16[512,384]{1,0:T(8,128)(2,1)S(1)}, bf16[512,384]{1,0:T(8,128)(2,1)S(1)}, u32[]{:S(2)}, u32[]{:S(2)}) collective-permute-start(bf16[512,384]{1,0:T(8,128)(2,1)S(1)} %get-tuple-element.57), channel_id=1, source_target_pairs={{0,2},{1,3},{2,0},{3,1},{4,6},{5,7},{6,4},{7,5},{8,10},{9,11},{10,... | collective-permute-start | bytes 1179656 | tf_op jit(solution)/shard_map/ppermute | solution.py:367
  5.6 6.1 %copy-start.2 = (bf16[1,384,512]{2,1,0:T(8,128)(2,1)S(1)}, bf16[1,384,512]{2,1,0:T(8,128)(2,1)}, u32[]{:S(2)}) copy-start(bf16[1,384,512]{2,1,0:T(8,128)(2,1)} %param.13) | copy-start | bytes 1179652
  7.5 13.0 %collective-permute-start.2 = (bf16[32,2048]{1,0:T(8,128)(2,1)S(1)}, bf16[32,2048]{1,0:T(8,128)(2,1)S(1)}, u32[]{:S(2)}, u32[]{:S(2)}) collective-permute-start(bf16[32,2048]{1,0:T(8,128)(2,1)S(1)} %get-tuple-element.61), channel_id=1, source_target_pairs={{0,8},{4,12},{8,0},{12,4},{1,9},{5,13},{9,1},{13,5},{2,10},{6,14},... | collective-permute-start | bytes 393224 | tf_op jit(solution)/shard_map/ppermute | solution.py:377
  10.1 10.3 %collective-permute-start.3 = (bf16[32,2048]{1,0:T(8,128)(2,1)S(1)}, bf16[32,2048]{1,0:T(8,128)(2,1)S(1)}, u32[]{:S(2)}, u32[]{:S(2)}) collective-permute-start(bf16[32,2048]{1,0:T(8,128)(2,1)S(1)} %get-tuple-element.62), channel_id=1, source_target_pairs={{0,12},{4,8},{8,4},{12,0},{1,13},{5,9},{9,5},{13,1},{2,14},{6,10},... | collective-permute-start | bytes 393224 | tf_op jit(solution)/shard_map/ppermute | solution.py:377
  11.5 9.2 %collective-permute-start.4 = (bf16[32,2048]{1,0:T(8,128)(2,1)S(1)}, bf16[32,2048]{1,0:T(8,128)(2,1)S(1)}, u32[]{:S(2)}, u32[]{:S(2)}) collective-permute-start(bf16[32,2048]{1,0:T(8,128)(2,1)S(1)} %get-tuple-element.63), channel_id=1, source_target_pairs={{0,4},{4,0},{8,12},{12,8},{1,5},{5,1},{9,13},{13,9},{2,6},{6,2},{1... | collective-permute-start | bytes 393224 | tf_op jit(solution)/shard_map/ppermute | solution.py:377
  11.7 11.6 %collective-permute-start.7 = (bf16[384,512]{1,0:T(8,128)(2,1)S(1)}, bf16[384,512]{1,0:T(8,128)(2,1)S(1)}, u32[]{:S(2)}, u32[]{:S(2)}) collective-permute-start(bf16[384,512]{1,0:T(8,128)(2,1)S(1)} %bitcast.13), channel_id=1, source_target_pairs={{0,2},{1,3},{2,0},{3,1},{4,6},{5,7},{6,4},{7,5},{8,10},{9,11},{10,... | collective-permute-start | bytes 1179656 | tf_op jit(solution)/shard_map/ppermute | solution.py:367
  15.5 10.0 %collective-permute-start.9 = (bf16[512,384]{1,0:T(8,128)(2,1)S(1)}, bf16[512,384]{1,0:T(8,128)(2,1)S(1)}, u32[]{:S(2)}, u32[]{:S(2)}) collective-permute-start(bf16[512,384]{1,0:T(8,128)(2,1)S(1)} %collective-permute-done.5.refs_4_), channel_id=1, source_target_pairs={{0,16},{16,0},{1,17},{17,1},{2,18},{18,2},{3,19},{19,3},{4,20},{20... | collective-permute-start | bytes 1179656 | tf_op jit(solution)/shard_map/ppermute | solution.py:370
  20.4 5.0 %collective-permute-start.6 = (bf16[512,384]{1,0:T(8,128)(2,1)S(1)}, bf16[512,384]{1,0:T(8,128)(2,1)S(1)}, u32[]{:S(2)}, u32[]{:S(2)}) collective-permute-start(bf16[512,384]{1,0:T(8,128)(2,1)S(1)} %collective-permute-done.5.refs_4_), channel_id=1, source_target_pairs={{0,1},{1,0},{2,3},{3,2},{4,5},{5,4},{6,7},{7,6},{8,9},{9,8},{10,11... | collective-permute-start | bytes 1179656 | tf_op jit(solution)/shard_map/ppermute | solution.py:367
  20.7 12.6 %collective-permute-start.14 = (bf16[128,1024]{1,0:T(8,128)(2,1)S(1)}, bf16[128,1024]{1,0:T(8,128)(2,1)S(1)}, u32[]{:S(2)}, u32[]{:S(2)}) collective-permute-start(bf16[128,1024]{1,0:T(8,128)(2,1)S(1)} %get-tuple-element.74), channel_id=1, source_target_pairs={{0,2},{1,3},{2,0},{3,1},{4,6},{5,7},{6,4},{7,5},{8,10},{9,11},{10,... | collective-permute-start | bytes 786440 | tf_op jit(solution)/shard_map/ppermute | solution.py:367
  23.3 2.1 %collective-permute-start.8 = (bf16[384,512]{1,0:T(8,128)(2,1)S(1)}, bf16[384,512]{1,0:T(8,128)(2,1)S(1)}, u32[]{:S(2)}, u32[]{:S(2)}) collective-permute-start(bf16[384,512]{1,0:T(8,128)(2,1)S(1)} %collective-permute-done.7.refs_1_.refs_6_), channel_id=1, source_target_pairs={{0,1},{1,0},{2,3},{3,2},{4,5},{5,4},{6,7},{7,6},{8,9},{9,8},{10,11... | collective-permute-start | bytes 1179656 | tf_op jit(solution)/shard_map/ppermute | solution.py:367
  25.5 1.7 %collective-permute-start.10 = (bf16[512,384]{1,0:T(8,128)(2,1)S(1)}, bf16[512,384]{1,0:T(8,128)(2,1)S(1)}, u32[]{:S(2)}, u32[]{:S(2)}) collective-permute-start(bf16[512,384]{1,0:T(8,128)(2,1)S(1)} %collective-permute-done.9.refs_5_), channel_id=1, source_target_pairs={{0,1},{1,0},{2,3},{3,2},{4,5},{5,4},{6,7},{7,6},{8,9},{9,8},{10,11... | collective-permute-start | bytes 1179656 | tf_op jit(solution)/shard_map/ppermute | solution.py:367
  28.8 5.2 %collective-permute-start.15 = (bf16[64,1152]{1,0:T(8,128)(2,1)S(1)}, bf16[64,1152]{1,0:T(8,128)(2,1)S(1)}, u32[]{:S(2)}, u32[]{:S(2)}) collective-permute-start(bf16[64,1152]{1,0:T(8,128)(2,1)S(1)} %get-tuple-element.85.refs_4_), channel_id=1, source_target_pairs={{0,1},{1,0},{2,3},{3,2},{4,5},{5,4},{6,7},{7,6},{8,9},{9,8},{10,11... | collective-permute-start | bytes 442376 | tf_op jit(solution)/shard_map/ppermute | solution.py:367
  29.0 12.9 %collective-permute-start.11 = (bf16[32,2048]{1,0:T(8,128)(2,1)S(1)}, bf16[32,2048]{1,0:T(8,128)(2,1)S(1)}, u32[]{:S(2)}, u32[]{:S(2)}) collective-permute-start(bf16[32,2048]{1,0:T(8,128)(2,1)S(1)} %get-tuple-element.69), channel_id=1, source_target_pairs={{0,8},{4,12},{8,0},{12,4},{1,9},{5,13},{9,1},{13,5},{2,10},{6,14},... | collective-permute-start | bytes 393224 | tf_op jit(solution)/shard_map/ppermute | solution.py:377
  31.5 10.4 %collective-permute-start.12 = (bf16[32,2048]{1,0:T(8,128)(2,1)S(1)}, bf16[32,2048]{1,0:T(8,128)(2,1)S(1)}, u32[]{:S(2)}, u32[]{:S(2)}) collective-permute-start(bf16[32,2048]{1,0:T(8,128)(2,1)S(1)} %get-tuple-element.70), channel_id=1, source_target_pairs={{0,12},{4,8},{8,4},{12,0},{1,13},{5,9},{9,5},{13,1},{2,14},{6,10},... | collective-permute-start | bytes 393224 | tf_op jit(solution)/shard_map/ppermute | solution.py:377
  32.9 9.8 %collective-permute-start.13 = (bf16[32,2048]{1,0:T(8,128)(2,1)S(1)}, bf16[32,2048]{1,0:T(8,128)(2,1)S(1)}, u32[]{:S(2)}, u32[]{:S(2)}) collective-permute-start(bf16[32,2048]{1,0:T(8,128)(2,1)S(1)} %get-tuple-element.71), channel_id=1, source_target_pairs={{0,4},{4,0},{8,12},{12,8},{1,5},{5,1},{9,13},{13,9},{2,6},{6,2},{1... | collective-permute-start | bytes 393224 | tf_op jit(solution)/shard_map/ppermute | solution.py:377
  33.3 11.3 %collective-permute-start.18 = (bf16[64,1152]{1,0:T(8,128)(2,1)S(1)}, bf16[64,1152]{1,0:T(8,128)(2,1)S(1)}, u32[]{:S(2)}, u32[]{:S(2)}) collective-permute-start(bf16[64,1152]{1,0:T(8,128)(2,1)S(1)} %get-tuple-element.85.refs_4_), channel_id=1, source_target_pairs={{0,3},{1,2},{2,1},{3,0},{4,7},{5,6},{6,5},{7,4},{8,11},{9,10},{10,... | collective-permute-start | bytes 442376 | tf_op jit(solution)/shard_map/ppermute | solution.py:367
  34.0 10.6 %collective-permute-start.17 = (bf16[64,1152]{1,0:T(8,128)(2,1)S(1)}, bf16[64,1152]{1,0:T(8,128)(2,1)S(1)}, u32[]{:S(2)}, u32[]{:S(2)}) collective-permute-start(bf16[64,1152]{1,0:T(8,128)(2,1)S(1)} %get-tuple-element.85.refs_4_), channel_id=1, source_target_pairs={{0,2},{1,3},{2,0},{3,1},{4,6},{5,7},{6,4},{7,5},{8,10},{9,11},{10,... | collective-permute-start | bytes 442376 | tf_op jit(solution)/shard_map/ppermute | solution.py:367
  34.9 7.8 %copy-start.1 = (bf16[128,2048]{1,0:T(8,128)(2,1)S(1)}, bf16[128,2048]{1,0:T(8,128)(2,1)}, u32[]{:S(2)}) copy-start(bf16[128,2048]{1,0:T(8,128)(2,1)} %dy_ref.1) | copy-start | bytes 1572868
  41.9 2.7 %collective-permute-start.16 = (bf16[256,512]{1,0:T(8,128)(2,1)S(1)}, bf16[256,512]{1,0:T(8,128)(2,1)S(1)}, u32[]{:S(2)}, u32[]{:S(2)}) collective-permute-start(bf16[256,512]{1,0:T(8,128)(2,1)S(1)} %pad_maximum_fusion), channel_id=1, source_target_pairs={{0,1},{1,0},{2,3},{3,2},{4,5},{5,4},{6,7},{7,6},{8,9},{9,8},{10,11... | collective-permute-start | bytes 786440 | tf_op jit(solution)/shard_map/ppermute | solution.py:367

commit v10 on v8

--- a/solution.py
+++ b/solution.py
@@ -12,7 +12,7 @@
 VMEM_LIMIT = 16 << 20
 FIRST_WEIGHT = 9 * 10**9
 COLLECT_WEIGHT = 1 << 33
-BACK_WEIGHT = 1 << 33
+BACK_WEIGHT = 10**9
 ARRANGE_WEIGHT = 3500 * 10**6
 
 

time: 46.4 us -> 46.6 us (level)
  starting transfers between devices: 17 us -> 17.7 us
  waiting for transfers between devices: 18.2 us -> 17.6 us
    ppermute x12, starting transfers between devices: 6.55 us -> 7.22 us  [to_dp(): return lax.ppermute(array, 'dp', [(i, i ^ mask) for i in range(dp_count)])]
    ppermute x6, waiting for transfers between devices: 11.5 us -> 10.8 us  [to_expert(): return lax.ppermute(array, 'expert', pairs)]
where the time goes in v10:
time: 46.6 us; the launch traced here: 46.1 us
  starting transfers between devices  17.7 us (38%)
  waiting for transfers between devices  17.6 us (38%)
  Pallas kernels  9.27 us (20%)
  between operations  0.76 us (2%)
  local copies, waits for them, and re-layouts  0.67 us (1%)
    ppermute x6, waiting for transfers between devices, to_expert(): return lax.ppermute(array, 'expert', pairs)  10.8 us
    pallas_call x8, Pallas kernels, call(): pl.pallas_call(kernel, out_shape=out_shape, in_specs=specs, out_specs=jax...  9.27 us
    ppermute x6, starting transfers between devices, to_expert(): return lax.ppermute(array, 'expert', pairs)  8.4 us
    ppermute x12, starting transfers between devices, to_dp(): return lax.ppermute(array, 'dp', [(i, i ^ mask) for i in range(dp_count)])  7.22 us
    ppermute x12, waiting for transfers between devices, to_dp(): return lax.ppermute(array, 'dp', [(i, i ^ mask) for i in range(dp_count)])  5.35 us
    ppermute x1, starting transfers between devices, to_group(): return lax.ppermute(array, 'groups', [(0, 1), (1, 0)])  2.09 us
    ppermute x1, waiting for transfers between devices, to_group(): return lax.ppermute(array, 'groups', [(0, 1), (1, 0)])  1.44 us
  transfers between devices with their start and end apart: 19, of which 8 were waited for; matrix products, arithmetic and copies ran while one was open for 0% of the time, Pallas kernels for 14%

profile of v10, /device:TPU:0, one launch (start us, length us, event | category | flops | bytes accessed | tf_op | source)
XLA Modules:
  0.0 46.1 jit_solution(2799458163766285813)
XLA Ops:
  0.6 0.0 copy-start
  0.6 1.3 %shard_map.119 = (bf16[512,384]{1,0:T(8,128)(2,1)S(1)}, bf16[1024,384]{1,0:T(8,128)(2,1)S(1)}) custom-call(s32[1]{0:T(128)} %bitcast.4.flag_ref, bf16[512,384]{1,0:T(8,128)(2,1)} %bitcast.19, bf16[512,384]{1,0:T(8,128)(2,1)} %bitcast.20), custom_call_target="tpu_custom_call" | custom-call | flops 1 | bytes 1 | tf_op jit(solution)/shard_map/pallas_call | solution.py:49
  2.0 0.5 %collective-permute-start = (bf16[1024,384]{1,0:T(8,128)(2,1)S(1)}, bf16[1024,384]{1,0:T(8,128)(2,1)S(1)}, u32[]{:S(2)}, u32[]{:S(2)}) collective-permute-start(bf16[1024,384]{1,0:T(8,128)(2,1)S(1)} %get-tuple-element.55.refs_0_), channel_id=1, source_target_pairs={{0,1},{1,0},{2,3},{3,2},{4,5},{5,4},{6,7},{7,6},{8,9},{9,8},{10,11... | collective-permute-start | bytes 2359304 | tf_op jit(solution)/shard_map/ppermute | solution.py:359
  2.5 0.1 collective-permute-start.1
  2.6 2.9 %collective-permute-start.5 = (bf16[512,384]{1,0:T(8,128)(2,1)S(1)}, bf16[512,384]{1,0:T(8,128)(2,1)S(1)}, u32[]{:S(2)}, u32[]{:S(2)}) collective-permute-start(bf16[512,384]{1,0:T(8,128)(2,1)S(1)} %get-tuple-element.53), channel_id=1, source_target_pairs={{0,2},{1,3},{2,0},{3,1},{4,6},{5,7},{6,4},{7,5},{8,10},{9,11},{10,... | collective-permute-start | bytes 1179656 | tf_op jit(solution)/shard_map/ppermute | solution.py:359
  5.5 0.0 copy-start.4
  5.5 0.0 copy-start.3
  5.5 0.1 pad_add_fusion.place_ref
  5.6 0.0 copy-done
  5.6 0.6 %copy-done.4 = s32[128,8]{0,1:T(8,128)S(1)} copy-done((s32[128,8]{0,1:T(8,128)S(1)}, s32[128,8]{0,1:T(8,128)}, u32[]{:S(2)}) %copy-start.4) | copy-done | bytes 4120
  6.2 0.0 copy-done.3
  6.2 0.0 copy-start.2
  6.2 1.8 %shard_map.118 = (bf16[32,2048]{1,0:T(8,128)(2,1)S(1)}, bf16[32,2048]{1,0:T(8,128)(2,1)S(1)}, bf16[32,2048]{1,0:T(8,128)(2,1)S(1)}, bf16[32,2048]{1,0:T(8,128)(2...) custom-call(s32[2]{0:T(128)S(1)} %pad_add_fusion.place_ref, s32[8,128]{1,0:T(8,128)S(1)} %bitcast.17, ...), custom_call_target="tpu_custom_call" | custom-call | flops 1 | bytes 1 | tf_op jit(solution)/shard_map/pallas_call | solution.py:49
  8.0 0.0 collective-permute-done.1.refs_3_
  8.0 0.0 collective-permute-done.refs_2_
  8.1 2.7 %collective-permute-start.2 = (bf16[32,2048]{1,0:T(8,128)(2,1)S(1)}, bf16[32,2048]{1,0:T(8,128)(2,1)S(1)}, u32[]{:S(2)}, u32[]{:S(2)}) collective-permute-start(bf16[32,2048]{1,0:T(8,128)(2,1)S(1)} %get-tuple-element.57), channel_id=1, source_target_pairs={{0,8},{4,12},{8,0},{12,4},{1,9},{5,13},{9,1},{13,5},{2,10},{6,14},... | collective-permute-start | bytes 393224 | tf_op jit(solution)/shard_map/ppermute | solution.py:369
  10.7 1.3 %collective-permute-start.3 = (bf16[32,2048]{1,0:T(8,128)(2,1)S(1)}, bf16[32,2048]{1,0:T(8,128)(2,1)S(1)}, u32[]{:S(2)}, u32[]{:S(2)}) collective-permute-start(bf16[32,2048]{1,0:T(8,128)(2,1)S(1)} %get-tuple-element.58), channel_id=1, source_target_pairs={{0,12},{4,8},{8,4},{12,0},{1,13},{5,9},{9,5},{13,1},{2,14},{6,10},... | collective-permute-start | bytes 393224 | tf_op jit(solution)/shard_map/ppermute | solution.py:369
  12.1 0.2 collective-permute-start.4
  12.3 0.0 copy-done.2
  12.3 0.5 %collective-permute-start.7 = (bf16[384,512]{1,0:T(8,128)(2,1)S(1)}, bf16[384,512]{1,0:T(8,128)(2,1)S(1)}, u32[]{:S(2)}, u32[]{:S(2)}) collective-permute-start(bf16[384,512]{1,0:T(8,128)(2,1)S(1)} %bitcast.13), channel_id=1, source_target_pairs={{0,2},{1,3},{2,0},{3,1},{4,6},{5,7},{6,4},{7,5},{8,10},{9,11},{10,... | collective-permute-start | bytes 1179656 | tf_op jit(solution)/shard_map/ppermute | solution.py:359
  12.8 2.6 %collective-permute-done.5.refs_4_ = bf16[512,384]{1,0:T(8,128)(2,1)S(1)} collective-permute-done((bf16[512,384]{1,0:T(8,128)(2,1)S(1)}, bf16[512,384]{1,0:T(8,128)(2,1)S(1)}, u32[]{:S(2)}, u32[]{:S(2)}) %collective-permute-start.5) | collective-permute-done | bytes 393248 | tf_op jit(solution)/shard_map/ppermute | solution.py:359
  15.4 2.1 %collective-permute-start.9 = (bf16[512,384]{1,0:T(8,128)(2,1)S(1)}, bf16[512,384]{1,0:T(8,128)(2,1)S(1)}, u32[]{:S(2)}, u32[]{:S(2)}) collective-permute-start(bf16[512,384]{1,0:T(8,128)(2,1)S(1)} %collective-permute-done.5.refs_4_), channel_id=1, source_target_pairs={{0,16},{16,0},{1,17},{17,1},{2,18},{18,2},{3,19},{19,3},{4,20},{20... | collective-permute-start | bytes 1179656 | tf_op jit(solution)/shard_map/ppermute | solution.py:362
  17.5 3.5 %collective-permute-done.2.refs_1_ = bf16[32,2048]{1,0:T(8,128)(2,1)S(1)} collective-permute-done((bf16[32,2048]{1,0:T(8,128)(2,1)S(1)}, bf16[32,2048]{1,0:T(8,128)(2,1)S(1)}, u32[]{:S(2)}, u32[]{:S(2)}) %collective-permute-start.2) | collective-permute-done | bytes 131104 | tf_op jit(solution)/shard_map/ppermute | solution.py:369
  21.0 0.0 collective-permute-start.6
  21.0 0.0 collective-permute-done.3.refs_2_
  21.0 0.2 collective-permute-done.4.refs_3_
  21.2 0.1 shard_map.120
  21.3 2.0 %collective-permute-done.7.refs_1_.refs_6_ = bf16[384,512]{1,0:T(8,128)(2,1)S(1)} collective-permute-done((bf16[384,512]{1,0:T(8,128)(2,1)S(1)}, bf16[384,512]{1,0:T(8,128)(2,1)S(1)}, u32[]{:S(2)}, u32[]{:S(2)}) %collective-permute-start.7) | collective-permute-done | bytes 393248 | tf_op jit(solution)/shard_map/ppermute | solution.py:359
  23.3 0.0 collective-permute-start.8
  23.3 0.7 %shard_map.121.sums_ref = f32[64,1536]{1,0:T(8,128)S(1)} custom-call(bf16[128,2048]{1,0:T(8,128)(2,1)S(1)} %get-tuple-element.60.rows_ref, bf16[1024,384]{1,0:T(8,128)(2,1)S(1)} %get-tuple-element.55.refs_0_, bf16[384,512]{1,0:T(8,128)(2,1)S(1)} %bitcast.14, bf16[1024,384]{1,0:T(8,128)(2,1)S(1)} %collective-permute-done.refs_2_, ...), custom_call_target="tpu_custom_call" | custom-call | flops 8999999488 | bytes 1 | tf_op jit(solution)/shard_map/pallas_call | solution.py:49
  24.0 1.4 %collective-permute-done.9.refs_5_ = bf16[512,384]{1,0:T(8,128)(2,1)S(1)} collective-permute-done((bf16[512,384]{1,0:T(8,128)(2,1)S(1)}, bf16[512,384]{1,0:T(8,128)(2,1)S(1)}, u32[]{:S(2)}, u32[]{:S(2)}) %collective-permute-start.9) | collective-permute-done | bytes 393248 | tf_op jit(solution)/shard_map/ppermute | solution.py:362
  25.4 0.0 collective-permute-start.10
  25.4 1.4 %collective-permute-start.14 = (bf16[128,1024]{1,0:T(8,128)(2,1)S(1)}, bf16[128,1024]{1,0:T(8,128)(2,1)S(1)}, u32[]{:S(2)}, u32[]{:S(2)}) collective-permute-start(bf16[128,1024]{1,0:T(8,128)(2,1)S(1)} %get-tuple-element.70), channel_id=1, source_target_pairs={{0,2},{1,3},{2,0},{3,1},{4,6},{5,7},{6,4},{7,5},{8,10},{9,11},{10,... | collective-permute-start | bytes 786440 | tf_op jit(solution)/shard_map/ppermute | solution.py:359
  26.8 0.0 collective-permute-done.6.refs_0_.refs_7_
  26.9 0.0 collective-permute-done.8.refs_2_.refs_9_
  26.9 0.4 shard_map.122.back_ref
  27.3 0.0 collective-permute-done.10.refs_8_
  27.3 1.6 %shard_map.123 = (bf16[32,2048]{1,0:T(8,128)(2,1)S(1)}, bf16[32,2048]{1,0:T(8,128)(2,1)S(1)}, bf16[32,2048]{1,0:T(8,128)(2,1)S(1)}, bf16[32,2048]{1,0:T(8,128)(2,1)S(1)}, bf16[64,1152]{1,0:T(8,128)(2,1)S(1)}) custom-call(s32[1]{0:T(128)} %bitcast.4.flag_ref, bf16[128,2048]{1,0:T(8,128)(2,1)S(1)} %get-tuple-element.60.rows_ref, ...), custom_call_target="tpu_custom_call" | custom-call | flops 1 | bytes 1 | tf_op jit(solution)/shard_map/pallas_call | solution.py:49
  28.9 0.3 collective-permute-start.15
  29.2 2.6 %collective-permute-start.11 = (bf16[32,2048]{1,0:T(8,128)(2,1)S(1)}, bf16[32,2048]{1,0:T(8,128)(2,1)S(1)}, u32[]{:S(2)}, u32[]{:S(2)}) collective-permute-start(bf16[32,2048]{1,0:T(8,128)(2,1)S(1)} %get-tuple-element.65), channel_id=1, source_target_pairs={{0,8},{4,12},{8,0},{12,4},{1,9},{5,13},{9,1},{13,5},{2,10},{6,14},... | collective-permute-start | bytes 393224 | tf_op jit(solution)/shard_map/ppermute | solution.py:369
  31.8 1.3 %collective-permute-start.12 = (bf16[32,2048]{1,0:T(8,128)(2,1)S(1)}, bf16[32,2048]{1,0:T(8,128)(2,1)S(1)}, u32[]{:S(2)}, u32[]{:S(2)}) collective-permute-start(bf16[32,2048]{1,0:T(8,128)(2,1)S(1)} %get-tuple-element.66), channel_id=1, source_target_pairs={{0,12},{4,8},{8,4},{12,0},{1,13},{5,9},{9,5},{13,1},{2,14},{6,10},... | collective-permute-start | bytes 393224 | tf_op jit(solution)/shard_map/ppermute | solution.py:369
  33.1 0.2 collective-permute-start.13
  33.4 0.8 %collective-permute-done.14.refs_1_ = bf16[128,1024]{1,0:T(8,128)(2,1)S(1)} collective-permute-done((bf16[128,1024]{1,0:T(8,128)(2,1)S(1)}, bf16[128,1024]{1,0:T(8,128)(2,1)S(1)}, u32[]{:S(2)}, u32[]{:S(2)}) %collective-permute-start.14) | collective-permute-done | bytes 262176 | tf_op jit(solution)/shard_map/ppermute | solution.py:359
  34.1 0.8 %collective-permute-start.18 = (bf16[64,1152]{1,0:T(8,128)(2,1)S(1)}, bf16[64,1152]{1,0:T(8,128)(2,1)S(1)}, u32[]{:S(2)}, u32[]{:S(2)}) collective-permute-start(bf16[64,1152]{1,0:T(8,128)(2,1)S(1)} %get-tuple-element.81.refs_4_), channel_id=1, source_target_pairs={{0,3},{1,2},{2,1},{3,0},{4,7},{5,6},{6,5},{7,4},{8,11},{9,10},{10,... | collective-permute-start | bytes 442376 | tf_op jit(solution)/shard_map/ppermute | solution.py:359
  34.9 0.0 collective-permute-done.15.refs_6_
  34.9 0.7 %collective-permute-start.17 = (bf16[64,1152]{1,0:T(8,128)(2,1)S(1)}, bf16[64,1152]{1,0:T(8,128)(2,1)S(1)}, u32[]{:S(2)}, u32[]{:S(2)}) collective-permute-start(bf16[64,1152]{1,0:T(8,128)(2,1)S(1)} %get-tuple-element.81.refs_4_), channel_id=1, source_target_pairs={{0,2},{1,3},{2,0},{3,1},{4,6},{5,7},{6,4},{7,5},{8,10},{9,11},{10,... | collective-permute-start | bytes 442376 | tf_op jit(solution)/shard_map/ppermute | solution.py:359
  35.6 0.0 copy-start.1
  35.7 6.4 %collective-permute-done.11.refs_1_ = bf16[32,2048]{1,0:T(8,128)(2,1)S(1)} collective-permute-done((bf16[32,2048]{1,0:T(8,128)(2,1)S(1)}, bf16[32,2048]{1,0:T(8,128)(2,1)S(1)}, u32[]{:S(2)}, u32[]{:S(2)}) %collective-permute-start.11) | collective-permute-done | bytes 131104 | tf_op jit(solution)/shard_map/ppermute | solution.py:369
  42.1 0.0 collective-permute-start.16
  42.1 0.0 collective-permute-done.12.refs_2_
  42.1 0.7 %collective-permute-done.13.refs_3_ = bf16[32,2048]{1,0:T(8,128)(2,1)S(1)} collective-permute-done((bf16[32,2048]{1,0:T(8,128)(2,1)S(1)}, bf16[32,2048]{1,0:T(8,128)(2,1)S(1)}, u32[]{:S(2)}, u32[]{:S(2)}) %collective-permute-start.13) | collective-permute-done | bytes 131104 | tf_op jit(solution)/shard_map/ppermute | solution.py:369
  42.8 0.0 copy-done.1
  42.8 2.0 %shard_map.124 = (bf16[128,2048]{1,0:T(8,128)(2,1)}, bf16[128,2048]{1,0:T(8,128)(2,1)}, f32[8,128]{1,0:T(8,128)}) custom-call(s32[2]{0:T(128)S(1)} %pad_add_fusion.place_ref, s32[8,128]{1,0:T(8,128)S(1)} %bitcast.18, bf16[64,128]{1,0:T(8,128)(2,1)S(1)} %get-tuple-element.47.select_ref, bf16[128,128]{1,0:T(8,128)(2,1)S(1)} %get-tuple-element.48.table_ref, ...), custom_call_target="tpu_custom_call" | custom-call | flops 8589934592 | bytes 1 | tf_op jit(solution)/shard_map/pallas_call | solution.py:49
  44.7 0.0 collective-permute-done.16
  44.8 0.0 collective-permute-done.18.refs_7_
  44.8 0.0 collective-permute-done.17.refs_5_
  44.8 1.4 %shard_map.125 = (bf16[512,384]{1,0:T(8,128)(2,1)}, bf16[512,384]{1,0:T(8,128)(2,1)}, bf16[384,512]{1,0:T(8,128)(2,1)}) custom-call(bf16[128,1024]{1,0:T(8,128)(2,1)S(1)} %get-tuple-element.77.refs_0_, bf16[128,1024]{1,0:T(8,128)(2,1)S(1)} %collective-permute-done.14.refs_1_, bf16[128,512]{1,0:T(8,128)(2,1)S(1)} %get-tuple-element.79.refs_2_, ...), custom_call_target="tpu_custom_call" | custom-call | flops 1 | bytes 1 | tf_op jit(solution)/shard_map/pallas_call | solution.py:49
  (4 shorter events, 0.1 us)
Async XLA Ops:
  0.6 4.9 %copy-start = (bf16[128,2048]{1,0:T(8,128)(2,1)S(1)}, bf16[128,2048]{1,0:T(8,128)(2,1)}, u32[]{:S(2)}) copy-start(bf16[128,2048]{1,0:T(8,128)(2,1)} %x_ref.1) | copy-start | bytes 1572868
  2.0 6.1 %collective-permute-start = (bf16[1024,384]{1,0:T(8,128)(2,1)S(1)}, bf16[1024,384]{1,0:T(8,128)(2,1)S(1)}, u32[]{:S(2)}, u32[]{:S(2)}) collective-permute-start(bf16[1024,384]{1,0:T(8,128)(2,1)S(1)} %get-tuple-element.55.refs_0_), channel_id=1, source_target_pairs={{0,1},{1,0},{2,3},{3,2},{4,5},{5,4},{6,7},{7,6},{8,9},{9,8},{10,11... | collective-permute-start | bytes 2359304 | tf_op jit(solution)/shard_map/ppermute | solution.py:359
  2.5 5.5 %collective-permute-start.1 = (bf16[384,512]{1,0:T(8,128)(2,1)}, bf16[384,512]{1,0:T(8,128)(2,1)S(1)}, u32[]{:S(2)}, u32[]{:S(2)}) collective-permute-start(bf16[384,512]{1,0:T(8,128)(2,1)} %bitcast.12), channel_id=1, source_target_pairs={{0,1},{1,0},{2,3},{3,2},{4,5},{5,4},{6,7},{7,6},{8,9},{9,8},{10,11... | collective-permute-start | bytes 1179656 | tf_op jit(solution)/shard_map/ppermute | solution.py:359
  2.6 12.8 %collective-permute-start.5 = (bf16[512,384]{1,0:T(8,128)(2,1)S(1)}, bf16[512,384]{1,0:T(8,128)(2,1)S(1)}, u32[]{:S(2)}, u32[]{:S(2)}) collective-permute-start(bf16[512,384]{1,0:T(8,128)(2,1)S(1)} %get-tuple-element.53), channel_id=1, source_target_pairs={{0,2},{1,3},{2,0},{3,1},{4,6},{5,7},{6,4},{7,5},{8,10},{9,11},{10,... | collective-permute-start | bytes 1179656 | tf_op jit(solution)/shard_map/ppermute | solution.py:359
  5.5 0.7 %copy-start.4 = (s32[128,8]{0,1:T(8,128)S(1)}, s32[128,8]{0,1:T(8,128)}, u32[]{:S(2)}) copy-start(s32[128,8]{0,1:T(8,128)} %param.9) | copy-start | bytes 12292
  5.5 0.7 %copy-start.3 = (f32[128,8]{0,1:T(8,128)S(1)}, f32[128,8]{0,1:T(8,128)}, u32[]{:S(2)}) copy-start(f32[128,8]{0,1:T(8,128)} %param.10) | copy-start | bytes 12292
  6.2 6.1 %copy-start.2 = (bf16[1,384,512]{2,1,0:T(8,128)(2,1)S(1)}, bf16[1,384,512]{2,1,0:T(8,128)(2,1)}, u32[]{:S(2)}) copy-start(bf16[1,384,512]{2,1,0:T(8,128)(2,1)} %param.13) | copy-start | bytes 1179652
  8.1 13.0 %collective-permute-start.2 = (bf16[32,2048]{1,0:T(8,128)(2,1)S(1)}, bf16[32,2048]{1,0:T(8,128)(2,1)S(1)}, u32[]{:S(2)}, u32[]{:S(2)}) collective-permute-start(bf16[32,2048]{1,0:T(8,128)(2,1)S(1)} %get-tuple-element.57), channel_id=1, source_target_pairs={{0,8},{4,12},{8,0},{12,4},{1,9},{5,13},{9,1},{13,5},{2,10},{6,14},... | collective-permute-start | bytes 393224 | tf_op jit(solution)/shard_map/ppermute | solution.py:369
  10.7 10.3 %collective-permute-start.3 = (bf16[32,2048]{1,0:T(8,128)(2,1)S(1)}, bf16[32,2048]{1,0:T(8,128)(2,1)S(1)}, u32[]{:S(2)}, u32[]{:S(2)}) collective-permute-start(bf16[32,2048]{1,0:T(8,128)(2,1)S(1)} %get-tuple-element.58), channel_id=1, source_target_pairs={{0,12},{4,8},{8,4},{12,0},{1,13},{5,9},{9,5},{13,1},{2,14},{6,10},... | collective-permute-start | bytes 393224 | tf_op jit(solution)/shard_map/ppermute | solution.py:369
  12.1 9.2 %collective-permute-start.4 = (bf16[32,2048]{1,0:T(8,128)(2,1)S(1)}, bf16[32,2048]{1,0:T(8,128)(2,1)S(1)}, u32[]{:S(2)}, u32[]{:S(2)}) collective-permute-start(bf16[32,2048]{1,0:T(8,128)(2,1)S(1)} %get-tuple-element.59), channel_id=1, source_target_pairs={{0,4},{4,0},{8,12},{12,8},{1,5},{5,1},{9,13},{13,9},{2,6},{6,2},{1... | collective-permute-start | bytes 393224 | tf_op jit(solution)/shard_map/ppermute | solution.py:369
  12.3 11.0 %collective-permute-start.7 = (bf16[384,512]{1,0:T(8,128)(2,1)S(1)}, bf16[384,512]{1,0:T(8,128)(2,1)S(1)}, u32[]{:S(2)}, u32[]{:S(2)}) collective-permute-start(bf16[384,512]{1,0:T(8,128)(2,1)S(1)} %bitcast.13), channel_id=1, source_target_pairs={{0,2},{1,3},{2,0},{3,1},{4,6},{5,7},{6,4},{7,5},{8,10},{9,11},{10,... | collective-permute-start | bytes 1179656 | tf_op jit(solution)/shard_map/ppermute | solution.py:359
  15.4 10.0 %collective-permute-start.9 = (bf16[512,384]{1,0:T(8,128)(2,1)S(1)}, bf16[512,384]{1,0:T(8,128)(2,1)S(1)}, u32[]{:S(2)}, u32[]{:S(2)}) collective-permute-start(bf16[512,384]{1,0:T(8,128)(2,1)S(1)} %collective-permute-done.5.refs_4_), channel_id=1, source_target_pairs={{0,16},{16,0},{1,17},{17,1},{2,18},{18,2},{3,19},{19,3},{4,20},{20... | collective-permute-start | bytes 1179656 | tf_op jit(solution)/shard_map/ppermute | solution.py:362
  21.0 5.8 %collective-permute-start.6 = (bf16[512,384]{1,0:T(8,128)(2,1)S(1)}, bf16[512,384]{1,0:T(8,128)(2,1)S(1)}, u32[]{:S(2)}, u32[]{:S(2)}) collective-permute-start(bf16[512,384]{1,0:T(8,128)(2,1)S(1)} %collective-permute-done.5.refs_4_), channel_id=1, source_target_pairs={{0,1},{1,0},{2,3},{3,2},{4,5},{5,4},{6,7},{7,6},{8,9},{9,8},{10,11... | collective-permute-start | bytes 1179656 | tf_op jit(solution)/shard_map/ppermute | solution.py:359
  23.3 3.6 %collective-permute-start.8 = (bf16[384,512]{1,0:T(8,128)(2,1)S(1)}, bf16[384,512]{1,0:T(8,128)(2,1)S(1)}, u32[]{:S(2)}, u32[]{:S(2)}) collective-permute-start(bf16[384,512]{1,0:T(8,128)(2,1)S(1)} %collective-permute-done.7.refs_1_.refs_6_), channel_id=1, source_target_pairs={{0,1},{1,0},{2,3},{3,2},{4,5},{5,4},{6,7},{7,6},{8,9},{9,8},{10,11... | collective-permute-start | bytes 1179656 | tf_op jit(solution)/shard_map/ppermute | solution.py:359
  25.4 1.9 %collective-permute-start.10 = (bf16[512,384]{1,0:T(8,128)(2,1)S(1)}, bf16[512,384]{1,0:T(8,128)(2,1)S(1)}, u32[]{:S(2)}, u32[]{:S(2)}) collective-permute-start(bf16[512,384]{1,0:T(8,128)(2,1)S(1)} %collective-permute-done.9.refs_5_), channel_id=1, source_target_pairs={{0,1},{1,0},{2,3},{3,2},{4,5},{5,4},{6,7},{7,6},{8,9},{9,8},{10,11... | collective-permute-start | bytes 1179656 | tf_op jit(solution)/shard_map/ppermute | solution.py:359
  25.4 8.7 %collective-permute-start.14 = (bf16[128,1024]{1,0:T(8,128)(2,1)S(1)}, bf16[128,1024]{1,0:T(8,128)(2,1)S(1)}, u32[]{:S(2)}, u32[]{:S(2)}) collective-permute-start(bf16[128,1024]{1,0:T(8,128)(2,1)S(1)} %get-tuple-element.70), channel_id=1, source_target_pairs={{0,2},{1,3},{2,0},{3,1},{4,6},{5,7},{6,4},{7,5},{8,10},{9,11},{10,... | collective-permute-start | bytes 786440 | tf_op jit(solution)/shard_map/ppermute | solution.py:359
  28.9 6.0 %collective-permute-start.15 = (bf16[64,1152]{1,0:T(8,128)(2,1)S(1)}, bf16[64,1152]{1,0:T(8,128)(2,1)S(1)}, u32[]{:S(2)}, u32[]{:S(2)}) collective-permute-start(bf16[64,1152]{1,0:T(8,128)(2,1)S(1)} %get-tuple-element.81.refs_4_), channel_id=1, source_target_pairs={{0,1},{1,0},{2,3},{3,2},{4,5},{5,4},{6,7},{7,6},{8,9},{9,8},{10,11... | collective-permute-start | bytes 442376 | tf_op jit(solution)/shard_map/ppermute | solution.py:359
  29.2 12.9 %collective-permute-start.11 = (bf16[32,2048]{1,0:T(8,128)(2,1)S(1)}, bf16[32,2048]{1,0:T(8,128)(2,1)S(1)}, u32[]{:S(2)}, u32[]{:S(2)}) collective-permute-start(bf16[32,2048]{1,0:T(8,128)(2,1)S(1)} %get-tuple-element.65), channel_id=1, source_target_pairs={{0,8},{4,12},{8,0},{12,4},{1,9},{5,13},{9,1},{13,5},{2,10},{6,14},... | collective-permute-start | bytes 393224 | tf_op jit(solution)/shard_map/ppermute | solution.py:369
  31.8 10.3 %collective-permute-start.12 = (bf16[32,2048]{1,0:T(8,128)(2,1)S(1)}, bf16[32,2048]{1,0:T(8,128)(2,1)S(1)}, u32[]{:S(2)}, u32[]{:S(2)}) collective-permute-start(bf16[32,2048]{1,0:T(8,128)(2,1)S(1)} %get-tuple-element.66), channel_id=1, source_target_pairs={{0,12},{4,8},{8,4},{12,0},{1,13},{5,9},{9,5},{13,1},{2,14},{6,10},... | collective-permute-start | bytes 393224 | tf_op jit(solution)/shard_map/ppermute | solution.py:369
  33.1 9.6 %collective-permute-start.13 = (bf16[32,2048]{1,0:T(8,128)(2,1)S(1)}, bf16[32,2048]{1,0:T(8,128)(2,1)S(1)}, u32[]{:S(2)}, u32[]{:S(2)}) collective-permute-start(bf16[32,2048]{1,0:T(8,128)(2,1)S(1)} %get-tuple-element.67), channel_id=1, source_target_pairs={{0,4},{4,0},{8,12},{12,8},{1,5},{5,1},{9,13},{13,9},{2,6},{6,2},{1... | collective-permute-start | bytes 393224 | tf_op jit(solution)/shard_map/ppermute | solution.py:369
  34.1 10.6 %collective-permute-start.18 = (bf16[64,1152]{1,0:T(8,128)(2,1)S(1)}, bf16[64,1152]{1,0:T(8,128)(2,1)S(1)}, u32[]{:S(2)}, u32[]{:S(2)}) collective-permute-start(bf16[64,1152]{1,0:T(8,128)(2,1)S(1)} %get-tuple-element.81.refs_4_), channel_id=1, source_target_pairs={{0,3},{1,2},{2,1},{3,0},{4,7},{5,6},{6,5},{7,4},{8,11},{9,10},{10,... | collective-permute-start | bytes 442376 | tf_op jit(solution)/shard_map/ppermute | solution.py:359
  34.9 9.9 %collective-permute-start.17 = (bf16[64,1152]{1,0:T(8,128)(2,1)S(1)}, bf16[64,1152]{1,0:T(8,128)(2,1)S(1)}, u32[]{:S(2)}, u32[]{:S(2)}) collective-permute-start(bf16[64,1152]{1,0:T(8,128)(2,1)S(1)} %get-tuple-element.81.refs_4_), channel_id=1, source_target_pairs={{0,2},{1,3},{2,0},{3,1},{4,6},{5,7},{6,4},{7,5},{8,10},{9,11},{10,... | collective-permute-start | bytes 442376 | tf_op jit(solution)/shard_map/ppermute | solution.py:359
  35.6 7.2 %copy-start.1 = (bf16[128,2048]{1,0:T(8,128)(2,1)S(1)}, bf16[128,2048]{1,0:T(8,128)(2,1)}, u32[]{:S(2)}) copy-start(bf16[128,2048]{1,0:T(8,128)(2,1)} %dy_ref.1) | copy-start | bytes 1572868
  42.1 2.7 %collective-permute-start.16 = (bf16[256,512]{1,0:T(8,128)(2,1)S(1)}, bf16[256,512]{1,0:T(8,128)(2,1)S(1)}, u32[]{:S(2)}, u32[]{:S(2)}) collective-permute-start(bf16[256,512]{1,0:T(8,128)(2,1)S(1)} %pad_maximum_fusion), channel_id=1, source_target_pairs={{0,1},{1,0},{2,3},{3,2},{4,5},{5,4},{6,7},{7,6},{8,9},{9,8},{10,11... | collective-permute-start | bytes 786440 | tf_op jit(solution)/shard_map/ppermute | solution.py:359
